TPU v7x, 128 devices: a whole 4x4x4 slice. The times are simulated.
128 devices in a mesh: dp: 2 (over y_lo), outer: 4 (over z), inner: 16 (over x, y_hi, core).
Axes of the slice: x: 4, y: 4 (y_hi: 2, y_lo: 2; y = y_hi * 2 + y_lo), z: 4, core: 2. Of those that a mesh axis runs over, the one named last changes fastest.
Arguments:
- inputs: bfloat16 [2, 10240, 4096], P('dp', ('outer', 'inner')), may hold values from -6 to 6
- block_order: int32 [2, 128], P('dp'), may hold values from 0 to 127, each once within a row
- w_query: bfloat16 [4096, 512], replicated, may hold values from -0.09375 to 0.09375
- w_key: bfloat16 [4096, 128], replicated, may hold values from -1.875 to 1.875
- w_value: bfloat16 [4096, 128], replicated, may hold values from -0.09375 to 0.09375
- grad_out: bfloat16 [2, 10240, 512], P('dp', ('outer', 'inner')), may hold values from -6 to 6
Outputs:
- grad_w_query: float32 [4096, 512], P(('dp', 'outer', 'inner'))
- grad_w_key: float32 [4096, 128], P(('dp', 'outer', 'inner'))
- grad_w_value: float32 [4096, 128], P(('dp', 'outer', 'inner'))
Inputs may be any that keep to these rules, and one draw needn't show every extreme that they name: Each row of block_order is a permutation of the sequence's 128 blocks; block slot b holds rows b * 80 to (b + 1) * 80 - 1 of the stored sequence.
All inputs are finite; a program needn't handle non-finite values.
Results may differ from a plain program's by a relative error of at most 0.012.
The roundings to bfloat16 on the way count: a program that leaves them out, or rounds other values in their place, can miss the bound.
Values may be sent and summed in bfloat16 or wider, within the bound.
No kernel may reach another device: no remote copies, remote signals or barrier semaphores. Data moves between devices by JAX's collectives and lax.ppermute only.
A program may use at most 192 MiB of HBM per device.

v0:
```python
import math

import jax
import jax.numpy as jnp
from jax import lax
from jax.sharding import PartitionSpec as P

masked_fill = -1e30


def from_behind(block, axis, distance):
    devices = range(lax.axis_size(axis))
    route = [((i - distance) % len(devices), i) for i in devices]
    return lax.ppermute(block, axis, route)


def attend_stats(carry, query, dout, key_rows, value_rows, key_pos, row_pos, scale):
    row_max, total, weighted = carry
    score = jnp.einsum("qhd,kd->hqk", query, key_rows, preferred_element_type=jnp.float32) * scale
    allowed = key_pos[None, None, :] <= row_pos[None, :, None]
    score = jnp.where(allowed, score, masked_fill)
    new_max = jnp.maximum(row_max, jnp.max(score, axis=2))
    factor = jnp.exp(row_max - new_max)
    weights = jnp.where(allowed, jnp.exp(score - new_max[:, :, None]), 0.0)
    dprob = jnp.einsum("qhd,kd->hqk", dout, value_rows, preferred_element_type=jnp.float32)
    total = total * factor + jnp.sum(weights, axis=2)
    weighted = weighted * factor + jnp.sum(weights * dprob, axis=2)
    return (new_max, total, weighted)


def group_grads(query, dout, key_rows, value_rows, key_pos, row_pos, lse, delta, scale):
    score = jnp.einsum("qhd,kd->hqk", query, key_rows, preferred_element_type=jnp.float32) * scale
    allowed = key_pos[None, None, :] <= row_pos[None, :, None]
    score = jnp.where(allowed, score, masked_fill)
    prob = jnp.where(allowed, jnp.exp(score - lse[:, :, None]), 0.0)
    dprob = jnp.einsum("qhd,kd->hqk", dout, value_rows, preferred_element_type=jnp.float32)
    dscore = (prob * (dprob - delta[:, :, None])).astype(jnp.bfloat16)
    prob_low = prob.astype(jnp.bfloat16)
    grad_query = (
        jnp.einsum("hqk,kd->qhd", dscore, key_rows, preferred_element_type=jnp.float32) * scale
    )
    grad_key = jnp.einsum("hqk,qhd->kd", dscore, query, preferred_element_type=jnp.float32) * scale
    grad_value = jnp.einsum("hqk,qhd->kd", prob_low, dout, preferred_element_type=jnp.float32)
    return (grad_query, grad_key, grad_value)


def per_device(inputs, block_order, w_query, w_key, w_value, grad_out):
    tokens = inputs[0]
    order = block_order[0]
    rows_dev = tokens.shape[0]
    half = rows_dev // 2
    head_dim = w_key.shape[1]
    heads = w_query.shape[1] // head_dim
    scale = 1.0 / math.sqrt(head_dim)
    n_outer = lax.axis_size("outer")
    n_inner = lax.axis_size("inner")
    outer_place = lax.axis_index("outer")
    inner_place = lax.axis_index("inner")
    group_rows = n_inner * rows_dev
    positions = (order[:, None] * half + jnp.arange(half, dtype=jnp.int32)[None, :]).reshape(-1)
    row_pos = lax.dynamic_slice_in_dim(
        positions, (outer_place * n_inner + inner_place) * rows_dev, rows_dev
    )
    query = (
        jnp.dot(tokens, w_query, preferred_element_type=jnp.float32)
        .astype(jnp.bfloat16)
        .reshape(rows_dev, heads, head_dim)
    )
    key_own = jnp.dot(tokens, w_key, preferred_element_type=jnp.float32).astype(jnp.bfloat16)
    value_own = jnp.dot(tokens, w_value, preferred_element_type=jnp.float32).astype(jnp.bfloat16)
    dout = grad_out[0].reshape(rows_dev, heads, head_dim)

    def group_start(turn):
        return (outer_place - turn) % n_outer * group_rows

    empty_stats = jnp.zeros((heads, rows_dev), jnp.float32)
    carry = (jnp.full((heads, rows_dev), masked_fill, jnp.float32), empty_stats, empty_stats)
    moving = (key_own, value_own)
    for turn in range(n_outer):
        start_row = group_start(turn)

        def fold_keys(state, pieces, start, start_row=start_row):
            key_pos = lax.dynamic_slice_in_dim(positions, start_row, pieces[0].shape[0])
            return attend_stats(state, query, dout, pieces[0], pieces[1], key_pos, row_pos, scale)

        carry = fold_keys(
            carry,
            (
                lax.all_gather(moving[0], "inner", axis=0, tiled=True),
                lax.all_gather(moving[1], "inner", axis=0, tiled=True),
            ),
            jnp.int32(0),
        )
        if turn + 1 < n_outer:
            moving = from_behind((moving[0], moving[1]), "outer", 1)
    row_max, total, weighted = carry
    lse = row_max + jnp.log(total)
    delta = weighted / total
    grad_query = jnp.zeros((rows_dev, heads, head_dim), jnp.float32)
    moving = (key_own, value_own)
    empty_rows = jnp.zeros((rows_dev, head_dim), jnp.float32)
    travel = (empty_rows, empty_rows)
    for turn in range(n_outer):
        start_row = group_start(turn)
        whole = (
            lax.all_gather(moving[0], "inner", axis=0, tiled=True),
            lax.all_gather(moving[1], "inner", axis=0, tiled=True),
        )
        if turn + 1 < n_outer:
            moving = from_behind((moving[0], moving[1]), "outer", 1)
        group_pos = lax.dynamic_slice_in_dim(positions, start_row, group_rows)
        part_query, part_key, part_value = group_grads(
            query, dout, whole[0], whole[1], group_pos, row_pos, lse, delta, scale
        )
        grad_query = grad_query + part_query
        summed = (
            lax.psum_scatter(part_key, "inner", scatter_dimension=0, tiled=True),
            lax.psum_scatter(part_value, "inner", scatter_dimension=0, tiled=True),
        )
        travel = (travel[0] + summed[0], travel[1] + summed[1])
        travel = from_behind((travel[0], travel[1]), "outer", 1)
    grad_key, grad_value = travel
    query_width = heads * head_dim
    grads = jnp.concatenate(
        [
            grad_query.reshape(rows_dev, query_width).astype(jnp.bfloat16),
            grad_key.astype(jnp.bfloat16),
            grad_value.astype(jnp.bfloat16),
        ],
        axis=1,
    )
    gathered = lax.psum_scatter(
        lax.dot_general(
            tokens, grads, (((0,), (0,)), ((), ())), preferred_element_type=jnp.float32
        ),
        ("dp", "outer", "inner"),
        scatter_dimension=0,
        tiled=True,
    )
    return (
        gathered[:, :query_width],
        gathered[:, query_width : query_width + head_dim],
        gathered[:, query_width + head_dim :],
    )


def solution(mesh):
    in_specs = (
        P("dp", ("outer", "inner"), None),
        P("dp", None),
        P(),
        P(),
        P(),
        P("dp", ("outer", "inner"), None),
    )
    out_specs = (
        P(("dp", "outer", "inner"), None),
        P(("dp", "outer", "inner"), None),
        P(("dp", "outer", "inner"), None),
    )
    return jax.shard_map(
        per_device, mesh=mesh, in_specs=in_specs, out_specs=out_specs, check_vma=False
    )
```

profile of v0, /device:TPU:0, one launch (start us, length us, event | category | flops | bytes accessed | tf_op | source)
XLA Modules:
  0.0 1493.8 jit_solution(7305101961773089652)
XLA Ops:
  8.5 1.7 fusion.56
  10.2 2.1 collective-permute-start
  12.3 1.7 fusion.59
  14.0 2.0 collective-permute-start.3
  16.0 27.5 %all_gather.32 = bf16[2560,128]{1,0:T(8,128)(2,1)} all-gather(bf16[160,128]{1,0:T(8,128)(2,1)S(1)} %fusion.56), channel_id=1, replica_groups=mesh['dp'=2,'outer'=4,'inner'=16] {'inner'}, dimensions={0}, use_global_device_ids=true | all-gather | bytes 696320 | tf_op jit(solution)/shard_map/all_gather | solution.py:106
  43.5 3.0 fusion.53
  48.0 5.2 fusion.121
  53.2 22.4 %all_gather.36 = bf16[2560,128]{1,0:T(8,128)(2,1)} all-gather(bf16[160,128]{1,0:T(8,128)(2,1)S(1)} %fusion.59), channel_id=1, replica_groups=mesh['dp'=2,'outer'=4,'inner'=16] {'inner'}, dimensions={0}, use_global_device_ids=true | all-gather | bytes 696320 | tf_op jit(solution)/shard_map/all_gather | solution.py:107
  75.7 24.5 %all_gather.33 = bf16[2560,128]{1,0:T(8,128)(2,1)S(1)} all-gather(bf16[160,128]{1,0:T(8,128)(2,1)} %collective-permute-done), channel_id=1, replica_groups=mesh['dp'=2,'outer'=4,'inner'=16] {'inner'}, dimensions={0}, use_global_device_ids=true | all-gather | bytes 696320 | tf_op jit(solution)/shard_map/all_gather | solution.py:89
  101.7 1.7 collective-permute-start.1
  103.5 21.2 %all_gather.37 = bf16[2560,128]{1,0:T(8,128)(2,1)S(1)} all-gather(bf16[160,128]{1,0:T(8,128)(2,1)} %collective-permute-done.3), channel_id=1, replica_groups=mesh['dp'=2,'outer'=4,'inner'=16] {'inner'}, dimensions={0}, use_global_device_ids=true | all-gather | bytes 696320 | tf_op jit(solution)/shard_map/all_gather | solution.py:90
  124.7 24.2 %all_gather.34 = bf16[2560,128]{1,0:T(8,128)(2,1)S(1)} all-gather(bf16[160,128]{1,0:T(8,128)(2,1)S(1)} %collective-permute-done.1), channel_id=1, replica_groups=mesh['dp'=2,'outer'=4,'inner'=16] {'inner'}, dimensions={0}, use_global_device_ids=true | all-gather | bytes 696320 | tf_op jit(solution)/shard_map/all_gather | solution.py:89
  151.2 1.9 collective-permute-start.5
  153.2 21.0 %all_gather.38 = bf16[2560,128]{1,0:T(8,128)(2,1)S(1)} all-gather(bf16[160,128]{1,0:T(8,128)(2,1)S(1)} %collective-permute-done.4), channel_id=1, replica_groups=mesh['dp'=2,'outer'=4,'inner'=16] {'inner'}, dimensions={0}, use_global_device_ids=true | all-gather | bytes 696320 | tf_op jit(solution)/shard_map/all_gather | solution.py:90
  174.1 24.7 %all_gather.35 = bf16[2560,128]{1,0:T(8,128)(2,1)S(1)} all-gather(bf16[160,128]{1,0:T(8,128)(2,1)S(1)} %collective-permute-done.2), channel_id=1, replica_groups=mesh['dp'=2,'outer'=4,'inner'=16] {'inner'}, dimensions={0}, use_global_device_ids=true | all-gather | bytes 696320 | tf_op jit(solution)/shard_map/all_gather | solution.py:89
  200.4 21.1 %all_gather.39 = bf16[2560,128]{1,0:T(8,128)(2,1)S(1)} all-gather(bf16[160,128]{1,0:T(8,128)(2,1)S(1)} %collective-permute-done.5), channel_id=1, replica_groups=mesh['dp'=2,'outer'=4,'inner'=16] {'inner'}, dimensions={0}, use_global_device_ids=true | all-gather | bytes 696320 | tf_op jit(solution)/shard_map/all_gather | solution.py:90
  221.4 4.1 fusion
  225.5 4.1 fusion.3
  229.6 4.1 fusion.6
  233.7 4.1 fusion.9
  237.8 2.7 convolution_bitcast_fusion.4
  240.6 22.9 %fusion.2 = (bf16[4,160,2560]{2,1,0:T(8,128)(2,1)}, bf16[4,160,2560]{2,1,0:T(8,128)(2,1)}, bf16[4,160,2560]{2,1,0:T(8,128)(2,1)}, bf16[4,160,2560]{2,1,0:T(8,128)(2,1)S(1)}) fusion(f32[2560,160,4]{0,1,2:T(8,128)} %get-tuple-element.48, f32[4,160,2560]{2,1,0:T(8,128)} %copy-done.1, f32[4,160]{1,0:T(4,128)S(1)} %get-tuple-element.20, ...), kind=kLoop, calls=%fused_computation.5 | loop fusion | flops 32768000 | bytes 67179520 | tf_op jit(solution)/shard_map/convert_element_type | solution.py:37
  263.5 1.7 copy-done.4
  265.2 2.2 fusion.23
  267.6 5.5 convolution_bitcast_fusion.3
  273.3 4.0 fusion.22
  277.4 5.6 convolution_bitcast_fusion.2
  283.0 4.1 fusion.21
  287.2 5.5 convolution_bitcast_fusion.1
  292.8 4.2 fusion.20
  297.1 9.2 reduce-scatter.20.cloned.1.call-done
  307.8 69.2 %reduce-scatter.12.cloned.1.call-done = f32[160,128]{1,0:T(8,128)} async-done(((f32[2560,128]{1,0:T(8,128)}), f32[160,128]{1,0:T(8,128)}) %reduce-scatter.12.cloned.1.call-update) | async-done | bytes 81936 | tf_op jit(solution)/shard_map/reduce_scatter | solution.py:117
  378.5 3.7 fusion.76
  382.2 65.5 %reduce-scatter.22.cloned.1.call-done = f32[160,128]{1,0:T(8,128)} async-done(((f32[2560,128]{1,0:T(8,128)}), f32[160,128]{1,0:T(8,128)}) %reduce-scatter.22.cloned.1.call-update) | async-done | bytes 81936 | tf_op jit(solution)/shard_map/reduce_scatter | solution.py:118
  450.2 68.0 %reduce-scatter.14.cloned.1.call-done = f32[160,128]{1,0:T(8,128)} async-done(((f32[2560,128]{1,0:T(8,128)}), f32[160,128]{1,0:T(8,128)}) %reduce-scatter.14.cloned.1.call-update) | async-done | bytes 81936 | tf_op jit(solution)/shard_map/reduce_scatter | solution.py:117
  520.8 3.7 convolution_add_fusion.2
  524.5 64.3 %reduce-scatter.24.cloned.1.call-done = f32[160,128]{1,0:T(8,128)} async-done(((f32[2560,128]{1,0:T(8,128)}), f32[160,128]{1,0:T(8,128)}) %reduce-scatter.24.cloned.1.call-update) | async-done | bytes 81936 | tf_op jit(solution)/shard_map/reduce_scatter | solution.py:118
  589.7 1.8 collective-permute-start.12
  591.5 67.9 %reduce-scatter.16.cloned.1.call-done = f32[160,128]{1,0:T(8,128)} async-done(((f32[2560,128]{1,0:T(8,128)}), f32[160,128]{1,0:T(8,128)}) %reduce-scatter.16.cloned.1.call-update) | async-done | bytes 81936 | tf_op jit(solution)/shard_map/reduce_scatter | solution.py:117
  661.9 3.0 convolution_add_fusion.1
  664.9 65.2 %reduce-scatter.26.cloned.1.call-done = f32[160,128]{1,0:T(8,128)} async-done(((f32[2560,128]{1,0:T(8,128)}), f32[160,128]{1,0:T(8,128)}) %reduce-scatter.26.cloned.1.call-update) | async-done | bytes 81936 | tf_op jit(solution)/shard_map/reduce_scatter | solution.py:118
  731.0 1.6 collective-permute-start.13
  732.6 68.2 %reduce-scatter.18.cloned.1.call-done = f32[160,128]{1,0:T(8,128)} async-done(((f32[2560,128]{1,0:T(8,128)}), f32[160,128]{1,0:T(8,128)}) %reduce-scatter.18.cloned.1.call-update) | async-done | bytes 81936 | tf_op jit(solution)/shard_map/reduce_scatter | solution.py:117
  801.7 1.6 collective-permute-start.9
  803.4 2.9 fusion.52
  807.0 6.3 convolution_bitcast_fusion
  813.3 12.6 copy.52
  826.0 658.2 %reduce-scatter.28.cloned.1.call-done = f32[32,768]{1,0:T(8,128)} async-done(((f32[4096,768]{1,0:T(8,128)}), f32[32,768]{1,0:T(8,128)}) %reduce-scatter.28.cloned.1.call-update) | async-done | bytes 98320
  (95 shorter events, 25.8 us)
Async XLA Ops:
  7.2 1.3 copy-start
  7.2 39.4 %copy-start.14 = (s32[1,128]{1,0:T(1,128)S(1)}, s32[1,128]{1,0:T(1,128)}, u32[]{:S(2)}) copy-start(s32[1,128]{1,0:T(1,128)} %param.7) | copy-start | bytes 1540
  7.2 299.1 %reduce-scatter.20.cloned.1.call-start = ((), (), s32[]{:S(2)}) async-start(), calls=%async_computation.13 | async-start | bytes 1392640 | tf_op jit(solution)/shard_map/reduce_scatter | solution.py:118
  10.2 65.5 %collective-permute-start = (bf16[160,128]{1,0:T(8,128)(2,1)S(1)}, bf16[160,128]{1,0:T(8,128)(2,1)}, u32[]{:S(2)}, u32[]{:S(2)}) collective-permute-start(bf16[160,128]{1,0:T(8,128)(2,1)S(1)} %fusion.56), channel_id=1, source_target_pairs={{48,0},{0,16},{16,32},{32,48},{49,1},{1,17},{17,33},{33,49},{50,2}... | collective-permute-start | bytes 122888 | tf_op jit(solution)/shard_map/ppermute | solution.py:14
  14.0 89.4 %collective-permute-start.3 = (bf16[160,128]{1,0:T(8,128)(2,1)S(1)}, bf16[160,128]{1,0:T(8,128)(2,1)}, u32[]{:S(2)}, u32[]{:S(2)}) collective-permute-start(bf16[160,128]{1,0:T(8,128)(2,1)S(1)} %fusion.59), channel_id=1, source_target_pairs={{48,0},{0,16},{16,32},{32,48},{49,1},{1,17},{17,33},{33,49},{50,2}... | collective-permute-start | bytes 122888 | tf_op jit(solution)/shard_map/ppermute | solution.py:14
  47.9 27.7 %copy-start.13 = (bf16[1,160,512]{2,1,0:T(8,128)(2,1)S(1)}, bf16[1,160,512]{2,1,0:T(8,128)(2,1)}, u32[]{:S(2)}) copy-start(bf16[1,160,512]{2,1,0:T(8,128)(2,1)} %param.11) | copy-start | bytes 491524
  100.2 3.2 copy-start.8
  101.7 127.9 %copy-start.3 = (f32[4,160,2560]{2,1,0:T(8,128)}, f32[4,160,2560]{2,1,0:T(8,128)S(1)}, u32[]{:S(2)}) copy-start(f32[4,160,2560]{2,1,0:T(8,128)S(1)} %get-tuple-element.45) | copy-start | bytes 19660804
  101.7 23.0 %collective-permute-start.1 = (bf16[160,128]{1,0:T(8,128)(2,1)}, bf16[160,128]{1,0:T(8,128)(2,1)S(1)}, u32[]{:S(2)}, u32[]{:S(2)}) collective-permute-start(bf16[160,128]{1,0:T(8,128)(2,1)} %collective-permute-done), channel_id=1, source_target_pairs={{48,0},{0,16},{16,32},{32,48},{49,1},{1,17},{17,33},{33,49},{50,2}... | collective-permute-start | bytes 122888 | tf_op jit(solution)/shard_map/ppermute | solution.py:14
  103.4 47.9 %collective-permute-start.4 = (bf16[160,128]{1,0:T(8,128)(2,1)}, bf16[160,128]{1,0:T(8,128)(2,1)S(1)}, u32[]{:S(2)}, u32[]{:S(2)}) collective-permute-start(bf16[160,128]{1,0:T(8,128)(2,1)} %collective-permute-done.3), channel_id=1, source_target_pairs={{48,0},{0,16},{16,32},{32,48},{49,1},{1,17},{17,33},{33,49},{50,2}... | collective-permute-start | bytes 122888 | tf_op jit(solution)/shard_map/ppermute | solution.py:14
  148.9 50.0 %copy-start.6 = (bf16[2560,128]{1,0:T(8,128)(2,1)}, bf16[2560,128]{1,0:T(8,128)(2,1)S(1)}, u32[]{:S(2)}) copy-start(bf16[2560,128]{1,0:T(8,128)(2,1)S(1)} %all_gather.34) | copy-start | bytes 1966084
  150.3 75.2 %copy-start.2 = (f32[4,160,2560]{2,1,0:T(8,128)}, f32[4,160,2560]{2,1,0:T(8,128)S(1)}, u32[]{:S(2)}) copy-start(f32[4,160,2560]{2,1,0:T(8,128)S(1)} %get-tuple-element.43) | copy-start | bytes 19660804
  150.3 23.8 %collective-permute-start.2 = (bf16[160,128]{1,0:T(8,128)(2,1)S(1)}, bf16[160,128]{1,0:T(8,128)(2,1)S(1)}, u32[]{:S(2)}, u32[]{:S(2)}) collective-permute-start(bf16[160,128]{1,0:T(8,128)(2,1)S(1)} %collective-permute-done.1), channel_id=1, source_target_pairs={{48,0},{0,16},{16,32},{32,48},{49,1},{1,17},{17,33},{33,49},{50,2}... | collective-permute-start | bytes 122888 | tf_op jit(solution)/shard_map/ppermute | solution.py:14
  151.2 49.1 %collective-permute-start.5 = (bf16[160,128]{1,0:T(8,128)(2,1)S(1)}, bf16[160,128]{1,0:T(8,128)(2,1)S(1)}, u32[]{:S(2)}, u32[]{:S(2)}) collective-permute-start(bf16[160,128]{1,0:T(8,128)(2,1)S(1)} %collective-permute-done.4), channel_id=1, source_target_pairs={{48,0},{0,16},{16,32},{32,48},{49,1},{1,17},{17,33},{33,49},{50,2}... | collective-permute-start | bytes 122888 | tf_op jit(solution)/shard_map/ppermute | solution.py:14
  198.8 1.5 copy-start.11
  200.3 25.2 %copy-start.1 = (f32[4,160,2560]{2,1,0:T(8,128)}, f32[4,160,2560]{2,1,0:T(8,128)S(1)}, u32[]{:S(2)}) copy-start(f32[4,160,2560]{2,1,0:T(8,128)S(1)} %get-tuple-element.41) | copy-start | bytes 19660804
  225.5 8.1 slice-start
  229.6 4.1 slice-start.1
  229.6 4.1 copy-start.5
  240.5 136.5 %reduce-scatter.12.cloned.1.call-start = ((), (), s32[]{:S(2)}) async-start(), calls=%async_computation.9 | async-start | bytes 1392640 | tf_op jit(solution)/shard_map/reduce_scatter | solution.py:117
  263.5 1.7 copy-start.4
  267.4 180.2 %reduce-scatter.22.cloned.1.call-start = ((), (), s32[]{:S(2)}) async-start(), calls=%async_computation.14 | async-start | bytes 1392640 | tf_op jit(solution)/shard_map/reduce_scatter | solution.py:118
  273.2 245.0 %reduce-scatter.14.cloned.1.call-start = ((), (), s32[]{:S(2)}) async-start(), calls=%async_computation.10 | async-start | bytes 1392640 | tf_op jit(solution)/shard_map/reduce_scatter | solution.py:117
  277.3 311.5 %reduce-scatter.24.cloned.1.call-start = ((), (), s32[]{:S(2)}) async-start(), calls=%async_computation.15 | async-start | bytes 1392640 | tf_op jit(solution)/shard_map/reduce_scatter | solution.py:118
  283.0 376.4 %reduce-scatter.16.cloned.1.call-start = ((), (), s32[]{:S(2)}) async-start(), calls=%async_computation.11 | async-start | bytes 1392640 | tf_op jit(solution)/shard_map/reduce_scatter | solution.py:117
  287.2 442.9 %reduce-scatter.26.cloned.1.call-start = ((), (), s32[]{:S(2)}) async-start(), calls=%async_computation.16 | async-start | bytes 1392640 | tf_op jit(solution)/shard_map/reduce_scatter | solution.py:118
  292.8 85.7 %copy-start.10 = (bf16[2560,128]{1,0:T(8,128)(2,1)S(1)}, bf16[2560,128]{1,0:T(8,128)(2,1)}, u32[]{:S(2)}) copy-start(bf16[2560,128]{1,0:T(8,128)(2,1)} %all_gather.32) | copy-start | bytes 1966084
  292.8 228.0 %copy-start.9 = (bf16[2560,128]{1,0:T(8,128)(2,1)S(1)}, bf16[2560,128]{1,0:T(8,128)(2,1)}, u32[]{:S(2)}) copy-start(bf16[2560,128]{1,0:T(8,128)(2,1)} %copy-done.8) | copy-start | bytes 1966084
  292.8 508.1 %reduce-scatter.18.cloned.1.call-start = ((), (), s32[]{:S(2)}) async-start(), calls=%async_computation.12 | async-start | bytes 1392640 | tf_op jit(solution)/shard_map/reduce_scatter | solution.py:117
  297.0 364.9 %copy-start.7 = (bf16[2560,128]{1,0:T(8,128)(2,1)S(1)}, bf16[2560,128]{1,0:T(8,128)(2,1)}, u32[]{:S(2)}) copy-start(bf16[2560,128]{1,0:T(8,128)(2,1)} %copy-done.6) | copy-start | bytes 1966084
  297.0 1187.2 %reduce-scatter.28.cloned.1.call-start = ((), (), s32[]{:S(2)}) async-start(), calls=%async_computation.17 | async-start | bytes 12681216
  306.3 141.4 %collective-permute-start.10 = (f32[160,128]{1,0:T(8,128)}, f32[160,128]{1,0:T(8,128)S(1)}, u32[]{:S(2)}, u32[]{:S(2)}) collective-permute-start(f32[160,128]{1,0:T(8,128)} %reduce-scatter.20.cloned.1.call-done), channel_id=1, source_target_pairs={{48,0},{0,16},{16,32},{32,48},{49,1},{1,17},{17,33},{33,49},{50,2}... | collective-permute-start | bytes 245768 | tf_op jit(solution)/shard_map/ppermute | solution.py:14
  377.0 141.3 %collective-permute-start.6 = (f32[160,128]{1,0:T(8,128)}, f32[160,128]{1,0:T(8,128)}, u32[]{:S(2)}, u32[]{:S(2)}) collective-permute-start(f32[160,128]{1,0:T(8,128)} %reduce-scatter.12.cloned.1.call-done), channel_id=1, source_target_pairs={{48,0},{0,16},{16,32},{32,48},{49,1},{1,17},{17,33},{33,49},{50,2}... | collective-permute-start | bytes 245768 | tf_op jit(solution)/shard_map/ppermute | solution.py:14
  382.2 421.2 %copy-start.12 = (bf16[2560,128]{1,0:T(8,128)(2,1)S(1)}, bf16[2560,128]{1,0:T(8,128)(2,1)}, u32[]{:S(2)}) copy-start(bf16[2560,128]{1,0:T(8,128)(2,1)} %copy-done.11) | copy-start | bytes 1966084
  448.6 140.2 %collective-permute-start.11 = (f32[160,128]{1,0:T(8,128)S(1)}, f32[160,128]{1,0:T(8,128)S(1)}, u32[]{:S(2)}, u32[]{:S(2)}) collective-permute-start(f32[160,128]{1,0:T(8,128)S(1)} %add.214), channel_id=1, source_target_pairs={{48,0},{0,16},{16,32},{32,48},{49,1},{1,17},{17,33},{33,49},{50,2}... | collective-permute-start | bytes 245768 | tf_op jit(solution)/shard_map/ppermute | solution.py:14
  519.2 140.2 %collective-permute-start.7 = (f32[160,128]{1,0:T(8,128)S(1)}, f32[160,128]{1,0:T(8,128)}, u32[]{:S(2)}, u32[]{:S(2)}) collective-permute-start(f32[160,128]{1,0:T(8,128)S(1)} %add.211), channel_id=1, source_target_pairs={{48,0},{0,16},{16,32},{32,48},{49,1},{1,17},{17,33},{33,49},{50,2}... | collective-permute-start | bytes 245768 | tf_op jit(solution)/shard_map/ppermute | solution.py:14
  589.7 140.4 %collective-permute-start.12 = (f32[160,128]{1,0:T(8,128)S(1)}, f32[160,128]{1,0:T(8,128)S(1)}, u32[]{:S(2)}, u32[]{:S(2)}) collective-permute-start(f32[160,128]{1,0:T(8,128)S(1)} %add.215), channel_id=1, source_target_pairs={{48,0},{0,16},{16,32},{32,48},{49,1},{1,17},{17,33},{33,49},{50,2}... | collective-permute-start | bytes 245768 | tf_op jit(solution)/shard_map/ppermute | solution.py:14
  660.3 140.5 %collective-permute-start.8 = (f32[160,128]{1,0:T(8,128)S(1)}, f32[160,128]{1,0:T(8,128)S(1)}, u32[]{:S(2)}, u32[]{:S(2)}) collective-permute-start(f32[160,128]{1,0:T(8,128)S(1)} %add.212), channel_id=1, source_target_pairs={{48,0},{0,16},{16,32},{32,48},{49,1},{1,17},{17,33},{33,49},{50,2}... | collective-permute-start | bytes 245768 | tf_op jit(solution)/shard_map/ppermute | solution.py:14
  731.0 75.3 %collective-permute-start.13 = (bf16[160,128]{1,0:T(8,128)(2,1)S(1)}, bf16[160,128]{1,0:T(8,128)(2,1)S(1)}, u32[]{:S(2)}, u32[]{:S(2)}) collective-permute-start(bf16[160,128]{1,0:T(8,128)(2,1)S(1)} %add.216), channel_id=1, source_target_pairs={{48,0},{0,16},{16,32},{32,48},{49,1},{1,17},{17,33},{33,49},{50,2}... | collective-permute-start | bytes 122888 | tf_op jit(solution)/shard_map/ppermute | solution.py:14
  801.7 5.3 collective-permute-start.9
Sparse Core Ops, SparseCore 0:
  240.6 65.5 reduce-scatter.19
  310.1 66.8 reduce-scatter.11
  380.8 66.8 reduce-scatter.21
  451.3 66.8 reduce-scatter.13
  521.9 66.8 reduce-scatter.23
  592.5 66.8 reduce-scatter.15
  663.2 66.8 reduce-scatter.25
  733.9 66.8 reduce-scatter.17
  826.1 658.0 reduce-scatter.27
where the time goes:
time: 1500 us; the launch traced here: 1490 us
  waiting for transfers between devices  1140 us (76%)
  blocking collectives  187 us (12%)
  matrix products  85.8 us (6%)
  other arithmetic  29.5 us (2%)
  starting transfers between devices  22.1 us (1%)
  local copies, waits for them, and re-layouts  18.8 us (1%)
    unnamed x10, waiting for transfers between devices  658 us
    reduce_scatter x4, waiting for transfers between devices, per_device(): lax.psum_scatter(part_key, 'inner', scatter_dimension=0, tiled=True)  273 us
    reduce_scatter x4, waiting for transfers between devices, per_device(): lax.psum_scatter(part_value, 'inner', scatter_dimension=0, tiled=True)  204 us
    all_gather x4, blocking collectives, per_device(): lax.all_gather(moving[0], 'inner', axis=0, tiled=True)  101 us
    all_gather x4, blocking collectives, per_device(): lax.all_gather(moving[1], 'inner', axis=0, tiled=True)  85.7 us
  transfers between devices with their start and end apart: 23, of which 10 were waited for; matrix products, arithmetic and copies ran while one was open for 6% of the time, Pallas kernels for 0%

commit v1 on v0

v1 whole, which is shorter than its diff:
```python
import functools
import math

import jax
import jax.numpy as jnp
import numpy as np
from jax import lax
from jax.experimental import pallas as pl
from jax.experimental.pallas import tpu as pltpu
from jax.sharding import Mesh, PartitionSpec as P

masked_fill = -1e30
HEADS = 4
HEAD = 128
ROWS = 160
HALF = 80
N_OUT = 4
N_X = 4
SLOT = HEADS * ROWS
ALL_ROWS = N_OUT * SLOT
KEYS = 16 * ROWS
KHALF = KEYS // 2
RT = 512
KC = 640
SCALE = 1.0 / math.sqrt(HEAD)
SCALE2 = SCALE * math.log2(math.e)
f32 = jnp.float32
bf16 = jnp.bfloat16
NT = (((1,), (1,)), ((), ()))
NN = (((1,), (0,)), ((), ()))
TN = (((0,), (0,)), ((), ()))


def dot(a, b, dims):
    return lax.dot_general(a, b, dims, preferred_element_type=f32)


def fill_rows(pieces, rows_ref):
    for d in range(N_OUT):
        for h in range(HEADS):
            rows_ref[d * SLOT + h * ROWS : d * SLOT + (h + 1) * ROWS, :] = pieces[d][
                :, h * HEAD : (h + 1) * HEAD
            ]


def masked_scores(key_rows, q, posq, ordk_ref, chunk):
    score = dot(key_rows, q, NT)
    place = lax.broadcasted_iota(jnp.int32, (HALF, RT), 0)
    parts = []
    for b in range(KC // HALF):
        limit = posq - ordk_ref[chunk * (KC // HALF) + b] * HALF
        part = score[b * HALF : (b + 1) * HALF] * SCALE2
        parts.append(jnp.where(place <= limit, part, masked_fill))
    return jnp.concatenate(parts, axis=0)


def stats_kernel(ordk_ref, posq_ref, q0, q1, q2, q3, g0, g1, g2, g3, kva, kvb, out_ref, qr, gr):
    fill_rows((q0, q1, q2, q3), qr)
    fill_rows((g0, g1, g2, g3), gr)

    def row_tile(rt, _):
        r0 = pl.multiple_of(rt * RT, RT)
        q = qr[pl.ds(r0, RT), :]
        g = gr[pl.ds(r0, RT), :]
        posq = posq_ref[:, pl.ds(r0, RT)]
        top = jnp.full((8, RT), masked_fill, f32)
        total = jnp.zeros((8, RT), f32)
        weighted = jnp.zeros((8, RT), f32)
        for chunk in range(KEYS // KC):
            kv = kva if chunk * KC < KHALF else kvb
            k0 = chunk * KC % KHALF
            score = masked_scores(kv[k0 : k0 + KC, :HEAD], q, posq, ordk_ref, chunk)
            dprob = dot(kv[k0 : k0 + KC, HEAD:], g, NT)
            score = score.reshape(KC // 8, 8, RT)
            new_top = jnp.maximum(top, jnp.max(score, axis=0))
            weights = jnp.exp2(score - new_top[None])
            factor = jnp.exp2(top - new_top)
            total = total * factor + jnp.sum(weights, axis=0)
            weighted = weighted * factor + jnp.sum(weights * dprob.reshape(KC // 8, 8, RT), axis=0)
            top = new_top
        row_top = jnp.max(top, axis=0, keepdims=True)
        factor = jnp.exp2(top - row_top)
        out_ref[0:1, pl.ds(r0, RT)] = row_top
        out_ref[1:2, pl.ds(r0, RT)] = jnp.sum(total * factor, axis=0, keepdims=True)
        out_ref[2:3, pl.ds(r0, RT)] = jnp.sum(weighted * factor, axis=0, keepdims=True)
        return 0

    lax.fori_loop(0, ALL_ROWS // RT, row_tile, 0)


def grads_kernel(
    ordk_ref, posq_ref, s0, s1, s2, s3, q0, q1, q2, q3, g0, g1, g2, g3, kva, kvb,
    dq0, dq1, dq2, dq3, dkv_keep, dkv_send, qr, gr, dqr, dkr, dvr, lse_ref, delta_ref,
):
    fill_rows((q0, q1, q2, q3), qr)
    fill_rows((g0, g1, g2, g3), gr)
    stats = (s0, s1, s2, s3)
    for d in range(N_OUT):
        parts = []
        for e in range(N_OUT):
            c0 = (d - e) % N_OUT * SLOT
            parts.append(stats[e][:, c0 : c0 + SLOT])
        row_top = parts[0][0:1]
        for part in parts[1:]:
            row_top = jnp.maximum(row_top, part[0:1])
        total = jnp.zeros_like(row_top)
        weighted = jnp.zeros_like(row_top)
        for part in parts:
            factor = jnp.exp2(part[0:1] - row_top)
            total = total + part[1:2] * factor
            weighted = weighted + part[2:3] * factor
        lse_ref[0:1, d * SLOT : (d + 1) * SLOT] = row_top + jnp.log2(total)
        delta_ref[0:1, d * SLOT : (d + 1) * SLOT] = weighted / total
    dkr[...] = jnp.zeros_like(dkr)
    dvr[...] = jnp.zeros_like(dvr)

    def row_tile(rt, _):
        r0 = pl.multiple_of(rt * RT, RT)
        q = qr[pl.ds(r0, RT), :]
        g = gr[pl.ds(r0, RT), :]
        posq = posq_ref[:, pl.ds(r0, RT)]
        lse = lse_ref[:, pl.ds(r0, RT)]
        delta = delta_ref[:, pl.ds(r0, RT)]
        dq = jnp.zeros((RT, HEAD), f32)
        for chunk in range(KEYS // KC):
            kv = kva if chunk * KC < KHALF else kvb
            k0 = chunk * KC % KHALF
            key_rows = kv[k0 : k0 + KC, :HEAD]
            score = masked_scores(key_rows, q, posq, ordk_ref, chunk)
            prob = jnp.exp2(score - lse)
            dprob = dot(kv[k0 : k0 + KC, HEAD:], g, NT)
            dscore = (prob * (dprob - delta)).astype(bf16)
            prob_low = prob.astype(bf16)
            dvr[chunk * KC : (chunk + 1) * KC, :] += dot(prob_low, g, NN)
            dkr[chunk * KC : (chunk + 1) * KC, :] += dot(dscore, q, NN)
            dq = dq + dot(dscore, key_rows, TN)
        dqr[pl.ds(r0, RT), :] = dq * SCALE
        return 0

    lax.fori_loop(0, ALL_ROWS // RT, row_tile, 0)
    for d, out in enumerate((dq0, dq1, dq2, dq3)):
        for h in range(HEADS):
            out[:, h * HEAD : (h + 1) * HEAD] = dqr[
                d * SLOT + h * ROWS : d * SLOT + (h + 1) * ROWS, :
            ].astype(out.dtype)
    dkv_keep[:, :HEAD] = dkr[:KHALF] * SCALE
    dkv_keep[:, HEAD:] = dvr[:KHALF]
    dkv_send[:, :HEAD] = dkr[KHALF:] * SCALE
    dkv_send[:, HEAD:] = dvr[KHALF:]


smem = pl.BlockSpec(memory_space=pltpu.SMEM)
vmem = pl.BlockSpec(memory_space=pltpu.VMEM)
params = pltpu.CompilerParams(vmem_limit_bytes=50 * 1024 * 1024)


def stats_call(ordk, posq, qs, gs, kva, kvb):
    return pl.pallas_call(
        stats_kernel,
        out_shape=jax.ShapeDtypeStruct((3, ALL_ROWS), f32),
        in_specs=[smem] + [vmem] * 11,
        out_specs=vmem,
        scratch_shapes=[pltpu.VMEM((ALL_ROWS, HEAD), bf16)] * 2,
        compiler_params=params,
        name="stats",
    )(ordk, posq, *qs, *gs, kva, kvb)


def grads_call(ordk, posq, stats, qs, gs, kva, kvb):
    wide = HEADS * HEAD
    return pl.pallas_call(
        grads_kernel,
        out_shape=(
            jax.ShapeDtypeStruct((ROWS, wide), f32),
            jax.ShapeDtypeStruct((ROWS, wide), bf16),
            jax.ShapeDtypeStruct((ROWS, wide), bf16),
            jax.ShapeDtypeStruct((ROWS, wide), bf16),
            jax.ShapeDtypeStruct((KHALF, 2 * HEAD), f32),
            jax.ShapeDtypeStruct((KHALF, 2 * HEAD), f32),
        ),
        in_specs=[smem] + [vmem] * 15,
        out_specs=[vmem] * 6,
        scratch_shapes=[
            pltpu.VMEM((ALL_ROWS, HEAD), bf16),
            pltpu.VMEM((ALL_ROWS, HEAD), bf16),
            pltpu.VMEM((ALL_ROWS, HEAD), f32),
            pltpu.VMEM((KEYS, HEAD), f32),
            pltpu.VMEM((KEYS, HEAD), f32),
            pltpu.VMEM((1, ALL_ROWS), f32),
            pltpu.VMEM((1, ALL_ROWS), f32),
        ],
        compiler_params=params,
        name="grads",
    )(ordk, posq, *stats, *qs, *gs, kva, kvb)


def shift(x, axis, d, n):
    return lax.ppermute(x, axis, [(i, (i + d) % n) for i in range(n)])


def from_behind(x, axis, n):
    return [x] + [shift(x, axis, d, n) for d in range(1, n)]


def per_device(inputs, block_order, w_query, w_key, w_value, grad_out):
    tokens = inputs[0]
    order = block_order[0]
    dout = grad_out[0]
    o, ix, iy, ic = (lax.axis_index(a) for a in ("outer", "x", "yh", "core"))

    gs = from_behind(dout, "outer", N_OUT)
    kv = jnp.concatenate(
        [
            dot(tokens, w_key, NN).astype(bf16),
            dot(tokens, w_value, NN).astype(bf16),
        ],
        axis=1,
    )
    query = dot(tokens, w_query, NN).astype(bf16)

    kv = jnp.concatenate(from_behind(kv, "yh", 2), axis=0)
    qs = from_behind(query, "outer", N_OUT)
    kva = jnp.concatenate(from_behind(kv, "x", N_X), axis=0)
    kvb = shift(kva, "core", 1, 2)

    inner = np.arange(2)[:, None, None, None], np.arange(N_X)[None, :, None, None], np.arange(2)[None, None, :, None]
    step = np.arange(2)[None, None, None, :]
    key_dev = ((o * N_X + (ix - inner[1]) % N_X) * 2 + (iy - inner[2]) % 2) * 2 + (ic - inner[0]) % 2
    key_blocks = (key_dev * 2 + step).reshape(-1)
    query_dev = (((o - np.arange(N_OUT)) % N_OUT * N_X + ix) * 2 + iy) * 2 + ic
    query_blocks = (query_dev[:, None] * 2 + np.arange(2)[None, :]).reshape(-1)

    def look_up(blocks):
        hit = blocks[:, None] == jnp.arange(order.shape[0], dtype=jnp.int32)[None, :]
        return jnp.sum(jnp.where(hit, order[None, :], 0), axis=1)

    ordk = look_up(key_blocks)
    ordq = look_up(query_blocks).reshape(N_OUT, 1, 2, 1)
    posq = ordq * HALF + jnp.arange(HALF, dtype=jnp.int32)
    posq = jnp.broadcast_to(posq, (N_OUT, HEADS, 2, HALF)).reshape(1, ALL_ROWS)

    stats = stats_call(ordk, posq, qs, gs, kva, kvb)
    columns = tokens.reshape(ROWS, 2, N_OUT, -1)
    xs = []
    for d in range(N_OUT):
        part = lax.dynamic_index_in_dim(columns, (o + d) % N_OUT, axis=2, keepdims=False)
        part = part.reshape(ROWS, -1)
        xs.append(part if d == 0 else shift(part, "outer", d, N_OUT))
    all_stats = from_behind(stats, "outer", N_OUT)
    dq0, dq1, dq2, dq3, dkv_keep, dkv_send = grads_call(ordk, posq, all_stats, qs, gs, kva, kvb)

    dkv_got = shift(dkv_send, "core", 1, 2)
    dq = dq0
    for d, part in ((1, dq1), (2, dq2), (3, dq3)):
        dq = dq + shift(part, "outer", -d, N_OUT).astype(f32)
    dq_all = from_behind(dq.astype(bf16), "outer", N_OUT)

    dkv = (dkv_keep + dkv_got).reshape(N_X, 2 * ROWS, 2 * HEAD)
    low = dkv.astype(bf16)
    part = dkv[0]
    for d in range(1, N_X):
        part = part + shift(low[d], "x", -d, N_X).astype(f32)
    dkv = part[:ROWS] + shift(part[ROWS:].astype(bf16), "yh", 1, 2).astype(f32)
    dkv_all = from_behind(dkv.astype(bf16), "outer", N_OUT)

    grads = jnp.concatenate(
        [jnp.concatenate(dq_all, axis=0), jnp.concatenate(dkv_all, axis=0)], axis=1
    )
    dw = dot(jnp.concatenate(xs, axis=0), grads, TN)
    dw = dw.reshape(16, 2, -1, dw.shape[1])
    mine = lax.dynamic_index_in_dim(dw, ic, axis=1, keepdims=False)
    other = lax.dynamic_index_in_dim(dw, 1 - ic, axis=1, keepdims=False)
    dw = (mine + shift(other, "core", 1, 2)).astype(bf16)
    dw = lax.all_to_all(dw, ("dp", "x", "yh"), 0, 0, tiled=True)
    dw = jnp.sum(dw.astype(f32), axis=0)
    wide = HEADS * HEAD
    return dw[:, :wide], dw[:, wide : wide + HEAD], dw[:, wide + HEAD :]


def solution(mesh):
    devices = np.asarray(mesh.devices).reshape(2, N_OUT, N_X, 2, 2)
    fine = Mesh(devices, ("dp", "outer", "x", "yh", "core"))
    seq = ("outer", "x", "yh", "core")
    rows = P(("dp",) + seq, None)
    return jax.shard_map(
        per_device,
        mesh=fine,
        in_specs=(
            P("dp", seq, None),
            P("dp", None),
            P(None, None),
            P(None, None),
            P(None, None),
            P("dp", seq, None),
        ),
        out_specs=(rows, rows, rows),
        check_vma=False,
    )
```

time: 1500 us -> 178 us (0.12)
  waiting for transfers between devices: 1140 us -> 44.3 us
  blocking collectives: 187 us -> 20.8 us
  matrix products: 85.8 us -> 6.94 us
  Pallas kernels: 0 us -> 34 us
  other arithmetic: 29.5 us -> 4.61 us
  starting transfers between devices: 22.1 us -> 46.9 us
    unnamed x10 -> x0, waiting for transfers between devices: 658 us -> none
    reduce_scatter x8 -> x0, waiting for transfers between devices: 477 us -> none  [the longest x4 273 us: per_device(): lax.psum_scatter(part_key, 'inner', scatter_dimension=0, tiled=True)]
    all_gather x8 -> x0, blocking collectives: 187 us -> none  [the longest x4 101 us: per_device(): lax.all_gather(moving[0], 'inner', axis=0, tiled=True)]
    dot_general x24 -> x4, matrix products: 85.8 us -> 6.94 us  [dot(): return lax.dot_general(a, b, dims, preferred_element_type=f32)]
    ppermute x14 -> x32, waiting for transfers between devices: 0.71 us -> 44.3 us  [shift(): return lax.ppermute(x, axis, [(i, (i + d) % n) for i in range(n)])]
    pallas_call x0 -> x2, Pallas kernels: none -> 34 us  [the longest x1 22.7 us: grads_call(): pl.pallas_call(grads_kernel, out_shape=(jax.ShapeDtypeStruct((ROWS, wide)...]
    ppermute x14 -> x32, starting transfers between devices: 21.6 us -> 46.9 us  [shift(): return lax.ppermute(x, axis, [(i, (i + d) % n) for i in range(n)])]
    all_to_all x0 -> x1, blocking collectives: none -> 20.8 us  [per_device(): dw = lax.all_to_all(dw, ('dp', 'x', 'yh'), 0, 0, tiled=True)]
  transfers between devices with their start and end apart: 23 -> 32, of which waited for: 10 -> 17; matrix products, arithmetic and copies ran while one was open for 6% -> 8% of each run, Pallas kernels for 0% -> 0%
where the time goes in v1:
time: 178 us
  starting transfers between devices  46.9 us (26%)
  waiting for transfers between devices  44.3 us (25%)
  Pallas kernels  34 us (19%)
  blocking collectives  20.8 us (12%)
  local copies, waits for them, and re-layouts  19.2 us (11%)
  matrix products  6.94 us (4%)
  other arithmetic  4.61 us (3%)
    ppermute x32, starting transfers between devices, shift(): return lax.ppermute(x, axis, [(i, (i + d) % n) for i in range(n)])  46.9 us
    ppermute x32, waiting for transfers between devices, shift(): return lax.ppermute(x, axis, [(i, (i + d) % n) for i in range(n)])  44.3 us
    pallas_call x1, Pallas kernels, grads_call(): pl.pallas_call(grads_kernel, out_shape=(jax.ShapeDtypeStruct((ROWS, wide)...  22.7 us
    all_to_all x1, blocking collectives, per_device(): dw = lax.all_to_all(dw, ('dp', 'x', 'yh'), 0, 0, tiled=True)  20.8 us
    pallas_call x1, Pallas kernels, stats_call(): pl.pallas_call(stats_kernel, out_shape=jax.ShapeDtypeStruct((3, ALL_ROWS)...  11.3 us
    dynamic_slice x1, local copies, waits for them, and re-layouts, per_device(): lax.dynamic_index_in_dim(columns, (o + d) % N_OUT, axis=2, keepdims=False)  9.14 us
    dot_general x4, matrix products, dot(): return lax.dot_general(a, b, dims, preferred_element_type=f32)  6.94 us
    unnamed x41, local copies, waits for them, and re-layouts  3.78 us
  transfers between devices with their start and end apart: 32, of which 17 were waited for; matrix products, arithmetic and copies ran while one was open for 8% of the time, Pallas kernels for 0%

profile of v1, /device:TPU:0, one launch (start us, length us, event | category | flops | bytes accessed | tf_op | source)
XLA Modules:
  0.0 177.7 jit_solution(13224416441254094892)
XLA Ops:
  0.7 3.6 %fusion.15.q0 = bf16[160,512]{1,0:T(8,128)(2,1)S(1)} fusion(bf16[4096,512]{1,0:T(8,128)(2,1)} %param.14, bf16[1,160,4096]{2,1,0:T(8,128)(2,1)} %param.12), kind=kOutput, calls=%fused_computation.18 | convolution fusion | flops 671170560 | bytes 5668864 | tf_op jit(solution)/shard_map/dot_general | solution.py:35
  4.3 2.1 %collective-permute-start.3 = (bf16[160,512]{1,0:T(8,128)(2,1)S(1)}, bf16[160,512]{1,0:T(8,128)(2,1)S(1)}, u32[]{:S(2)}, u32[]{:S(2)}) collective-permute-start(bf16[160,512]{1,0:T(8,128)(2,1)S(1)} %fusion.15.q0), channel_id=1, source_target_pairs={{0,16},{16,32},{32,48},{48,0},{1,17},{17,33},{33,49},{49,1},{2,18}... | collective-permute-start | bytes 491528 | tf_op jit(solution)/shard_map/ppermute | solution.py:198
  6.3 3.6 %collective-permute-start.4 = (bf16[160,512]{1,0:T(8,128)(2,1)S(1)}, bf16[160,512]{1,0:T(8,128)(2,1)S(1)}, u32[]{:S(2)}, u32[]{:S(2)}) collective-permute-start(bf16[160,512]{1,0:T(8,128)(2,1)S(1)} %fusion.15.q0), channel_id=1, source_target_pairs={{0,32},{16,48},{32,0},{48,16},{1,33},{17,49},{33,1},{49,17},{2,34}... | collective-permute-start | bytes 491528 | tf_op jit(solution)/shard_map/ppermute | solution.py:198
  9.9 1.0 collective-permute-start.5
  12.0 3.3 %collective-permute-start.9 = (bf16[160,256]{1,0:T(8,128)(2,1)S(1)}, bf16[160,256]{1,0:T(8,128)(2,1)S(1)}, u32[]{:S(2)}, u32[]{:S(2)}) collective-permute-start(bf16[160,256]{1,0:T(8,128)(2,1)S(1)} %get-tuple-element.26), channel_id=1, source_target_pairs={{0,2},{2,0},{1,3},{3,1},{4,6},{6,4},{5,7},{7,5},{8,10},{10,8},{9,1... | collective-permute-start | bytes 245768 | tf_op jit(solution)/shard_map/ppermute | solution.py:198
  15.7 2.4 %collective-permute-done.9 = bf16[160,256]{1,0:T(8,128)(2,1)S(1)} collective-permute-done((bf16[160,256]{1,0:T(8,128)(2,1)S(1)}, bf16[160,256]{1,0:T(8,128)(2,1)S(1)}, u32[]{:S(2)}, u32[]{:S(2)}) %collective-permute-start.9) | collective-permute-done | bytes 81952 | tf_op jit(solution)/shard_map/ppermute | solution.py:198
  18.1 1.6 collective-permute-start.10
  19.8 2.8 %collective-permute-start.11 = (bf16[320,256]{1,0:T(8,128)(2,1)S(1)}, bf16[320,256]{1,0:T(8,128)(2,1)S(1)}, u32[]{:S(2)}, u32[]{:S(2)}) collective-permute-start(bf16[320,256]{1,0:T(8,128)(2,1)S(1)} %pad_maximum_fusion), channel_id=1, source_target_pairs={{0,8},{4,12},{8,0},{12,4},{1,9},{5,13},{9,1},{13,5},{2,10},{6,14},... | collective-permute-start | bytes 491528 | tf_op jit(solution)/shard_map/ppermute | solution.py:198
  22.6 3.7 %collective-permute-done.10 = bf16[320,256]{1,0:T(8,128)(2,1)S(1)} collective-permute-done((bf16[320,256]{1,0:T(8,128)(2,1)S(1)}, bf16[320,256]{1,0:T(8,128)(2,1)S(1)}, u32[]{:S(2)}, u32[]{:S(2)}) %collective-permute-start.10) | collective-permute-done | bytes 163872 | tf_op jit(solution)/shard_map/ppermute | solution.py:198
  26.9 1.2 collective-permute-done.11
  28.1 0.7 collective-permute-start.6
  28.8 2.8 %collective-permute-done.12 = bf16[320,256]{1,0:T(8,128)(2,1)S(1)} collective-permute-done((bf16[320,256]{1,0:T(8,128)(2,1)S(1)}, bf16[320,256]{1,0:T(8,128)(2,1)S(1)}, u32[]{:S(2)}, u32[]{:S(2)}) %collective-permute-start.12) | collective-permute-done | bytes 163872 | tf_op jit(solution)/shard_map/ppermute | solution.py:198
  32.6 2.9 %collective-permute-start.8 = (bf16[160,512]{1,0:T(8,128)(2,1)S(1)}, bf16[160,512]{1,0:T(8,128)(2,1)}, u32[]{:S(2)}, u32[]{:S(2)}) collective-permute-start(bf16[160,512]{1,0:T(8,128)(2,1)S(1)} %bitcast.41), channel_id=1, source_target_pairs={{0,48},{16,0},{32,16},{48,32},{1,49},{17,1},{33,17},{49,33},{2,50}... | collective-permute-start | bytes 491528 | tf_op jit(solution)/shard_map/ppermute | solution.py:198
  35.9 4.2 %collective-permute-done.7.g2 = bf16[160,512]{1,0:T(8,128)(2,1)S(1)} collective-permute-done((bf16[160,512]{1,0:T(8,128)(2,1)S(1)}, bf16[160,512]{1,0:T(8,128)(2,1)S(1)}, u32[]{:S(2)}, u32[]{:S(2)}) %collective-permute-start.7) | collective-permute-done | bytes 163872 | tf_op jit(solution)/shard_map/ppermute | solution.py:198
  40.1 1.1 collective-permute-done.8.g3
  41.2 11.3 %stats.1.s0 = f32[3,2560]{1,0:T(4,128)S(1)} custom-call(s32[32]{0:T(128)S(1)} %select_reduce_fusion.ordk_ref, s32[1,2560]{1,0:T(1,128)S(1)} %reshape.137.posq_ref, bf16[160,512]{1,0:T(8,128)(2,1)S(1)} %fusion.15.q0, bf16[160,512]{1,0:T(8,128)(2,1)S(1)} %collective-permute-done.3.q1, bf16[160,512]{1,0:T(8,128)(2,1)S(1)} %collective-permute-done.4.q2, ...), custom_call_target="tpu_custom_call" | custom-call | tf_op jit(solution)/shard_map/stats/pallas_call | solution.py:158
  52.5 2.5 %collective-permute-start.14 = (f32[3,2560]{1,0:T(4,128)S(1)}, f32[3,2560]{1,0:T(4,128)S(1)}, u32[]{:S(2)}, u32[]{:S(2)}) collective-permute-start(f32[3,2560]{1,0:T(4,128)S(1)} %stats.1.s0), channel_id=1, source_target_pairs={{0,16},{16,32},{32,48},{48,0},{1,17},{17,33},{33,49},{49,1},{2,18}... | collective-permute-start | bytes 92168 | tf_op jit(solution)/shard_map/ppermute | solution.py:198
  55.0 1.6 collective-permute-start.15
  56.7 2.4 %collective-permute-start.16 = (f32[3,2560]{1,0:T(4,128)S(1)}, f32[3,2560]{1,0:T(4,128)S(1)}, u32[]{:S(2)}, u32[]{:S(2)}) collective-permute-start(f32[3,2560]{1,0:T(4,128)S(1)} %stats.1.s0), channel_id=1, source_target_pairs={{0,48},{16,0},{32,16},{48,32},{1,49},{17,1},{33,17},{49,33},{2,50}... | collective-permute-start | bytes 92168 | tf_op jit(solution)/shard_map/ppermute | solution.py:198
  59.1 1.5 collective-permute-done.15.s2
  60.8 22.7 %grads.1 = (f32[160,512]{1,0:T(8,128)S(1)}, bf16[160,512]{1,0:T(8,128)(2,1)S(1)}, bf16[160,512]{1,0:T(8,128)(2,1)S(1)}, bf16[160,512]{1,0:T(8,128)(2,1)S(1)}, f32[1280,256]{1,0:T(8,128)}, /*index=5*/f32[1280,256]{1,0:T(8,128)}) custom-call(s32[32]{0:T(128)S(1)} %select_reduce_fusion.ordk_ref, s32[1,2560]{1,0:T(1,128)S(1)} %reshape.137.posq_ref, ...), custom_call_target="tpu_custom_call" | custom-call | tf_op jit(solution)/shard_map/grads/pallas_call | solution.py:171
  83.4 0.7 copy-done.2
  86.2 3.2 %reshape_squeeze.3 = bf16[160,2,4,512]{3,2,1,0:T(4,128)(2,1)S(1)} reshape(bf16[1,160,4096]{2,1,0:T(8,128)(2,1)} %param.12) | data formatting | bytes 2621440 | tf_op jit(solution)/shard_map/reshape;squeeze | solution.py:243
  89.6 2.0 %fusion.59 = (bf16[1280,256]{1,0:T(8,128)(2,1)S(1)}, f32[1280,256]{1,0:T(8,128)S(1)}) fusion(f32[1280,256]{1,0:T(8,128)} %get-tuple-element.13, f32[1280,256]{1,0:T(8,128)} %collective-permute-done.23), kind=kLoop, calls=%fused_computation.93 | loop fusion | flops 655360 | bytes 4587520 | tf_op jit(solution)/shard_map/convert_element_type | solution.py:259
  91.6 1.9 %collective-permute-start.24 = (bf16[320,256]{1,0:T(8,128)(2,1)S(1)}, bf16[320,256]{1,0:T(8,128)(2,1)S(1)}, u32[]{:S(2)}, u32[]{:S(2)}) collective-permute-start(bf16[320,256]{1,0:T(8,128)(2,1)S(1)} %get-tuple-element.21), channel_id=1, source_target_pairs={{0,12},{4,0},{8,4},{12,8},{1,13},{5,1},{9,5},{13,9},{2,14},{6,2},{... | collective-permute-start | bytes 491528 | tf_op jit(solution)/shard_map/ppermute | solution.py:198
  94.1 0.8 collective-permute-start.26
  94.9 9.1 %dynamic-slice_reduce_fusion.3 = (bf16[160,2,512]{2,1,0:T(2,128)(2,1)S(1)}, bf16[160,2,512]{2,1,0:T(2,128)(2,1)S(1)}, bf16[160,2,512]{2,1,0:T(2,128)(2,1)S(1)}, bf16[160,2,512]{2,1,0:T(2,128)(2,1)S(1)}) fusion(bf16[160,2,4,512]{3,2,1,0:T(4,128)(2,1)S(1)} %reshape_squeeze.3, s32[]{:T(128)S(6)} %select_n.72, s32[]{:T(128)S(6)} %select_n.76, s32[]{:T(128)S(6)} %select_n.74, ...), kind=kLoop, calls=%fused_computation.39 | loop fusion | bytes 2621456 | tf_op jit(solution)/shard_map/jit(dynamic_index_in_dim)/dynamic_slice | solution.py:246
  104.1 1.2 collective-permute-start
  105.4 3.9 %collective-permute-start.1 = (bf16[160,1024]{1,0:T(8,128)(2,1)S(1)}, bf16[160,1024]{1,0:T(8,128)(2,1)S(1)}, u32[]{:S(2)}, u32[]{:S(2)}) collective-permute-start(bf16[160,1024]{1,0:T(8,128)(2,1)S(1)} %bitcast.51), channel_id=1, source_target_pairs={{0,32},{16,48},{32,0},{48,16},{1,33},{17,49},{33,1},{49,17},{2,34}... | collective-permute-start | bytes 983048 | tf_op jit(solution)/shard_map/ppermute | solution.py:198
  109.4 1.4 collective-permute-start.18
  111.6 9.2 %collective-permute-done.17 = bf16[160,512]{1,0:T(8,128)(2,1)S(1)} collective-permute-done((bf16[160,512]{1,0:T(8,128)(2,1)S(1)}, bf16[160,512]{1,0:T(8,128)(2,1)S(1)}, u32[]{:S(2)}, u32[]{:S(2)}) %collective-permute-start.17) | collective-permute-done | bytes 163872 | tf_op jit(solution)/shard_map/ppermute | solution.py:198
  120.9 2.6 %collective-permute-start.2 = (bf16[160,1024]{1,0:T(8,128)(2,1)S(1)}, bf16[160,1024]{1,0:T(8,128)(2,1)S(1)}, u32[]{:S(2)}, u32[]{:S(2)}) collective-permute-start(bf16[160,1024]{1,0:T(8,128)(2,1)S(1)} %bitcast.50), channel_id=1, source_target_pairs={{0,48},{16,0},{32,16},{48,32},{1,49},{17,1},{33,17},{49,33},{2,50}... | collective-permute-start | bytes 983048 | tf_op jit(solution)/shard_map/ppermute | solution.py:198
  123.4 4.9 %collective-permute-done.18 = bf16[160,512]{1,0:T(8,128)(2,1)S(1)} collective-permute-done((bf16[160,512]{1,0:T(8,128)(2,1)S(1)}, bf16[160,512]{1,0:T(8,128)(2,1)S(1)}, u32[]{:S(2)}, u32[]{:S(2)}) %collective-permute-start.18) | collective-permute-done | bytes 163872 | tf_op jit(solution)/shard_map/ppermute | solution.py:198
  128.3 3.3 %collective-permute-start.27 = (bf16[160,256]{1,0:T(8,128)(2,1)S(1)}, bf16[160,256]{1,0:T(8,128)(2,1)S(1)}, u32[]{:S(2)}, u32[]{:S(2)}) collective-permute-start(bf16[160,256]{1,0:T(8,128)(2,1)S(1)} %slice.59), channel_id=1, source_target_pairs={{0,2},{2,0},{1,3},{3,1},{4,6},{6,4},{5,7},{7,5},{8,10},{10,8},{9,1... | collective-permute-start | bytes 245768 | tf_op jit(solution)/shard_map/ppermute | solution.py:198
  131.8 0.8 collective-permute-start.21
  132.6 1.7 collective-permute-done.27
  134.3 0.8 collective-permute-start.22
  135.1 1.3 collective-permute-start.28
  136.4 1.7 collective-permute-start.29
  138.1 3.2 %collective-permute-done.20 = bf16[160,512]{1,0:T(8,128)(2,1)S(1)} collective-permute-done((bf16[160,512]{1,0:T(8,128)(2,1)S(1)}, bf16[160,512]{1,0:T(8,128)(2,1)S(1)}, u32[]{:S(2)}, u32[]{:S(2)}) %collective-permute-start.20) | collective-permute-done | bytes 163872 | tf_op jit(solution)/shard_map/ppermute | solution.py:198
  142.0 1.1 collective-permute-done.28
  143.1 2.8 %collective-permute-done.30 = bf16[160,256]{1,0:T(8,128)(2,1)} collective-permute-done((bf16[160,256]{1,0:T(8,128)(2,1)S(1)}, bf16[160,256]{1,0:T(8,128)(2,1)}, u32[]{:S(2)}, u32[]{:S(2)}) %collective-permute-start.30) | collective-permute-done | bytes 81952 | tf_op jit(solution)/shard_map/ppermute | solution.py:198
  145.9 2.4 %fusion.1 = f32[1024,768]{1,0:T(8,128)S(1)} fusion(bf16[160,1024]{1,0:T(8,128)(2,1)S(1)} %collective-permute-done.2, bf16[160,1024]{1,0:T(8,128)(2,1)S(1)} %collective-permute-done.1, bf16[160,1024]{1,0:T(8,128)(2,1)S(1)} %collective-permute-done, bf16[160,1024]{1,0:T(8,128)(2,1)S(1)} %bitcast.53, bf16[160,256]{1,0:T(8,128)(2,1)} %collective-permute-done.30, ...), kind=kOutput, calls=%fused_computation.4 | convolution fusion | flops 1019740160 | bytes 5439488 | tf_op jit(solution)/shard_map/dot_general | solution.py:35
  148.3 1.4 dynamic-slice_bitcast_fusion
  149.6 0.8 copy-done.11
  150.4 3.6 %collective-permute-done.31 = f32[16,32,768]{2,1,0:T(8,128)S(1)} collective-permute-done((f32[16,32,768]{2,1,0:T(8,128)}, f32[16,32,768]{2,1,0:T(8,128)S(1)}, u32[]{:S(2)}, u32[]{:S(2)}) %collective-permute-start.31) | collective-permute-done | bytes 1572896 | tf_op jit(solution)/shard_map/ppermute | solution.py:198
  154.0 1.6 fusion
  155.6 20.8 %all_to_all.5 = bf16[16,32,768]{2,1,0:T(8,128)(2,1)S(1)} all-to-all(bf16[16,32,768]{2,1,0:T(8,128)(2,1)S(1)} %fusion), channel_id=1, replica_groups=mesh['dp'=2,'outer'=4,'x'=4,'yh'=2,'core'=2] {'dp','x','yh'}, dimensions={0} | all-to-all | bytes 1572864 | tf_op jit(solution)/shard_map/all_to_all | solution.py:274
  (97 shorter events, 9.6 us)
Async XLA Ops:
  0.6 10.3 %copy-start = (bf16[4096,128]{1,0:T(8,128)(2,1)S(1)}, bf16[4096,128]{1,0:T(8,128)(2,1)}, u32[]{:S(2)}) copy-start(bf16[4096,128]{1,0:T(8,128)(2,1)} %param.15) | copy-start | bytes 3145732
  0.6 10.3 %copy-start.10 = (bf16[1,160,4096]{2,1,0:T(8,128)(2,1)S(1)}, bf16[1,160,4096]{2,1,0:T(8,128)(2,1)}, u32[]{:S(2)}) copy-start(bf16[1,160,4096]{2,1,0:T(8,128)(2,1)} %param.12) | copy-start | bytes 3932164
  4.2 7.2 %copy-start.12 = (bf16[4096,128]{1,0:T(8,128)(2,1)S(1)}, bf16[4096,128]{1,0:T(8,128)(2,1)}, u32[]{:S(2)}) copy-start(bf16[4096,128]{1,0:T(8,128)(2,1)} %param.16) | copy-start | bytes 3145732
  4.3 27.7 %collective-permute-start.3 = (bf16[160,512]{1,0:T(8,128)(2,1)S(1)}, bf16[160,512]{1,0:T(8,128)(2,1)S(1)}, u32[]{:S(2)}, u32[]{:S(2)}) collective-permute-start(bf16[160,512]{1,0:T(8,128)(2,1)S(1)} %fusion.15.q0), channel_id=1, source_target_pairs={{0,16},{16,32},{32,48},{48,0},{1,17},{17,33},{33,49},{49,1},{2,18}... | collective-permute-start | bytes 491528 | tf_op jit(solution)/shard_map/ppermute | solution.py:198
  6.3 26.2 %collective-permute-start.4 = (bf16[160,512]{1,0:T(8,128)(2,1)S(1)}, bf16[160,512]{1,0:T(8,128)(2,1)S(1)}, u32[]{:S(2)}, u32[]{:S(2)}) collective-permute-start(bf16[160,512]{1,0:T(8,128)(2,1)S(1)} %fusion.15.q0), channel_id=1, source_target_pairs={{0,32},{16,48},{32,0},{48,16},{1,33},{17,49},{33,1},{49,17},{2,34}... | collective-permute-start | bytes 491528 | tf_op jit(solution)/shard_map/ppermute | solution.py:198
  9.9 26.0 %collective-permute-start.5 = (bf16[160,512]{1,0:T(8,128)(2,1)S(1)}, bf16[160,512]{1,0:T(8,128)(2,1)S(1)}, u32[]{:S(2)}, u32[]{:S(2)}) collective-permute-start(bf16[160,512]{1,0:T(8,128)(2,1)S(1)} %fusion.15.q0), channel_id=1, source_target_pairs={{0,48},{16,0},{32,16},{48,32},{1,49},{17,1},{33,17},{49,33},{2,50}... | collective-permute-start | bytes 491528 | tf_op jit(solution)/shard_map/ppermute | solution.py:198
  11.4 3.9 %copy-start.16 = (s32[1,1,2,1]{2,3,1,0:T(1,128)S(1)}, s32[1,1,2,1]{2,3,1,0:T(1,128)}, u32[]{:S(2)}) copy-start(s32[1,1,2,1]{2,3,1,0:T(1,128)} %constant.129) | copy-start | bytes 28
  11.5 3.9 %copy-start.15 = (s32[2,1,1,1]{0,3,2,1:T(1,128)S(1)}, s32[2,1,1,1]{0,3,2,1:T(1,128)}, u32[]{:S(2)}) copy-start(s32[2,1,1,1]{0,3,2,1:T(1,128)} %constant.130) | copy-start | bytes 28
  11.5 3.9 %copy-start.13 = (s32[1,4,1,1]{1,3,2,0:T(1,128)S(1)}, s32[1,4,1,1]{1,3,2,0:T(1,128)}, u32[]{:S(2)}) copy-start(s32[1,4,1,1]{1,3,2,0:T(1,128)} %constant.128) | copy-start | bytes 52
  11.5 8.2 %copy-start.14 = (s32[1,128]{1,0:T(1,128)S(1)}, s32[1,128]{1,0:T(1,128)}, u32[]{:S(2)}) copy-start(s32[1,128]{1,0:T(1,128)} %param.13) | copy-start | bytes 1540
  11.5 16.6 %copy-start.1 = (bf16[1,160,512]{2,1,0:T(8,128)(2,1)S(1)}, bf16[1,160,512]{2,1,0:T(8,128)(2,1)}, u32[]{:S(2)}) copy-start(bf16[1,160,512]{2,1,0:T(8,128)(2,1)} %param.17) | copy-start | bytes 491524
  12.0 6.0 %collective-permute-start.9 = (bf16[160,256]{1,0:T(8,128)(2,1)S(1)}, bf16[160,256]{1,0:T(8,128)(2,1)S(1)}, u32[]{:S(2)}, u32[]{:S(2)}) collective-permute-start(bf16[160,256]{1,0:T(8,128)(2,1)S(1)} %get-tuple-element.26), channel_id=1, source_target_pairs={{0,2},{2,0},{1,3},{3,1},{4,6},{6,4},{5,7},{7,5},{8,10},{10,8},{9,1... | collective-permute-start | bytes 245768 | tf_op jit(solution)/shard_map/ppermute | solution.py:198
  18.1 8.3 %collective-permute-start.10 = (bf16[320,256]{1,0:T(8,128)(2,1)S(1)}, bf16[320,256]{1,0:T(8,128)(2,1)S(1)}, u32[]{:S(2)}, u32[]{:S(2)}) collective-permute-start(bf16[320,256]{1,0:T(8,128)(2,1)S(1)} %pad_maximum_fusion), channel_id=1, source_target_pairs={{0,4},{4,8},{8,12},{12,0},{1,5},{5,9},{9,13},{13,1},{2,6},{6,10},{... | collective-permute-start | bytes 491528 | tf_op jit(solution)/shard_map/ppermute | solution.py:198
  19.8 8.3 %collective-permute-start.11 = (bf16[320,256]{1,0:T(8,128)(2,1)S(1)}, bf16[320,256]{1,0:T(8,128)(2,1)S(1)}, u32[]{:S(2)}, u32[]{:S(2)}) collective-permute-start(bf16[320,256]{1,0:T(8,128)(2,1)S(1)} %pad_maximum_fusion), channel_id=1, source_target_pairs={{0,8},{4,12},{8,0},{12,4},{1,9},{5,13},{9,1},{13,5},{2,10},{6,14},... | collective-permute-start | bytes 491528 | tf_op jit(solution)/shard_map/ppermute | solution.py:198
  26.3 5.3 %collective-permute-start.12 = (bf16[320,256]{1,0:T(8,128)(2,1)S(1)}, bf16[320,256]{1,0:T(8,128)(2,1)S(1)}, u32[]{:S(2)}, u32[]{:S(2)}) collective-permute-start(bf16[320,256]{1,0:T(8,128)(2,1)S(1)} %pad_maximum_fusion), channel_id=1, source_target_pairs={{0,12},{4,0},{8,4},{12,8},{1,13},{5,1},{9,5},{13,9},{2,14},{6,2},{... | collective-permute-start | bytes 491528 | tf_op jit(solution)/shard_map/ppermute | solution.py:198
  28.1 7.8 %collective-permute-start.6 = (bf16[160,512]{1,0:T(8,128)(2,1)S(1)}, bf16[160,512]{1,0:T(8,128)(2,1)S(1)}, u32[]{:S(2)}, u32[]{:S(2)}) collective-permute-start(bf16[160,512]{1,0:T(8,128)(2,1)S(1)} %bitcast.39), channel_id=1, source_target_pairs={{0,16},{16,32},{32,48},{48,0},{1,17},{17,33},{33,49},{49,1},{2,18}... | collective-permute-start | bytes 491528 | tf_op jit(solution)/shard_map/ppermute | solution.py:198
  31.7 9.5 %collective-permute-start.13 = (bf16[1280,256]{1,0:T(8,128)(2,1)S(1)}, bf16[1280,256]{1,0:T(8,128)(2,1)S(1)}, u32[]{:S(2)}, u32[]{:S(2)}) collective-permute-start(bf16[1280,256]{1,0:T(8,128)(2,1)S(1)} %constant_dynamic-update-slice_fusion.kva), channel_id=1, source_target_pairs={{0,1},{1,0},{2,3},{3,2},{4,5},{5,4},{6,7},{7,6},{8,9},{9,8},{10,11... | collective-permute-start | bytes 1966088 | tf_op jit(solution)/shard_map/ppermute | solution.py:198
  31.9 8.2 %collective-permute-start.7 = (bf16[160,512]{1,0:T(8,128)(2,1)S(1)}, bf16[160,512]{1,0:T(8,128)(2,1)S(1)}, u32[]{:S(2)}, u32[]{:S(2)}) collective-permute-start(bf16[160,512]{1,0:T(8,128)(2,1)S(1)} %bitcast.40), channel_id=1, source_target_pairs={{0,32},{16,48},{32,0},{48,16},{1,33},{17,49},{33,1},{49,17},{2,34}... | collective-permute-start | bytes 491528 | tf_op jit(solution)/shard_map/ppermute | solution.py:198
  32.6 8.7 %collective-permute-start.8 = (bf16[160,512]{1,0:T(8,128)(2,1)S(1)}, bf16[160,512]{1,0:T(8,128)(2,1)}, u32[]{:S(2)}, u32[]{:S(2)}) collective-permute-start(bf16[160,512]{1,0:T(8,128)(2,1)S(1)} %bitcast.41), channel_id=1, source_target_pairs={{0,48},{16,0},{32,16},{48,32},{1,49},{17,1},{33,17},{49,33},{2,50}... | collective-permute-start | bytes 491528 | tf_op jit(solution)/shard_map/ppermute | solution.py:198
  52.5 6.6 %collective-permute-start.14 = (f32[3,2560]{1,0:T(4,128)S(1)}, f32[3,2560]{1,0:T(4,128)S(1)}, u32[]{:S(2)}, u32[]{:S(2)}) collective-permute-start(f32[3,2560]{1,0:T(4,128)S(1)} %stats.1.s0), channel_id=1, source_target_pairs={{0,16},{16,32},{32,48},{48,0},{1,17},{17,33},{33,49},{49,1},{2,18}... | collective-permute-start | bytes 92168 | tf_op jit(solution)/shard_map/ppermute | solution.py:198
  55.0 5.5 %collective-permute-start.15 = (f32[3,2560]{1,0:T(4,128)S(1)}, f32[3,2560]{1,0:T(4,128)S(1)}, u32[]{:S(2)}, u32[]{:S(2)}) collective-permute-start(f32[3,2560]{1,0:T(4,128)S(1)} %stats.1.s0), channel_id=1, source_target_pairs={{0,32},{16,48},{32,0},{48,16},{1,33},{17,49},{33,1},{49,17},{2,34}... | collective-permute-start | bytes 92168 | tf_op jit(solution)/shard_map/ppermute | solution.py:198
  56.7 4.1 %collective-permute-start.16 = (f32[3,2560]{1,0:T(4,128)S(1)}, f32[3,2560]{1,0:T(4,128)S(1)}, u32[]{:S(2)}, u32[]{:S(2)}) collective-permute-start(f32[3,2560]{1,0:T(4,128)S(1)} %stats.1.s0), channel_id=1, source_target_pairs={{0,48},{16,0},{32,16},{48,32},{1,49},{17,1},{33,17},{49,33},{2,50}... | collective-permute-start | bytes 92168 | tf_op jit(solution)/shard_map/ppermute | solution.py:198
  83.4 0.7 copy-start.2
  84.8 0.7 copy-start.6
  85.5 0.7 copy-start.8
  86.2 3.4 %collective-permute-start.23 = (f32[1280,256]{1,0:T(8,128)}, f32[1280,256]{1,0:T(8,128)}, u32[]{:S(2)}, u32[]{:S(2)}) collective-permute-start(f32[1280,256]{1,0:T(8,128)} %get-tuple-element.14), channel_id=1, source_target_pairs={{0,1},{1,0},{2,3},{3,2},{4,5},{5,4},{6,7},{7,6},{8,9},{9,8},{10,11... | collective-permute-start | bytes 3932168 | tf_op jit(solution)/shard_map/ppermute | solution.py:198
  91.6 17.7 %collective-permute-start.24 = (bf16[320,256]{1,0:T(8,128)(2,1)S(1)}, bf16[320,256]{1,0:T(8,128)(2,1)S(1)}, u32[]{:S(2)}, u32[]{:S(2)}) collective-permute-start(bf16[320,256]{1,0:T(8,128)(2,1)S(1)} %get-tuple-element.21), channel_id=1, source_target_pairs={{0,12},{4,0},{8,4},{12,8},{1,13},{5,1},{9,5},{13,9},{2,14},{6,2},{... | collective-permute-start | bytes 491528 | tf_op jit(solution)/shard_map/ppermute | solution.py:198
  93.5 15.9 %collective-permute-start.25 = (bf16[320,256]{1,0:T(8,128)(2,1)S(1)}, bf16[320,256]{1,0:T(8,128)(2,1)S(1)}, u32[]{:S(2)}, u32[]{:S(2)}) collective-permute-start(bf16[320,256]{1,0:T(8,128)(2,1)S(1)} %get-tuple-element.23), channel_id=1, source_target_pairs={{0,8},{4,12},{8,0},{12,4},{1,9},{5,13},{9,1},{13,5},{2,10},{6,14},... | collective-permute-start | bytes 491528 | tf_op jit(solution)/shard_map/ppermute | solution.py:198
  94.1 16.8 %collective-permute-start.26 = (bf16[320,256]{1,0:T(8,128)(2,1)S(1)}, bf16[320,256]{1,0:T(8,128)(2,1)S(1)}, u32[]{:S(2)}, u32[]{:S(2)}) collective-permute-start(bf16[320,256]{1,0:T(8,128)(2,1)S(1)} %get-tuple-element.22), channel_id=1, source_target_pairs={{0,4},{4,8},{8,12},{12,0},{1,5},{5,9},{9,13},{13,1},{2,6},{6,10},{... | collective-permute-start | bytes 491528 | tf_op jit(solution)/shard_map/ppermute | solution.py:198
  104.0 5.3 %copy-start.9 = (bf16[160,512]{1,0:T(8,128)(2,1)S(1)}, bf16[160,512]{1,0:T(8,128)(2,1)}, u32[]{:S(2)}) copy-start(bf16[160,512]{1,0:T(8,128)(2,1)} %copy-done.8) | copy-start | bytes 491524
  104.0 5.4 %copy-start.7 = (bf16[160,512]{1,0:T(8,128)(2,1)S(1)}, bf16[160,512]{1,0:T(8,128)(2,1)}, u32[]{:S(2)}) copy-start(bf16[160,512]{1,0:T(8,128)(2,1)} %copy-done.6) | copy-start | bytes 491524
  104.0 6.9 %copy-start.5 = (bf16[160,512]{1,0:T(8,128)(2,1)S(1)}, bf16[160,512]{1,0:T(8,128)(2,1)}, u32[]{:S(2)}) copy-start(bf16[160,512]{1,0:T(8,128)(2,1)} %copy-done.4) | copy-start | bytes 491524
  104.0 27.6 %copy-start.3 = (f32[160,512]{1,0:T(8,128)S(1)}, f32[160,512]{1,0:T(8,128)}, u32[]{:S(2)}) copy-start(f32[160,512]{1,0:T(8,128)} %copy-done.2) | copy-start | bytes 983044
  104.1 27.7 %collective-permute-start = (bf16[160,1024]{1,0:T(8,128)(2,1)S(1)}, bf16[160,1024]{1,0:T(8,128)(2,1)S(1)}, u32[]{:S(2)}, u32[]{:S(2)}) collective-permute-start(bf16[160,1024]{1,0:T(8,128)(2,1)S(1)} %bitcast.52), channel_id=1, source_target_pairs={{0,16},{16,32},{32,48},{48,0},{1,17},{17,33},{33,49},{49,1},{2,18}... | collective-permute-start | bytes 983048 | tf_op jit(solution)/shard_map/ppermute | solution.py:198
  105.4 29.7 %collective-permute-start.1 = (bf16[160,1024]{1,0:T(8,128)(2,1)S(1)}, bf16[160,1024]{1,0:T(8,128)(2,1)S(1)}, u32[]{:S(2)}, u32[]{:S(2)}) collective-permute-start(bf16[160,1024]{1,0:T(8,128)(2,1)S(1)} %bitcast.51), channel_id=1, source_target_pairs={{0,32},{16,48},{32,0},{48,16},{1,33},{17,49},{33,1},{49,17},{2,34}... | collective-permute-start | bytes 983048 | tf_op jit(solution)/shard_map/ppermute | solution.py:198
  109.3 11.5 %collective-permute-start.17 = (bf16[160,512]{1,0:T(8,128)(2,1)S(1)}, bf16[160,512]{1,0:T(8,128)(2,1)S(1)}, u32[]{:S(2)}, u32[]{:S(2)}) collective-permute-start(bf16[160,512]{1,0:T(8,128)(2,1)S(1)} %copy-done.9), channel_id=1, source_target_pairs={{0,48},{16,0},{32,16},{48,32},{1,49},{17,1},{33,17},{49,33},{2,50}... | collective-permute-start | bytes 491528 | tf_op jit(solution)/shard_map/ppermute | solution.py:198
  109.4 18.9 %collective-permute-start.18 = (bf16[160,512]{1,0:T(8,128)(2,1)S(1)}, bf16[160,512]{1,0:T(8,128)(2,1)S(1)}, u32[]{:S(2)}, u32[]{:S(2)}) collective-permute-start(bf16[160,512]{1,0:T(8,128)(2,1)S(1)} %copy-done.7), channel_id=1, source_target_pairs={{0,32},{16,48},{32,0},{48,16},{1,33},{17,49},{33,1},{49,17},{2,34}... | collective-permute-start | bytes 491528 | tf_op jit(solution)/shard_map/ppermute | solution.py:198
  110.9 20.7 %collective-permute-start.19 = (bf16[160,512]{1,0:T(8,128)(2,1)S(1)}, bf16[160,512]{1,0:T(8,128)(2,1)S(1)}, u32[]{:S(2)}, u32[]{:S(2)}) collective-permute-start(bf16[160,512]{1,0:T(8,128)(2,1)S(1)} %copy-done.5), channel_id=1, source_target_pairs={{0,16},{16,32},{32,48},{48,0},{1,17},{17,33},{33,49},{49,1},{2,18}... | collective-permute-start | bytes 491528 | tf_op jit(solution)/shard_map/ppermute | solution.py:198
  120.9 15.6 %collective-permute-start.2 = (bf16[160,1024]{1,0:T(8,128)(2,1)S(1)}, bf16[160,1024]{1,0:T(8,128)(2,1)S(1)}, u32[]{:S(2)}, u32[]{:S(2)}) collective-permute-start(bf16[160,1024]{1,0:T(8,128)(2,1)S(1)} %bitcast.50), channel_id=1, source_target_pairs={{0,48},{16,0},{32,16},{48,32},{1,49},{17,1},{33,17},{49,33},{2,50}... | collective-permute-start | bytes 983048 | tf_op jit(solution)/shard_map/ppermute | solution.py:198
  128.3 5.9 %collective-permute-start.27 = (bf16[160,256]{1,0:T(8,128)(2,1)S(1)}, bf16[160,256]{1,0:T(8,128)(2,1)S(1)}, u32[]{:S(2)}, u32[]{:S(2)}) collective-permute-start(bf16[160,256]{1,0:T(8,128)(2,1)S(1)} %slice.59), channel_id=1, source_target_pairs={{0,2},{2,0},{1,3},{3,1},{4,6},{6,4},{5,7},{7,5},{8,10},{10,8},{9,1... | collective-permute-start | bytes 245768 | tf_op jit(solution)/shard_map/ppermute | solution.py:198
  131.7 9.6 %collective-permute-start.20 = (bf16[160,512]{1,0:T(8,128)(2,1)S(1)}, bf16[160,512]{1,0:T(8,128)(2,1)S(1)}, u32[]{:S(2)}, u32[]{:S(2)}) collective-permute-start(bf16[160,512]{1,0:T(8,128)(2,1)S(1)} %add_convert_fusion), channel_id=1, source_target_pairs={{0,16},{16,32},{32,48},{48,0},{1,17},{17,33},{33,49},{49,1},{2,18}... | collective-permute-start | bytes 491528 | tf_op jit(solution)/shard_map/ppermute | solution.py:198
  131.8 9.6 %collective-permute-start.21 = (bf16[160,512]{1,0:T(8,128)(2,1)S(1)}, bf16[160,512]{1,0:T(8,128)(2,1)S(1)}, u32[]{:S(2)}, u32[]{:S(2)}) collective-permute-start(bf16[160,512]{1,0:T(8,128)(2,1)S(1)} %add_convert_fusion), channel_id=1, source_target_pairs={{0,32},{16,48},{32,0},{48,16},{1,33},{17,49},{33,1},{49,17},{2,34}... | collective-permute-start | bytes 491528 | tf_op jit(solution)/shard_map/ppermute | solution.py:198
  134.3 7.7 %collective-permute-start.22 = (bf16[160,512]{1,0:T(8,128)(2,1)S(1)}, bf16[160,512]{1,0:T(8,128)(2,1)S(1)}, u32[]{:S(2)}, u32[]{:S(2)}) collective-permute-start(bf16[160,512]{1,0:T(8,128)(2,1)S(1)} %add_convert_fusion), channel_id=1, source_target_pairs={{0,48},{16,0},{32,16},{48,32},{1,49},{17,1},{33,17},{49,33},{2,50}... | collective-permute-start | bytes 491528 | tf_op jit(solution)/shard_map/ppermute | solution.py:198
  135.1 8.0 %collective-permute-start.28 = (bf16[160,256]{1,0:T(8,128)(2,1)S(1)}, bf16[160,256]{1,0:T(8,128)(2,1)S(1)}, u32[]{:S(2)}, u32[]{:S(2)}) collective-permute-start(bf16[160,256]{1,0:T(8,128)(2,1)S(1)} %fusion.41), channel_id=1, source_target_pairs={{0,16},{16,32},{32,48},{48,0},{1,17},{17,33},{33,49},{49,1},{2,18}... | collective-permute-start | bytes 245768 | tf_op jit(solution)/shard_map/ppermute | solution.py:198
  136.4 6.7 %collective-permute-start.29 = (bf16[160,256]{1,0:T(8,128)(2,1)S(1)}, bf16[160,256]{1,0:T(8,128)(2,1)}, u32[]{:S(2)}, u32[]{:S(2)}) collective-permute-start(bf16[160,256]{1,0:T(8,128)(2,1)S(1)} %fusion.41), channel_id=1, source_target_pairs={{0,32},{16,48},{32,0},{48,16},{1,33},{17,49},{33,1},{49,17},{2,34}... | collective-permute-start | bytes 245768 | tf_op jit(solution)/shard_map/ppermute | solution.py:198
  141.3 4.5 %collective-permute-start.30 = (bf16[160,256]{1,0:T(8,128)(2,1)S(1)}, bf16[160,256]{1,0:T(8,128)(2,1)}, u32[]{:S(2)}, u32[]{:S(2)}) collective-permute-start(bf16[160,256]{1,0:T(8,128)(2,1)S(1)} %fusion.41), channel_id=1, source_target_pairs={{0,48},{16,0},{32,16},{48,32},{1,49},{17,1},{33,17},{49,33},{2,50}... | collective-permute-start | bytes 245768 | tf_op jit(solution)/shard_map/ppermute | solution.py:198
  148.2 2.2 %copy-start.11 = (f32[1024,768]{1,0:T(8,128)}, f32[1024,768]{1,0:T(8,128)S(1)}, u32[]{:S(2)}) copy-start(f32[1024,768]{1,0:T(8,128)S(1)} %fusion.1) | copy-start | bytes 9437188
  150.4 3.6 %collective-permute-start.31 = (f32[16,32,768]{2,1,0:T(8,128)}, f32[16,32,768]{2,1,0:T(8,128)S(1)}, u32[]{:S(2)}, u32[]{:S(2)}) collective-permute-start(f32[16,32,768]{2,1,0:T(8,128)} %dynamic-slice_bitcast_fusion), channel_id=1, source_target_pairs={{0,1},{1,0},{2,3},{3,2},{4,5},{5,4},{6,7},{7,6},{8,9},{9,8},{10,11... | collective-permute-start | bytes 4718600 | tf_op jit(solution)/shard_map/ppermute | solution.py:198
  (1 other events, 0.7 us)

commit v2 on v1

--- a/solution.py
+++ b/solution.py
@@ -149,6 +149,43 @@
     dkv_send[:, HEAD:] = dvr[KHALF:]
 
 
+def columns_kernel(place_ref, tok, keep, send):
+    o = place_ref[0]
+    ic = place_ref[1]
+    src = lax.broadcasted_iota(jnp.int32, (512, 256), 0)
+    dst = lax.broadcasted_iota(jnp.int32, (512, 256), 1)
+    home = dst // 32 * 64 + dst % 32
+    for out, c in ((keep, ic), (send, 1 - ic)):
+        pick = jnp.where(src == home + c * 32, 1.0, 0.0).astype(bf16)
+        for d in range(N_OUT):
+            base = lax.rem(o + d, N_OUT) * 512
+            for p in range(2):
+                start = pl.multiple_of(base + p * 2048, 512)
+                cols = tok[:, pl.ds(start, 512)]
+                out[d, :, p * 256 : (p + 1) * 256] = dot(cols, pick, NN).astype(bf16)
+
+
+def weights_kernel(keep, got, x1, x2, x3, q0, q1, q2, q3, k0, k1, k2, k3, qo, ko, out, xr, gr):
+    wide = HEADS * HEAD
+    for d in range(N_OUT):
+        rows = slice(d * ROWS, (d + 1) * ROWS)
+        other = slice((N_OUT + d) * ROWS, (N_OUT + d + 1) * ROWS)
+        if d == 0:
+            xr[rows, :] = keep[0]
+            xr[other, :] = got[0]
+        else:
+            x = (x1, x2, x3)[d - 1]
+            xr[rows, :] = x[0]
+            xr[other, :] = x[1]
+        gr[rows, :wide] = (q0, q1, q2, q3)[d][...]
+        gr[rows, wide:] = (k0, k1, k2, k3)[d][...]
+        gr[other, :wide] = qo[d]
+        gr[other, wide:] = ko[d]
+    dw = dot(xr[...], gr[...], TN).astype(bf16)
+    for p in range(16):
+        out[p] = dw[p * 32 : (p + 1) * 32]
+
+
 smem = pl.BlockSpec(memory_space=pltpu.SMEM)
 vmem = pl.BlockSpec(memory_space=pltpu.VMEM)
 params = pltpu.CompilerParams(vmem_limit_bytes=50 * 1024 * 1024)
@@ -194,6 +231,33 @@
     )(ordk, posq, *stats, *qs, *gs, kva, kvb)
 
 
+def columns_call(place, tokens):
+    shape = jax.ShapeDtypeStruct((N_OUT, ROWS, 512), bf16)
+    return pl.pallas_call(
+        columns_kernel,
+        out_shape=(shape, shape),
+        in_specs=[smem, vmem],
+        out_specs=[vmem] * 2,
+        compiler_params=params,
+        name="columns",
+    )(place, tokens)
+
+
+def weights_call(*args):
+    return pl.pallas_call(
+        weights_kernel,
+        out_shape=jax.ShapeDtypeStruct((16, 32, 768), bf16),
+        in_specs=[vmem] * len(args),
+        out_specs=vmem,
+        scratch_shapes=[
+            pltpu.VMEM((2 * N_OUT * ROWS, 512), bf16),
+            pltpu.VMEM((2 * N_OUT * ROWS, 768), bf16),
+        ],
+        compiler_params=params,
+        name="weights",
+    )(*args)
+
+
 def shift(x, axis, d, n):
     return lax.ppermute(x, axis, [(i, (i + d) % n) for i in range(n)])
 
@@ -208,7 +272,6 @@
     dout = grad_out[0]
     o, ix, iy, ic = (lax.axis_index(a) for a in ("outer", "x", "yh", "core"))
 
-    gs = from_behind(dout, "outer", N_OUT)
     kv = jnp.concatenate(
         [
             dot(tokens, w_key, NN).astype(bf16),
@@ -216,12 +279,15 @@
         ],
         axis=1,
     )
-    query = dot(tokens, w_query, NN).astype(bf16)
-
-    kv = jnp.concatenate(from_behind(kv, "yh", 2), axis=0)
+    kv, later, dout = lax.optimization_barrier((kv, tokens, dout))
+    pair = jnp.concatenate(from_behind(kv, "yh", 2), axis=0)
+    query = dot(later, w_query, NN).astype(bf16)
     qs = from_behind(query, "outer", N_OUT)
-    kva = jnp.concatenate(from_behind(kv, "x", N_X), axis=0)
+    gs = from_behind(dout, "outer", N_OUT)
+    keep, send = columns_call(jnp.stack([o, ic]), later)
+    kva = jnp.concatenate(from_behind(pair, "x", N_X), axis=0)
     kvb = shift(kva, "core", 1, 2)
+    got = shift(send, "core", 1, 2)
 
     inner = np.arange(2)[:, None, None, None], np.arange(N_X)[None, :, None, None], np.arange(2)[None, None, :, None]
     step = np.arange(2)[None, None, None, :]
@@ -239,14 +305,13 @@
     posq = ordq * HALF + jnp.arange(HALF, dtype=jnp.int32)
     posq = jnp.broadcast_to(posq, (N_OUT, HEADS, 2, HALF)).reshape(1, ALL_ROWS)
 
+    keep, got, kva = lax.optimization_barrier((keep, got, kva))
+    xs = [
+        shift(jnp.stack([keep[d], got[d]]), "outer", d, N_OUT) for d in range(1, N_OUT)
+    ]
     stats = stats_call(ordk, posq, qs, gs, kva, kvb)
-    columns = tokens.reshape(ROWS, 2, N_OUT, -1)
-    xs = []
-    for d in range(N_OUT):
-        part = lax.dynamic_index_in_dim(columns, (o + d) % N_OUT, axis=2, keepdims=False)
-        part = part.reshape(ROWS, -1)
-        xs.append(part if d == 0 else shift(part, "outer", d, N_OUT))
     all_stats = from_behind(stats, "outer", N_OUT)
+    all_stats, xs = lax.optimization_barrier((all_stats, xs))
     dq0, dq1, dq2, dq3, dkv_keep, dkv_send = grads_call(ordk, posq, all_stats, qs, gs, kva, kvb)
 
     dkv_got = shift(dkv_send, "core", 1, 2)
@@ -263,14 +328,9 @@
     dkv = part[:ROWS] + shift(part[ROWS:].astype(bf16), "yh", 1, 2).astype(f32)
     dkv_all = from_behind(dkv.astype(bf16), "outer", N_OUT)
 
-    grads = jnp.concatenate(
-        [jnp.concatenate(dq_all, axis=0), jnp.concatenate(dkv_all, axis=0)], axis=1
-    )
-    dw = dot(jnp.concatenate(xs, axis=0), grads, TN)
-    dw = dw.reshape(16, 2, -1, dw.shape[1])
-    mine = lax.dynamic_index_in_dim(dw, ic, axis=1, keepdims=False)
-    other = lax.dynamic_index_in_dim(dw, 1 - ic, axis=1, keepdims=False)
-    dw = (mine + shift(other, "core", 1, 2)).astype(bf16)
+    dq_other = shift(jnp.stack(dq_all), "core", 1, 2)
+    dkv_other = shift(jnp.stack(dkv_all), "core", 1, 2)
+    dw = weights_call(keep, got, *xs, *dq_all, *dkv_all, dq_other, dkv_other)
     dw = lax.all_to_all(dw, ("dp", "x", "yh"), 0, 0, tiled=True)
     dw = jnp.sum(dw.astype(f32), axis=0)
     wide = HEADS * HEAD

time: 178 us -> 158 us (0.89)
  starting transfers between devices: 46.9 us -> 38.1 us
  local copies, waits for them, and re-layouts: 19.2 us -> 10.7 us
  Pallas kernels: 34 us -> 40.1 us
  waiting for transfers between devices: 44.3 us -> 38.2 us
  blocking collectives: 20.8 us -> 18.5 us
    dynamic_slice x1 -> x0, local copies, waits for them, and re-layouts: 9.14 us -> none  [per_device(): lax.dynamic_index_in_dim(columns, (o + d) % N_OUT, axis=2, keepdims=False)]
    ppermute x32 -> x34, starting transfers between devices: 46.9 us -> 38.1 us  [shift(): return lax.ppermute(x, axis, [(i, (i + d) % n) for i in range(n)])]
    ppermute x32 -> x34, waiting for transfers between devices: 44.3 us -> 38.2 us  [shift(): return lax.ppermute(x, axis, [(i, (i + d) % n) for i in range(n)])]
    pallas_call x0 -> x2, Pallas kernels: none -> 5.97 us  [the longest x1 3.72 us: weights_call(): pl.pallas_call(weights_kernel, out_shape=jax.ShapeDtypeStruct((16, 32, 76...]
    another operation x1 -> x0, local copies, waits for them, and re-layouts: 3.22 us -> none  [per_device(): columns = tokens.reshape(ROWS, 2, N_OUT, -1)]
    unnamed x41 -> x33, local copies, waits for them, and re-layouts: 3.78 us -> 6.92 us
    another operation x0 -> x6, other arithmetic: none -> 2.48 us  [the longest x3 2.28 us: per_device(): jnp.stack([keep[d], got[d]])]
    all_to_all x1, blocking collectives: 20.8 us -> 18.5 us  [per_device(): dw = lax.all_to_all(dw, ('dp', 'x', 'yh'), 0, 0, tiled=True)]
  transfers between devices with their start and end apart: 32 -> 34, of which waited for: 17 -> 17; matrix products, arithmetic and copies ran while one was open for 8% -> 5% of each run, Pallas kernels for 0% -> 9%
where the time goes in v2:
time: 158 us
  Pallas kernels  40.1 us (25%)
  waiting for transfers between devices  38.2 us (24%)
  starting transfers between devices  38.1 us (24%)
  blocking collectives  18.5 us (12%)
  local copies, waits for them, and re-layouts  10.7 us (7%)
  other arithmetic  5.74 us (4%)
  matrix products  5.32 us (3%)
    ppermute x34, waiting for transfers between devices, shift(): return lax.ppermute(x, axis, [(i, (i + d) % n) for i in range(n)])  38.2 us
    ppermute x34, starting transfers between devices, shift(): return lax.ppermute(x, axis, [(i, (i + d) % n) for i in range(n)])  38.1 us
    pallas_call x1, Pallas kernels, grads_call(): pl.pallas_call(grads_kernel, out_shape=(jax.ShapeDtypeStruct((ROWS, wide)...  22.8 us
    all_to_all x1, blocking collectives, per_device(): dw = lax.all_to_all(dw, ('dp', 'x', 'yh'), 0, 0, tiled=True)  18.5 us
    pallas_call x1, Pallas kernels, stats_call(): pl.pallas_call(stats_kernel, out_shape=jax.ShapeDtypeStruct((3, ALL_ROWS)...  11.3 us
    unnamed x33, local copies, waits for them, and re-layouts  6.92 us
    dot_general x3, matrix products, dot(): return lax.dot_general(a, b, dims, preferred_element_type=f32)  5.32 us
    pallas_call x1, Pallas kernels, weights_call(): pl.pallas_call(weights_kernel, out_shape=jax.ShapeDtypeStruct((16, 32, 76...  3.72 us
  transfers between devices with their start and end apart: 34, of which 17 were waited for; matrix products, arithmetic and copies ran while one was open for 5% of the time, Pallas kernels for 9%

profile of v2, /device:TPU:0, one launch (start us, length us, event | category | flops | bytes accessed | tf_op | source)
XLA Modules:
  0.0 157.6 jit_solution(14349556454413898433)
XLA Ops:
  0.7 1.2 copy-done
  1.9 1.8 %convolution_convert_fusion.2 = bf16[160,128]{1,0:T(8,128)(2,1)S(1)} fusion(bf16[4096,128]{1,0:T(8,128)(2,1)S(1)} %copy-done, bf16[1,160,4096]{2,1,0:T(8,128)(2,1)} %param.12), kind=kOutput, calls=%fused_computation.3 | convolution fusion | flops 167792640 | bytes 2400256 | tf_op jit(solution)/shard_map/dot_general | solution.py:35
  4.8 3.0 %convolution_convert_fusion.q0 = bf16[160,512]{1,0:T(8,128)(2,1)S(1)} fusion(bf16[160,4096]{1,0:T(8,128)(2,1)S(1)} %bitcast.27, bf16[4096,512]{1,0:T(8,128)(2,1)} %param.14), kind=kOutput, calls=%fused_computation.1 | convolution fusion | flops 671170560 | bytes 5668864 | tf_op jit(solution)/shard_map/dot_general | solution.py:35
  7.9 4.2 %collective-permute-start.7 = (bf16[160,512]{1,0:T(8,128)(2,1)S(1)}, bf16[160,512]{1,0:T(8,128)(2,1)S(1)}, u32[]{:S(2)}, u32[]{:S(2)}) collective-permute-start(bf16[160,512]{1,0:T(8,128)(2,1)S(1)} %convolution_convert_fusion.q0), channel_id=1, source_target_pairs={{0,48},{16,0},{32,16},{48,32},{1,49},{17,1},{33,17},{49,33},{2,50}... | collective-permute-start | bytes 491528 | tf_op jit(solution)/shard_map/ppermute | solution.py:262
  12.1 3.2 %collective-permute-start.1 = (bf16[160,256]{1,0:T(8,128)(2,1)}, bf16[160,256]{1,0:T(8,128)(2,1)}, u32[]{:S(2)}, u32[]{:S(2)}) collective-permute-start(bf16[160,256]{1,0:T(8,128)(2,1)} %pad_maximum_fusion.5), channel_id=1, source_target_pairs={{0,2},{2,0},{1,3},{3,1},{4,6},{6,4},{5,7},{7,5},{8,10},{10,8},{9,1... | collective-permute-start | bytes 245768 | tf_op jit(solution)/shard_map/ppermute | solution.py:262
  15.4 2.3 %columns.1 = (bf16[4,160,512]{2,1,0:T(8,128)(2,1)S(1)}, bf16[4,160,512]{2,1,0:T(8,128)(2,1)}) custom-call(s32[2]{0:T(128)S(1)} %pad_add_fusion.place_ref, bf16[160,4096]{1,0:T(8,128)(2,1)S(1)} %bitcast.28), custom_call_target="tpu_custom_call" | custom-call | tf_op jit(solution)/shard_map/columns/pallas_call | solution.py:236
  17.7 0.9 constant_dynamic-update-slice_fusion.1
  19.2 0.9 constant_dynamic-update-slice_fusion
  20.1 3.1 %collective-permute-start.3 = (bf16[320,256]{1,0:T(8,128)(2,1)S(1)}, bf16[320,256]{1,0:T(8,128)(2,1)S(1)}, u32[]{:S(2)}, u32[]{:S(2)}) collective-permute-start(bf16[320,256]{1,0:T(8,128)(2,1)S(1)} %get-tuple-element.58), channel_id=1, source_target_pairs={{0,8},{4,12},{8,0},{12,4},{1,9},{5,13},{9,1},{13,5},{2,10},{6,14},... | collective-permute-start | bytes 491528 | tf_op jit(solution)/shard_map/ppermute | solution.py:262
  23.9 7.9 %collective-permute-done.2 = bf16[320,256]{1,0:T(8,128)(2,1)S(1)} collective-permute-done((bf16[320,256]{1,0:T(8,128)(2,1)S(1)}, bf16[320,256]{1,0:T(8,128)(2,1)S(1)}, u32[]{:S(2)}, u32[]{:S(2)}) %collective-permute-start.2) | collective-permute-done | bytes 163872 | tf_op jit(solution)/shard_map/ppermute | solution.py:262
  32.4 1.3 collective-permute-start.5
  33.8 4.2 %collective-permute-done.4 = bf16[320,256]{1,0:T(8,128)(2,1)S(1)} collective-permute-done((bf16[320,256]{1,0:T(8,128)(2,1)S(1)}, bf16[320,256]{1,0:T(8,128)(2,1)S(1)}, u32[]{:S(2)}, u32[]{:S(2)}) %collective-permute-start.4) | collective-permute-done | bytes 163872 | tf_op jit(solution)/shard_map/ppermute | solution.py:262
  38.8 1.2 fusion.23
  40.7 2.9 %collective-permute-start.9 = (bf16[160,512]{1,0:T(8,128)(2,1)S(1)}, bf16[160,512]{1,0:T(8,128)(2,1)S(1)}, u32[]{:S(2)}, u32[]{:S(2)}) collective-permute-start(bf16[160,512]{1,0:T(8,128)(2,1)S(1)} %bitcast.35), channel_id=1, source_target_pairs={{0,32},{16,48},{32,0},{48,16},{1,33},{17,49},{33,1},{49,17},{2,34}... | collective-permute-start | bytes 491528 | tf_op jit(solution)/shard_map/ppermute | solution.py:262
  43.6 0.8 pad_maximum_fusion.2
  45.1 1.4 collective-permute-start.8
  47.9 3.3 %collective-permute-start.16 = (bf16[2,160,512]{2,1,0:T(8,128)(2,1)}, bf16[2,160,512]{2,1,0:T(8,128)(2,1)}, u32[]{:S(2)}, u32[]{:S(2)}) collective-permute-start(bf16[2,160,512]{2,1,0:T(8,128)(2,1)} %pad_maximum_fusion.2), channel_id=1, source_target_pairs={{0,32},{16,48},{32,0},{48,16},{1,33},{17,49},{33,1},{49,17},{2,34}... | collective-permute-start | bytes 983048 | tf_op jit(solution)/shard_map/ppermute | solution.py:262
  51.8 1.1 collective-permute-start.17
  53.5 0.9 copy-done.4
  54.4 0.9 copy-done.6
  55.3 0.9 copy-done.8
  56.2 11.3 %stats.1.s0 = f32[3,2560]{1,0:T(4,128)S(1)} custom-call(s32[32]{0:T(128)S(1)} %select_reduce_fusion.ordk_ref, s32[1,2560]{1,0:T(1,128)S(1)} %reshape.114.posq_ref, bf16[160,512]{1,0:T(8,128)(2,1)S(1)} %convolution_convert_fusion.q0, bf16[160,512]{1,0:T(8,128)(2,1)S(1)} %copy-done.4, bf16[160,512]{1,0:T(8,128)(2,1)} %collective-permute-done.6.q2, ...), custom_call_target="tpu_custom_call" | custom-call | tf_op jit(solution)/shard_map/stats/pallas_call | solution.py:195
  68.0 2.6 %collective-permute-start.13 = (f32[3,2560]{1,0:T(4,128)S(1)}, f32[3,2560]{1,0:T(4,128)S(1)}, u32[]{:S(2)}, u32[]{:S(2)}) collective-permute-start(f32[3,2560]{1,0:T(4,128)S(1)} %stats.1.s0), channel_id=1, source_target_pairs={{0,32},{16,48},{32,0},{48,16},{1,33},{17,49},{33,1},{49,17},{2,34}... | collective-permute-start | bytes 92168 | tf_op jit(solution)/shard_map/ppermute | solution.py:262
  70.6 1.4 collective-permute-done.14.s3
  72.5 1.1 collective-permute-done.13.s2
  73.6 3.6 %collective-permute-done.12.s1 = f32[3,2560]{1,0:T(4,128)S(1)} collective-permute-done((f32[3,2560]{1,0:T(4,128)S(1)}, f32[3,2560]{1,0:T(4,128)S(1)}, u32[]{:S(2)}, u32[]{:S(2)}) %collective-permute-start.12) | collective-permute-done | bytes 30752 | tf_op jit(solution)/shard_map/ppermute | solution.py:262
  77.2 22.8 %grads.1 = (f32[160,512]{1,0:T(8,128)S(1)}, bf16[160,512]{1,0:T(8,128)(2,1)S(1)}, bf16[160,512]{1,0:T(8,128)(2,1)S(1)}, bf16[160,512]{1,0:T(8,128)(2,1)S(1)}, f32[1280,256]{1,0:T(8,128)}, /*index=5*/f32[1280,256]{1,0:T(8,128)}) custom-call(s32[32]{0:T(128)S(1)} %select_reduce_fusion.ordk_ref, s32[1,2560]{1,0:T(1,128)S(1)} %reshape.114.posq_ref, ...), custom_call_target="tpu_custom_call" | custom-call | tf_op jit(solution)/shard_map/grads/pallas_call | solution.py:208
  100.0 1.3 collective-permute-start.19
  102.1 1.2 collective-permute-done.24
  103.3 1.5 fusion.21
  104.8 1.6 collective-permute-start.25
  107.0 1.8 %collective-permute-start.26 = (bf16[320,256]{1,0:T(8,128)(2,1)S(1)}, bf16[320,256]{1,0:T(8,128)(2,1)S(1)}, u32[]{:S(2)}, u32[]{:S(2)}) collective-permute-start(bf16[320,256]{1,0:T(8,128)(2,1)S(1)} %get-tuple-element.49), channel_id=1, source_target_pairs={{0,8},{4,12},{8,0},{12,4},{1,9},{5,13},{9,1},{13,5},{2,10},{6,14},... | collective-permute-start | bytes 491528 | tf_op jit(solution)/shard_map/ppermute | solution.py:262
  108.9 2.8 %collective-permute-done.20 = bf16[160,512]{1,0:T(8,128)(2,1)S(1)} collective-permute-done((bf16[160,512]{1,0:T(8,128)(2,1)S(1)}, bf16[160,512]{1,0:T(8,128)(2,1)S(1)}, u32[]{:S(2)}, u32[]{:S(2)}) %collective-permute-start.20) | collective-permute-done | bytes 163872 | tf_op jit(solution)/shard_map/ppermute | solution.py:262
  111.8 1.2 collective-permute-start.23
  113.5 0.8 collective-permute-start.21
  114.3 2.8 %collective-permute-done.27 = bf16[320,256]{1,0:T(8,128)(2,1)S(1)} collective-permute-done((bf16[320,256]{1,0:T(8,128)(2,1)S(1)}, bf16[320,256]{1,0:T(8,128)(2,1)S(1)}, u32[]{:S(2)}, u32[]{:S(2)}) %collective-permute-start.27) | collective-permute-done | bytes 163872 | tf_op jit(solution)/shard_map/ppermute | solution.py:262
  117.3 1.6 %collective-permute-done.23.q3 = bf16[160,512]{1,0:T(8,128)(2,1)S(1)} collective-permute-done((bf16[160,512]{1,0:T(8,128)(2,1)S(1)}, bf16[160,512]{1,0:T(8,128)(2,1)S(1)}, u32[]{:S(2)}, u32[]{:S(2)}) %collective-permute-start.23) | collective-permute-done | bytes 163872 | tf_op jit(solution)/shard_map/ppermute | solution.py:262
  118.9 2.7 %collective-permute-done.22.q2 = bf16[160,512]{1,0:T(8,128)(2,1)S(1)} collective-permute-done((bf16[160,512]{1,0:T(8,128)(2,1)S(1)}, bf16[160,512]{1,0:T(8,128)(2,1)S(1)}, u32[]{:S(2)}, u32[]{:S(2)}) %collective-permute-start.22) | collective-permute-done | bytes 163872 | tf_op jit(solution)/shard_map/ppermute | solution.py:262
  121.6 1.9 %collective-permute-done.21.q1 = bf16[160,512]{1,0:T(8,128)(2,1)S(1)} collective-permute-done((bf16[160,512]{1,0:T(8,128)(2,1)S(1)}, bf16[160,512]{1,0:T(8,128)(2,1)S(1)}, u32[]{:S(2)}, u32[]{:S(2)}) %collective-permute-start.21) | collective-permute-done | bytes 163872 | tf_op jit(solution)/shard_map/ppermute | solution.py:262
  123.8 0.8 collective-permute-start.31
  124.6 1.3 collective-permute-start.30
  125.9 1.3 collective-permute-start.29
  127.2 1.9 %collective-permute-done.31.k3 = bf16[160,256]{1,0:T(8,128)(2,1)S(1)} collective-permute-done((bf16[160,256]{1,0:T(8,128)(2,1)S(1)}, bf16[160,256]{1,0:T(8,128)(2,1)S(1)}, u32[]{:S(2)}, u32[]{:S(2)}) %collective-permute-start.31) | collective-permute-done | bytes 81952 | tf_op jit(solution)/shard_map/ppermute | solution.py:262
  129.1 1.5 collective-permute-done.30.k2
  130.6 1.7 %collective-permute-done.29.k1 = bf16[160,256]{1,0:T(8,128)(2,1)S(1)} collective-permute-done((bf16[160,256]{1,0:T(8,128)(2,1)S(1)}, bf16[160,256]{1,0:T(8,128)(2,1)S(1)}, u32[]{:S(2)}, u32[]{:S(2)}) %collective-permute-start.29) | collective-permute-done | bytes 81952 | tf_op jit(solution)/shard_map/ppermute | solution.py:262
  132.4 1.6 %collective-permute-done.33.ko = bf16[4,160,256]{2,1,0:T(8,128)(2,1)S(1)} collective-permute-done((bf16[4,160,256]{2,1,0:T(8,128)(2,1)S(1)}, bf16[4,160,256]{2,1,0:T(8,128)(2,1)S(1)}, u32[]{:S(2)}, u32[]{:S(2)}) %collective-permute-start.33) | collective-permute-done | bytes 327712 | tf_op jit(solution)/shard_map/ppermute | solution.py:262
  134.0 3.7 %weights.1 = bf16[16,32,768]{2,1,0:T(8,128)(2,1)} custom-call(bf16[4,160,512]{2,1,0:T(8,128)(2,1)S(1)} %get-tuple-element.28.keep, bf16[4,160,512]{2,1,0:T(8,128)(2,1)} %collective-permute-done.got, bf16[2,160,512]{2,1,0:T(8,128)(2,1)} %collective-permute-done.15.x1, bf16[2,160,512]{2,1,0:T(8,128)(2,1)} %collective-permute-done.16.x2, ...), custom_call_target="tpu_custom_call" | custom-call | tf_op jit(solution)/shard_map/weights/pallas_call | solution.py:247
  137.7 18.5 %all_to_all.5 = bf16[16,32,768]{2,1,0:T(8,128)(2,1)S(1)} all-to-all(bf16[16,32,768]{2,1,0:T(8,128)(2,1)} %weights.1), channel_id=1, replica_groups=mesh['dp'=2,'outer'=4,'x'=4,'yh'=2,'core'=2] {'dp','x','yh'}, dimensions={0} | all-to-all | bytes 1572864 | tf_op jit(solution)/shard_map/all_to_all | solution.py:334
  (97 shorter events, 12.7 us)
Async XLA Ops:
  0.6 1.2 copy-start
  0.6 3.0 %copy-start.1 = (bf16[1,160,4096]{2,1,0:T(8,128)(2,1)S(1)}, bf16[1,160,4096]{2,1,0:T(8,128)(2,1)}, u32[]{:S(2)}) copy-start(bf16[1,160,4096]{2,1,0:T(8,128)(2,1)} %param.12) | copy-start | bytes 3932164
  0.7 3.0 %copy-start.9 = (bf16[4096,128]{1,0:T(8,128)(2,1)S(1)}, bf16[4096,128]{1,0:T(8,128)(2,1)}, u32[]{:S(2)}) copy-start(bf16[4096,128]{1,0:T(8,128)(2,1)} %param.16) | copy-start | bytes 3145732
  7.9 10.7 %copy-start.14 = (s32[1,1,2,1]{2,3,1,0:T(1,128)S(1)}, s32[1,1,2,1]{2,3,1,0:T(1,128)}, u32[]{:S(2)}) copy-start(s32[1,1,2,1]{2,3,1,0:T(1,128)} %constant.92) | copy-start | bytes 28
  7.9 10.7 %copy-start.13 = (s32[2,1,1,1]{0,3,2,1:T(1,128)S(1)}, s32[2,1,1,1]{0,3,2,1:T(1,128)}, u32[]{:S(2)}) copy-start(s32[2,1,1,1]{0,3,2,1:T(1,128)} %constant.93) | copy-start | bytes 28
  7.9 10.9 %copy-start.11 = (s32[1,4,1,1]{1,3,2,0:T(1,128)S(1)}, s32[1,4,1,1]{1,3,2,0:T(1,128)}, u32[]{:S(2)}) copy-start(s32[1,4,1,1]{1,3,2,0:T(1,128)} %constant.91) | copy-start | bytes 52
  7.9 11.1 %copy-start.12 = (s32[1,128]{1,0:T(1,128)S(1)}, s32[1,128]{1,0:T(1,128)}, u32[]{:S(2)}) copy-start(s32[1,128]{1,0:T(1,128)} %param.13) | copy-start | bytes 1540
  7.9 30.1 %copy-start.2 = (bf16[1,160,512]{2,1,0:T(8,128)(2,1)S(1)}, bf16[1,160,512]{2,1,0:T(8,128)(2,1)}, u32[]{:S(2)}) copy-start(bf16[1,160,512]{2,1,0:T(8,128)(2,1)} %param.17) | copy-start | bytes 491524
  7.9 32.8 %collective-permute-start.7 = (bf16[160,512]{1,0:T(8,128)(2,1)S(1)}, bf16[160,512]{1,0:T(8,128)(2,1)S(1)}, u32[]{:S(2)}, u32[]{:S(2)}) collective-permute-start(bf16[160,512]{1,0:T(8,128)(2,1)S(1)} %convolution_convert_fusion.q0), channel_id=1, source_target_pairs={{0,48},{16,0},{32,16},{48,32},{1,49},{17,1},{33,17},{49,33},{2,50}... | collective-permute-start | bytes 491528 | tf_op jit(solution)/shard_map/ppermute | solution.py:262
  12.1 33.0 %collective-permute-start.6 = (bf16[160,512]{1,0:T(8,128)(2,1)S(1)}, bf16[160,512]{1,0:T(8,128)(2,1)}, u32[]{:S(2)}, u32[]{:S(2)}) collective-permute-start(bf16[160,512]{1,0:T(8,128)(2,1)S(1)} %convolution_convert_fusion.q0), channel_id=1, source_target_pairs={{0,32},{16,48},{32,0},{48,16},{1,33},{17,49},{33,1},{49,17},{2,34}... | collective-permute-start | bytes 491528 | tf_op jit(solution)/shard_map/ppermute | solution.py:262
  12.1 7.1 %collective-permute-start.1 = (bf16[160,256]{1,0:T(8,128)(2,1)}, bf16[160,256]{1,0:T(8,128)(2,1)}, u32[]{:S(2)}, u32[]{:S(2)}) collective-permute-start(bf16[160,256]{1,0:T(8,128)(2,1)} %pad_maximum_fusion.5), channel_id=1, source_target_pairs={{0,2},{2,0},{1,3},{3,1},{4,6},{6,4},{5,7},{7,5},{8,10},{10,8},{9,1... | collective-permute-start | bytes 245768 | tf_op jit(solution)/shard_map/ppermute | solution.py:262
  17.7 21.0 %collective-permute-start = (bf16[4,160,512]{2,1,0:T(8,128)(2,1)}, bf16[4,160,512]{2,1,0:T(8,128)(2,1)}, u32[]{:S(2)}, u32[]{:S(2)}) collective-permute-start(bf16[4,160,512]{2,1,0:T(8,128)(2,1)} %get-tuple-element.26), channel_id=1, source_target_pairs={{0,1},{1,0},{2,3},{3,2},{4,5},{5,4},{6,7},{7,6},{8,9},{9,8},{10,11... | collective-permute-start | bytes 1966088 | tf_op jit(solution)/shard_map/ppermute | solution.py:262
  20.1 12.3 %collective-permute-start.3 = (bf16[320,256]{1,0:T(8,128)(2,1)S(1)}, bf16[320,256]{1,0:T(8,128)(2,1)S(1)}, u32[]{:S(2)}, u32[]{:S(2)}) collective-permute-start(bf16[320,256]{1,0:T(8,128)(2,1)S(1)} %get-tuple-element.58), channel_id=1, source_target_pairs={{0,8},{4,12},{8,0},{12,4},{1,9},{5,13},{9,1},{13,5},{2,10},{6,14},... | collective-permute-start | bytes 491528 | tf_op jit(solution)/shard_map/ppermute | solution.py:262
  23.2 8.6 %collective-permute-start.2 = (bf16[320,256]{1,0:T(8,128)(2,1)S(1)}, bf16[320,256]{1,0:T(8,128)(2,1)S(1)}, u32[]{:S(2)}, u32[]{:S(2)}) collective-permute-start(bf16[320,256]{1,0:T(8,128)(2,1)S(1)} %get-tuple-element.58), channel_id=1, source_target_pairs={{0,4},{4,8},{8,12},{12,0},{1,5},{5,9},{9,13},{13,1},{2,6},{6,10},{... | collective-permute-start | bytes 491528 | tf_op jit(solution)/shard_map/ppermute | solution.py:262
  31.8 6.1 %collective-permute-start.4 = (bf16[320,256]{1,0:T(8,128)(2,1)S(1)}, bf16[320,256]{1,0:T(8,128)(2,1)S(1)}, u32[]{:S(2)}, u32[]{:S(2)}) collective-permute-start(bf16[320,256]{1,0:T(8,128)(2,1)S(1)} %get-tuple-element.58), channel_id=1, source_target_pairs={{0,12},{4,0},{8,4},{12,8},{1,13},{5,1},{9,5},{13,9},{2,14},{6,2},{... | collective-permute-start | bytes 491528 | tf_op jit(solution)/shard_map/ppermute | solution.py:262
  32.4 14.1 %collective-permute-start.5 = (bf16[160,512]{1,0:T(8,128)(2,1)S(1)}, bf16[160,512]{1,0:T(8,128)(2,1)S(1)}, u32[]{:S(2)}, u32[]{:S(2)}) collective-permute-start(bf16[160,512]{1,0:T(8,128)(2,1)S(1)} %convolution_convert_fusion.q0), channel_id=1, source_target_pairs={{0,16},{16,32},{32,48},{48,0},{1,17},{17,33},{33,49},{49,1},{2,18}... | collective-permute-start | bytes 491528 | tf_op jit(solution)/shard_map/ppermute | solution.py:262
  38.0 9.2 %collective-permute-start.10 = (bf16[160,512]{1,0:T(8,128)(2,1)S(1)}, bf16[160,512]{1,0:T(8,128)(2,1)S(1)}, u32[]{:S(2)}, u32[]{:S(2)}) collective-permute-start(bf16[160,512]{1,0:T(8,128)(2,1)S(1)} %bitcast.34), channel_id=1, source_target_pairs={{0,48},{16,0},{32,16},{48,32},{1,49},{17,1},{33,17},{49,33},{2,50}... | collective-permute-start | bytes 491528 | tf_op jit(solution)/shard_map/ppermute | solution.py:262
  38.7 14.8 %collective-permute-start.11 = (bf16[1280,256]{1,0:T(8,128)(2,1)S(1)}, bf16[1280,256]{1,0:T(8,128)(2,1)S(1)}, u32[]{:S(2)}, u32[]{:S(2)}) collective-permute-start(bf16[1280,256]{1,0:T(8,128)(2,1)S(1)} %constant_dynamic-update-slice_fusion.2.kva), channel_id=1, source_target_pairs={{0,1},{1,0},{2,3},{3,2},{4,5},{5,4},{6,7},{7,6},{8,9},{9,8},{10,11... | collective-permute-start | bytes 1966088 | tf_op jit(solution)/shard_map/ppermute | solution.py:262
  40.7 10.4 %collective-permute-start.9 = (bf16[160,512]{1,0:T(8,128)(2,1)S(1)}, bf16[160,512]{1,0:T(8,128)(2,1)S(1)}, u32[]{:S(2)}, u32[]{:S(2)}) collective-permute-start(bf16[160,512]{1,0:T(8,128)(2,1)S(1)} %bitcast.35), channel_id=1, source_target_pairs={{0,32},{16,48},{32,0},{48,16},{1,33},{17,49},{33,1},{49,17},{2,34}... | collective-permute-start | bytes 491528 | tf_op jit(solution)/shard_map/ppermute | solution.py:262
  45.1 8.4 %collective-permute-start.8 = (bf16[160,512]{1,0:T(8,128)(2,1)S(1)}, bf16[160,512]{1,0:T(8,128)(2,1)}, u32[]{:S(2)}, u32[]{:S(2)}) collective-permute-start(bf16[160,512]{1,0:T(8,128)(2,1)S(1)} %bitcast.36), channel_id=1, source_target_pairs={{0,16},{16,32},{32,48},{48,0},{1,17},{17,33},{33,49},{49,1},{2,18}... | collective-permute-start | bytes 491528 | tf_op jit(solution)/shard_map/ppermute | solution.py:262
  47.2 30.0 %collective-permute-start.15 = (bf16[2,160,512]{2,1,0:T(8,128)(2,1)}, bf16[2,160,512]{2,1,0:T(8,128)(2,1)}, u32[]{:S(2)}, u32[]{:S(2)}) collective-permute-start(bf16[2,160,512]{2,1,0:T(8,128)(2,1)} %pad_maximum_fusion.1), channel_id=1, source_target_pairs={{0,16},{16,32},{32,48},{48,0},{1,17},{17,33},{33,49},{49,1},{2,18}... | collective-permute-start | bytes 983048 | tf_op jit(solution)/shard_map/ppermute | solution.py:262
  47.2 0.7 copy-start.5
  47.9 29.4 %collective-permute-start.16 = (bf16[2,160,512]{2,1,0:T(8,128)(2,1)}, bf16[2,160,512]{2,1,0:T(8,128)(2,1)}, u32[]{:S(2)}, u32[]{:S(2)}) collective-permute-start(bf16[2,160,512]{2,1,0:T(8,128)(2,1)} %pad_maximum_fusion.2), channel_id=1, source_target_pairs={{0,32},{16,48},{32,0},{48,16},{1,33},{17,49},{33,1},{49,17},{2,34}... | collective-permute-start | bytes 983048 | tf_op jit(solution)/shard_map/ppermute | solution.py:262
  51.1 0.7 copy-start.7
  51.8 25.4 %collective-permute-start.17 = (bf16[2,160,512]{2,1,0:T(8,128)(2,1)}, bf16[2,160,512]{2,1,0:T(8,128)(2,1)}, u32[]{:S(2)}, u32[]{:S(2)}) collective-permute-start(bf16[2,160,512]{2,1,0:T(8,128)(2,1)} %pad_maximum_fusion.3), channel_id=1, source_target_pairs={{0,48},{16,0},{32,16},{48,32},{1,49},{17,1},{33,17},{49,33},{2,50}... | collective-permute-start | bytes 983048 | tf_op jit(solution)/shard_map/ppermute | solution.py:262
  53.5 0.9 copy-start.4
  54.4 0.9 copy-start.6
  55.3 0.9 copy-start.8
  67.6 4.5 %collective-permute-start.14 = (f32[3,2560]{1,0:T(4,128)S(1)}, f32[3,2560]{1,0:T(4,128)S(1)}, u32[]{:S(2)}, u32[]{:S(2)}) collective-permute-start(f32[3,2560]{1,0:T(4,128)S(1)} %stats.1.s0), channel_id=1, source_target_pairs={{0,48},{16,0},{32,16},{48,32},{1,49},{17,1},{33,17},{49,33},{2,50}... | collective-permute-start | bytes 92168 | tf_op jit(solution)/shard_map/ppermute | solution.py:262
  68.0 5.6 %collective-permute-start.13 = (f32[3,2560]{1,0:T(4,128)S(1)}, f32[3,2560]{1,0:T(4,128)S(1)}, u32[]{:S(2)}, u32[]{:S(2)}) collective-permute-start(f32[3,2560]{1,0:T(4,128)S(1)} %stats.1.s0), channel_id=1, source_target_pairs={{0,32},{16,48},{32,0},{48,16},{1,33},{17,49},{33,1},{49,17},{2,34}... | collective-permute-start | bytes 92168 | tf_op jit(solution)/shard_map/ppermute | solution.py:262
  72.0 5.2 %collective-permute-start.12 = (f32[3,2560]{1,0:T(4,128)S(1)}, f32[3,2560]{1,0:T(4,128)S(1)}, u32[]{:S(2)}, u32[]{:S(2)}) collective-permute-start(f32[3,2560]{1,0:T(4,128)S(1)} %stats.1.s0), channel_id=1, source_target_pairs={{0,16},{16,32},{32,48},{48,0},{1,17},{17,33},{33,49},{49,1},{2,18}... | collective-permute-start | bytes 92168 | tf_op jit(solution)/shard_map/ppermute | solution.py:262
  100.0 3.2 %collective-permute-start.24 = (f32[1280,256]{1,0:T(8,128)}, f32[1280,256]{1,0:T(8,128)S(1)}, u32[]{:S(2)}, u32[]{:S(2)}) collective-permute-start(f32[1280,256]{1,0:T(8,128)} %get-tuple-element.44), channel_id=1, source_target_pairs={{0,1},{1,0},{2,3},{3,2},{4,5},{5,4},{6,7},{7,6},{8,9},{9,8},{10,11... | collective-permute-start | bytes 3932168 | tf_op jit(solution)/shard_map/ppermute | solution.py:262
  100.0 7.0 %collective-permute-start.18 = (bf16[160,512]{1,0:T(8,128)(2,1)S(1)}, bf16[160,512]{1,0:T(8,128)(2,1)S(1)}, u32[]{:S(2)}, u32[]{:S(2)}) collective-permute-start(bf16[160,512]{1,0:T(8,128)(2,1)S(1)} %get-tuple-element.40), channel_id=1, source_target_pairs={{0,48},{16,0},{32,16},{48,32},{1,49},{17,1},{33,17},{49,33},{2,50}... | collective-permute-start | bytes 491528 | tf_op jit(solution)/shard_map/ppermute | solution.py:262
  100.0 8.8 %collective-permute-start.19 = (bf16[160,512]{1,0:T(8,128)(2,1)S(1)}, bf16[160,512]{1,0:T(8,128)(2,1)S(1)}, u32[]{:S(2)}, u32[]{:S(2)}) collective-permute-start(bf16[160,512]{1,0:T(8,128)(2,1)S(1)} %get-tuple-element.41), channel_id=1, source_target_pairs={{0,32},{16,48},{32,0},{48,16},{1,33},{17,49},{33,1},{49,17},{2,34}... | collective-permute-start | bytes 491528 | tf_op jit(solution)/shard_map/ppermute | solution.py:262
  101.4 10.3 %collective-permute-start.20 = (bf16[160,512]{1,0:T(8,128)(2,1)S(1)}, bf16[160,512]{1,0:T(8,128)(2,1)S(1)}, u32[]{:S(2)}, u32[]{:S(2)}) collective-permute-start(bf16[160,512]{1,0:T(8,128)(2,1)S(1)} %get-tuple-element.42), channel_id=1, source_target_pairs={{0,16},{16,32},{32,48},{48,0},{1,17},{17,33},{33,49},{49,1},{2,18}... | collective-permute-start | bytes 491528 | tf_op jit(solution)/shard_map/ppermute | solution.py:262
  104.8 8.6 %collective-permute-start.25 = (bf16[320,256]{1,0:T(8,128)(2,1)S(1)}, bf16[320,256]{1,0:T(8,128)(2,1)S(1)}, u32[]{:S(2)}, u32[]{:S(2)}) collective-permute-start(bf16[320,256]{1,0:T(8,128)(2,1)S(1)} %get-tuple-element.47), channel_id=1, source_target_pairs={{0,12},{4,0},{8,4},{12,8},{1,13},{5,1},{9,5},{13,9},{2,14},{6,2},{... | collective-permute-start | bytes 491528 | tf_op jit(solution)/shard_map/ppermute | solution.py:262
  106.4 10.7 %collective-permute-start.27 = (bf16[320,256]{1,0:T(8,128)(2,1)S(1)}, bf16[320,256]{1,0:T(8,128)(2,1)S(1)}, u32[]{:S(2)}, u32[]{:S(2)}) collective-permute-start(bf16[320,256]{1,0:T(8,128)(2,1)S(1)} %get-tuple-element.48), channel_id=1, source_target_pairs={{0,4},{4,8},{8,12},{12,0},{1,5},{5,9},{9,13},{13,1},{2,6},{6,10},{... | collective-permute-start | bytes 491528 | tf_op jit(solution)/shard_map/ppermute | solution.py:262
  107.0 10.1 %collective-permute-start.26 = (bf16[320,256]{1,0:T(8,128)(2,1)S(1)}, bf16[320,256]{1,0:T(8,128)(2,1)S(1)}, u32[]{:S(2)}, u32[]{:S(2)}) collective-permute-start(bf16[320,256]{1,0:T(8,128)(2,1)S(1)} %get-tuple-element.49), channel_id=1, source_target_pairs={{0,8},{4,12},{8,0},{12,4},{1,9},{5,13},{9,1},{13,5},{2,10},{6,14},... | collective-permute-start | bytes 491528 | tf_op jit(solution)/shard_map/ppermute | solution.py:262
  111.8 7.1 %collective-permute-start.23 = (bf16[160,512]{1,0:T(8,128)(2,1)S(1)}, bf16[160,512]{1,0:T(8,128)(2,1)S(1)}, u32[]{:S(2)}, u32[]{:S(2)}) collective-permute-start(bf16[160,512]{1,0:T(8,128)(2,1)S(1)} %add_convert_fusion.q0), channel_id=1, source_target_pairs={{0,48},{16,0},{32,16},{48,32},{1,49},{17,1},{33,17},{49,33},{2,50}... | collective-permute-start | bytes 491528 | tf_op jit(solution)/shard_map/ppermute | solution.py:262
  113.0 8.7 %collective-permute-start.22 = (bf16[160,512]{1,0:T(8,128)(2,1)S(1)}, bf16[160,512]{1,0:T(8,128)(2,1)S(1)}, u32[]{:S(2)}, u32[]{:S(2)}) collective-permute-start(bf16[160,512]{1,0:T(8,128)(2,1)S(1)} %add_convert_fusion.q0), channel_id=1, source_target_pairs={{0,32},{16,48},{32,0},{48,16},{1,33},{17,49},{33,1},{49,17},{2,34}... | collective-permute-start | bytes 491528 | tf_op jit(solution)/shard_map/ppermute | solution.py:262
  113.5 10.1 %collective-permute-start.21 = (bf16[160,512]{1,0:T(8,128)(2,1)S(1)}, bf16[160,512]{1,0:T(8,128)(2,1)S(1)}, u32[]{:S(2)}, u32[]{:S(2)}) collective-permute-start(bf16[160,512]{1,0:T(8,128)(2,1)S(1)} %add_convert_fusion.q0), channel_id=1, source_target_pairs={{0,16},{16,32},{32,48},{48,0},{1,17},{17,33},{33,49},{49,1},{2,18}... | collective-permute-start | bytes 491528 | tf_op jit(solution)/shard_map/ppermute | solution.py:262
  117.2 6.5 %collective-permute-start.28 = (bf16[160,256]{1,0:T(8,128)(2,1)S(1)}, bf16[160,256]{1,0:T(8,128)(2,1)S(1)}, u32[]{:S(2)}, u32[]{:S(2)}) collective-permute-start(bf16[160,256]{1,0:T(8,128)(2,1)S(1)} %slice.83), channel_id=1, source_target_pairs={{0,2},{2,0},{1,3},{3,1},{4,6},{6,4},{5,7},{7,5},{8,10},{10,8},{9,1... | collective-permute-start | bytes 245768 | tf_op jit(solution)/shard_map/ppermute | solution.py:262
  123.6 8.8 %collective-permute-start.32 = (bf16[4,160,512]{2,1,0:T(8,128)(2,1)S(1)}, bf16[4,160,512]{2,1,0:T(8,128)(2,1)S(1)}, u32[]{:S(2)}, u32[]{:S(2)}) collective-permute-start(bf16[4,160,512]{2,1,0:T(8,128)(2,1)S(1)} %pad_maximum_fusion), channel_id=1, source_target_pairs={{0,1},{1,0},{2,3},{3,2},{4,5},{5,4},{6,7},{7,6},{8,9},{9,8},{10,11... | collective-permute-start | bytes 1966088 | tf_op jit(solution)/shard_map/ppermute | solution.py:262
  123.8 5.3 %collective-permute-start.31 = (bf16[160,256]{1,0:T(8,128)(2,1)S(1)}, bf16[160,256]{1,0:T(8,128)(2,1)S(1)}, u32[]{:S(2)}, u32[]{:S(2)}) collective-permute-start(bf16[160,256]{1,0:T(8,128)(2,1)S(1)} %fusion.2.k0), channel_id=1, source_target_pairs={{0,48},{16,0},{32,16},{48,32},{1,49},{17,1},{33,17},{49,33},{2,50}... | collective-permute-start | bytes 245768 | tf_op jit(solution)/shard_map/ppermute | solution.py:262
  124.6 6.0 %collective-permute-start.30 = (bf16[160,256]{1,0:T(8,128)(2,1)S(1)}, bf16[160,256]{1,0:T(8,128)(2,1)S(1)}, u32[]{:S(2)}, u32[]{:S(2)}) collective-permute-start(bf16[160,256]{1,0:T(8,128)(2,1)S(1)} %fusion.2.k0), channel_id=1, source_target_pairs={{0,32},{16,48},{32,0},{48,16},{1,33},{17,49},{33,1},{49,17},{2,34}... | collective-permute-start | bytes 245768 | tf_op jit(solution)/shard_map/ppermute | solution.py:262
  125.9 6.4 %collective-permute-start.29 = (bf16[160,256]{1,0:T(8,128)(2,1)S(1)}, bf16[160,256]{1,0:T(8,128)(2,1)S(1)}, u32[]{:S(2)}, u32[]{:S(2)}) collective-permute-start(bf16[160,256]{1,0:T(8,128)(2,1)S(1)} %fusion.2.k0), channel_id=1, source_target_pairs={{0,16},{16,32},{32,48},{48,0},{1,17},{17,33},{33,49},{49,1},{2,18}... | collective-permute-start | bytes 245768 | tf_op jit(solution)/shard_map/ppermute | solution.py:262
  132.3 1.7 %collective-permute-start.33 = (bf16[4,160,256]{2,1,0:T(8,128)(2,1)S(1)}, bf16[4,160,256]{2,1,0:T(8,128)(2,1)S(1)}, u32[]{:S(2)}, u32[]{:S(2)}) collective-permute-start(bf16[4,160,256]{2,1,0:T(8,128)(2,1)S(1)} %pad_maximum_fusion.4), channel_id=1, source_target_pairs={{0,1},{1,0},{2,3},{3,2},{4,5},{5,4},{6,7},{7,6},{8,9},{9,8},{10,11... | collective-permute-start | bytes 983048 | tf_op jit(solution)/shard_map/ppermute | solution.py:262
  132.4 1.6 %copy-start.10 = (bf16[4,160,512]{2,1,0:T(8,128)(2,1)}, bf16[4,160,512]{2,1,0:T(8,128)(2,1)S(1)}, u32[]{:S(2)}) copy-start(bf16[4,160,512]{2,1,0:T(8,128)(2,1)S(1)} %collective-permute-done.32.qo) | copy-start | bytes 1966084
  (1 other events, 0.7 us)

commit v3 on v1

v3 whole, which is shorter than its diff:
```python
import functools
import math

import jax
import jax.numpy as jnp
import numpy as np
from jax import lax
from jax.experimental import pallas as pl
from jax.experimental.pallas import tpu as pltpu
from jax.sharding import Mesh, PartitionSpec as P

masked_fill = -1e30
HEADS = 4
HEAD = 128
ROWS = 160
HALF = 80
N_OUT = 4
N_X = 4
SLOT = HEADS * ROWS
ALL_ROWS = N_OUT * SLOT
KEYS = 16 * ROWS
KHALF = KEYS // 2
RT = 512
KC = 640
SCALE = 1.0 / math.sqrt(HEAD)
SCALE2 = SCALE * math.log2(math.e)
f32 = jnp.float32
bf16 = jnp.bfloat16
NT = (((1,), (1,)), ((), ()))
NN = (((1,), (0,)), ((), ()))
TN = (((0,), (0,)), ((), ()))


def dot(a, b, dims):
    return lax.dot_general(a, b, dims, preferred_element_type=f32)


def fill_rows(pieces, rows_ref):
    for d in range(N_OUT):
        for h in range(HEADS):
            rows_ref[d * SLOT + h * ROWS : d * SLOT + (h + 1) * ROWS, :] = pieces[d][
                :, h * HEAD : (h + 1) * HEAD
            ]


def masked_scores(key_rows, q, posq, ordk_ref, block):
    score = dot(key_rows, q, NT)
    place = lax.broadcasted_iota(jnp.int32, (HALF, RT), 0)
    parts = []
    for b in range(score.shape[0] // HALF):
        limit = posq - ordk_ref[block + b] * HALF
        part = score[b * HALF : (b + 1) * HALF] * SCALE2
        parts.append(jnp.where(place <= limit, part, masked_fill))
    return jnp.concatenate(parts, axis=0)


def stats_kernel(ordk_ref, posq_ref, q0, q1, q2, q3, g0, g1, g2, g3, kva, kvb, out_ref, qr, gr):
    fill_rows((q0, q1, q2, q3), qr)
    fill_rows((g0, g1, g2, g3), gr)

    def row_tile(rt, _):
        r0 = pl.multiple_of(rt * RT, RT)
        q = qr[pl.ds(r0, RT), :]
        g = gr[pl.ds(r0, RT), :]
        posq = posq_ref[:, pl.ds(r0, RT)]
        top = jnp.full((8, RT), masked_fill, f32)
        total = jnp.zeros((8, RT), f32)
        weighted = jnp.zeros((8, RT), f32)
        for chunk in range(KEYS // KC):
            kv = kva if chunk * KC < KHALF else kvb
            k0 = chunk * KC % KHALF
            score = masked_scores(kv[k0 : k0 + KC, :HEAD], q, posq, ordk_ref, chunk * (KC // HALF))
            dprob = dot(kv[k0 : k0 + KC, HEAD:], g, NT)
            score = score.reshape(KC // 8, 8, RT)
            new_top = jnp.maximum(top, jnp.max(score, axis=0))
            weights = jnp.exp2(score - new_top[None])
            factor = jnp.exp2(top - new_top)
            total = total * factor + jnp.sum(weights, axis=0)
            weighted = weighted * factor + jnp.sum(weights * dprob.reshape(KC // 8, 8, RT), axis=0)
            top = new_top
        row_top = jnp.max(top, axis=0, keepdims=True)
        factor = jnp.exp2(top - row_top)
        out_ref[0:1, pl.ds(r0, RT)] = row_top
        out_ref[1:2, pl.ds(r0, RT)] = jnp.sum(total * factor, axis=0, keepdims=True)
        out_ref[2:3, pl.ds(r0, RT)] = jnp.sum(weighted * factor, axis=0, keepdims=True)
        return 0

    lax.fori_loop(0, ALL_ROWS // RT, row_tile, 0)


def combine_stats(stats, rowstat_ref):
    for d in range(N_OUT):
        parts = []
        for e in range(N_OUT):
            c0 = (d - e) % N_OUT * SLOT
            parts.append(stats[e][:, c0 : c0 + SLOT])
        row_top = parts[0][0:1]
        for part in parts[1:]:
            row_top = jnp.maximum(row_top, part[0:1])
        total = jnp.zeros_like(row_top)
        weighted = jnp.zeros_like(row_top)
        for part in parts:
            factor = jnp.exp2(part[0:1] - row_top)
            total = total + part[1:2] * factor
            weighted = weighted + part[2:3] * factor
        rowstat_ref[0:1, d * SLOT : (d + 1) * SLOT] = row_top + jnp.log2(total)
        rowstat_ref[1:2, d * SLOT : (d + 1) * SLOT] = weighted / total


def grads_pass(segments, ordk_ref, posq_ref, rowstat_ref, kvs, dq_in, dq_out, dkvs, qr, gr):
    for out in dkvs:
        out[...] = jnp.zeros_like(out)

    def row_tile(rt, _):
        r0 = pl.multiple_of(rt * RT, RT)
        q = qr[pl.ds(r0, RT), :]
        g = gr[pl.ds(r0, RT), :]
        posq = posq_ref[:, pl.ds(r0, RT)]
        lse = rowstat_ref[0:1, pl.ds(r0, RT)]
        delta = rowstat_ref[1:2, pl.ds(r0, RT)]
        dq = jnp.zeros((RT, HEAD), f32) if dq_in is None else dq_in[pl.ds(r0, RT), :]
        for which, k0, size, block, to, t0 in segments:
            kv = kvs[which]
            key_rows = kv[k0 : k0 + size, :HEAD]
            score = masked_scores(key_rows, q, posq, ordk_ref, block)
            prob = jnp.exp2(score - lse)
            dprob = dot(kv[k0 : k0 + size, HEAD:], g, NT)
            dscore = (prob * (dprob - delta)).astype(bf16)
            prob_low = prob.astype(bf16)
            dkvs[to][t0 : t0 + size, HEAD:] += dot(prob_low, g, NN)
            dkvs[to][t0 : t0 + size, :HEAD] += dot(dscore, q, NN)
            dq = dq + dot(dscore, key_rows, TN)
        dq_out[pl.ds(r0, RT), :] = dq
        return 0

    lax.fori_loop(0, ALL_ROWS // RT, row_tile, 0)
    for out in dkvs:
        out[:, :HEAD] = out[:, :HEAD] * SCALE


HOME = 2 * ROWS
AWAY = KHALF - HOME


def away_segments(half):
    size = AWAY // 2
    first = half * (KHALF // HALF)
    return [
        (0, HOME + j * size, size, first + (HOME + j * size) // HALF, 0, j * size) for j in range(2)
    ]


def grads_first(ordk, posq, s0, s1, s2, s3, q0, q1, q2, q3, g0, g1, g2, g3, kvb, rowstat, dq, send, qr, gr):
    fill_rows((q0, q1, q2, q3), qr)
    fill_rows((g0, g1, g2, g3), gr)
    combine_stats((s0, s1, s2, s3), rowstat)
    grads_pass(away_segments(1), ordk, posq, rowstat, (kvb,), None, dq, (send,), qr, gr)


def grads_second(ordk, posq, rowstat, q0, q1, q2, q3, g0, g1, g2, g3, kva, dq_in, dq, keep, qr, gr):
    fill_rows((q0, q1, q2, q3), qr)
    fill_rows((g0, g1, g2, g3), gr)
    grads_pass(away_segments(0), ordk, posq, rowstat, (kva,), dq_in, dq, (keep,), qr, gr)


def grads_third(
    ordk, posq, rowstat, q0, q1, q2, q3, g0, g1, g2, g3, kva, kvb, dq_in,
    dq0, dq1, dq2, dq3, keep, send, qr, gr, dqr,
):
    fill_rows((q0, q1, q2, q3), qr)
    fill_rows((g0, g1, g2, g3), gr)
    segments = [(0, 0, HOME, 0, 0, 0), (1, 0, HOME, KHALF // HALF, 1, 0)]
    grads_pass(segments, ordk, posq, rowstat, (kva, kvb), dq_in, dqr, (keep, send), qr, gr)
    for d, out in enumerate((dq0, dq1, dq2, dq3)):
        for h in range(HEADS):
            rows = dqr[d * SLOT + h * ROWS : d * SLOT + (h + 1) * ROWS, :] * SCALE
            out[:, h * HEAD : (h + 1) * HEAD] = rows.astype(out.dtype)


def columns_kernel(place_ref, own, other, out):
    ic = place_ref[1]
    src = lax.broadcasted_iota(jnp.int32, (512, 256), 0)
    dst = lax.broadcasted_iota(jnp.int32, (512, 256), 1)
    home = dst // 32 * 64 + dst % 32 + ic * 32
    pick = jnp.where(src == home, 1.0, 0.0).astype(bf16)
    for t, tok in enumerate((own, other)):
        for o in range(N_OUT):
            for p in range(2):
                start = p * 2048 + o * 512
                cols = tok[:, start : start + 512]
                out[o, t, :, p * 256 : (p + 1) * 256] = dot(cols, pick, NN).astype(bf16)


def weights_kernel(place_ref, x, q0, q1, q2, q3, k0, k1, k2, k3, qo, ko, out, xr, gr):
    wide = HEADS * HEAD
    for d in range(N_OUT):
        rows = slice(d * ROWS, (d + 1) * ROWS)
        other = slice((N_OUT + d) * ROWS, (N_OUT + d + 1) * ROWS)
        source = lax.rem(place_ref[0] + N_OUT - d, N_OUT)
        xr[rows, :] = x[source, 0]
        xr[other, :] = x[source, 1]
        gr[rows, :wide] = (q0, q1, q2, q3)[d][...]
        gr[rows, wide:] = (k0, k1, k2, k3)[d][...]
        gr[other, :wide] = qo[d]
        gr[other, wide:] = ko[d]
    dw = dot(xr[...], gr[...], TN).astype(bf16)
    for p in range(16):
        out[p] = dw[p * 32 : (p + 1) * 32]


smem = pl.BlockSpec(memory_space=pltpu.SMEM)
vmem = pl.BlockSpec(memory_space=pltpu.VMEM)
params = pltpu.CompilerParams(vmem_limit_bytes=50 * 1024 * 1024)


def cost(pairs, matmuls, size):
    return pl.CostEstimate(
        flops=2 * pairs * HEAD * matmuls, transcendentals=pairs, bytes_accessed=size
    )


def kernel_call(body, name, outs, scratch, estimate, aliases, scalars, *args):
    return pl.pallas_call(
        body,
        out_shape=tuple(jax.ShapeDtypeStruct(*o) for o in outs),
        in_specs=[smem] * scalars + [vmem] * (len(args) - scalars),
        out_specs=tuple(vmem for _ in outs),
        scratch_shapes=[pltpu.VMEM(*s) for s in scratch],
        compiler_params=params,
        cost_estimate=estimate,
        input_output_aliases=aliases,
        name=name,
    )(*args)


WIDE = HEADS * HEAD
row_scratch = [((ALL_ROWS, HEAD), bf16)] * 2
acc_rows = ((ALL_ROWS, HEAD), f32)


def shift(x, axis, d, n):
    return lax.ppermute(x, axis, [(i, (i + d) % n) for i in range(n)])


def from_behind(x, axis, n):
    return [x] + [shift(x, axis, d, n) for d in range(1, n)]


def both_ways(x, axis, way):
    behind = shift(x, axis, 1, 4)
    ahead = shift(x, axis, -1, 4)
    far = shift(behind if way == 1 else ahead, axis, way, 4)
    return [x, behind, far, ahead]


def per_device(inputs, block_order, w_query, w_key, w_value, grad_out):
    tokens = inputs[0]
    order = block_order[0]
    dout = grad_out[0]
    o, ix, iy, ic = (lax.axis_index(a) for a in ("outer", "x", "yh", "core"))

    kv = jnp.concatenate(
        [
            dot(tokens, w_key, NN).astype(bf16),
            dot(tokens, w_value, NN).astype(bf16),
        ],
        axis=1,
    )
    kv, later, dout = lax.optimization_barrier((kv, tokens, dout))
    pair = shift(kv, "yh", 1, 2)
    own_x = both_ways(kv, "x", 1)
    pair_x = both_ways(pair, "x", -1)
    query = dot(later, w_query, NN).astype(bf16)
    qs = both_ways(query, "outer", 1)
    gs = both_ways(dout, "outer", -1)
    kva = jnp.concatenate([part for d in range(N_X) for part in (own_x[d], pair_x[d])], axis=0)
    kvb = shift(kva, "core", 1, 2)

    inner = np.arange(2)[:, None, None, None], np.arange(N_X)[None, :, None, None], np.arange(2)[None, None, :, None]
    step = np.arange(2)[None, None, None, :]
    key_dev = ((o * N_X + (ix - inner[1]) % N_X) * 2 + (iy - inner[2]) % 2) * 2 + (ic - inner[0]) % 2
    key_blocks = (key_dev * 2 + step).reshape(-1)
    query_dev = (((o - np.arange(N_OUT)) % N_OUT * N_X + ix) * 2 + iy) * 2 + ic
    query_blocks = (query_dev[:, None] * 2 + np.arange(2)[None, :]).reshape(-1)

    def look_up(blocks):
        hit = blocks[:, None] == jnp.arange(order.shape[0], dtype=jnp.int32)[None, :]
        return jnp.sum(jnp.where(hit, order[None, :], 0), axis=1)

    ordk = look_up(key_blocks)
    ordq = look_up(query_blocks).reshape(N_OUT, 1, 2, 1)
    posq = ordq * HALF + jnp.arange(HALF, dtype=jnp.int32)
    posq = jnp.broadcast_to(posq, (N_OUT, HEADS, 2, HALF)).reshape(1, ALL_ROWS)

    place = jnp.stack([o, ic])
    later, kva = lax.optimization_barrier((later, kva))
    other_tokens = shift(later, "core", 1, 2)
    (stats,) = kernel_call(
        stats_kernel, "stats", [((3, ALL_ROWS), f32)], row_scratch,
        cost(ALL_ROWS * KEYS, 2, 4 << 20), {}, 1, ordk, posq, *qs, *gs, kva, kvb,
    )
    all_stats = from_behind(stats, "outer", N_OUT)
    later, other_tokens, stats = lax.optimization_barrier((later, other_tokens, stats))
    (columns,) = kernel_call(
        columns_kernel, "columns", [((N_OUT, 2, ROWS, 512), bf16)], [],
        cost(ROWS * 4096, 4, 5 << 20), {}, 1, place, later, other_tokens,
    )
    columns = lax.all_to_all(columns, "outer", 0, 0, tiled=True)

    rowstat, dq, send = kernel_call(
        grads_first, "grads_first",
        [((2, ALL_ROWS), f32), acc_rows, ((AWAY, 2 * HEAD), f32)], row_scratch,
        cost(ALL_ROWS * AWAY, 5, 8 << 20), {}, 1, ordk, posq, *all_stats, *qs, *gs, kvb,
    )
    got = shift(send, "core", 1, 2)
    dq, keep = kernel_call(
        grads_second, "grads_second", [acc_rows, ((AWAY, 2 * HEAD), f32)], row_scratch,
        cost(ALL_ROWS * AWAY, 5, 8 << 20), {12: 0}, 1, ordk, posq, rowstat, *qs, *gs, kva, dq,
    )
    away = (keep + got).astype(bf16).reshape(N_X - 1, HOME, 2 * HEAD)
    away, dq = lax.optimization_barrier((away, dq))
    away = [shift(away[d - 1], "x", -d, N_X) for d in range(1, N_X)]
    dq0, dq1, dq2, dq3, keep, send = kernel_call(
        grads_third, "grads_third",
        [((ROWS, WIDE), f32)] + [((ROWS, WIDE), bf16)] * 3 + [((HOME, 2 * HEAD), f32)] * 2,
        row_scratch + [acc_rows],
        cost(ALL_ROWS * 2 * HOME, 5, 8 << 20), {}, 1, ordk, posq, rowstat, *qs, *gs, kva, kvb, dq,
    )
    got = shift(send, "core", 1, 2)
    dq1, dq2, dq3, columns = lax.optimization_barrier((dq1, dq2, dq3, columns))
    dq = dq0
    for d, part in ((1, dq1), (2, dq2), (3, dq3)):
        dq = dq + shift(part, "outer", -d, N_OUT).astype(f32)
    dq_all = from_behind(dq.astype(bf16), "outer", N_OUT)

    part = keep + got
    for arrived in away:
        part = part + arrived.astype(f32)
    dkv = part[:ROWS] + shift(part[ROWS:].astype(bf16), "yh", 1, 2).astype(f32)
    dkv_all = both_ways(dkv.astype(bf16), "outer", 1)

    dq_other = shift(jnp.stack(dq_all), "core", 1, 2)
    dkv_other = shift(jnp.stack(dkv_all), "core", 1, 2)
    (dw,) = kernel_call(
        weights_kernel, "weights", [((16, 32, 768), bf16)],
        [((2 * N_OUT * ROWS, 512), bf16), ((2 * N_OUT * ROWS, 768), bf16)],
        cost(1280 * 512, 6, 4 << 20), {}, 1,
        place, columns, *dq_all, *dkv_all, dq_other, dkv_other,
    )
    dw = lax.all_to_all(dw, ("dp", "x", "yh"), 0, 0, tiled=True)
    dw = jnp.sum(dw.astype(f32), axis=0)
    wide = HEADS * HEAD
    return dw[:, :wide], dw[:, wide : wide + HEAD], dw[:, wide + HEAD :]


def solution(mesh):
    devices = np.asarray(mesh.devices).reshape(2, N_OUT, N_X, 2, 2)
    fine = Mesh(devices, ("dp", "outer", "x", "yh", "core"))
    seq = ("outer", "x", "yh", "core")
    rows = P(("dp",) + seq, None)
    return jax.shard_map(
        per_device,
        mesh=fine,
        in_specs=(
            P("dp", seq, None),
            P("dp", None),
            P(None, None),
            P(None, None),
            P(None, None),
            P("dp", seq, None),
        ),
        out_specs=(rows, rows, rows),
        check_vma=False,
    )
```

time: 178 us -> 178 us (level)
  Pallas kernels: 34 us -> 47 us
  waiting for transfers between devices: 44.3 us -> 31.3 us
  local copies, waits for them, and re-layouts: 19.2 us -> 9.86 us
  starting transfers between devices: 46.9 us -> 56 us
    pallas_call x2 -> x6, Pallas kernels: 34 us -> 47 us  [kernel_call(): pl.pallas_call(body, out_shape=tuple((jax.ShapeDtypeStruct(*o) for o in o...]
    ppermute x32 -> x35, waiting for transfers between devices: 44.3 us -> 31.3 us  [shift(): return lax.ppermute(x, axis, [(i, (i + d) % n) for i in range(n)])]
    dynamic_slice x1 -> x0, local copies, waits for them, and re-layouts: 9.14 us -> none  [per_device(): lax.dynamic_index_in_dim(columns, (o + d) % N_OUT, axis=2, keepdims=False)]
    ppermute x32 -> x35, starting transfers between devices: 46.9 us -> 52.4 us  [shift(): return lax.ppermute(x, axis, [(i, (i + d) % n) for i in range(n)])]
    all_to_all x0 -> x1, starting transfers between devices: none -> 3.54 us  [per_device(): columns = lax.all_to_all(columns, 'outer', 0, 0, tiled=True)]
    unnamed x41, local copies, waits for them, and re-layouts: 3.78 us -> 7.13 us
    another operation x1 -> x0, local copies, waits for them, and re-layouts: 3.22 us -> none  [per_device(): columns = tokens.reshape(ROWS, 2, N_OUT, -1)]
    dot_general x4 -> x3, matrix products: 6.94 us -> 5.38 us  [dot(): return lax.dot_general(a, b, dims, preferred_element_type=f32)]
  transfers between devices with their start and end apart: 32 -> 36, of which waited for: 17 -> 19; matrix products, arithmetic and copies ran while one was open for 8% -> 5% of each run, Pallas kernels for 0% -> 26%
where the time goes in v3:
time: 178 us; the launch traced here: 177 us
  starting transfers between devices  56 us (31%)
  Pallas kernels  47 us (26%)
  waiting for transfers between devices  31.3 us (18%)
  blocking collectives  21.4 us (12%)
  local copies, waits for them, and re-layouts  9.86 us (6%)
  matrix products  5.38 us (3%)
  other arithmetic  5.05 us (3%)
    ppermute x35, starting transfers between devices, shift(): return lax.ppermute(x, axis, [(i, (i + d) % n) for i in range(n)])  52.4 us
    pallas_call x6, Pallas kernels, kernel_call(): pl.pallas_call(body, out_shape=tuple((jax.ShapeDtypeStruct(*o) for o in o...  47 us
    ppermute x35, waiting for transfers between devices, shift(): return lax.ppermute(x, axis, [(i, (i + d) % n) for i in range(n)])  31.3 us
    all_to_all x1, blocking collectives, per_device(): dw = lax.all_to_all(dw, ('dp', 'x', 'yh'), 0, 0, tiled=True)  21.4 us
    unnamed x41, local copies, waits for them, and re-layouts  7.13 us
    dot_general x3, matrix products, dot(): return lax.dot_general(a, b, dims, preferred_element_type=f32)  5.38 us
  transfers between devices with their start and end apart: 36, of which 19 were waited for; matrix products, arithmetic and copies ran while one was open for 5% of the time, Pallas kernels for 26%

profile of v3, /device:TPU:0, one launch (start us, length us, event | category | flops | bytes accessed | tf_op | source)
XLA Modules:
  0.0 177.0 jit_solution(12432156327289955216)
XLA Ops:
  0.7 1.2 copy-done
  1.9 1.8 %convolution_convert_fusion.1 = bf16[160,128]{1,0:T(8,128)(2,1)S(1)} fusion(bf16[4096,128]{1,0:T(8,128)(2,1)S(1)} %copy-done, bf16[1,160,4096]{2,1,0:T(8,128)(2,1)} %param.12), kind=kOutput, calls=%fused_computation.2 | convolution fusion | flops 167792640 | bytes 2400256 | tf_op jit(solution)/shard_map/dot_general | solution.py:35
  4.9 3.1 %convolution_convert_fusion.q0 = bf16[160,512]{1,0:T(8,128)(2,1)S(1)} fusion(bf16[160,4096]{1,0:T(8,128)(2,1)S(1)} %bitcast.34, bf16[4096,512]{1,0:T(8,128)(2,1)} %param.14), kind=kOutput, calls=%fused_computation.1 | convolution fusion | flops 671170560 | bytes 5668864 | tf_op jit(solution)/shard_map/dot_general | solution.py:35
  7.9 2.1 %collective-permute-start = (bf16[160,512]{1,0:T(8,128)(2,1)S(1)}, bf16[160,512]{1,0:T(8,128)(2,1)S(1)}, u32[]{:S(2)}, u32[]{:S(2)}) collective-permute-start(bf16[160,512]{1,0:T(8,128)(2,1)S(1)} %convolution_convert_fusion.q0), channel_id=1, source_target_pairs={{0,16},{16,32},{32,48},{48,0},{1,17},{17,33},{33,49},{49,1},{2,18}... | collective-permute-start | bytes 491528 | tf_op jit(solution)/shard_map/ppermute | solution.py:242
  10.0 2.2 %collective-permute-start.2 = (bf16[160,512]{1,0:T(8,128)(2,1)S(1)}, bf16[160,512]{1,0:T(8,128)(2,1)}, u32[]{:S(2)}, u32[]{:S(2)}) collective-permute-start(bf16[160,512]{1,0:T(8,128)(2,1)S(1)} %convolution_convert_fusion.q0), channel_id=1, source_target_pairs={{0,48},{16,0},{32,16},{48,32},{1,49},{17,1},{33,17},{49,33},{2,50}... | collective-permute-start | bytes 491528 | tf_op jit(solution)/shard_map/ppermute | solution.py:242
  12.2 3.2 %collective-permute-start.6 = (bf16[160,256]{1,0:T(8,128)(2,1)}, bf16[160,256]{1,0:T(8,128)(2,1)}, u32[]{:S(2)}, u32[]{:S(2)}) collective-permute-start(bf16[160,256]{1,0:T(8,128)(2,1)} %pad_maximum_fusion.2), channel_id=1, source_target_pairs={{0,2},{2,0},{1,3},{3,1},{4,6},{6,4},{5,7},{7,5},{8,10},{10,8},{9,1... | collective-permute-start | bytes 245768 | tf_op jit(solution)/shard_map/ppermute | solution.py:242
  15.4 1.5 collective-permute-start.7
  18.5 1.5 collective-permute-start.8
  21.4 1.1 collective-permute-start.9
  23.4 1.6 collective-permute-done.8
  26.0 1.2 collective-permute-done.9
  27.2 2.8 %collective-permute-start.4 = (bf16[160,512]{1,0:T(8,128)(2,1)S(1)}, bf16[160,512]{1,0:T(8,128)(2,1)}, u32[]{:S(2)}, u32[]{:S(2)}) collective-permute-start(bf16[160,512]{1,0:T(8,128)(2,1)S(1)} %bitcast.46), channel_id=1, source_target_pairs={{0,48},{16,0},{32,16},{48,32},{1,49},{17,1},{33,17},{49,33},{2,50}... | collective-permute-start | bytes 491528 | tf_op jit(solution)/shard_map/ppermute | solution.py:242
  30.0 1.8 %collective-permute-start.11 = (bf16[160,256]{1,0:T(8,128)(2,1)S(1)}, bf16[160,256]{1,0:T(8,128)(2,1)S(1)}, u32[]{:S(2)}, u32[]{:S(2)}) collective-permute-start(bf16[160,256]{1,0:T(8,128)(2,1)S(1)} %collective-permute-done.10), channel_id=1, source_target_pairs={{0,12},{4,0},{8,4},{12,8},{1,13},{5,1},{9,5},{13,9},{2,14},{6,2},{... | collective-permute-start | bytes 245768 | tf_op jit(solution)/shard_map/ppermute | solution.py:242
  31.9 2.6 %collective-permute-done.11 = bf16[160,256]{1,0:T(8,128)(2,1)S(1)} collective-permute-done((bf16[160,256]{1,0:T(8,128)(2,1)S(1)}, bf16[160,256]{1,0:T(8,128)(2,1)S(1)}, u32[]{:S(2)}, u32[]{:S(2)}) %collective-permute-start.11) | collective-permute-done | bytes 81952 | tf_op jit(solution)/shard_map/ppermute | solution.py:242
  34.5 3.4 %collective-permute-start.12 = (bf16[160,256]{1,0:T(8,128)(2,1)}, bf16[160,256]{1,0:T(8,128)(2,1)S(1)}, u32[]{:S(2)}, u32[]{:S(2)}) collective-permute-start(bf16[160,256]{1,0:T(8,128)(2,1)} %pad_maximum_fusion.2), channel_id=1, source_target_pairs={{0,12},{4,0},{8,4},{12,8},{1,13},{5,1},{9,5},{13,9},{2,14},{6,2},{... | collective-permute-start | bytes 245768 | tf_op jit(solution)/shard_map/ppermute | solution.py:242
  37.8 2.4 %collective-permute-done.12 = bf16[160,256]{1,0:T(8,128)(2,1)S(1)} collective-permute-done((bf16[160,256]{1,0:T(8,128)(2,1)}, bf16[160,256]{1,0:T(8,128)(2,1)S(1)}, u32[]{:S(2)}, u32[]{:S(2)}) %collective-permute-start.12) | collective-permute-done | bytes 81952 | tf_op jit(solution)/shard_map/ppermute | solution.py:242
  40.5 1.5 collective-permute-start.1
  42.0 1.8 %collective-permute-start.5 = (bf16[160,512]{1,0:T(8,128)(2,1)}, bf16[160,512]{1,0:T(8,128)(2,1)}, u32[]{:S(2)}, u32[]{:S(2)}) collective-permute-start(bf16[160,512]{1,0:T(8,128)(2,1)} %collective-permute-done.4.g3), channel_id=1, source_target_pairs={{0,48},{16,0},{32,16},{48,32},{1,49},{17,1},{33,17},{49,33},{2,50}... | collective-permute-start | bytes 491528 | tf_op jit(solution)/shard_map/ppermute | solution.py:242
  44.3 4.2 %collective-permute-done.1.q2 = bf16[160,512]{1,0:T(8,128)(2,1)} collective-permute-done((bf16[160,512]{1,0:T(8,128)(2,1)S(1)}, bf16[160,512]{1,0:T(8,128)(2,1)}, u32[]{:S(2)}, u32[]{:S(2)}) %collective-permute-start.1) | collective-permute-done | bytes 163872 | tf_op jit(solution)/shard_map/ppermute | solution.py:242
  48.7 11.8 %stats.1.s0 = f32[3,2560]{1,0:T(4,128)S(1)} custom-call(s32[32]{0:T(128)S(1)} %select_reduce_fusion.ordk_ref.ordk, s32[1,2560]{1,0:T(1,128)S(1)} %reshape.107.posq_ref.posq, bf16[160,512]{1,0:T(8,128)(2,1)S(1)} %convolution_convert_fusion.q0, bf16[160,512]{1,0:T(8,128)(2,1)S(1)} %collective-permute-done.q1, bf16[160,512]{1,0:T(8,128)(2,1)} %collective-permute-done.1.q2, ...), custom_call_target="tpu_custom_call" | custom-call | flops 3355443200 | bytes 4194304 | tf_op jit(solution)/shard_map/stats/pallas_call | solution.py:223
  60.5 1.7 collective-permute-start.14
  62.2 2.8 %collective-permute-start.15 = (f32[3,2560]{1,0:T(4,128)S(1)}, f32[3,2560]{1,0:T(4,128)S(1)}, u32[]{:S(2)}, u32[]{:S(2)}) collective-permute-start(f32[3,2560]{1,0:T(4,128)S(1)} %stats.1.s0), channel_id=1, source_target_pairs={{0,32},{16,48},{32,0},{48,16},{1,33},{17,49},{33,1},{49,17},{2,34}... | collective-permute-start | bytes 92168 | tf_op jit(solution)/shard_map/ppermute | solution.py:242
  65.0 1.1 collective-permute-start.16
  66.2 1.5 collective-permute-done.15.s2
  67.7 1.3 collective-permute-done.16.s3
  69.0 11.5 %grads_first.1 = (f32[2,2560]{1,0:T(2,128)S(1)}, f32[2560,128]{1,0:T(8,128)}, f32[960,256]{1,0:T(8,128)}) custom-call(s32[32]{0:T(128)S(1)} %select_reduce_fusion.ordk_ref.ordk, s32[1,2560]{1,0:T(1,128)S(1)} %reshape.107.posq_ref.posq, f32[3,2560]{1,0:T(4,128)S(1)} %stats.1.s0, f32[3,2560]{1,0:T(4,128)S(1)} %collective-permute-done.14.s1, ...), custom_call_target="tpu_custom_call" | custom-call | flops 3145728000 | bytes 8388608 | tf_op jit(solution)/shard_map/grads_first/pallas_call | solution.py:223
  80.6 2.2 %columns.1 = bf16[4,2,160,512]{3,2,1,0:T(8,128)(2,1)S(1)} custom-call(s32[2]{0:T(128)S(1)} %pad_add_fusion.place_ref, bf16[160,4096]{1,0:T(8,128)(2,1)S(1)} %bitcast.36, bf16[160,4096]{1,0:T(8,128)(2,1)} %collective-permute-done.18.other), custom_call_target="tpu_custom_call" | custom-call | flops 671088640 | bytes 5242880 | tf_op jit(solution)/shard_map/columns/pallas_call | solution.py:223
  82.9 1.1 copy-done.2
  84.0 3.5 %all-to-all-start = ((bf16[4,2,160,512]{3,2,1,0:T(8,128)(2,1)}), bf16[4,2,160,512]{3,2,1,0:T(8,128)(2,1)S(1)}, u32[]{:S(2)}, u32[]{:S(2)}) async-start(bf16[4,2,160,512]{3,2,1,0:T(8,128)(2,1)} %copy-done.2), calls=%async_computation | async-start | bytes 2621440 | tf_op jit(solution)/shard_map/all_to_all | solution.py:308
  87.5 11.7 %grads_second.1 = (f32[2560,128]{1,0:T(8,128)}, f32[960,256]{1,0:T(8,128)S(1)}) custom-call(s32[32]{0:T(128)S(1)} %select_reduce_fusion.ordk_ref.ordk, s32[1,2560]{1,0:T(1,128)S(1)} %reshape.107.posq_ref.posq, f32[2,2560]{1,0:T(2,128)S(1)} %get-tuple-element.31.rowstat, ...), custom_call_target="tpu_custom_call", output_to_operand_aliasing={{0}: (12, {})} | custom-call | flops 3145728000 | bytes 8388608 | tf_op jit(solution)/shard_map/grads_second/pallas_call | solution.py:223
  99.3 2.2 %add_convert_fusion = bf16[960,256]{1,0:T(8,128)(2,1)} fusion(f32[960,256]{1,0:T(8,128)S(1)} %get-tuple-element.33, f32[960,256]{1,0:T(8,128)} %collective-permute-done.17), kind=kLoop, calls=%fused_computation.4 | loop fusion | flops 491520 | bytes 2457600 | tf_op jit(solution)/shard_map/convert_element_type | solution.py:320
  101.5 8.0 %grads_third.1 = (f32[160,512]{1,0:T(8,128)S(1)}, bf16[160,512]{1,0:T(8,128)(2,1)S(1)}, bf16[160,512]{1,0:T(8,128)(2,1)S(1)}, bf16[160,512]{1,0:T(8,128)(2,1)S(1...) custom-call(s32[32]{0:T(128)S(1)} %select_reduce_fusion.ordk_ref.ordk, s32[1,2560]{1,0:T(1,128)S(1)} %reshape.107.posq_ref.posq, ...), custom_call_target="tpu_custom_call" | custom-call | flops 2097152000 | bytes 8388608 | tf_op jit(solution)/shard_map/grads_third/pallas_call | solution.py:223
  111.9 1.7 collective-permute-start.21
  113.6 2.7 %collective-permute-start.20 = (bf16[160,512]{1,0:T(8,128)(2,1)}, bf16[160,512]{1,0:T(8,128)(2,1)S(1)}, u32[]{:S(2)}, u32[]{:S(2)}) collective-permute-start(bf16[160,512]{1,0:T(8,128)(2,1)} %copy-done.10), channel_id=1, source_target_pairs={{0,32},{16,48},{32,0},{48,16},{1,33},{17,49},{33,1},{49,17},{2,34}... | collective-permute-start | bytes 491528 | tf_op jit(solution)/shard_map/ppermute | solution.py:242
  116.3 1.5 collective-permute-start.19
  117.8 1.1 slice_bitcast_fusion.2
  119.7 4.2 %collective-permute-start.27 = (bf16[320,256]{1,0:T(8,128)(2,1)S(1)}, bf16[320,256]{1,0:T(8,128)(2,1)S(1)}, u32[]{:S(2)}, u32[]{:S(2)}) collective-permute-start(bf16[320,256]{1,0:T(8,128)(2,1)S(1)} %get-tuple-element.53), channel_id=1, source_target_pairs={{0,8},{4,12},{8,0},{12,4},{1,9},{5,13},{9,1},{13,5},{2,10},{6,14},... | collective-permute-start | bytes 491528 | tf_op jit(solution)/shard_map/ppermute | solution.py:242
  124.4 3.5 %collective-permute-start.26 = (bf16[320,256]{1,0:T(8,128)(2,1)S(1)}, bf16[320,256]{1,0:T(8,128)(2,1)S(1)}, u32[]{:S(2)}, u32[]{:S(2)}) collective-permute-start(bf16[320,256]{1,0:T(8,128)(2,1)S(1)} %get-tuple-element.51), channel_id=1, source_target_pairs={{0,12},{4,0},{8,4},{12,8},{1,13},{5,1},{9,5},{13,9},{2,14},{6,2},{... | collective-permute-start | bytes 491528 | tf_op jit(solution)/shard_map/ppermute | solution.py:242
  129.1 1.9 %collective-permute-done.27 = bf16[320,256]{1,0:T(8,128)(2,1)S(1)} collective-permute-done((bf16[320,256]{1,0:T(8,128)(2,1)S(1)}, bf16[320,256]{1,0:T(8,128)(2,1)S(1)}, u32[]{:S(2)}, u32[]{:S(2)}) %collective-permute-start.27) | collective-permute-done | bytes 163872 | tf_op jit(solution)/shard_map/ppermute | solution.py:242
  132.6 3.6 %collective-permute-start.29 = (bf16[160,256]{1,0:T(8,128)(2,1)S(1)}, bf16[160,256]{1,0:T(8,128)(2,1)S(1)}, u32[]{:S(2)}, u32[]{:S(2)}) collective-permute-start(bf16[160,256]{1,0:T(8,128)(2,1)S(1)} %slice.45), channel_id=1, source_target_pairs={{0,2},{2,0},{1,3},{3,1},{4,6},{6,4},{5,7},{7,5},{8,10},{10,8},{9,1... | collective-permute-start | bytes 245768 | tf_op jit(solution)/shard_map/ppermute | solution.py:242
  136.3 1.8 %collective-permute-done.22.q1 = bf16[160,512]{1,0:T(8,128)(2,1)S(1)} collective-permute-done((bf16[160,512]{1,0:T(8,128)(2,1)S(1)}, bf16[160,512]{1,0:T(8,128)(2,1)S(1)}, u32[]{:S(2)}, u32[]{:S(2)}) %collective-permute-start.22) | collective-permute-done | bytes 163872 | tf_op jit(solution)/shard_map/ppermute | solution.py:242
  138.9 1.3 collective-permute-start.30
  140.2 2.0 %collective-permute-start.32 = (bf16[160,256]{1,0:T(8,128)(2,1)S(1)}, bf16[160,256]{1,0:T(8,128)(2,1)S(1)}, u32[]{:S(2)}, u32[]{:S(2)}) collective-permute-start(bf16[160,256]{1,0:T(8,128)(2,1)S(1)} %fusion.k0), channel_id=1, source_target_pairs={{0,48},{16,0},{32,16},{48,32},{1,49},{17,1},{33,17},{49,33},{2,50}... | collective-permute-start | bytes 245768 | tf_op jit(solution)/shard_map/ppermute | solution.py:242
  142.2 2.8 %collective-permute-done.30.k1 = bf16[160,256]{1,0:T(8,128)(2,1)S(1)} collective-permute-done((bf16[160,256]{1,0:T(8,128)(2,1)S(1)}, bf16[160,256]{1,0:T(8,128)(2,1)S(1)}, u32[]{:S(2)}, u32[]{:S(2)}) %collective-permute-start.30) | collective-permute-done | bytes 81952 | tf_op jit(solution)/shard_map/ppermute | solution.py:242
  145.1 5.6 %collective-permute-done.31.k2 = bf16[160,256]{1,0:T(8,128)(2,1)S(1)} collective-permute-done((bf16[160,256]{1,0:T(8,128)(2,1)S(1)}, bf16[160,256]{1,0:T(8,128)(2,1)S(1)}, u32[]{:S(2)}, u32[]{:S(2)}) %collective-permute-start.31) | collective-permute-done | bytes 81952 | tf_op jit(solution)/shard_map/ppermute | solution.py:242
  150.8 1.6 collective-permute-done.34.ko
  152.5 1.8 %weights.1 = bf16[16,32,768]{2,1,0:T(8,128)(2,1)S(1)} custom-call(s32[2]{0:T(128)S(1)} %pad_add_fusion.place_ref, bf16[4,2,160,512]{3,2,1,0:T(8,128)(2,1)S(1)} %all-to-all-done.x, bf16[160,512]{1,0:T(8,128)(2,1)S(1)} %add_convert_fusion.1.q0, bf16[160,512]{1,0:T(8,128)(2,1)S(1)} %collective-permute-done.22.q1, ...), custom_call_target="tpu_custom_call" | custom-call | flops 1006632960 | bytes 4194304 | tf_op jit(solution)/shard_map/weights/pallas_call | solution.py:223
  154.2 21.4 %all_to_all.10 = bf16[16,32,768]{2,1,0:T(8,128)(2,1)S(1)} all-to-all(bf16[16,32,768]{2,1,0:T(8,128)(2,1)S(1)} %weights.1), channel_id=1, replica_groups=mesh['dp'=2,'outer'=4,'x'=4,'yh'=2,'core'=2] {'dp','x','yh'}, dimensions={0} | all-to-all | bytes 1572864 | tf_op jit(solution)/shard_map/all_to_all | solution.py:350
  (106 shorter events, 16.2 us)
Async XLA Ops:
  0.6 3.0 %copy-start.1 = (bf16[1,160,4096]{2,1,0:T(8,128)(2,1)S(1)}, bf16[1,160,4096]{2,1,0:T(8,128)(2,1)}, u32[]{:S(2)}) copy-start(bf16[1,160,4096]{2,1,0:T(8,128)(2,1)} %param.12) | copy-start | bytes 3932164
  0.7 3.0 %copy-start.12 = (bf16[4096,128]{1,0:T(8,128)(2,1)S(1)}, bf16[4096,128]{1,0:T(8,128)(2,1)}, u32[]{:S(2)}) copy-start(bf16[4096,128]{1,0:T(8,128)(2,1)} %param.15) | copy-start | bytes 3145732
  4.8 12.1 %copy-start.5 = (bf16[1,160,512]{2,1,0:T(8,128)(2,1)S(1)}, bf16[1,160,512]{2,1,0:T(8,128)(2,1)}, u32[]{:S(2)}) copy-start(bf16[1,160,512]{2,1,0:T(8,128)(2,1)} %param.17) | copy-start | bytes 491524
  4.9 13.0 %copy-start.16 = (s32[2,1,1,1]{0,3,2,1:T(1,128)S(1)}, s32[2,1,1,1]{0,3,2,1:T(1,128)}, u32[]{:S(2)}) copy-start(s32[2,1,1,1]{0,3,2,1:T(1,128)} %constant.93) | copy-start | bytes 28
  4.9 13.0 %copy-start.15 = (s32[1,1,2,1]{2,3,1,0:T(1,128)S(1)}, s32[1,1,2,1]{2,3,1,0:T(1,128)}, u32[]{:S(2)}) copy-start(s32[1,1,2,1]{2,3,1,0:T(1,128)} %constant.92) | copy-start | bytes 28
  4.9 13.2 %copy-start.13 = (s32[1,4,1,1]{1,3,2,0:T(1,128)S(1)}, s32[1,4,1,1]{1,3,2,0:T(1,128)}, u32[]{:S(2)}) copy-start(s32[1,4,1,1]{1,3,2,0:T(1,128)} %constant.91) | copy-start | bytes 52
  4.9 13.4 %copy-start.14 = (s32[1,128]{1,0:T(1,128)S(1)}, s32[1,128]{1,0:T(1,128)}, u32[]{:S(2)}) copy-start(s32[1,128]{1,0:T(1,128)} %param.13) | copy-start | bytes 1540
  7.9 32.6 %collective-permute-start = (bf16[160,512]{1,0:T(8,128)(2,1)S(1)}, bf16[160,512]{1,0:T(8,128)(2,1)S(1)}, u32[]{:S(2)}, u32[]{:S(2)}) collective-permute-start(bf16[160,512]{1,0:T(8,128)(2,1)S(1)} %convolution_convert_fusion.q0), channel_id=1, source_target_pairs={{0,16},{16,32},{32,48},{48,0},{1,17},{17,33},{33,49},{49,1},{2,18}... | collective-permute-start | bytes 491528 | tf_op jit(solution)/shard_map/ppermute | solution.py:242
  10.0 33.8 %collective-permute-start.2 = (bf16[160,512]{1,0:T(8,128)(2,1)S(1)}, bf16[160,512]{1,0:T(8,128)(2,1)}, u32[]{:S(2)}, u32[]{:S(2)}) collective-permute-start(bf16[160,512]{1,0:T(8,128)(2,1)S(1)} %convolution_convert_fusion.q0), channel_id=1, source_target_pairs={{0,48},{16,0},{32,16},{48,32},{1,49},{17,1},{33,17},{49,33},{2,50}... | collective-permute-start | bytes 491528 | tf_op jit(solution)/shard_map/ppermute | solution.py:242
  12.2 6.3 %collective-permute-start.6 = (bf16[160,256]{1,0:T(8,128)(2,1)}, bf16[160,256]{1,0:T(8,128)(2,1)}, u32[]{:S(2)}, u32[]{:S(2)}) collective-permute-start(bf16[160,256]{1,0:T(8,128)(2,1)} %pad_maximum_fusion.2), channel_id=1, source_target_pairs={{0,2},{2,0},{1,3},{3,1},{4,6},{6,4},{5,7},{7,5},{8,10},{10,8},{9,1... | collective-permute-start | bytes 245768 | tf_op jit(solution)/shard_map/ppermute | solution.py:242
  15.4 6.0 %collective-permute-start.7 = (bf16[160,256]{1,0:T(8,128)(2,1)}, bf16[160,256]{1,0:T(8,128)(2,1)}, u32[]{:S(2)}, u32[]{:S(2)}) collective-permute-start(bf16[160,256]{1,0:T(8,128)(2,1)} %pad_maximum_fusion.2), channel_id=1, source_target_pairs={{0,4},{4,8},{8,12},{12,0},{1,5},{5,9},{9,13},{13,1},{2,6},{6,10},{... | collective-permute-start | bytes 245768 | tf_op jit(solution)/shard_map/ppermute | solution.py:242
  16.9 27.4 %collective-permute-start.3 = (bf16[160,512]{1,0:T(8,128)(2,1)S(1)}, bf16[160,512]{1,0:T(8,128)(2,1)}, u32[]{:S(2)}, u32[]{:S(2)}) collective-permute-start(bf16[160,512]{1,0:T(8,128)(2,1)S(1)} %bitcast.45), channel_id=1, source_target_pairs={{0,16},{16,32},{32,48},{48,0},{1,17},{17,33},{33,49},{49,1},{2,18}... | collective-permute-start | bytes 491528 | tf_op jit(solution)/shard_map/ppermute | solution.py:242
  18.5 6.5 %collective-permute-start.8 = (bf16[160,256]{1,0:T(8,128)(2,1)}, bf16[160,256]{1,0:T(8,128)(2,1)S(1)}, u32[]{:S(2)}, u32[]{:S(2)}) collective-permute-start(bf16[160,256]{1,0:T(8,128)(2,1)} %collective-permute-done.6), channel_id=1, source_target_pairs={{0,4},{4,8},{8,12},{12,0},{1,5},{5,9},{9,13},{13,1},{2,6},{6,10},{... | collective-permute-start | bytes 245768 | tf_op jit(solution)/shard_map/ppermute | solution.py:242
  21.4 5.9 %collective-permute-start.9 = (bf16[160,256]{1,0:T(8,128)(2,1)}, bf16[160,256]{1,0:T(8,128)(2,1)S(1)}, u32[]{:S(2)}, u32[]{:S(2)}) collective-permute-start(bf16[160,256]{1,0:T(8,128)(2,1)} %collective-permute-done.7), channel_id=1, source_target_pairs={{0,4},{4,8},{8,12},{12,0},{1,5},{5,9},{9,13},{13,1},{2,6},{6,10},{... | collective-permute-start | bytes 245768 | tf_op jit(solution)/shard_map/ppermute | solution.py:242
  25.0 5.0 %collective-permute-start.10 = (bf16[160,256]{1,0:T(8,128)(2,1)}, bf16[160,256]{1,0:T(8,128)(2,1)S(1)}, u32[]{:S(2)}, u32[]{:S(2)}) collective-permute-start(bf16[160,256]{1,0:T(8,128)(2,1)} %collective-permute-done.6), channel_id=1, source_target_pairs={{0,12},{4,0},{8,4},{12,8},{1,13},{5,1},{9,5},{13,9},{2,14},{6,2},{... | collective-permute-start | bytes 245768 | tf_op jit(solution)/shard_map/ppermute | solution.py:242
  27.2 14.8 %collective-permute-start.4 = (bf16[160,512]{1,0:T(8,128)(2,1)S(1)}, bf16[160,512]{1,0:T(8,128)(2,1)}, u32[]{:S(2)}, u32[]{:S(2)}) collective-permute-start(bf16[160,512]{1,0:T(8,128)(2,1)S(1)} %bitcast.46), channel_id=1, source_target_pairs={{0,48},{16,0},{32,16},{48,32},{1,49},{17,1},{33,17},{49,33},{2,50}... | collective-permute-start | bytes 491528 | tf_op jit(solution)/shard_map/ppermute | solution.py:242
  30.0 4.4 %collective-permute-start.11 = (bf16[160,256]{1,0:T(8,128)(2,1)S(1)}, bf16[160,256]{1,0:T(8,128)(2,1)S(1)}, u32[]{:S(2)}, u32[]{:S(2)}) collective-permute-start(bf16[160,256]{1,0:T(8,128)(2,1)S(1)} %collective-permute-done.10), channel_id=1, source_target_pairs={{0,12},{4,0},{8,4},{12,8},{1,13},{5,1},{9,5},{13,9},{2,14},{6,2},{... | collective-permute-start | bytes 245768 | tf_op jit(solution)/shard_map/ppermute | solution.py:242
  34.5 5.7 %collective-permute-start.12 = (bf16[160,256]{1,0:T(8,128)(2,1)}, bf16[160,256]{1,0:T(8,128)(2,1)S(1)}, u32[]{:S(2)}, u32[]{:S(2)}) collective-permute-start(bf16[160,256]{1,0:T(8,128)(2,1)} %pad_maximum_fusion.2), channel_id=1, source_target_pairs={{0,12},{4,0},{8,4},{12,8},{1,13},{5,1},{9,5},{13,9},{2,14},{6,2},{... | collective-permute-start | bytes 245768 | tf_op jit(solution)/shard_map/ppermute | solution.py:242
  40.2 47.3 %copy-start.3 = (bf16[1280,256]{1,0:T(8,128)(2,1)}, bf16[1280,256]{1,0:T(8,128)(2,1)S(1)}, u32[]{:S(2)}) copy-start(bf16[1280,256]{1,0:T(8,128)(2,1)S(1)} %constant_dynamic-update-slice_fusion.kva) | copy-start | bytes 1966084
  40.2 8.4 %collective-permute-start.13 = (bf16[1280,256]{1,0:T(8,128)(2,1)S(1)}, bf16[1280,256]{1,0:T(8,128)(2,1)}, u32[]{:S(2)}, u32[]{:S(2)}) collective-permute-start(bf16[1280,256]{1,0:T(8,128)(2,1)S(1)} %constant_dynamic-update-slice_fusion.kva), channel_id=1, source_target_pairs={{0,1},{1,0},{2,3},{3,2},{4,5},{5,4},{6,7},{7,6},{8,9},{9,8},{10,11... | collective-permute-start | bytes 1966088 | tf_op jit(solution)/shard_map/ppermute | solution.py:242
  40.5 47.0 %copy-start.7 = (bf16[160,512]{1,0:T(8,128)(2,1)}, bf16[160,512]{1,0:T(8,128)(2,1)S(1)}, u32[]{:S(2)}) copy-start(bf16[160,512]{1,0:T(8,128)(2,1)S(1)} %collective-permute-done.q1) | copy-start | bytes 491524
  40.5 8.0 %collective-permute-start.1 = (bf16[160,512]{1,0:T(8,128)(2,1)S(1)}, bf16[160,512]{1,0:T(8,128)(2,1)}, u32[]{:S(2)}, u32[]{:S(2)}) collective-permute-start(bf16[160,512]{1,0:T(8,128)(2,1)S(1)} %collective-permute-done.q1), channel_id=1, source_target_pairs={{0,16},{16,32},{32,48},{48,0},{1,17},{17,33},{33,49},{49,1},{2,18}... | collective-permute-start | bytes 491528 | tf_op jit(solution)/shard_map/ppermute | solution.py:242
  42.0 6.6 %collective-permute-start.5 = (bf16[160,512]{1,0:T(8,128)(2,1)}, bf16[160,512]{1,0:T(8,128)(2,1)}, u32[]{:S(2)}, u32[]{:S(2)}) collective-permute-start(bf16[160,512]{1,0:T(8,128)(2,1)} %collective-permute-done.4.g3), channel_id=1, source_target_pairs={{0,48},{16,0},{32,16},{48,32},{1,49},{17,1},{33,17},{49,33},{2,50}... | collective-permute-start | bytes 491528 | tf_op jit(solution)/shard_map/ppermute | solution.py:242
  43.8 36.8 %collective-permute-start.18 = (bf16[160,4096]{1,0:T(8,128)(2,1)S(1)}, bf16[160,4096]{1,0:T(8,128)(2,1)}, u32[]{:S(2)}, u32[]{:S(2)}) collective-permute-start(bf16[160,4096]{1,0:T(8,128)(2,1)S(1)} %bitcast.35), channel_id=1, source_target_pairs={{0,1},{1,0},{2,3},{3,2},{4,5},{5,4},{6,7},{7,6},{8,9},{9,8},{10,11... | collective-permute-start | bytes 3932168 | tf_op jit(solution)/shard_map/ppermute | solution.py:242
  60.5 5.7 %collective-permute-start.14 = (f32[3,2560]{1,0:T(4,128)S(1)}, f32[3,2560]{1,0:T(4,128)S(1)}, u32[]{:S(2)}, u32[]{:S(2)}) collective-permute-start(f32[3,2560]{1,0:T(4,128)S(1)} %stats.1.s0), channel_id=1, source_target_pairs={{0,16},{16,32},{32,48},{48,0},{1,17},{17,33},{33,49},{49,1},{2,18}... | collective-permute-start | bytes 92168 | tf_op jit(solution)/shard_map/ppermute | solution.py:242
  62.2 5.5 %collective-permute-start.15 = (f32[3,2560]{1,0:T(4,128)S(1)}, f32[3,2560]{1,0:T(4,128)S(1)}, u32[]{:S(2)}, u32[]{:S(2)}) collective-permute-start(f32[3,2560]{1,0:T(4,128)S(1)} %stats.1.s0), channel_id=1, source_target_pairs={{0,32},{16,48},{32,0},{48,16},{1,33},{17,49},{33,1},{49,17},{2,34}... | collective-permute-start | bytes 92168 | tf_op jit(solution)/shard_map/ppermute | solution.py:242
  65.0 4.0 %collective-permute-start.16 = (f32[3,2560]{1,0:T(4,128)S(1)}, f32[3,2560]{1,0:T(4,128)S(1)}, u32[]{:S(2)}, u32[]{:S(2)}) collective-permute-start(f32[3,2560]{1,0:T(4,128)S(1)} %stats.1.s0), channel_id=1, source_target_pairs={{0,48},{16,0},{32,16},{48,32},{1,49},{17,1},{33,17},{49,33},{2,50}... | collective-permute-start | bytes 92168 | tf_op jit(solution)/shard_map/ppermute | solution.py:242
  80.6 18.7 %collective-permute-start.17 = (f32[960,256]{1,0:T(8,128)}, f32[960,256]{1,0:T(8,128)}, u32[]{:S(2)}, u32[]{:S(2)}) collective-permute-start(f32[960,256]{1,0:T(8,128)} %get-tuple-element.34), channel_id=1, source_target_pairs={{0,1},{1,0},{2,3},{3,2},{4,5},{5,4},{6,7},{7,6},{8,9},{9,8},{10,11... | collective-permute-start | bytes 2949128 | tf_op jit(solution)/shard_map/ppermute | solution.py:242
  84.0 28.0 %all-to-all-start = ((bf16[4,2,160,512]{3,2,1,0:T(8,128)(2,1)}), bf16[4,2,160,512]{3,2,1,0:T(8,128)(2,1)S(1)}, u32[]{:S(2)}, u32[]{:S(2)}) async-start(bf16[4,2,160,512]{3,2,1,0:T(8,128)(2,1)} %copy-done.2), calls=%async_computation | async-start | bytes 2621440 | tf_op jit(solution)/shard_map/all_to_all | solution.py:308
  99.3 2.2 %copy-start.4 = (bf16[1280,256]{1,0:T(8,128)(2,1)S(1)}, bf16[1280,256]{1,0:T(8,128)(2,1)}, u32[]{:S(2)}) copy-start(bf16[1280,256]{1,0:T(8,128)(2,1)} %copy-done.3) | copy-start | bytes 1966084
  99.3 2.2 %copy-start.6 = (bf16[1,160,512]{2,1,0:T(8,128)(2,1)S(1)}, bf16[1,160,512]{2,1,0:T(8,128)(2,1)}, u32[]{:S(2)}) copy-start(bf16[1,160,512]{2,1,0:T(8,128)(2,1)} %param.17) | copy-start | bytes 491524
  99.3 2.2 %copy-start.8 = (bf16[160,512]{1,0:T(8,128)(2,1)S(1)}, bf16[160,512]{1,0:T(8,128)(2,1)}, u32[]{:S(2)}) copy-start(bf16[160,512]{1,0:T(8,128)(2,1)} %copy-done.7) | copy-start | bytes 491524
  111.4 20.1 %collective-permute-start.25 = (f32[320,256]{1,0:T(8,128)S(1)}, f32[320,256]{1,0:T(8,128)}, u32[]{:S(2)}, u32[]{:S(2)}) collective-permute-start(f32[320,256]{1,0:T(8,128)S(1)} %get-tuple-element.49), channel_id=1, source_target_pairs={{0,1},{1,0},{2,3},{3,2},{4,5},{5,4},{6,7},{7,6},{8,9},{9,8},{10,11... | collective-permute-start | bytes 983048 | tf_op jit(solution)/shard_map/ppermute | solution.py:242
  111.9 7.8 %collective-permute-start.21 = (bf16[160,512]{1,0:T(8,128)(2,1)}, bf16[160,512]{1,0:T(8,128)(2,1)S(1)}, u32[]{:S(2)}, u32[]{:S(2)}) collective-permute-start(bf16[160,512]{1,0:T(8,128)(2,1)} %copy-done.11), channel_id=1, source_target_pairs={{0,16},{16,32},{32,48},{48,0},{1,17},{17,33},{33,49},{49,1},{2,18}... | collective-permute-start | bytes 491528 | tf_op jit(solution)/shard_map/ppermute | solution.py:242
  113.6 10.8 %collective-permute-start.20 = (bf16[160,512]{1,0:T(8,128)(2,1)}, bf16[160,512]{1,0:T(8,128)(2,1)S(1)}, u32[]{:S(2)}, u32[]{:S(2)}) collective-permute-start(bf16[160,512]{1,0:T(8,128)(2,1)} %copy-done.10), channel_id=1, source_target_pairs={{0,32},{16,48},{32,0},{48,16},{1,33},{17,49},{33,1},{49,17},{2,34}... | collective-permute-start | bytes 491528 | tf_op jit(solution)/shard_map/ppermute | solution.py:242
  116.3 11.6 %collective-permute-start.19 = (bf16[160,512]{1,0:T(8,128)(2,1)}, bf16[160,512]{1,0:T(8,128)(2,1)S(1)}, u32[]{:S(2)}, u32[]{:S(2)}) collective-permute-start(bf16[160,512]{1,0:T(8,128)(2,1)} %copy-done.9), channel_id=1, source_target_pairs={{0,48},{16,0},{32,16},{48,32},{1,49},{17,1},{33,17},{49,33},{2,50}... | collective-permute-start | bytes 491528 | tf_op jit(solution)/shard_map/ppermute | solution.py:242
  118.9 9.2 %collective-permute-start.28 = (bf16[320,256]{1,0:T(8,128)(2,1)S(1)}, bf16[320,256]{1,0:T(8,128)(2,1)S(1)}, u32[]{:S(2)}, u32[]{:S(2)}) collective-permute-start(bf16[320,256]{1,0:T(8,128)(2,1)S(1)} %get-tuple-element.52), channel_id=1, source_target_pairs={{0,4},{4,8},{8,12},{12,0},{1,5},{5,9},{9,13},{13,1},{2,6},{6,10},{... | collective-permute-start | bytes 491528 | tf_op jit(solution)/shard_map/ppermute | solution.py:242
  119.7 11.2 %collective-permute-start.27 = (bf16[320,256]{1,0:T(8,128)(2,1)S(1)}, bf16[320,256]{1,0:T(8,128)(2,1)S(1)}, u32[]{:S(2)}, u32[]{:S(2)}) collective-permute-start(bf16[320,256]{1,0:T(8,128)(2,1)S(1)} %get-tuple-element.53), channel_id=1, source_target_pairs={{0,8},{4,12},{8,0},{12,4},{1,9},{5,13},{9,1},{13,5},{2,10},{6,14},... | collective-permute-start | bytes 491528 | tf_op jit(solution)/shard_map/ppermute | solution.py:242
  124.4 7.2 %collective-permute-start.26 = (bf16[320,256]{1,0:T(8,128)(2,1)S(1)}, bf16[320,256]{1,0:T(8,128)(2,1)S(1)}, u32[]{:S(2)}, u32[]{:S(2)}) collective-permute-start(bf16[320,256]{1,0:T(8,128)(2,1)S(1)} %get-tuple-element.51), channel_id=1, source_target_pairs={{0,12},{4,0},{8,4},{12,8},{1,13},{5,1},{9,5},{13,9},{2,14},{6,2},{... | collective-permute-start | bytes 491528 | tf_op jit(solution)/shard_map/ppermute | solution.py:242
  128.0 10.1 %collective-permute-start.22 = (bf16[160,512]{1,0:T(8,128)(2,1)S(1)}, bf16[160,512]{1,0:T(8,128)(2,1)S(1)}, u32[]{:S(2)}, u32[]{:S(2)}) collective-permute-start(bf16[160,512]{1,0:T(8,128)(2,1)S(1)} %add_convert_fusion.1.q0), channel_id=1, source_target_pairs={{0,16},{16,32},{32,48},{48,0},{1,17},{17,33},{33,49},{49,1},{2,18}... | collective-permute-start | bytes 491528 | tf_op jit(solution)/shard_map/ppermute | solution.py:242
  128.1 10.0 %collective-permute-start.23 = (bf16[160,512]{1,0:T(8,128)(2,1)S(1)}, bf16[160,512]{1,0:T(8,128)(2,1)S(1)}, u32[]{:S(2)}, u32[]{:S(2)}) collective-permute-start(bf16[160,512]{1,0:T(8,128)(2,1)S(1)} %add_convert_fusion.1.q0), channel_id=1, source_target_pairs={{0,32},{16,48},{32,0},{48,16},{1,33},{17,49},{33,1},{49,17},{2,34}... | collective-permute-start | bytes 491528 | tf_op jit(solution)/shard_map/ppermute | solution.py:242
  131.0 7.8 %collective-permute-start.24 = (bf16[160,512]{1,0:T(8,128)(2,1)S(1)}, bf16[160,512]{1,0:T(8,128)(2,1)S(1)}, u32[]{:S(2)}, u32[]{:S(2)}) collective-permute-start(bf16[160,512]{1,0:T(8,128)(2,1)S(1)} %add_convert_fusion.1.q0), channel_id=1, source_target_pairs={{0,48},{16,0},{32,16},{48,32},{1,49},{17,1},{33,17},{49,33},{2,50}... | collective-permute-start | bytes 491528 | tf_op jit(solution)/shard_map/ppermute | solution.py:242
  132.6 6.3 %collective-permute-start.29 = (bf16[160,256]{1,0:T(8,128)(2,1)S(1)}, bf16[160,256]{1,0:T(8,128)(2,1)S(1)}, u32[]{:S(2)}, u32[]{:S(2)}) collective-permute-start(bf16[160,256]{1,0:T(8,128)(2,1)S(1)} %slice.45), channel_id=1, source_target_pairs={{0,2},{2,0},{1,3},{3,1},{4,6},{6,4},{5,7},{7,5},{8,10},{10,8},{9,1... | collective-permute-start | bytes 245768 | tf_op jit(solution)/shard_map/ppermute | solution.py:242
  138.8 13.7 %collective-permute-start.33 = (bf16[4,160,512]{2,1,0:T(8,128)(2,1)S(1)}, bf16[4,160,512]{2,1,0:T(8,128)(2,1)S(1)}, u32[]{:S(2)}, u32[]{:S(2)}) collective-permute-start(bf16[4,160,512]{2,1,0:T(8,128)(2,1)S(1)} %pad_maximum_fusion), channel_id=1, source_target_pairs={{0,1},{1,0},{2,3},{3,2},{4,5},{5,4},{6,7},{7,6},{8,9},{9,8},{10,11... | collective-permute-start | bytes 1966088 | tf_op jit(solution)/shard_map/ppermute | solution.py:242
  138.9 6.1 %collective-permute-start.30 = (bf16[160,256]{1,0:T(8,128)(2,1)S(1)}, bf16[160,256]{1,0:T(8,128)(2,1)S(1)}, u32[]{:S(2)}, u32[]{:S(2)}) collective-permute-start(bf16[160,256]{1,0:T(8,128)(2,1)S(1)} %fusion.k0), channel_id=1, source_target_pairs={{0,16},{16,32},{32,48},{48,0},{1,17},{17,33},{33,49},{49,1},{2,18}... | collective-permute-start | bytes 245768 | tf_op jit(solution)/shard_map/ppermute | solution.py:242
  140.2 4.9 %collective-permute-start.32 = (bf16[160,256]{1,0:T(8,128)(2,1)S(1)}, bf16[160,256]{1,0:T(8,128)(2,1)S(1)}, u32[]{:S(2)}, u32[]{:S(2)}) collective-permute-start(bf16[160,256]{1,0:T(8,128)(2,1)S(1)} %fusion.k0), channel_id=1, source_target_pairs={{0,48},{16,0},{32,16},{48,32},{1,49},{17,1},{33,17},{49,33},{2,50}... | collective-permute-start | bytes 245768 | tf_op jit(solution)/shard_map/ppermute | solution.py:242
  145.1 5.7 %collective-permute-start.31 = (bf16[160,256]{1,0:T(8,128)(2,1)S(1)}, bf16[160,256]{1,0:T(8,128)(2,1)S(1)}, u32[]{:S(2)}, u32[]{:S(2)}) collective-permute-start(bf16[160,256]{1,0:T(8,128)(2,1)S(1)} %collective-permute-done.30.k1), channel_id=1, source_target_pairs={{0,16},{16,32},{32,48},{48,0},{1,17},{17,33},{33,49},{49,1},{2,18}... | collective-permute-start | bytes 245768 | tf_op jit(solution)/shard_map/ppermute | solution.py:242
  150.7 1.7 collective-permute-start.34
  (5 other events, 4.3 us)

commit v4 on v3

v4 whole, which is shorter than its diff:
```python
import functools
import math

import jax
import jax.numpy as jnp
import numpy as np
from jax import lax
from jax.experimental import pallas as pl
from jax.experimental.pallas import tpu as pltpu
from jax.sharding import Mesh, PartitionSpec as P

masked_fill = -1e30
HEADS = 4
HEAD = 128
ROWS = 160
HALF = 80
N_OUT = 4
N_X = 4
SLOT = HEADS * ROWS
ALL_ROWS = N_OUT * SLOT
KEYS = 16 * ROWS
KHALF = KEYS // 2
RT = 512
KC = 640
SCALE = 1.0 / math.sqrt(HEAD)
SCALE2 = SCALE * math.log2(math.e)
f32 = jnp.float32
bf16 = jnp.bfloat16
NT = (((1,), (1,)), ((), ()))
NN = (((1,), (0,)), ((), ()))
TN = (((0,), (0,)), ((), ()))


def dot(a, b, dims):
    return lax.dot_general(a, b, dims, preferred_element_type=f32)


def slot_start(d):
    return (d - 1) % N_OUT * SLOT


def fill_rows(pieces, q_ref, g_ref):
    for d in range(N_OUT):
        for h in range(HEADS):
            r0 = slot_start(d) + h * ROWS
            q_ref[r0 : r0 + ROWS, :] = pieces[d][:, h * HEAD : (h + 1) * HEAD]
            g_ref[r0 : r0 + ROWS, :] = pieces[d][:, (HEADS + h) * HEAD : (HEADS + h + 1) * HEAD]


def masked_scores(key_rows, q, posq, ordk_ref, block):
    score = dot(key_rows, q, NT)
    place = lax.broadcasted_iota(jnp.int32, (HALF, RT), 0)
    parts = []
    for b in range(score.shape[0] // HALF):
        limit = posq - ordk_ref[block + b] * HALF
        part = score[b * HALF : (b + 1) * HALF] * SCALE2
        parts.append(jnp.where(place <= limit, part, masked_fill))
    return jnp.concatenate(parts, axis=0)


def stats_kernel(ordk_ref, posq_ref, p0, p1, p2, p3, kva, kvb, out_ref, qr, gr):
    fill_rows((p0, p1, p2, p3), qr, gr)

    def row_tile(rt, _):
        r0 = pl.multiple_of(rt * RT, RT)
        q = qr[pl.ds(r0, RT), :]
        g = gr[pl.ds(r0, RT), :]
        posq = posq_ref[:, pl.ds(r0, RT)]
        top = jnp.full((8, RT), masked_fill, f32)
        total = jnp.zeros((8, RT), f32)
        weighted = jnp.zeros((8, RT), f32)
        for chunk in range(KEYS // KC):
            kv = kva if chunk * KC < KHALF else kvb
            k0 = chunk * KC % KHALF
            score = masked_scores(kv[k0 : k0 + KC, :HEAD], q, posq, ordk_ref, chunk * (KC // HALF))
            dprob = dot(kv[k0 : k0 + KC, HEAD:], g, NT)
            score = score.reshape(KC // 8, 8, RT)
            new_top = jnp.maximum(top, jnp.max(score, axis=0))
            weights = jnp.exp2(score - new_top[None])
            factor = jnp.exp2(top - new_top)
            total = total * factor + jnp.sum(weights, axis=0)
            weighted = weighted * factor + jnp.sum(weights * dprob.reshape(KC // 8, 8, RT), axis=0)
            top = new_top
        row_top = jnp.max(top, axis=0, keepdims=True)
        factor = jnp.exp2(top - row_top)
        out_ref[0:1, pl.ds(r0, RT)] = row_top
        out_ref[1:2, pl.ds(r0, RT)] = jnp.sum(total * factor, axis=0, keepdims=True)
        out_ref[2:3, pl.ds(r0, RT)] = jnp.sum(weighted * factor, axis=0, keepdims=True)
        return 0

    lax.fori_loop(0, ALL_ROWS // RT, row_tile, 0)


def combine_stats(stats, rowstat_ref):
    for d in range(N_OUT):
        parts = []
        for e in range(N_OUT):
            c0 = slot_start(d - e)
            parts.append(stats[e][:, c0 : c0 + SLOT])
        row_top = parts[0][0:1]
        for part in parts[1:]:
            row_top = jnp.maximum(row_top, part[0:1])
        total = jnp.zeros_like(row_top)
        weighted = jnp.zeros_like(row_top)
        for part in parts:
            factor = jnp.exp2(part[0:1] - row_top)
            total = total + part[1:2] * factor
            weighted = weighted + part[2:3] * factor
        r0 = slot_start(d)
        rowstat_ref[0:1, r0 : r0 + SLOT] = row_top + jnp.log2(total)
        rowstat_ref[1:2, r0 : r0 + SLOT] = weighted / total


def grads_pass(block, ordk_ref, posq_ref, rowstat_ref, kv, dq_in, dqr, dkv, qr, gr):
    dkv[...] = jnp.zeros_like(dkv)

    def row_tile(rt, _):
        r0 = pl.multiple_of(rt * RT, RT)
        q = qr[pl.ds(r0, RT), :]
        g = gr[pl.ds(r0, RT), :]
        posq = posq_ref[:, pl.ds(r0, RT)]
        lse = rowstat_ref[0:1, pl.ds(r0, RT)]
        delta = rowstat_ref[1:2, pl.ds(r0, RT)]
        dq = jnp.zeros((RT, HEAD), f32) if dq_in is None else dq_in[pl.ds(r0, RT), :]
        for k0 in range(0, KHALF, KC):
            key_rows = kv[k0 : k0 + KC, :HEAD]
            score = masked_scores(key_rows, q, posq, ordk_ref, block + k0 // HALF)
            prob = jnp.exp2(score - lse)
            dprob = dot(kv[k0 : k0 + KC, HEAD:], g, NT)
            dscore = (prob * (dprob - delta)).astype(bf16)
            prob_low = prob.astype(bf16)
            dkv[k0 : k0 + KC, HEAD:] += dot(prob_low, g, NN)
            dkv[k0 : k0 + KC, :HEAD] += dot(dscore, q, NN)
            dq = dq + dot(dscore, key_rows, TN)
        dqr[pl.ds(r0, RT), :] = dq
        return 0

    lax.fori_loop(0, ALL_ROWS // RT, row_tile, 0)
    dkv[:, :HEAD] = dkv[:, :HEAD] * SCALE


def grads_first(ordk, posq, s0, s1, s2, s3, p0, p1, p2, p3, kvb, rowstat, dq, dkvb, qr, gr):
    fill_rows((p0, p1, p2, p3), qr, gr)
    combine_stats((s0, s1, s2, s3), rowstat)
    grads_pass(KHALF // HALF, ordk, posq, rowstat, kvb, None, dq, dkvb, qr, gr)


def grads_second(
    ordk, posq, rowstat, p0, p1, p2, p3, kva, dq_in, dq0, dq1, dq2, dq3, dkva, qr, gr, dqr
):
    fill_rows((p0, p1, p2, p3), qr, gr)
    grads_pass(0, ordk, posq, rowstat, kva, dq_in, dqr, dkva, qr, gr)
    for d, out in enumerate((dq0, dq1, dq2, dq3)):
        for h in range(HEADS):
            r0 = slot_start(d) + h * ROWS
            out[:, h * HEAD : (h + 1) * HEAD] = (dqr[r0 : r0 + ROWS, :] * SCALE).astype(out.dtype)


def columns_kernel(place_ref, own, other, x0, x1, x2, x3):
    ic = place_ref[1]
    src = lax.broadcasted_iota(jnp.int32, (512, 256), 0)
    dst = lax.broadcasted_iota(jnp.int32, (512, 256), 1)
    home = dst // 32 * 64 + dst % 32 + ic * 32
    pick = jnp.where(src == home, 1.0, 0.0).astype(bf16)
    for d, out in enumerate((x0, x1, x2, x3)):
        base = lax.rem(place_ref[0] + d, N_OUT) * 512
        for t, tok in enumerate((own, other)):
            for p in range(2):
                cols = tok[:, pl.ds(pl.multiple_of(base + p * 2048, 512), 512)]
                out[t, :, p * 256 : (p + 1) * 256] = dot(cols, pick, NN).astype(bf16)


def weights_kernel(x0, x1, x2, x3, q0, q1, q2, q3, k0, k1, k2, k3, qo, ko, out, xr, gr):
    wide = HEADS * HEAD
    for d, x in enumerate((x0, x1, x2, x3)):
        rows = slice(d * ROWS, (d + 1) * ROWS)
        other = slice((N_OUT + d) * ROWS, (N_OUT + d + 1) * ROWS)
        xr[rows, :] = x[0]
        xr[other, :] = x[1]
        gr[rows, :wide] = (q0, q1, q2, q3)[d][...]
        gr[rows, wide:] = (k0, k1, k2, k3)[d][...]
        gr[other, :wide] = qo[d]
        gr[other, wide:] = ko[d]
    dw = dot(xr[...], gr[...], TN).astype(bf16)
    for p in range(16):
        out[p] = dw[p * 32 : (p + 1) * 32]


smem = pl.BlockSpec(memory_space=pltpu.SMEM)
vmem = pl.BlockSpec(memory_space=pltpu.VMEM)
params = pltpu.CompilerParams(vmem_limit_bytes=50 * 1024 * 1024)


def cost(pairs, matmuls, size):
    return pl.CostEstimate(
        flops=2 * pairs * HEAD * matmuls, transcendentals=pairs, bytes_accessed=size
    )


def kernel_call(body, name, outs, scratch, estimate, aliases, scalars, *args):
    return pl.pallas_call(
        body,
        out_shape=tuple(jax.ShapeDtypeStruct(*o) for o in outs),
        in_specs=[smem] * scalars + [vmem] * (len(args) - scalars),
        out_specs=tuple(vmem for _ in outs),
        scratch_shapes=[pltpu.VMEM(*s) for s in scratch],
        compiler_params=params,
        cost_estimate=estimate,
        input_output_aliases=aliases,
        name=name,
    )(*args)


WIDE = HEADS * HEAD
row_scratch = [((ALL_ROWS, HEAD), bf16)] * 2
acc_rows = ((ALL_ROWS, HEAD), f32)


def shift(x, axis, d, n):
    return lax.ppermute(x, axis, [(i, (i + d) % n) for i in range(n)])


def from_behind(x, axis, n):
    return [x] + [shift(x, axis, d, n) for d in range(1, n)]


def per_device(inputs, block_order, w_query, w_key, w_value, grad_out):
    tokens = inputs[0]
    order = block_order[0]
    dout = grad_out[0]
    o, ix, iy, ic = (lax.axis_index(a) for a in ("outer", "x", "yh", "core"))

    query = dot(tokens, w_query, NN).astype(bf16)
    ps = from_behind(jnp.concatenate([query, dout], axis=1), "outer", N_OUT)
    kv = jnp.concatenate(
        [
            dot(tokens, w_key, NN).astype(bf16),
            dot(tokens, w_value, NN).astype(bf16),
        ],
        axis=1,
    )
    kva = jnp.broadcast_to(kv[None], (8,) + kv.shape)
    kva = lax.all_to_all(kva, ("x", "yh"), 0, 0, tiled=True).reshape(KHALF, 2 * HEAD)
    kvb = shift(kva, "core", 1, 2)

    key_dev = (o * 8 + np.arange(8)[None, :, None]) * 2 + (ic + np.arange(2)[:, None, None]) % 2
    key_blocks = (key_dev * 2 + np.arange(2)[None, None, :]).reshape(-1)
    query_dev = (((o - np.array([1, 2, 3, 0])) % N_OUT * N_X + ix) * 2 + iy) * 2 + ic
    query_blocks = (query_dev[:, None] * 2 + np.arange(2)[None, :]).reshape(-1)

    def look_up(blocks):
        hit = blocks[:, None] == jnp.arange(order.shape[0], dtype=jnp.int32)[None, :]
        return jnp.sum(jnp.where(hit, order[None, :], 0), axis=1)

    ordk = look_up(key_blocks)
    ordq = look_up(query_blocks).reshape(N_OUT, 1, 2, 1)
    posq = ordq * HALF + jnp.arange(HALF, dtype=jnp.int32)
    posq = jnp.broadcast_to(posq, (N_OUT, HEADS, 2, HALF)).reshape(1, ALL_ROWS)

    place = jnp.stack([o, ic])
    later, kv = lax.optimization_barrier((tokens, kv))
    other_tokens = shift(later, "core", 1, 2)
    xs = kernel_call(
        columns_kernel, "columns", [((2, ROWS, 512), bf16)] * N_OUT, [],
        cost(ROWS * 4096, 4, 5 << 20), {}, 1, place, later, other_tokens,
    )
    xs, ps, kva = lax.optimization_barrier((xs, ps, kva))
    xs = [xs[0]] + [shift(xs[d], "outer", d, N_OUT) for d in range(1, N_OUT)]
    (stats,) = kernel_call(
        stats_kernel, "stats", [((3, ALL_ROWS), f32)], row_scratch,
        cost(ALL_ROWS * KEYS, 2, 4 << 20), {}, 1, ordk, posq, *ps, kva, kvb,
    )
    all_stats = from_behind(stats, "outer", N_OUT)
    all_stats, xs = lax.optimization_barrier((all_stats, xs))

    half = ((KHALF, 2 * HEAD), f32)
    rowstat, dq, dkvb = kernel_call(
        grads_first, "grads_first", [((2, ALL_ROWS), f32), acc_rows, half], row_scratch,
        cost(ALL_ROWS * KHALF, 5, 8 << 20), {}, 1, ordk, posq, *all_stats, *ps, kvb,
    )
    got = shift(dkvb, "core", 1, 2)
    dq0, dq1, dq2, dq3, dkva = kernel_call(
        grads_second, "grads_second",
        [((ROWS, WIDE), f32)] + [((ROWS, WIDE), bf16)] * 3 + [half], row_scratch + [acc_rows],
        cost(ALL_ROWS * KHALF, 5, 8 << 20), {}, 1, ordk, posq, rowstat, *ps, kva, dq,
    )
    dq1, dq2, dq3, got = lax.optimization_barrier((dq1, dq2, dq3, got))
    dq_parts = [shift(part, "outer", -d, N_OUT) for d, part in ((1, dq1), (2, dq2), (3, dq3))]
    dq = dq0
    dkv = (dkva + got).astype(bf16).reshape(8, ROWS, 2 * HEAD)
    dkv = lax.all_to_all(dkv, ("x", "yh"), 0, 0, tiled=True)
    dkv = jnp.sum(dkv.astype(f32), axis=0)
    dkv_all = from_behind(dkv.astype(bf16), "outer", N_OUT)
    for part in dq_parts:
        dq = dq + part.astype(f32)
    dq_all = from_behind(dq.astype(bf16), "outer", N_OUT)

    dq_other = shift(jnp.stack(dq_all), "core", 1, 2)
    dkv_other = shift(jnp.stack(dkv_all), "core", 1, 2)
    (dw,) = kernel_call(
        weights_kernel, "weights", [((16, 32, 768), bf16)],
        [((2 * N_OUT * ROWS, 512), bf16), ((2 * N_OUT * ROWS, 768), bf16)],
        cost(1280 * 512, 6, 4 << 20), {}, 0,
        *xs, *dq_all, *dkv_all, dq_other, dkv_other,
    )
    dw = lax.all_to_all(dw, ("dp", "x", "yh"), 0, 0, tiled=True)
    dw = jnp.sum(dw.astype(f32), axis=0)
    wide = HEADS * HEAD
    return dw[:, :wide], dw[:, wide : wide + HEAD], dw[:, wide + HEAD :]


def solution(mesh):
    devices = np.asarray(mesh.devices).reshape(2, N_OUT, N_X, 2, 2)
    fine = Mesh(devices, ("dp", "outer", "x", "yh", "core"))
    seq = ("outer", "x", "yh", "core")
    rows = P(("dp",) + seq, None)
    return jax.shard_map(
        per_device,
        mesh=fine,
        in_specs=(
            P("dp", seq, None),
            P("dp", None),
            P(None, None),
            P(None, None),
            P(None, None),
            P("dp", seq, None),
        ),
        out_specs=(rows, rows, rows),
        check_vma=False,
    )
```

time: 178 us -> 149 us (0.84)
  starting transfers between devices: 56 us -> 31.6 us
  waiting for transfers between devices: 31.3 us -> 38 us
  Pallas kernels: 47 us -> 41.9 us
  local copies, waits for them, and re-layouts: 9.86 us -> 6.83 us
  blocking collectives: 21.4 us -> 19.3 us
    ppermute x35 -> x23, starting transfers between devices: 52.4 us -> 20.5 us  [shift(): return lax.ppermute(x, axis, [(i, (i + d) % n) for i in range(n)])]
    all_to_all x1 -> x2, waiting for transfers between devices: 0.01 us -> 10.8 us  [the longest x1 10.8 us: per_device(): lax.all_to_all(kva, ('x', 'yh'), 0, 0, tiled=True).reshape(KHALF, 2 * HEAD)]
    all_to_all x1 -> x2, starting transfers between devices: 3.54 us -> 11.1 us  [the longest x1 6.93 us: per_device(): lax.all_to_all(kva, ('x', 'yh'), 0, 0, tiled=True).reshape(KHALF, 2 * HEAD)]
    pallas_call x6 -> x5, Pallas kernels: 47 us -> 41.9 us  [kernel_call(): pl.pallas_call(body, out_shape=tuple((jax.ShapeDtypeStruct(*o) for o in o...]
    ppermute x35 -> x23, waiting for transfers between devices: 31.3 us -> 27.2 us  [shift(): return lax.ppermute(x, axis, [(i, (i + d) % n) for i in range(n)])]
    unnamed x41 -> x34, local copies, waits for them, and re-layouts: 7.13 us -> 4.36 us
    all_to_all x1, blocking collectives: 21.4 us -> 19.3 us  [per_device(): dw = lax.all_to_all(dw, ('dp', 'x', 'yh'), 0, 0, tiled=True)]
  transfers between devices with their start and end apart: 36 -> 25, of which waited for: 19 -> 13; matrix products, arithmetic and copies ran while one was open for 5% -> 5% of each run, Pallas kernels for 26% -> 18%
where the time goes in v4:
time: 149 us
  Pallas kernels  41.9 us (28%)
  waiting for transfers between devices  38 us (26%)
  starting transfers between devices  31.6 us (21%)
  blocking collectives  19.3 us (13%)
  local copies, waits for them, and re-layouts  6.83 us (5%)
  other arithmetic  5.46 us (4%)
  matrix products  4.59 us (3%)
    pallas_call x5, Pallas kernels, kernel_call(): pl.pallas_call(body, out_shape=tuple((jax.ShapeDtypeStruct(*o) for o in o...  41.9 us
    ppermute x23, waiting for transfers between devices, shift(): return lax.ppermute(x, axis, [(i, (i + d) % n) for i in range(n)])  27.2 us
    ppermute x23, starting transfers between devices, shift(): return lax.ppermute(x, axis, [(i, (i + d) % n) for i in range(n)])  20.5 us
    all_to_all x1, blocking collectives, per_device(): dw = lax.all_to_all(dw, ('dp', 'x', 'yh'), 0, 0, tiled=True)  19.3 us
    all_to_all x1, waiting for transfers between devices, per_device(): lax.all_to_all(kva, ('x', 'yh'), 0, 0, tiled=True).reshape(KHALF, 2 * HEAD)  10.8 us
    all_to_all x1, starting transfers between devices, per_device(): lax.all_to_all(kva, ('x', 'yh'), 0, 0, tiled=True).reshape(KHALF, 2 * HEAD)  6.93 us
    dot_general x3, matrix products, dot(): return lax.dot_general(a, b, dims, preferred_element_type=f32)  4.59 us
    unnamed x34, local copies, waits for them, and re-layouts  4.36 us
  transfers between devices with their start and end apart: 25, of which 13 were waited for; matrix products, arithmetic and copies ran while one was open for 5% of the time, Pallas kernels for 18%

profile of v4, /device:TPU:0, one launch (start us, length us, event | category | flops | bytes accessed | tf_op | source)
XLA Modules:
  0.0 148.7 jit_solution(15221745120489548423)
XLA Ops:
  0.7 3.6 %convolution_convert_fusion = bf16[160,512]{1,0:T(8,128)(2,1)S(1)} fusion(bf16[4096,512]{1,0:T(8,128)(2,1)} %param.13, bf16[1,160,4096]{2,1,0:T(8,128)(2,1)} %param.11), kind=kOutput, calls=%fused_computation.2 | convolution fusion | flops 671170560 | bytes 5668864 | tf_op jit(solution)/shard_map/dot_general | solution.py:35
  4.3 4.2 %collective-permute-start.3 = (bf16[160,1024]{1,0:T(8,128)(2,1)S(1)}, bf16[160,1024]{1,0:T(8,128)(2,1)}, u32[]{:S(2)}, u32[]{:S(2)}) collective-permute-start(bf16[160,1024]{1,0:T(8,128)(2,1)S(1)} %pad_maximum_fusion.1.p0), channel_id=1, source_target_pairs={{0,48},{16,0},{32,16},{48,32},{1,49},{17,1},{33,17},{49,33},{2,50}... | collective-permute-start | bytes 983048 | tf_op jit(solution)/shard_map/ppermute | solution.py:220
  8.5 1.3 collective-permute-start.1
  10.3 0.5 convolution_convert_fusion.1
  10.9 0.9 broadcast_in_dim.47
  11.7 6.9 %all-to-all-start = ((bf16[8,160,256]{2,1,0:T(8,128)(2,1)}), bf16[8,160,256]{2,1,0:T(8,128)(2,1)S(1)}, u32[]{:S(2)}, u32[]{:S(2)}) async-start(bf16[8,160,256]{2,1,0:T(8,128)(2,1)} %broadcast_in_dim.47), calls=%async_computation | async-start | bytes 1310720 | tf_op jit(solution)/shard_map/all_to_all | solution.py:243
  19.3 10.8 %all-to-all-done = bf16[8,160,256]{2,1,0:T(8,128)(2,1)S(1)} async-done(((bf16[8,160,256]{2,1,0:T(8,128)(2,1)}), bf16[8,160,256]{2,1,0:T(8,128)(2,1)S(1)}, u32[]{:S(2)}, u32[]{:S(2)}) %all-to-all-start) | async-done | bytes 655392 | tf_op jit(solution)/shard_map/all_to_all | solution.py:243
  30.7 2.2 %columns.1 = (bf16[2,160,512]{2,1,0:T(8,128)(2,1)S(1)}, bf16[2,160,512]{2,1,0:T(8,128)(2,1)S(1)}, bf16[2,160,512]{2,1,0:T(8,128)(2,1)S(1)}, bf16[2,160,512]{2,1,0:T(8,128)(2,1)S(1)}) custom-call(s32[2]{0:T(128)S(1)} %pad_add_fusion.place_ref, bf16[160,4096]{1,0:T(8,128)(2,1)S(1)} %bitcast.29, bf16[160,4096]{1,0:T(8,128)(2,1)} %collective-permute-done.other), custom_call_target="tpu_custom_call" | custom-call | flops 671088640 | bytes 5242880 | tf_op jit(solution)/shard_map/columns/pallas_call | solution.py:201
  32.9 0.7 copy-done.2
  33.7 2.3 %collective-permute-start.8 = (bf16[2,160,512]{2,1,0:T(8,128)(2,1)S(1)}, bf16[2,160,512]{2,1,0:T(8,128)(2,1)S(1)}, u32[]{:S(2)}, u32[]{:S(2)}) collective-permute-start(bf16[2,160,512]{2,1,0:T(8,128)(2,1)S(1)} %get-tuple-element.48), channel_id=1, source_target_pairs={{0,16},{16,32},{32,48},{48,0},{1,17},{17,33},{33,49},{49,1},{2,18}... | collective-permute-start | bytes 983048 | tf_op jit(solution)/shard_map/ppermute | solution.py:220
  36.0 1.4 collective-permute-start.9
  37.3 1.5 collective-permute-start.10
  38.8 11.7 %stats.1.s0 = f32[3,2560]{1,0:T(4,128)S(1)} custom-call(s32[32]{0:T(128)S(1)} %select_reduce_fusion.ordk_ref.ordk, s32[1,2560]{1,0:T(1,128)S(1)} %reshape.101.posq_ref.posq, bf16[160,1024]{1,0:T(8,128)(2,1)S(1)} %pad_maximum_fusion.1.p0, bf16[160,1024]{1,0:T(8,128)(2,1)} %collective-permute-done.1.p1, bf16[160,1024]{1,0:T(8,128)(2,1)} %collective-permute-done.2.p2, ...), custom_call_target="tpu_custom_call" | custom-call | flops 3355443200 | bytes 4194304 | tf_op jit(solution)/shard_map/stats/pallas_call | solution.py:201
  50.5 1.3 collective-permute-start.7
  51.9 1.4 collective-permute-start.6
  53.2 1.4 collective-permute-done.7.s3
  54.6 0.7 collective-permute-start.5
  55.3 2.1 %collective-permute-done.6.s2 = f32[3,2560]{1,0:T(4,128)S(1)} collective-permute-done((f32[3,2560]{1,0:T(4,128)S(1)}, f32[3,2560]{1,0:T(4,128)S(1)}, u32[]{:S(2)}, u32[]{:S(2)}) %collective-permute-start.6) | collective-permute-done | bytes 30752 | tf_op jit(solution)/shard_map/ppermute | solution.py:220
  57.4 2.4 %collective-permute-done.5.s1 = f32[3,2560]{1,0:T(4,128)S(1)} collective-permute-done((f32[3,2560]{1,0:T(4,128)S(1)}, f32[3,2560]{1,0:T(4,128)S(1)}, u32[]{:S(2)}, u32[]{:S(2)}) %collective-permute-start.5) | collective-permute-done | bytes 30752 | tf_op jit(solution)/shard_map/ppermute | solution.py:220
  59.8 0.8 copy-done.6
  60.6 0.7 copy-done.8
  61.4 13.4 %grads_first.1 = (f32[2,2560]{1,0:T(2,128)S(1)}, f32[2560,128]{1,0:T(8,128)S(1)}, f32[1280,256]{1,0:T(8,128)}) custom-call(s32[32]{0:T(128)S(1)} %select_reduce_fusion.ordk_ref.ordk, s32[1,2560]{1,0:T(1,128)S(1)} %reshape.101.posq_ref.posq, f32[3,2560]{1,0:T(4,128)S(1)} %stats.1.s0, f32[3,2560]{1,0:T(4,128)S(1)} %collective-permute-done.5.s1, ...), custom_call_target="tpu_custom_call" | custom-call | flops 4194304000 | bytes 8388608 | tf_op jit(solution)/shard_map/grads_first/pallas_call | solution.py:201
  74.7 1.1 copy-done.10
  75.8 13.3 %grads_second.1 = (f32[160,512]{1,0:T(8,128)S(1)}, bf16[160,512]{1,0:T(8,128)(2,1)S(1)}, bf16[160,512]{1,0:T(8,128)(2,1)S(1)}, bf16[160,512]{1,0:T(8,128)(2,1)S(1)}, f32[1280,256]{1,0:T(8,128)}) custom-call(s32[32]{0:T(128)S(1)} %select_reduce_fusion.ordk_ref.ordk, s32[1,2560]{1,0:T(1,128)S(1)} %reshape.101.posq_ref.posq, ...), custom_call_target="tpu_custom_call" | custom-call | flops 4194304000 | bytes 8388608 | tf_op jit(solution)/shard_map/grads_second/pallas_call | solution.py:201
  89.1 1.3 collective-permute-start.12
  90.7 0.7 collective-permute-start.14
  91.4 2.3 %add_convert_fusion = bf16[1280,256]{1,0:T(8,128)(2,1)} fusion(f32[1280,256]{1,0:T(8,128)} %get-tuple-element.69, f32[1280,256]{1,0:T(8,128)S(1)} %collective-permute-done.11), kind=kLoop, calls=%fused_computation.1 | loop fusion | flops 655360 | bytes 3276800 | tf_op jit(solution)/shard_map/convert_element_type | solution.py:290
  93.7 4.2 %all-to-all-start.1 = ((bf16[8,160,256]{2,1,0:T(8,128)(2,1)}), bf16[8,160,256]{2,1,0:T(8,128)(2,1)}, u32[]{:S(2)}, u32[]{:S(2)}) async-start(bf16[8,160,256]{2,1,0:T(8,128)(2,1)} %bitcast.8), calls=%async_computation.1 | async-start | bytes 1310720 | tf_op jit(solution)/shard_map/all_to_all | solution.py:291
  97.9 1.1 collective-permute-done.13
  99.0 2.7 %collective-permute-done.14 = bf16[160,512]{1,0:T(8,128)(2,1)S(1)} collective-permute-done((bf16[160,512]{1,0:T(8,128)(2,1)S(1)}, bf16[160,512]{1,0:T(8,128)(2,1)S(1)}, u32[]{:S(2)}, u32[]{:S(2)}) %collective-permute-start.14) | collective-permute-done | bytes 163872 | tf_op jit(solution)/shard_map/ppermute | solution.py:220
  101.7 0.8 collective-permute-start.17
  102.8 1.1 collective-permute-start.15
  103.8 5.0 %collective-permute-done.17.q3 = bf16[160,512]{1,0:T(8,128)(2,1)S(1)} collective-permute-done((bf16[160,512]{1,0:T(8,128)(2,1)S(1)}, bf16[160,512]{1,0:T(8,128)(2,1)S(1)}, u32[]{:S(2)}, u32[]{:S(2)}) %collective-permute-start.17) | collective-permute-done | bytes 163872 | tf_op jit(solution)/shard_map/ppermute | solution.py:220
  108.9 2.1 %collective-permute-done.16.q2 = bf16[160,512]{1,0:T(8,128)(2,1)S(1)} collective-permute-done((bf16[160,512]{1,0:T(8,128)(2,1)S(1)}, bf16[160,512]{1,0:T(8,128)(2,1)S(1)}, u32[]{:S(2)}, u32[]{:S(2)}) %collective-permute-start.16) | collective-permute-done | bytes 163872 | tf_op jit(solution)/shard_map/ppermute | solution.py:220
  111.0 2.0 %collective-permute-done.15.q1 = bf16[160,512]{1,0:T(8,128)(2,1)S(1)} collective-permute-done((bf16[160,512]{1,0:T(8,128)(2,1)S(1)}, bf16[160,512]{1,0:T(8,128)(2,1)S(1)}, u32[]{:S(2)}, u32[]{:S(2)}) %collective-permute-start.15) | collective-permute-done | bytes 163872 | tf_op jit(solution)/shard_map/ppermute | solution.py:220
  112.9 0.9 pad_maximum_fusion
  113.9 1.2 reduce_sum.41.k0
  115.0 1.1 collective-permute-start.20
  116.2 1.0 collective-permute-start.18
  117.1 3.2 %collective-permute-done.20.k3 = bf16[160,256]{1,0:T(8,128)(2,1)S(1)} collective-permute-done((bf16[160,256]{1,0:T(8,128)(2,1)S(1)}, bf16[160,256]{1,0:T(8,128)(2,1)S(1)}, u32[]{:S(2)}, u32[]{:S(2)}) %collective-permute-start.20) | collective-permute-done | bytes 81952 | tf_op jit(solution)/shard_map/ppermute | solution.py:220
  120.4 2.5 %collective-permute-done.19.k2 = bf16[160,256]{1,0:T(8,128)(2,1)S(1)} collective-permute-done((bf16[160,256]{1,0:T(8,128)(2,1)S(1)}, bf16[160,256]{1,0:T(8,128)(2,1)S(1)}, u32[]{:S(2)}, u32[]{:S(2)}) %collective-permute-start.19) | collective-permute-done | bytes 81952 | tf_op jit(solution)/shard_map/ppermute | solution.py:220
  122.8 1.2 collective-permute-done.18.k1
  124.2 1.6 %collective-permute-done.22.ko = bf16[4,160,256]{2,1,0:T(8,128)(2,1)S(1)} collective-permute-done((bf16[4,160,256]{2,1,0:T(8,128)(2,1)S(1)}, bf16[4,160,256]{2,1,0:T(8,128)(2,1)S(1)}, u32[]{:S(2)}, u32[]{:S(2)}) %collective-permute-start.22) | collective-permute-done | bytes 327712 | tf_op jit(solution)/shard_map/ppermute | solution.py:220
  125.8 1.0 copy-done.9
  126.8 1.2 weights.1
  128.0 19.3 %all_to_all.15 = bf16[16,32,768]{2,1,0:T(8,128)(2,1)S(1)} all-to-all(bf16[16,32,768]{2,1,0:T(8,128)(2,1)S(1)} %weights.1), channel_id=1, replica_groups=mesh['dp'=2,'outer'=4,'x'=4,'yh'=2,'core'=2] {'dp','x','yh'}, dimensions={0} | all-to-all | bytes 1572864 | tf_op jit(solution)/shard_map/all_to_all | solution.py:306
  147.5 0.6 fusion.13
  148.1 0.6 slice.12
  (72 shorter events, 2.6 us)
Async XLA Ops:
  0.6 9.1 %copy-start = (bf16[4096,128]{1,0:T(8,128)(2,1)S(1)}, bf16[4096,128]{1,0:T(8,128)(2,1)}, u32[]{:S(2)}) copy-start(bf16[4096,128]{1,0:T(8,128)(2,1)} %param.14) | copy-start | bytes 3145732
  0.6 9.1 %copy-start.1 = (bf16[1,160,4096]{2,1,0:T(8,128)(2,1)S(1)}, bf16[1,160,4096]{2,1,0:T(8,128)(2,1)}, u32[]{:S(2)}) copy-start(bf16[1,160,4096]{2,1,0:T(8,128)(2,1)} %param.11) | copy-start | bytes 3932164
  0.7 3.6 %copy-start.12 = (bf16[1,160,512]{2,1,0:T(8,128)(2,1)S(1)}, bf16[1,160,512]{2,1,0:T(8,128)(2,1)}, u32[]{:S(2)}) copy-start(bf16[1,160,512]{2,1,0:T(8,128)(2,1)} %param.16) | copy-start | bytes 491524
  4.3 6.0 %copy-start.11 = (bf16[4096,128]{1,0:T(8,128)(2,1)S(1)}, bf16[4096,128]{1,0:T(8,128)(2,1)}, u32[]{:S(2)}) copy-start(bf16[4096,128]{1,0:T(8,128)(2,1)} %param.15) | copy-start | bytes 3145732
  4.3 29.3 %collective-permute-start.3 = (bf16[160,1024]{1,0:T(8,128)(2,1)S(1)}, bf16[160,1024]{1,0:T(8,128)(2,1)}, u32[]{:S(2)}, u32[]{:S(2)}) collective-permute-start(bf16[160,1024]{1,0:T(8,128)(2,1)S(1)} %pad_maximum_fusion.1.p0), channel_id=1, source_target_pairs={{0,48},{16,0},{32,16},{48,32},{1,49},{17,1},{33,17},{49,33},{2,50}... | collective-permute-start | bytes 983048 | tf_op jit(solution)/shard_map/ppermute | solution.py:220
  8.5 25.2 %collective-permute-start.2 = (bf16[160,1024]{1,0:T(8,128)(2,1)S(1)}, bf16[160,1024]{1,0:T(8,128)(2,1)}, u32[]{:S(2)}, u32[]{:S(2)}) collective-permute-start(bf16[160,1024]{1,0:T(8,128)(2,1)S(1)} %pad_maximum_fusion.1.p0), channel_id=1, source_target_pairs={{0,32},{16,48},{32,0},{48,16},{1,33},{17,49},{33,1},{49,17},{2,34}... | collective-permute-start | bytes 983048 | tf_op jit(solution)/shard_map/ppermute | solution.py:220
  8.5 25.2 %collective-permute-start.1 = (bf16[160,1024]{1,0:T(8,128)(2,1)S(1)}, bf16[160,1024]{1,0:T(8,128)(2,1)}, u32[]{:S(2)}, u32[]{:S(2)}) collective-permute-start(bf16[160,1024]{1,0:T(8,128)(2,1)S(1)} %pad_maximum_fusion.1.p0), channel_id=1, source_target_pairs={{0,16},{16,32},{32,48},{48,0},{1,17},{17,33},{33,49},{49,1},{2,18}... | collective-permute-start | bytes 983048 | tf_op jit(solution)/shard_map/ppermute | solution.py:220
  10.8 7.9 %copy-start.13 = (s32[4]{0:T(128)S(1)}, s32[4]{0:T(128)}, u32[]{:S(2)}) copy-start(s32[4]{0:T(128)} %constant.77) | copy-start | bytes 52
  10.8 8.1 %copy-start.14 = (s32[1,128]{1,0:T(1,128)S(1)}, s32[1,128]{1,0:T(1,128)}, u32[]{:S(2)}) copy-start(s32[1,128]{1,0:T(1,128)} %param.12) | copy-start | bytes 1540
  10.8 8.3 %copy-start.16 = (s32[2,1,1]{0,2,1:T(1,128)S(1)}, s32[2,1,1]{0,2,1:T(1,128)}, u32[]{:S(2)}) copy-start(s32[2,1,1]{0,2,1:T(1,128)} %constant.69.clone) | copy-start | bytes 28
  10.8 8.3 %copy-start.15 = (s32[1,8,1]{1,2,0:T(1,128)S(1)}, s32[1,8,1]{1,2,0:T(1,128)}, u32[]{:S(2)}) copy-start(s32[1,8,1]{1,2,0:T(1,128)} %constant.68.clone) | copy-start | bytes 100
  11.7 18.3 %all-to-all-start = ((bf16[8,160,256]{2,1,0:T(8,128)(2,1)}), bf16[8,160,256]{2,1,0:T(8,128)(2,1)S(1)}, u32[]{:S(2)}, u32[]{:S(2)}) async-start(bf16[8,160,256]{2,1,0:T(8,128)(2,1)} %broadcast_in_dim.47), calls=%async_computation | async-start | bytes 1310720 | tf_op jit(solution)/shard_map/all_to_all | solution.py:243
  18.7 12.0 %collective-permute-start = (bf16[160,4096]{1,0:T(8,128)(2,1)S(1)}, bf16[160,4096]{1,0:T(8,128)(2,1)}, u32[]{:S(2)}, u32[]{:S(2)}) collective-permute-start(bf16[160,4096]{1,0:T(8,128)(2,1)S(1)} %bitcast.28), channel_id=1, source_target_pairs={{0,1},{1,0},{2,3},{3,2},{4,5},{5,4},{6,7},{7,6},{8,9},{9,8},{10,11... | collective-permute-start | bytes 3932168 | tf_op jit(solution)/shard_map/ppermute | solution.py:220
  30.1 8.7 %collective-permute-start.4 = (bf16[1280,256]{1,0:T(8,128)(2,1)S(1)}, bf16[1280,256]{1,0:T(8,128)(2,1)}, u32[]{:S(2)}, u32[]{:S(2)}) collective-permute-start(bf16[1280,256]{1,0:T(8,128)(2,1)S(1)} %bitcast.35), channel_id=1, source_target_pairs={{0,1},{1,0},{2,3},{3,2},{4,5},{5,4},{6,7},{7,6},{8,9},{9,8},{10,11... | collective-permute-start | bytes 1966088 | tf_op jit(solution)/shard_map/ppermute | solution.py:220
  32.9 0.7 copy-start.2
  33.7 26.1 %collective-permute-start.8 = (bf16[2,160,512]{2,1,0:T(8,128)(2,1)S(1)}, bf16[2,160,512]{2,1,0:T(8,128)(2,1)S(1)}, u32[]{:S(2)}, u32[]{:S(2)}) collective-permute-start(bf16[2,160,512]{2,1,0:T(8,128)(2,1)S(1)} %get-tuple-element.48), channel_id=1, source_target_pairs={{0,16},{16,32},{32,48},{48,0},{1,17},{17,33},{33,49},{49,1},{2,18}... | collective-permute-start | bytes 983048 | tf_op jit(solution)/shard_map/ppermute | solution.py:220
  36.0 23.9 %collective-permute-start.9 = (bf16[2,160,512]{2,1,0:T(8,128)(2,1)S(1)}, bf16[2,160,512]{2,1,0:T(8,128)(2,1)S(1)}, u32[]{:S(2)}, u32[]{:S(2)}) collective-permute-start(bf16[2,160,512]{2,1,0:T(8,128)(2,1)S(1)} %get-tuple-element.49), channel_id=1, source_target_pairs={{0,32},{16,48},{32,0},{48,16},{1,33},{17,49},{33,1},{49,17},{2,34}... | collective-permute-start | bytes 983048 | tf_op jit(solution)/shard_map/ppermute | solution.py:220
  37.3 23.3 %collective-permute-start.10 = (bf16[2,160,512]{2,1,0:T(8,128)(2,1)S(1)}, bf16[2,160,512]{2,1,0:T(8,128)(2,1)S(1)}, u32[]{:S(2)}, u32[]{:S(2)}) collective-permute-start(bf16[2,160,512]{2,1,0:T(8,128)(2,1)S(1)} %get-tuple-element.50), channel_id=1, source_target_pairs={{0,48},{16,0},{32,16},{48,32},{1,49},{17,1},{33,17},{49,33},{2,50}... | collective-permute-start | bytes 983048 | tf_op jit(solution)/shard_map/ppermute | solution.py:220
  50.5 4.1 %collective-permute-start.7 = (f32[3,2560]{1,0:T(4,128)S(1)}, f32[3,2560]{1,0:T(4,128)S(1)}, u32[]{:S(2)}, u32[]{:S(2)}) collective-permute-start(f32[3,2560]{1,0:T(4,128)S(1)} %stats.1.s0), channel_id=1, source_target_pairs={{0,48},{16,0},{32,16},{48,32},{1,49},{17,1},{33,17},{49,33},{2,50}... | collective-permute-start | bytes 92168 | tf_op jit(solution)/shard_map/ppermute | solution.py:220
  51.9 5.5 %collective-permute-start.6 = (f32[3,2560]{1,0:T(4,128)S(1)}, f32[3,2560]{1,0:T(4,128)S(1)}, u32[]{:S(2)}, u32[]{:S(2)}) collective-permute-start(f32[3,2560]{1,0:T(4,128)S(1)} %stats.1.s0), channel_id=1, source_target_pairs={{0,32},{16,48},{32,0},{48,16},{1,33},{17,49},{33,1},{49,17},{2,34}... | collective-permute-start | bytes 92168 | tf_op jit(solution)/shard_map/ppermute | solution.py:220
  54.6 5.2 %collective-permute-start.5 = (f32[3,2560]{1,0:T(4,128)S(1)}, f32[3,2560]{1,0:T(4,128)S(1)}, u32[]{:S(2)}, u32[]{:S(2)}) collective-permute-start(f32[3,2560]{1,0:T(4,128)S(1)} %stats.1.s0), channel_id=1, source_target_pairs={{0,16},{16,32},{32,48},{48,0},{1,17},{17,33},{33,49},{49,1},{2,18}... | collective-permute-start | bytes 92168 | tf_op jit(solution)/shard_map/ppermute | solution.py:220
  59.8 14.9 %copy-start.4 = (bf16[2,160,512]{2,1,0:T(8,128)(2,1)}, bf16[2,160,512]{2,1,0:T(8,128)(2,1)S(1)}, u32[]{:S(2)}) copy-start(bf16[2,160,512]{2,1,0:T(8,128)(2,1)S(1)} %collective-permute-done.8.x1) | copy-start | bytes 983044
  59.8 0.8 copy-start.6
  60.6 0.7 copy-start.8
  74.7 1.1 copy-start.10
  75.8 13.3 %collective-permute-start.11 = (f32[1280,256]{1,0:T(8,128)}, f32[1280,256]{1,0:T(8,128)S(1)}, u32[]{:S(2)}, u32[]{:S(2)}) collective-permute-start(f32[1280,256]{1,0:T(8,128)} %get-tuple-element.65), channel_id=1, source_target_pairs={{0,1},{1,0},{2,3},{3,2},{4,5},{5,4},{6,7},{7,6},{8,9},{9,8},{10,11... | collective-permute-start | bytes 3932168 | tf_op jit(solution)/shard_map/ppermute | solution.py:220
  89.1 8.8 %collective-permute-start.12 = (bf16[160,512]{1,0:T(8,128)(2,1)S(1)}, bf16[160,512]{1,0:T(8,128)(2,1)S(1)}, u32[]{:S(2)}, u32[]{:S(2)}) collective-permute-start(bf16[160,512]{1,0:T(8,128)(2,1)S(1)} %get-tuple-element.66), channel_id=1, source_target_pairs={{0,48},{16,0},{32,16},{48,32},{1,49},{17,1},{33,17},{49,33},{2,50}... | collective-permute-start | bytes 491528 | tf_op jit(solution)/shard_map/ppermute | solution.py:220
  90.4 8.6 %collective-permute-start.13 = (bf16[160,512]{1,0:T(8,128)(2,1)S(1)}, bf16[160,512]{1,0:T(8,128)(2,1)S(1)}, u32[]{:S(2)}, u32[]{:S(2)}) collective-permute-start(bf16[160,512]{1,0:T(8,128)(2,1)S(1)} %get-tuple-element.67), channel_id=1, source_target_pairs={{0,32},{16,48},{32,0},{48,16},{1,33},{17,49},{33,1},{49,17},{2,34}... | collective-permute-start | bytes 491528 | tf_op jit(solution)/shard_map/ppermute | solution.py:220
  90.7 11.0 %collective-permute-start.14 = (bf16[160,512]{1,0:T(8,128)(2,1)S(1)}, bf16[160,512]{1,0:T(8,128)(2,1)S(1)}, u32[]{:S(2)}, u32[]{:S(2)}) collective-permute-start(bf16[160,512]{1,0:T(8,128)(2,1)S(1)} %get-tuple-element.68), channel_id=1, source_target_pairs={{0,16},{16,32},{32,48},{48,0},{1,17},{17,33},{33,49},{49,1},{2,18}... | collective-permute-start | bytes 491528 | tf_op jit(solution)/shard_map/ppermute | solution.py:220
  93.7 20.2 %all-to-all-start.1 = ((bf16[8,160,256]{2,1,0:T(8,128)(2,1)}), bf16[8,160,256]{2,1,0:T(8,128)(2,1)}, u32[]{:S(2)}, u32[]{:S(2)}) async-start(bf16[8,160,256]{2,1,0:T(8,128)(2,1)} %bitcast.8), calls=%async_computation.1 | async-start | bytes 1310720 | tf_op jit(solution)/shard_map/all_to_all | solution.py:291
  101.7 7.1 %collective-permute-start.17 = (bf16[160,512]{1,0:T(8,128)(2,1)S(1)}, bf16[160,512]{1,0:T(8,128)(2,1)S(1)}, u32[]{:S(2)}, u32[]{:S(2)}) collective-permute-start(bf16[160,512]{1,0:T(8,128)(2,1)S(1)} %add_convert_fusion.1.q0), channel_id=1, source_target_pairs={{0,48},{16,0},{32,16},{48,32},{1,49},{17,1},{33,17},{49,33},{2,50}... | collective-permute-start | bytes 491528 | tf_op jit(solution)/shard_map/ppermute | solution.py:220
  102.5 8.4 %collective-permute-start.16 = (bf16[160,512]{1,0:T(8,128)(2,1)S(1)}, bf16[160,512]{1,0:T(8,128)(2,1)S(1)}, u32[]{:S(2)}, u32[]{:S(2)}) collective-permute-start(bf16[160,512]{1,0:T(8,128)(2,1)S(1)} %add_convert_fusion.1.q0), channel_id=1, source_target_pairs={{0,32},{16,48},{32,0},{48,16},{1,33},{17,49},{33,1},{49,17},{2,34}... | collective-permute-start | bytes 491528 | tf_op jit(solution)/shard_map/ppermute | solution.py:220
  102.8 10.2 %collective-permute-start.15 = (bf16[160,512]{1,0:T(8,128)(2,1)S(1)}, bf16[160,512]{1,0:T(8,128)(2,1)S(1)}, u32[]{:S(2)}, u32[]{:S(2)}) collective-permute-start(bf16[160,512]{1,0:T(8,128)(2,1)S(1)} %add_convert_fusion.1.q0), channel_id=1, source_target_pairs={{0,16},{16,32},{32,48},{48,0},{1,17},{17,33},{33,49},{49,1},{2,18}... | collective-permute-start | bytes 491528 | tf_op jit(solution)/shard_map/ppermute | solution.py:220
  112.9 12.9 %copy-start.3 = (bf16[2,160,512]{2,1,0:T(8,128)(2,1)S(1)}, bf16[2,160,512]{2,1,0:T(8,128)(2,1)}, u32[]{:S(2)}) copy-start(bf16[2,160,512]{2,1,0:T(8,128)(2,1)} %copy-done.2) | copy-start | bytes 983044
  112.9 12.9 %copy-start.5 = (bf16[2,160,512]{2,1,0:T(8,128)(2,1)S(1)}, bf16[2,160,512]{2,1,0:T(8,128)(2,1)}, u32[]{:S(2)}) copy-start(bf16[2,160,512]{2,1,0:T(8,128)(2,1)} %copy-done.4) | copy-start | bytes 983044
  112.9 12.9 %copy-start.7 = (bf16[2,160,512]{2,1,0:T(8,128)(2,1)S(1)}, bf16[2,160,512]{2,1,0:T(8,128)(2,1)}, u32[]{:S(2)}) copy-start(bf16[2,160,512]{2,1,0:T(8,128)(2,1)} %copy-done.6) | copy-start | bytes 983044
  113.8 11.9 %collective-permute-start.21 = (bf16[4,160,512]{2,1,0:T(8,128)(2,1)}, bf16[4,160,512]{2,1,0:T(8,128)(2,1)S(1)}, u32[]{:S(2)}, u32[]{:S(2)}) collective-permute-start(bf16[4,160,512]{2,1,0:T(8,128)(2,1)} %pad_maximum_fusion), channel_id=1, source_target_pairs={{0,1},{1,0},{2,3},{3,2},{4,5},{5,4},{6,7},{7,6},{8,9},{9,8},{10,11... | collective-permute-start | bytes 1966088 | tf_op jit(solution)/shard_map/ppermute | solution.py:220
  115.0 5.3 %collective-permute-start.20 = (bf16[160,256]{1,0:T(8,128)(2,1)S(1)}, bf16[160,256]{1,0:T(8,128)(2,1)S(1)}, u32[]{:S(2)}, u32[]{:S(2)}) collective-permute-start(bf16[160,256]{1,0:T(8,128)(2,1)S(1)} %reduce_sum.41.k0), channel_id=1, source_target_pairs={{0,48},{16,0},{32,16},{48,32},{1,49},{17,1},{33,17},{49,33},{2,50}... | collective-permute-start | bytes 245768 | tf_op jit(solution)/shard_map/ppermute | solution.py:220
  116.2 6.6 %collective-permute-start.19 = (bf16[160,256]{1,0:T(8,128)(2,1)S(1)}, bf16[160,256]{1,0:T(8,128)(2,1)S(1)}, u32[]{:S(2)}, u32[]{:S(2)}) collective-permute-start(bf16[160,256]{1,0:T(8,128)(2,1)S(1)} %reduce_sum.41.k0), channel_id=1, source_target_pairs={{0,32},{16,48},{32,0},{48,16},{1,33},{17,49},{33,1},{49,17},{2,34}... | collective-permute-start | bytes 245768 | tf_op jit(solution)/shard_map/ppermute | solution.py:220
  116.2 7.8 %collective-permute-start.18 = (bf16[160,256]{1,0:T(8,128)(2,1)S(1)}, bf16[160,256]{1,0:T(8,128)(2,1)S(1)}, u32[]{:S(2)}, u32[]{:S(2)}) collective-permute-start(bf16[160,256]{1,0:T(8,128)(2,1)S(1)} %reduce_sum.41.k0), channel_id=1, source_target_pairs={{0,16},{16,32},{32,48},{48,0},{1,17},{17,33},{33,49},{49,1},{2,18}... | collective-permute-start | bytes 245768 | tf_op jit(solution)/shard_map/ppermute | solution.py:220
  124.1 1.7 %collective-permute-start.22 = (bf16[4,160,256]{2,1,0:T(8,128)(2,1)S(1)}, bf16[4,160,256]{2,1,0:T(8,128)(2,1)S(1)}, u32[]{:S(2)}, u32[]{:S(2)}) collective-permute-start(bf16[4,160,256]{2,1,0:T(8,128)(2,1)S(1)} %pad_maximum_fusion.2), channel_id=1, source_target_pairs={{0,1},{1,0},{2,3},{3,2},{4,5},{5,4},{6,7},{7,6},{8,9},{9,8},{10,11... | collective-permute-start | bytes 983048 | tf_op jit(solution)/shard_map/ppermute | solution.py:220
  125.8 1.0 copy-start.9

commit v5 on v4

--- a/solution.py
+++ b/solution.py
@@ -20,8 +20,9 @@
 ALL_ROWS = N_OUT * SLOT
 KEYS = 16 * ROWS
 KHALF = KEYS // 2
-RT = 512
+RT = 1280
 KC = 640
+KS = 160
 SCALE = 1.0 / math.sqrt(HEAD)
 SCALE2 = SCALE * math.log2(math.e)
 f32 = jnp.float32
@@ -69,17 +70,17 @@
         top = jnp.full((8, RT), masked_fill, f32)
         total = jnp.zeros((8, RT), f32)
         weighted = jnp.zeros((8, RT), f32)
-        for chunk in range(KEYS // KC):
-            kv = kva if chunk * KC < KHALF else kvb
-            k0 = chunk * KC % KHALF
-            score = masked_scores(kv[k0 : k0 + KC, :HEAD], q, posq, ordk_ref, chunk * (KC // HALF))
-            dprob = dot(kv[k0 : k0 + KC, HEAD:], g, NT)
-            score = score.reshape(KC // 8, 8, RT)
+        for chunk in range(KEYS // KS):
+            kv = kva if chunk * KS < KHALF else kvb
+            k0 = chunk * KS % KHALF
+            score = masked_scores(kv[k0 : k0 + KS, :HEAD], q, posq, ordk_ref, chunk * (KS // HALF))
+            dprob = dot(kv[k0 : k0 + KS, HEAD:], g, NT)
+            score = score.reshape(KS // 8, 8, RT)
             new_top = jnp.maximum(top, jnp.max(score, axis=0))
             weights = jnp.exp2(score - new_top[None])
             factor = jnp.exp2(top - new_top)
             total = total * factor + jnp.sum(weights, axis=0)
-            weighted = weighted * factor + jnp.sum(weights * dprob.reshape(KC // 8, 8, RT), axis=0)
+            weighted = weighted * factor + jnp.sum(weights * dprob.reshape(KS // 8, 8, RT), axis=0)
             top = new_top
         row_top = jnp.max(top, axis=0, keepdims=True)
         factor = jnp.exp2(top - row_top)
@@ -111,7 +112,12 @@
         rowstat_ref[1:2, r0 : r0 + SLOT] = weighted / total
 
 
-def grads_pass(block, ordk_ref, posq_ref, rowstat_ref, kv, dq_in, dqr, dkv, qr, gr):
+def grads_kernel(
+    ordk, posq_ref, s0, s1, s2, s3, p0, p1, p2, p3, kva, kvb,
+    dq0, dq1, dq2, dq3, keep, send, qr, gr, rowstat, dqr, dkv,
+):
+    fill_rows((p0, p1, p2, p3), qr, gr)
+    combine_stats((s0, s1, s2, s3), rowstat)
     dkv[...] = jnp.zeros_like(dkv)
 
     def row_tile(rt, _):
@@ -119,41 +125,32 @@
         q = qr[pl.ds(r0, RT), :]
         g = gr[pl.ds(r0, RT), :]
         posq = posq_ref[:, pl.ds(r0, RT)]
-        lse = rowstat_ref[0:1, pl.ds(r0, RT)]
-        delta = rowstat_ref[1:2, pl.ds(r0, RT)]
-        dq = jnp.zeros((RT, HEAD), f32) if dq_in is None else dq_in[pl.ds(r0, RT), :]
-        for k0 in range(0, KHALF, KC):
+        lse = rowstat[0:1, pl.ds(r0, RT)]
+        delta = rowstat[1:2, pl.ds(r0, RT)]
+        dq = jnp.zeros((RT, HEAD), f32)
+        for chunk in range(KEYS // KC):
+            kv = kva if chunk * KC < KHALF else kvb
+            k0 = chunk * KC % KHALF
             key_rows = kv[k0 : k0 + KC, :HEAD]
-            score = masked_scores(key_rows, q, posq, ordk_ref, block + k0 // HALF)
+            score = masked_scores(key_rows, q, posq, ordk, chunk * (KC // HALF))
             prob = jnp.exp2(score - lse)
             dprob = dot(kv[k0 : k0 + KC, HEAD:], g, NT)
             dscore = (prob * (dprob - delta)).astype(bf16)
             prob_low = prob.astype(bf16)
-            dkv[k0 : k0 + KC, HEAD:] += dot(prob_low, g, NN)
-            dkv[k0 : k0 + KC, :HEAD] += dot(dscore, q, NN)
+            dkv[chunk * KC : (chunk + 1) * KC, HEAD:] += dot(prob_low, g, NN)
+            dkv[chunk * KC : (chunk + 1) * KC, :HEAD] += dot(dscore, q, NN)
             dq = dq + dot(dscore, key_rows, TN)
         dqr[pl.ds(r0, RT), :] = dq
         return 0
 
     lax.fori_loop(0, ALL_ROWS // RT, row_tile, 0)
-    dkv[:, :HEAD] = dkv[:, :HEAD] * SCALE
-
-
-def grads_first(ordk, posq, s0, s1, s2, s3, p0, p1, p2, p3, kvb, rowstat, dq, dkvb, qr, gr):
-    fill_rows((p0, p1, p2, p3), qr, gr)
-    combine_stats((s0, s1, s2, s3), rowstat)
-    grads_pass(KHALF // HALF, ordk, posq, rowstat, kvb, None, dq, dkvb, qr, gr)
-
-
-def grads_second(
-    ordk, posq, rowstat, p0, p1, p2, p3, kva, dq_in, dq0, dq1, dq2, dq3, dkva, qr, gr, dqr
-):
-    fill_rows((p0, p1, p2, p3), qr, gr)
-    grads_pass(0, ordk, posq, rowstat, kva, dq_in, dqr, dkva, qr, gr)
     for d, out in enumerate((dq0, dq1, dq2, dq3)):
         for h in range(HEADS):
             r0 = slot_start(d) + h * ROWS
             out[:, h * HEAD : (h + 1) * HEAD] = (dqr[r0 : r0 + ROWS, :] * SCALE).astype(out.dtype)
+    for out, k0 in ((keep, 0), (send, KHALF)):
+        out[:, :HEAD] = (dkv[k0 : k0 + KHALF, :HEAD] * SCALE).astype(out.dtype)
+        out[:, HEAD:] = dkv[k0 : k0 + KHALF, HEAD:].astype(out.dtype)
 
 
 def columns_kernel(place_ref, own, other, x0, x1, x2, x3):
@@ -186,9 +183,10 @@
         out[p] = dw[p * 32 : (p + 1) * 32]
 
 
+VM = 24
 smem = pl.BlockSpec(memory_space=pltpu.SMEM)
 vmem = pl.BlockSpec(memory_space=pltpu.VMEM)
-params = pltpu.CompilerParams(vmem_limit_bytes=50 * 1024 * 1024)
+params = pltpu.CompilerParams(vmem_limit_bytes=VM * 1024 * 1024)
 
 
 def cost(pairs, matmuls, size):
@@ -264,7 +262,7 @@
         columns_kernel, "columns", [((2, ROWS, 512), bf16)] * N_OUT, [],
         cost(ROWS * 4096, 4, 5 << 20), {}, 1, place, later, other_tokens,
     )
-    xs, ps, kva = lax.optimization_barrier((xs, ps, kva))
+    xs, kva = lax.optimization_barrier((xs, kva))
     xs = [xs[0]] + [shift(xs[d], "outer", d, N_OUT) for d in range(1, N_OUT)]
     (stats,) = kernel_call(
         stats_kernel, "stats", [((3, ALL_ROWS), f32)], row_scratch,
@@ -273,21 +271,17 @@
     all_stats = from_behind(stats, "outer", N_OUT)
     all_stats, xs = lax.optimization_barrier((all_stats, xs))
 
-    half = ((KHALF, 2 * HEAD), f32)
-    rowstat, dq, dkvb = kernel_call(
-        grads_first, "grads_first", [((2, ALL_ROWS), f32), acc_rows, half], row_scratch,
-        cost(ALL_ROWS * KHALF, 5, 8 << 20), {}, 1, ordk, posq, *all_stats, *ps, kvb,
-    )
-    got = shift(dkvb, "core", 1, 2)
-    dq0, dq1, dq2, dq3, dkva = kernel_call(
-        grads_second, "grads_second",
-        [((ROWS, WIDE), f32)] + [((ROWS, WIDE), bf16)] * 3 + [half], row_scratch + [acc_rows],
-        cost(ALL_ROWS * KHALF, 5, 8 << 20), {}, 1, ordk, posq, rowstat, *ps, kva, dq,
-    )
-    dq1, dq2, dq3, got = lax.optimization_barrier((dq1, dq2, dq3, got))
+    half = (KHALF, 2 * HEAD)
+    dq, dq1, dq2, dq3, keep, send = kernel_call(
+        grads_kernel, "grads",
+        [((ROWS, WIDE), f32)] + [((ROWS, WIDE), bf16)] * 3 + [(half, f32), (half, bf16)],
+        row_scratch + [((2, ALL_ROWS), f32), acc_rows, ((KEYS, 2 * HEAD), f32)],
+        cost(ALL_ROWS * KEYS, 5, 8 << 20), {}, 1,
+        ordk, posq, *all_stats, *ps, kva, kvb,
+    )
+    got = shift(send, "core", 1, 2)
     dq_parts = [shift(part, "outer", -d, N_OUT) for d, part in ((1, dq1), (2, dq2), (3, dq3))]
-    dq = dq0
-    dkv = (dkva + got).astype(bf16).reshape(8, ROWS, 2 * HEAD)
+    dkv = (keep + got.astype(f32)).astype(bf16).reshape(8, ROWS, 2 * HEAD)
     dkv = lax.all_to_all(dkv, ("x", "yh"), 0, 0, tiled=True)
     dkv = jnp.sum(dkv.astype(f32), axis=0)
     dkv_all = from_behind(dkv.astype(bf16), "outer", N_OUT)

time: 149 us -> 140 us (0.940)
  Pallas kernels: 41.9 us -> 36.1 us
  local copies, waits for them, and re-layouts: 6.83 us -> 4.26 us
    pallas_call x5 -> x4, Pallas kernels: 41.9 us -> 36.1 us  [kernel_call(): pl.pallas_call(body, out_shape=tuple((jax.ShapeDtypeStruct(*o) for o in o...]
    unnamed x34 -> x32, local copies, waits for them, and re-layouts: 4.36 us -> 1.77 us
  transfers between devices with their start and end apart: 25 -> 25, of which waited for: 13 -> 13; matrix products, arithmetic and copies ran while one was open for 5% -> 4% of each run, Pallas kernels for 18% -> 10%
where the time goes in v5:
time: 140 us; the launch traced here: 139 us
  waiting for transfers between devices  39.1 us (28%)
  Pallas kernels  36.1 us (26%)
  starting transfers between devices  32 us (23%)
  blocking collectives  18.3 us (13%)
  matrix products  4.59 us (3%)
  local copies, waits for them, and re-layouts  4.26 us (3%)
  other arithmetic  4.15 us (3%)
    pallas_call x4, Pallas kernels, kernel_call(): pl.pallas_call(body, out_shape=tuple((jax.ShapeDtypeStruct(*o) for o in o...  36.1 us
    ppermute x23, waiting for transfers between devices, shift(): return lax.ppermute(x, axis, [(i, (i + d) % n) for i in range(n)])  28.3 us
    ppermute x23, starting transfers between devices, shift(): return lax.ppermute(x, axis, [(i, (i + d) % n) for i in range(n)])  20.6 us
    all_to_all x1, blocking collectives, per_device(): dw = lax.all_to_all(dw, ('dp', 'x', 'yh'), 0, 0, tiled=True)  18.3 us
    all_to_all x1, waiting for transfers between devices, per_device(): lax.all_to_all(kva, ('x', 'yh'), 0, 0, tiled=True).reshape(KHALF, 2 * HEAD)  10.8 us
    all_to_all x1, starting transfers between devices, per_device(): lax.all_to_all(kva, ('x', 'yh'), 0, 0, tiled=True).reshape(KHALF, 2 * HEAD)  6.93 us
    dot_general x3, matrix products, dot(): return lax.dot_general(a, b, dims, preferred_element_type=f32)  4.59 us
    all_to_all x1, starting transfers between devices, per_device(): dkv = lax.all_to_all(dkv, ('x', 'yh'), 0, 0, tiled=True)  4.41 us
  transfers between devices with their start and end apart: 25, of which 13 were waited for; matrix products, arithmetic and copies ran while one was open for 4% of the time, Pallas kernels for 10%

profile of v5, /device:TPU:0, one launch (start us, length us, event | category | flops | bytes accessed | tf_op | source)
XLA Modules:
  0.0 139.5 jit_solution(342351576069237506)
XLA Ops:
  0.7 3.6 %convolution_convert_fusion = bf16[160,512]{1,0:T(8,128)(2,1)S(1)} fusion(bf16[4096,512]{1,0:T(8,128)(2,1)} %param.13, bf16[1,160,4096]{2,1,0:T(8,128)(2,1)} %param.11), kind=kOutput, calls=%fused_computation.2 | convolution fusion | flops 671170560 | bytes 5668864 | tf_op jit(solution)/shard_map/dot_general | solution.py:36
  4.3 4.2 %collective-permute-start.2 = (bf16[160,1024]{1,0:T(8,128)(2,1)S(1)}, bf16[160,1024]{1,0:T(8,128)(2,1)}, u32[]{:S(2)}, u32[]{:S(2)}) collective-permute-start(bf16[160,1024]{1,0:T(8,128)(2,1)S(1)} %pad_maximum_fusion.1.p0), channel_id=1, source_target_pairs={{0,48},{16,0},{32,16},{48,32},{1,49},{17,1},{33,17},{49,33},{2,50}... | collective-permute-start | bytes 983048 | tf_op jit(solution)/shard_map/ppermute | solution.py:218
  8.5 1.3 collective-permute-start
  9.8 0.5 convolution_convert_fusion.2
  10.3 0.5 convolution_convert_fusion.1
  10.9 0.9 broadcast_in_dim.47
  11.8 6.9 %all-to-all-start = ((bf16[8,160,256]{2,1,0:T(8,128)(2,1)}), bf16[8,160,256]{2,1,0:T(8,128)(2,1)S(1)}, u32[]{:S(2)}, u32[]{:S(2)}) async-start(bf16[8,160,256]{2,1,0:T(8,128)(2,1)} %broadcast_in_dim.47), calls=%async_computation | async-start | bytes 1310720 | tf_op jit(solution)/shard_map/all_to_all | solution.py:241
  18.9 0.2 select_reduce_fusion.1
  19.3 10.8 %all-to-all-done = bf16[8,160,256]{2,1,0:T(8,128)(2,1)S(1)} async-done(((bf16[8,160,256]{2,1,0:T(8,128)(2,1)}), bf16[8,160,256]{2,1,0:T(8,128)(2,1)S(1)}, u32[]{:S(2)}, u32[]{:S(2)}) %all-to-all-start) | async-done | bytes 655392 | tf_op jit(solution)/shard_map/all_to_all | solution.py:241
  30.7 2.2 %columns.1 = (bf16[2,160,512]{2,1,0:T(8,128)(2,1)S(1)}, bf16[2,160,512]{2,1,0:T(8,128)(2,1)S(1)}, bf16[2,160,512]{2,1,0:T(8,128)(2,1)S(1)}, bf16[2,160,512]{2,1,0:T(8,128)(2,1)S(1)}) custom-call(s32[2]{0:T(128)S(1)} %pad_add_fusion.place_ref, bf16[160,4096]{1,0:T(8,128)(2,1)S(1)} %bitcast.29, bf16[160,4096]{1,0:T(8,128)(2,1)} %collective-permute-done.3.other), custom_call_target="tpu_custom_call" | custom-call | flops 671088640 | bytes 5242880 | tf_op jit(solution)/shard_map/columns/pallas_call | solution.py:199
  32.9 0.7 copy-done.2
  33.7 2.2 %collective-permute-start.8 = (bf16[2,160,512]{2,1,0:T(8,128)(2,1)S(1)}, bf16[2,160,512]{2,1,0:T(8,128)(2,1)S(1)}, u32[]{:S(2)}, u32[]{:S(2)}) collective-permute-start(bf16[2,160,512]{2,1,0:T(8,128)(2,1)S(1)} %get-tuple-element.34), channel_id=1, source_target_pairs={{0,16},{16,32},{32,48},{48,0},{1,17},{17,33},{33,49},{49,1},{2,18}... | collective-permute-start | bytes 983048 | tf_op jit(solution)/shard_map/ppermute | solution.py:218
  35.9 1.4 collective-permute-start.9
  37.3 1.5 %collective-permute-start.10 = (bf16[2,160,512]{2,1,0:T(8,128)(2,1)S(1)}, bf16[2,160,512]{2,1,0:T(8,128)(2,1)S(1)}, u32[]{:S(2)}, u32[]{:S(2)}) collective-permute-start(bf16[2,160,512]{2,1,0:T(8,128)(2,1)S(1)} %get-tuple-element.36), channel_id=1, source_target_pairs={{0,48},{16,0},{32,16},{48,32},{1,49},{17,1},{33,17},{49,33},{2,50}... | collective-permute-start | bytes 983048 | tf_op jit(solution)/shard_map/ppermute | solution.py:218
  38.8 11.6 %stats.1.s0 = f32[3,2560]{1,0:T(4,128)S(1)} custom-call(s32[32]{0:T(128)S(1)} %select_reduce_fusion.ordk_ref.ordk, s32[1,2560]{1,0:T(1,128)S(1)} %reshape.101.posq_ref, bf16[160,1024]{1,0:T(8,128)(2,1)S(1)} %pad_maximum_fusion.1.p0, bf16[160,1024]{1,0:T(8,128)(2,1)} %collective-permute-done.p1, bf16[160,1024]{1,0:T(8,128)(2,1)} %collective-permute-done.1.p2, ...), custom_call_target="tpu_custom_call" | custom-call | flops 3355443200 | bytes 4194304 | tf_op jit(solution)/shard_map/stats/pallas_call | solution.py:199
  50.4 1.3 collective-permute-start.7
  51.7 1.3 collective-permute-start.6
  53.0 1.4 %collective-permute-done.7.s3 = f32[3,2560]{1,0:T(4,128)S(1)} collective-permute-done((f32[3,2560]{1,0:T(4,128)S(1)}, f32[3,2560]{1,0:T(4,128)S(1)}, u32[]{:S(2)}, u32[]{:S(2)}) %collective-permute-start.7) | collective-permute-done | bytes 30752 | tf_op jit(solution)/shard_map/ppermute | solution.py:218
  54.5 0.8 collective-permute-start.5
  55.2 2.0 %collective-permute-done.6.s2 = f32[3,2560]{1,0:T(4,128)S(1)} collective-permute-done((f32[3,2560]{1,0:T(4,128)S(1)}, f32[3,2560]{1,0:T(4,128)S(1)}, u32[]{:S(2)}, u32[]{:S(2)}) %collective-permute-start.6) | collective-permute-done | bytes 30752 | tf_op jit(solution)/shard_map/ppermute | solution.py:218
  57.2 2.4 %collective-permute-done.5.s1 = f32[3,2560]{1,0:T(4,128)S(1)} collective-permute-done((f32[3,2560]{1,0:T(4,128)S(1)}, f32[3,2560]{1,0:T(4,128)S(1)}, u32[]{:S(2)}, u32[]{:S(2)}) %collective-permute-start.5) | collective-permute-done | bytes 30752 | tf_op jit(solution)/shard_map/ppermute | solution.py:218
  59.7 21.1 %grads.1 = (f32[160,512]{1,0:T(8,128)S(1)}, bf16[160,512]{1,0:T(8,128)(2,1)S(1)}, bf16[160,512]{1,0:T(8,128)(2,1)S(1)}, bf16[160,512]{1,0:T(8,128)(2,1)S(1)}, f3...) custom-call(s32[32]{0:T(128)S(1)} %select_reduce_fusion.ordk_ref.ordk, s32[1,2560]{1,0:T(1,128)S(1)} %reshape.101.posq_ref, ...), custom_call_target="tpu_custom_call" | custom-call | flops 8388608000 | bytes 8388608 | tf_op jit(solution)/shard_map/grads/pallas_call | solution.py:199
  80.9 1.3 collective-permute-start.11
  82.2 0.4 collective-permute-start.12
  82.6 0.6 collective-permute-start.13
  83.2 1.0 add_convert_fusion
  84.2 4.4 %all-to-all-start.1 = ((bf16[8,160,256]{2,1,0:T(8,128)(2,1)}), bf16[8,160,256]{2,1,0:T(8,128)(2,1)}, u32[]{:S(2)}, u32[]{:S(2)}) async-start(bf16[8,160,256]{2,1,0:T(8,128)(2,1)} %bitcast.8), calls=%async_computation.1 | async-start | bytes 1310720 | tf_op jit(solution)/shard_map/all_to_all | solution.py:285
  88.6 2.2 %collective-permute-done.12 = bf16[160,512]{1,0:T(8,128)(2,1)S(1)} collective-permute-done((bf16[160,512]{1,0:T(8,128)(2,1)S(1)}, bf16[160,512]{1,0:T(8,128)(2,1)S(1)}, u32[]{:S(2)}, u32[]{:S(2)}) %collective-permute-start.12) | collective-permute-done | bytes 163872 | tf_op jit(solution)/shard_map/ppermute | solution.py:218
  90.8 2.6 %collective-permute-done.13 = bf16[160,512]{1,0:T(8,128)(2,1)S(1)} collective-permute-done((bf16[160,512]{1,0:T(8,128)(2,1)S(1)}, bf16[160,512]{1,0:T(8,128)(2,1)S(1)}, u32[]{:S(2)}, u32[]{:S(2)}) %collective-permute-start.13) | collective-permute-done | bytes 163872 | tf_op jit(solution)/shard_map/ppermute | solution.py:218
  93.5 0.8 collective-permute-start.16
  94.3 0.3 collective-permute-start.15
  94.6 1.0 collective-permute-start.14
  95.6 5.0 %collective-permute-done.16.q3 = bf16[160,512]{1,0:T(8,128)(2,1)S(1)} collective-permute-done((bf16[160,512]{1,0:T(8,128)(2,1)S(1)}, bf16[160,512]{1,0:T(8,128)(2,1)S(1)}, u32[]{:S(2)}, u32[]{:S(2)}) %collective-permute-start.16) | collective-permute-done | bytes 163872 | tf_op jit(solution)/shard_map/ppermute | solution.py:218
  100.7 2.1 %collective-permute-done.15.q2 = bf16[160,512]{1,0:T(8,128)(2,1)S(1)} collective-permute-done((bf16[160,512]{1,0:T(8,128)(2,1)S(1)}, bf16[160,512]{1,0:T(8,128)(2,1)S(1)}, u32[]{:S(2)}, u32[]{:S(2)}) %collective-permute-start.15) | collective-permute-done | bytes 163872 | tf_op jit(solution)/shard_map/ppermute | solution.py:218
  102.7 2.0 %collective-permute-done.14.q1 = bf16[160,512]{1,0:T(8,128)(2,1)S(1)} collective-permute-done((bf16[160,512]{1,0:T(8,128)(2,1)S(1)}, bf16[160,512]{1,0:T(8,128)(2,1)S(1)}, u32[]{:S(2)}, u32[]{:S(2)}) %collective-permute-start.14) | collective-permute-done | bytes 163872 | tf_op jit(solution)/shard_map/ppermute | solution.py:218
  104.7 0.9 pad_maximum_fusion
  105.7 1.2 reduce_sum.41.k0
  106.9 1.1 collective-permute-start.20
  108.0 0.9 collective-permute-start.18
  109.0 3.2 %collective-permute-done.20.k3 = bf16[160,256]{1,0:T(8,128)(2,1)S(1)} collective-permute-done((bf16[160,256]{1,0:T(8,128)(2,1)S(1)}, bf16[160,256]{1,0:T(8,128)(2,1)S(1)}, u32[]{:S(2)}, u32[]{:S(2)}) %collective-permute-start.20) | collective-permute-done | bytes 81952 | tf_op jit(solution)/shard_map/ppermute | solution.py:218
  112.2 2.5 %collective-permute-done.19.k2 = bf16[160,256]{1,0:T(8,128)(2,1)S(1)} collective-permute-done((bf16[160,256]{1,0:T(8,128)(2,1)S(1)}, bf16[160,256]{1,0:T(8,128)(2,1)S(1)}, u32[]{:S(2)}, u32[]{:S(2)}) %collective-permute-start.19) | collective-permute-done | bytes 81952 | tf_op jit(solution)/shard_map/ppermute | solution.py:218
  114.6 1.2 collective-permute-done.18.k1
  116.0 1.6 %collective-permute-done.22.ko = bf16[4,160,256]{2,1,0:T(8,128)(2,1)S(1)} collective-permute-done((bf16[4,160,256]{2,1,0:T(8,128)(2,1)S(1)}, bf16[4,160,256]{2,1,0:T(8,128)(2,1)S(1)}, u32[]{:S(2)}, u32[]{:S(2)}) %collective-permute-start.22) | collective-permute-done | bytes 327712 | tf_op jit(solution)/shard_map/ppermute | solution.py:218
  117.6 1.0 copy-done.9
  118.6 1.2 weights.1
  119.8 18.3 %all_to_all.15 = bf16[16,32,768]{2,1,0:T(8,128)(2,1)S(1)} all-to-all(bf16[16,32,768]{2,1,0:T(8,128)(2,1)S(1)} %weights.1), channel_id=1, replica_groups=mesh['dp'=2,'outer'=4,'x'=4,'yh'=2,'core'=2] {'dp','x','yh'}, dimensions={0} | all-to-all | bytes 1572864 | tf_op jit(solution)/shard_map/all_to_all | solution.py:300
  138.2 0.6 fusion.13
  138.8 0.6 slice.12
  (69 shorter events, 1.6 us)
Async XLA Ops:
  0.6 9.1 %copy-start = (bf16[4096,128]{1,0:T(8,128)(2,1)S(1)}, bf16[4096,128]{1,0:T(8,128)(2,1)}, u32[]{:S(2)}) copy-start(bf16[4096,128]{1,0:T(8,128)(2,1)} %param.14) | copy-start | bytes 3145732
  0.6 9.1 %copy-start.1 = (bf16[1,160,4096]{2,1,0:T(8,128)(2,1)S(1)}, bf16[1,160,4096]{2,1,0:T(8,128)(2,1)}, u32[]{:S(2)}) copy-start(bf16[1,160,4096]{2,1,0:T(8,128)(2,1)} %param.11) | copy-start | bytes 3932164
  0.7 3.6 %copy-start.11 = (bf16[1,160,512]{2,1,0:T(8,128)(2,1)S(1)}, bf16[1,160,512]{2,1,0:T(8,128)(2,1)}, u32[]{:S(2)}) copy-start(bf16[1,160,512]{2,1,0:T(8,128)(2,1)} %param.16) | copy-start | bytes 491524
  4.3 6.0 %copy-start.10 = (bf16[4096,128]{1,0:T(8,128)(2,1)S(1)}, bf16[4096,128]{1,0:T(8,128)(2,1)}, u32[]{:S(2)}) copy-start(bf16[4096,128]{1,0:T(8,128)(2,1)} %param.15) | copy-start | bytes 3145732
  4.3 31.6 %collective-permute-start.2 = (bf16[160,1024]{1,0:T(8,128)(2,1)S(1)}, bf16[160,1024]{1,0:T(8,128)(2,1)}, u32[]{:S(2)}, u32[]{:S(2)}) collective-permute-start(bf16[160,1024]{1,0:T(8,128)(2,1)S(1)} %pad_maximum_fusion.1.p0), channel_id=1, source_target_pairs={{0,48},{16,0},{32,16},{48,32},{1,49},{17,1},{33,17},{49,33},{2,50}... | collective-permute-start | bytes 983048 | tf_op jit(solution)/shard_map/ppermute | solution.py:218
  8.5 28.8 %collective-permute-start.1 = (bf16[160,1024]{1,0:T(8,128)(2,1)S(1)}, bf16[160,1024]{1,0:T(8,128)(2,1)}, u32[]{:S(2)}, u32[]{:S(2)}) collective-permute-start(bf16[160,1024]{1,0:T(8,128)(2,1)S(1)} %pad_maximum_fusion.1.p0), channel_id=1, source_target_pairs={{0,32},{16,48},{32,0},{48,16},{1,33},{17,49},{33,1},{49,17},{2,34}... | collective-permute-start | bytes 983048 | tf_op jit(solution)/shard_map/ppermute | solution.py:218
  8.5 30.2 %collective-permute-start = (bf16[160,1024]{1,0:T(8,128)(2,1)S(1)}, bf16[160,1024]{1,0:T(8,128)(2,1)}, u32[]{:S(2)}, u32[]{:S(2)}) collective-permute-start(bf16[160,1024]{1,0:T(8,128)(2,1)S(1)} %pad_maximum_fusion.1.p0), channel_id=1, source_target_pairs={{0,16},{16,32},{32,48},{48,0},{1,17},{17,33},{33,49},{49,1},{2,18}... | collective-permute-start | bytes 983048 | tf_op jit(solution)/shard_map/ppermute | solution.py:218
  10.8 7.9 %copy-start.12 = (s32[4]{0:T(128)S(1)}, s32[4]{0:T(128)}, u32[]{:S(2)}) copy-start(s32[4]{0:T(128)} %constant.77) | copy-start | bytes 52
  10.8 8.1 %copy-start.13 = (s32[1,128]{1,0:T(1,128)S(1)}, s32[1,128]{1,0:T(1,128)}, u32[]{:S(2)}) copy-start(s32[1,128]{1,0:T(1,128)} %param.12) | copy-start | bytes 1540
  10.8 8.4 %copy-start.15 = (s32[2,1,1]{0,2,1:T(1,128)S(1)}, s32[2,1,1]{0,2,1:T(1,128)}, u32[]{:S(2)}) copy-start(s32[2,1,1]{0,2,1:T(1,128)} %constant.69.clone) | copy-start | bytes 28
  10.8 8.4 %copy-start.14 = (s32[1,8,1]{1,2,0:T(1,128)S(1)}, s32[1,8,1]{1,2,0:T(1,128)}, u32[]{:S(2)}) copy-start(s32[1,8,1]{1,2,0:T(1,128)} %constant.68.clone) | copy-start | bytes 100
  11.8 18.3 %all-to-all-start = ((bf16[8,160,256]{2,1,0:T(8,128)(2,1)}), bf16[8,160,256]{2,1,0:T(8,128)(2,1)S(1)}, u32[]{:S(2)}, u32[]{:S(2)}) async-start(bf16[8,160,256]{2,1,0:T(8,128)(2,1)} %broadcast_in_dim.47), calls=%async_computation | async-start | bytes 1310720 | tf_op jit(solution)/shard_map/all_to_all | solution.py:241
  18.7 12.0 %collective-permute-start.3 = (bf16[160,4096]{1,0:T(8,128)(2,1)S(1)}, bf16[160,4096]{1,0:T(8,128)(2,1)}, u32[]{:S(2)}, u32[]{:S(2)}) collective-permute-start(bf16[160,4096]{1,0:T(8,128)(2,1)S(1)} %bitcast.28), channel_id=1, source_target_pairs={{0,1},{1,0},{2,3},{3,2},{4,5},{5,4},{6,7},{7,6},{8,9},{9,8},{10,11... | collective-permute-start | bytes 3932168 | tf_op jit(solution)/shard_map/ppermute | solution.py:218
  30.1 8.6 %collective-permute-start.4 = (bf16[1280,256]{1,0:T(8,128)(2,1)S(1)}, bf16[1280,256]{1,0:T(8,128)(2,1)}, u32[]{:S(2)}, u32[]{:S(2)}) collective-permute-start(bf16[1280,256]{1,0:T(8,128)(2,1)S(1)} %bitcast.35), channel_id=1, source_target_pairs={{0,1},{1,0},{2,3},{3,2},{4,5},{5,4},{6,7},{7,6},{8,9},{9,8},{10,11... | collective-permute-start | bytes 1966088 | tf_op jit(solution)/shard_map/ppermute | solution.py:218
  32.9 0.7 copy-start.2
  33.7 26.0 %collective-permute-start.8 = (bf16[2,160,512]{2,1,0:T(8,128)(2,1)S(1)}, bf16[2,160,512]{2,1,0:T(8,128)(2,1)S(1)}, u32[]{:S(2)}, u32[]{:S(2)}) collective-permute-start(bf16[2,160,512]{2,1,0:T(8,128)(2,1)S(1)} %get-tuple-element.34), channel_id=1, source_target_pairs={{0,16},{16,32},{32,48},{48,0},{1,17},{17,33},{33,49},{49,1},{2,18}... | collective-permute-start | bytes 983048 | tf_op jit(solution)/shard_map/ppermute | solution.py:218
  35.9 23.8 %collective-permute-start.9 = (bf16[2,160,512]{2,1,0:T(8,128)(2,1)S(1)}, bf16[2,160,512]{2,1,0:T(8,128)(2,1)S(1)}, u32[]{:S(2)}, u32[]{:S(2)}) collective-permute-start(bf16[2,160,512]{2,1,0:T(8,128)(2,1)S(1)} %get-tuple-element.35), channel_id=1, source_target_pairs={{0,32},{16,48},{32,0},{48,16},{1,33},{17,49},{33,1},{49,17},{2,34}... | collective-permute-start | bytes 983048 | tf_op jit(solution)/shard_map/ppermute | solution.py:218
  37.3 22.4 %collective-permute-start.10 = (bf16[2,160,512]{2,1,0:T(8,128)(2,1)S(1)}, bf16[2,160,512]{2,1,0:T(8,128)(2,1)S(1)}, u32[]{:S(2)}, u32[]{:S(2)}) collective-permute-start(bf16[2,160,512]{2,1,0:T(8,128)(2,1)S(1)} %get-tuple-element.36), channel_id=1, source_target_pairs={{0,48},{16,0},{32,16},{48,32},{1,49},{17,1},{33,17},{49,33},{2,50}... | collective-permute-start | bytes 983048 | tf_op jit(solution)/shard_map/ppermute | solution.py:218
  50.4 4.1 %collective-permute-start.7 = (f32[3,2560]{1,0:T(4,128)S(1)}, f32[3,2560]{1,0:T(4,128)S(1)}, u32[]{:S(2)}, u32[]{:S(2)}) collective-permute-start(f32[3,2560]{1,0:T(4,128)S(1)} %stats.1.s0), channel_id=1, source_target_pairs={{0,48},{16,0},{32,16},{48,32},{1,49},{17,1},{33,17},{49,33},{2,50}... | collective-permute-start | bytes 92168 | tf_op jit(solution)/shard_map/ppermute | solution.py:218
  51.7 5.5 %collective-permute-start.6 = (f32[3,2560]{1,0:T(4,128)S(1)}, f32[3,2560]{1,0:T(4,128)S(1)}, u32[]{:S(2)}, u32[]{:S(2)}) collective-permute-start(f32[3,2560]{1,0:T(4,128)S(1)} %stats.1.s0), channel_id=1, source_target_pairs={{0,32},{16,48},{32,0},{48,16},{1,33},{17,49},{33,1},{49,17},{2,34}... | collective-permute-start | bytes 92168 | tf_op jit(solution)/shard_map/ppermute | solution.py:218
  54.5 5.2 %collective-permute-start.5 = (f32[3,2560]{1,0:T(4,128)S(1)}, f32[3,2560]{1,0:T(4,128)S(1)}, u32[]{:S(2)}, u32[]{:S(2)}) collective-permute-start(f32[3,2560]{1,0:T(4,128)S(1)} %stats.1.s0), channel_id=1, source_target_pairs={{0,16},{16,32},{32,48},{48,0},{1,17},{17,33},{33,49},{49,1},{2,18}... | collective-permute-start | bytes 92168 | tf_op jit(solution)/shard_map/ppermute | solution.py:218
  59.7 21.1 %copy-start.4 = (bf16[2,160,512]{2,1,0:T(8,128)(2,1)}, bf16[2,160,512]{2,1,0:T(8,128)(2,1)S(1)}, u32[]{:S(2)}) copy-start(bf16[2,160,512]{2,1,0:T(8,128)(2,1)S(1)} %collective-permute-done.8.x1) | copy-start | bytes 983044
  59.7 21.1 %copy-start.6 = (bf16[2,160,512]{2,1,0:T(8,128)(2,1)}, bf16[2,160,512]{2,1,0:T(8,128)(2,1)S(1)}, u32[]{:S(2)}) copy-start(bf16[2,160,512]{2,1,0:T(8,128)(2,1)S(1)} %collective-permute-done.9.x2) | copy-start | bytes 983044
  59.7 21.1 %copy-start.8 = (bf16[2,160,512]{2,1,0:T(8,128)(2,1)}, bf16[2,160,512]{2,1,0:T(8,128)(2,1)S(1)}, u32[]{:S(2)}) copy-start(bf16[2,160,512]{2,1,0:T(8,128)(2,1)S(1)} %collective-permute-done.10.x3) | copy-start | bytes 983044
  80.8 2.4 %collective-permute-start.17 = (bf16[1280,256]{1,0:T(8,128)(2,1)S(1)}, bf16[1280,256]{1,0:T(8,128)(2,1)S(1)}, u32[]{:S(2)}, u32[]{:S(2)}) collective-permute-start(bf16[1280,256]{1,0:T(8,128)(2,1)S(1)} %get-tuple-element.50), channel_id=1, source_target_pairs={{0,1},{1,0},{2,3},{3,2},{4,5},{5,4},{6,7},{7,6},{8,9},{9,8},{10,11... | collective-permute-start | bytes 1966088 | tf_op jit(solution)/shard_map/ppermute | solution.py:218
  80.9 7.7 %collective-permute-start.11 = (bf16[160,512]{1,0:T(8,128)(2,1)S(1)}, bf16[160,512]{1,0:T(8,128)(2,1)S(1)}, u32[]{:S(2)}, u32[]{:S(2)}) collective-permute-start(bf16[160,512]{1,0:T(8,128)(2,1)S(1)} %get-tuple-element.46), channel_id=1, source_target_pairs={{0,48},{16,0},{32,16},{48,32},{1,49},{17,1},{33,17},{49,33},{2,50}... | collective-permute-start | bytes 491528 | tf_op jit(solution)/shard_map/ppermute | solution.py:218
  82.2 8.6 %collective-permute-start.12 = (bf16[160,512]{1,0:T(8,128)(2,1)S(1)}, bf16[160,512]{1,0:T(8,128)(2,1)S(1)}, u32[]{:S(2)}, u32[]{:S(2)}) collective-permute-start(bf16[160,512]{1,0:T(8,128)(2,1)S(1)} %get-tuple-element.47), channel_id=1, source_target_pairs={{0,32},{16,48},{32,0},{48,16},{1,33},{17,49},{33,1},{49,17},{2,34}... | collective-permute-start | bytes 491528 | tf_op jit(solution)/shard_map/ppermute | solution.py:218
  82.6 10.8 %collective-permute-start.13 = (bf16[160,512]{1,0:T(8,128)(2,1)S(1)}, bf16[160,512]{1,0:T(8,128)(2,1)S(1)}, u32[]{:S(2)}, u32[]{:S(2)}) collective-permute-start(bf16[160,512]{1,0:T(8,128)(2,1)S(1)} %get-tuple-element.48), channel_id=1, source_target_pairs={{0,16},{16,32},{32,48},{48,0},{1,17},{17,33},{33,49},{49,1},{2,18}... | collective-permute-start | bytes 491528 | tf_op jit(solution)/shard_map/ppermute | solution.py:218
  84.2 21.5 %all-to-all-start.1 = ((bf16[8,160,256]{2,1,0:T(8,128)(2,1)}), bf16[8,160,256]{2,1,0:T(8,128)(2,1)}, u32[]{:S(2)}, u32[]{:S(2)}) async-start(bf16[8,160,256]{2,1,0:T(8,128)(2,1)} %bitcast.8), calls=%async_computation.1 | async-start | bytes 1310720 | tf_op jit(solution)/shard_map/all_to_all | solution.py:285
  93.5 7.1 %collective-permute-start.16 = (bf16[160,512]{1,0:T(8,128)(2,1)S(1)}, bf16[160,512]{1,0:T(8,128)(2,1)S(1)}, u32[]{:S(2)}, u32[]{:S(2)}) collective-permute-start(bf16[160,512]{1,0:T(8,128)(2,1)S(1)} %add_convert_fusion.1.q0), channel_id=1, source_target_pairs={{0,48},{16,0},{32,16},{48,32},{1,49},{17,1},{33,17},{49,33},{2,50}... | collective-permute-start | bytes 491528 | tf_op jit(solution)/shard_map/ppermute | solution.py:218
  94.3 8.5 %collective-permute-start.15 = (bf16[160,512]{1,0:T(8,128)(2,1)S(1)}, bf16[160,512]{1,0:T(8,128)(2,1)S(1)}, u32[]{:S(2)}, u32[]{:S(2)}) collective-permute-start(bf16[160,512]{1,0:T(8,128)(2,1)S(1)} %add_convert_fusion.1.q0), channel_id=1, source_target_pairs={{0,32},{16,48},{32,0},{48,16},{1,33},{17,49},{33,1},{49,17},{2,34}... | collective-permute-start | bytes 491528 | tf_op jit(solution)/shard_map/ppermute | solution.py:218
  94.6 10.1 %collective-permute-start.14 = (bf16[160,512]{1,0:T(8,128)(2,1)S(1)}, bf16[160,512]{1,0:T(8,128)(2,1)S(1)}, u32[]{:S(2)}, u32[]{:S(2)}) collective-permute-start(bf16[160,512]{1,0:T(8,128)(2,1)S(1)} %add_convert_fusion.1.q0), channel_id=1, source_target_pairs={{0,16},{16,32},{32,48},{48,0},{1,17},{17,33},{33,49},{49,1},{2,18}... | collective-permute-start | bytes 491528 | tf_op jit(solution)/shard_map/ppermute | solution.py:218
  104.7 12.9 %copy-start.3 = (bf16[2,160,512]{2,1,0:T(8,128)(2,1)S(1)}, bf16[2,160,512]{2,1,0:T(8,128)(2,1)}, u32[]{:S(2)}) copy-start(bf16[2,160,512]{2,1,0:T(8,128)(2,1)} %copy-done.2) | copy-start | bytes 983044
  104.7 12.9 %copy-start.5 = (bf16[2,160,512]{2,1,0:T(8,128)(2,1)S(1)}, bf16[2,160,512]{2,1,0:T(8,128)(2,1)}, u32[]{:S(2)}) copy-start(bf16[2,160,512]{2,1,0:T(8,128)(2,1)} %copy-done.4) | copy-start | bytes 983044
  104.7 12.9 %copy-start.7 = (bf16[2,160,512]{2,1,0:T(8,128)(2,1)S(1)}, bf16[2,160,512]{2,1,0:T(8,128)(2,1)}, u32[]{:S(2)}) copy-start(bf16[2,160,512]{2,1,0:T(8,128)(2,1)} %copy-done.6) | copy-start | bytes 983044
  105.7 10.4 %collective-permute-start.21 = (bf16[4,160,512]{2,1,0:T(8,128)(2,1)}, bf16[4,160,512]{2,1,0:T(8,128)(2,1)S(1)}, u32[]{:S(2)}, u32[]{:S(2)}) collective-permute-start(bf16[4,160,512]{2,1,0:T(8,128)(2,1)} %pad_maximum_fusion), channel_id=1, source_target_pairs={{0,1},{1,0},{2,3},{3,2},{4,5},{5,4},{6,7},{7,6},{8,9},{9,8},{10,11... | collective-permute-start | bytes 1966088 | tf_op jit(solution)/shard_map/ppermute | solution.py:218
  106.9 5.3 %collective-permute-start.20 = (bf16[160,256]{1,0:T(8,128)(2,1)S(1)}, bf16[160,256]{1,0:T(8,128)(2,1)S(1)}, u32[]{:S(2)}, u32[]{:S(2)}) collective-permute-start(bf16[160,256]{1,0:T(8,128)(2,1)S(1)} %reduce_sum.41.k0), channel_id=1, source_target_pairs={{0,48},{16,0},{32,16},{48,32},{1,49},{17,1},{33,17},{49,33},{2,50}... | collective-permute-start | bytes 245768 | tf_op jit(solution)/shard_map/ppermute | solution.py:218
  108.0 6.6 %collective-permute-start.19 = (bf16[160,256]{1,0:T(8,128)(2,1)S(1)}, bf16[160,256]{1,0:T(8,128)(2,1)S(1)}, u32[]{:S(2)}, u32[]{:S(2)}) collective-permute-start(bf16[160,256]{1,0:T(8,128)(2,1)S(1)} %reduce_sum.41.k0), channel_id=1, source_target_pairs={{0,32},{16,48},{32,0},{48,16},{1,33},{17,49},{33,1},{49,17},{2,34}... | collective-permute-start | bytes 245768 | tf_op jit(solution)/shard_map/ppermute | solution.py:218
  108.0 7.8 %collective-permute-start.18 = (bf16[160,256]{1,0:T(8,128)(2,1)S(1)}, bf16[160,256]{1,0:T(8,128)(2,1)S(1)}, u32[]{:S(2)}, u32[]{:S(2)}) collective-permute-start(bf16[160,256]{1,0:T(8,128)(2,1)S(1)} %reduce_sum.41.k0), channel_id=1, source_target_pairs={{0,16},{16,32},{32,48},{48,0},{1,17},{17,33},{33,49},{49,1},{2,18}... | collective-permute-start | bytes 245768 | tf_op jit(solution)/shard_map/ppermute | solution.py:218
  115.9 1.7 %collective-permute-start.22 = (bf16[4,160,256]{2,1,0:T(8,128)(2,1)S(1)}, bf16[4,160,256]{2,1,0:T(8,128)(2,1)S(1)}, u32[]{:S(2)}, u32[]{:S(2)}) collective-permute-start(bf16[4,160,256]{2,1,0:T(8,128)(2,1)S(1)} %pad_maximum_fusion.2), channel_id=1, source_target_pairs={{0,1},{1,0},{2,3},{3,2},{4,5},{5,4},{6,7},{7,6},{8,9},{9,8},{10,11... | collective-permute-start | bytes 983048 | tf_op jit(solution)/shard_map/ppermute | solution.py:218
  117.6 1.0 copy-start.9

commit v6 on v5

--- a/solution.py
+++ b/solution.py
@@ -40,12 +40,11 @@
     return (d - 1) % N_OUT * SLOT
 
 
-def fill_rows(pieces, q_ref, g_ref):
+def fill_rows(pieces, rows_ref):
     for d in range(N_OUT):
         for h in range(HEADS):
             r0 = slot_start(d) + h * ROWS
-            q_ref[r0 : r0 + ROWS, :] = pieces[d][:, h * HEAD : (h + 1) * HEAD]
-            g_ref[r0 : r0 + ROWS, :] = pieces[d][:, (HEADS + h) * HEAD : (HEADS + h + 1) * HEAD]
+            rows_ref[r0 : r0 + ROWS, :] = pieces[d][:, h * HEAD : (h + 1) * HEAD]
 
 
 def masked_scores(key_rows, q, posq, ordk_ref, block):
@@ -59,8 +58,9 @@
     return jnp.concatenate(parts, axis=0)
 
 
-def stats_kernel(ordk_ref, posq_ref, p0, p1, p2, p3, kva, kvb, out_ref, qr, gr):
-    fill_rows((p0, p1, p2, p3), qr, gr)
+def stats_pass(block, ordk_ref, posq_ref, qs, gs, kv, before, out_ref, qr, gr):
+    fill_rows(qs, qr)
+    fill_rows(gs, gr)
 
     def row_tile(rt, _):
         r0 = pl.multiple_of(rt * RT, RT)
@@ -70,10 +70,8 @@
         top = jnp.full((8, RT), masked_fill, f32)
         total = jnp.zeros((8, RT), f32)
         weighted = jnp.zeros((8, RT), f32)
-        for chunk in range(KEYS // KS):
-            kv = kva if chunk * KS < KHALF else kvb
-            k0 = chunk * KS % KHALF
-            score = masked_scores(kv[k0 : k0 + KS, :HEAD], q, posq, ordk_ref, chunk * (KS // HALF))
+        for k0 in range(0, KHALF, KS):
+            score = masked_scores(kv[k0 : k0 + KS, :HEAD], q, posq, ordk_ref, block + k0 // HALF)
             dprob = dot(kv[k0 : k0 + KS, HEAD:], g, NT)
             score = score.reshape(KS // 8, 8, RT)
             new_top = jnp.maximum(top, jnp.max(score, axis=0))
@@ -83,13 +81,31 @@
             weighted = weighted * factor + jnp.sum(weights * dprob.reshape(KS // 8, 8, RT), axis=0)
             top = new_top
         row_top = jnp.max(top, axis=0, keepdims=True)
+        if before is not None:
+            row_top = jnp.maximum(row_top, before[0:1, pl.ds(r0, RT)])
         factor = jnp.exp2(top - row_top)
+        total = jnp.sum(total * factor, axis=0, keepdims=True)
+        weighted = jnp.sum(weighted * factor, axis=0, keepdims=True)
+        if before is not None:
+            factor = jnp.exp2(before[0:1, pl.ds(r0, RT)] - row_top)
+            total = total + before[1:2, pl.ds(r0, RT)] * factor
+            weighted = weighted + before[2:3, pl.ds(r0, RT)] * factor
         out_ref[0:1, pl.ds(r0, RT)] = row_top
-        out_ref[1:2, pl.ds(r0, RT)] = jnp.sum(total * factor, axis=0, keepdims=True)
-        out_ref[2:3, pl.ds(r0, RT)] = jnp.sum(weighted * factor, axis=0, keepdims=True)
+        out_ref[1:2, pl.ds(r0, RT)] = total
+        out_ref[2:3, pl.ds(r0, RT)] = weighted
         return 0
 
     lax.fori_loop(0, ALL_ROWS // RT, row_tile, 0)
+
+
+def stats_own(ordk, posq, q0, q1, q2, q3, g0, g1, g2, g3, kva, out, qr, gr):
+    stats_pass(0, ordk, posq, (q0, q1, q2, q3), (g0, g1, g2, g3), kva, None, out, qr, gr)
+
+
+def stats_other(ordk, posq, q0, q1, q2, q3, g0, g1, g2, g3, kvb, before, out, qr, gr):
+    stats_pass(
+        KHALF // HALF, ordk, posq, (q0, q1, q2, q3), (g0, g1, g2, g3), kvb, before, out, qr, gr
+    )
 
 
 def combine_stats(stats, rowstat_ref):
@@ -113,10 +129,11 @@
 
 
 def grads_kernel(
-    ordk, posq_ref, s0, s1, s2, s3, p0, p1, p2, p3, kva, kvb,
+    ordk, posq_ref, s0, s1, s2, s3, q0, q1, q2, q3, g0, g1, g2, g3, kva, kvb,
     dq0, dq1, dq2, dq3, keep, send, qr, gr, rowstat, dqr, dkv,
 ):
-    fill_rows((p0, p1, p2, p3), qr, gr)
+    fill_rows((q0, q1, q2, q3), qr)
+    fill_rows((g0, g1, g2, g3), gr)
     combine_stats((s0, s1, s2, s3), rowstat)
     dkv[...] = jnp.zeros_like(dkv)
 
@@ -183,6 +200,14 @@
         out[p] = dw[p * 32 : (p + 1) * 32]
 
 
+def last_sum(parts, dwq, dwk, dwv):
+    total = jnp.sum(parts[...].astype(f32), axis=0)
+    wide = HEADS * HEAD
+    dwq[...] = total[:, :wide]
+    dwk[...] = total[:, wide : wide + HEAD]
+    dwv[...] = total[:, wide + HEAD :]
+
+
 VM = 24
 smem = pl.BlockSpec(memory_space=pltpu.SMEM)
 vmem = pl.BlockSpec(memory_space=pltpu.VMEM)
@@ -229,7 +254,10 @@
     o, ix, iy, ic = (lax.axis_index(a) for a in ("outer", "x", "yh", "core"))
 
     query = dot(tokens, w_query, NN).astype(bf16)
-    ps = from_behind(jnp.concatenate([query, dout], axis=1), "outer", N_OUT)
+    q1, q3 = shift(query, "outer", 1, N_OUT), shift(query, "outer", -1, N_OUT)
+    g1, g3 = shift(dout, "outer", 1, N_OUT), shift(dout, "outer", -1, N_OUT)
+    qs = [query, q1, shift(q1, "outer", 1, N_OUT), q3]
+    gs = [dout, g1, shift(g3, "outer", -1, N_OUT), g3]
     kv = jnp.concatenate(
         [
             dot(tokens, w_key, NN).astype(bf16),
@@ -237,24 +265,6 @@
         ],
         axis=1,
     )
-    kva = jnp.broadcast_to(kv[None], (8,) + kv.shape)
-    kva = lax.all_to_all(kva, ("x", "yh"), 0, 0, tiled=True).reshape(KHALF, 2 * HEAD)
-    kvb = shift(kva, "core", 1, 2)
-
-    key_dev = (o * 8 + np.arange(8)[None, :, None]) * 2 + (ic + np.arange(2)[:, None, None]) % 2
-    key_blocks = (key_dev * 2 + np.arange(2)[None, None, :]).reshape(-1)
-    query_dev = (((o - np.array([1, 2, 3, 0])) % N_OUT * N_X + ix) * 2 + iy) * 2 + ic
-    query_blocks = (query_dev[:, None] * 2 + np.arange(2)[None, :]).reshape(-1)
-
-    def look_up(blocks):
-        hit = blocks[:, None] == jnp.arange(order.shape[0], dtype=jnp.int32)[None, :]
-        return jnp.sum(jnp.where(hit, order[None, :], 0), axis=1)
-
-    ordk = look_up(key_blocks)
-    ordq = look_up(query_blocks).reshape(N_OUT, 1, 2, 1)
-    posq = ordq * HALF + jnp.arange(HALF, dtype=jnp.int32)
-    posq = jnp.broadcast_to(posq, (N_OUT, HEADS, 2, HALF)).reshape(1, ALL_ROWS)
-
     place = jnp.stack([o, ic])
     later, kv = lax.optimization_barrier((tokens, kv))
     other_tokens = shift(later, "core", 1, 2)
@@ -262,14 +272,37 @@
         columns_kernel, "columns", [((2, ROWS, 512), bf16)] * N_OUT, [],
         cost(ROWS * 4096, 4, 5 << 20), {}, 1, place, later, other_tokens,
     )
-    xs, kva = lax.optimization_barrier((xs, kva))
+    kva = jnp.broadcast_to(kv[None], (8,) + kv.shape)
+    kva = lax.all_to_all(kva, ("x", "yh"), 0, 0, tiled=True).reshape(KHALF, 2 * HEAD)
+    kva, qs, gs, xs = lax.optimization_barrier((kva, qs, gs, xs))
+    kvb = shift(kva, "core", 1, 2)
+
+    key_dev = (o * 8 + np.arange(8)[None, :, None]) * 2 + (ic + np.arange(2)[:, None, None]) % 2
+    key_blocks = (key_dev * 2 + np.arange(2)[None, None, :]).reshape(-1)
+    query_dev = (((o - np.array([1, 2, 3, 0])) % N_OUT * N_X + ix) * 2 + iy) * 2 + ic
+    query_blocks = (query_dev[:, None] * 2 + np.arange(2)[None, :]).reshape(-1)
+
+    def look_up(blocks):
+        hit = blocks[:, None] == jnp.arange(order.shape[0], dtype=jnp.int32)[None, :]
+        return jnp.sum(jnp.where(hit, order[None, :], 0), axis=1)
+
+    ordk = look_up(key_blocks)
+    ordq = look_up(query_blocks).reshape(N_OUT, 1, 2, 1)
+    posq = ordq * HALF + jnp.arange(HALF, dtype=jnp.int32)
+    posq = jnp.broadcast_to(posq, (N_OUT, HEADS, 2, HALF)).reshape(1, ALL_ROWS)
+
+    pairs = cost(ALL_ROWS * KHALF, 2, 4 << 20)
+    row_stats = [((3, ALL_ROWS), f32)]
+    (stats,) = kernel_call(
+        stats_own, "stats_own", row_stats, row_scratch, pairs, {}, 1, ordk, posq, *qs, *gs, kva
+    )
+    (stats,) = kernel_call(
+        stats_other, "stats_other", row_stats, row_scratch, pairs, {}, 1,
+        ordk, posq, *qs, *gs, kvb, stats,
+    )
+    xs, stats = lax.optimization_barrier((xs, stats))
     xs = [xs[0]] + [shift(xs[d], "outer", d, N_OUT) for d in range(1, N_OUT)]
-    (stats,) = kernel_call(
-        stats_kernel, "stats", [((3, ALL_ROWS), f32)], row_scratch,
-        cost(ALL_ROWS * KEYS, 2, 4 << 20), {}, 1, ordk, posq, *ps, kva, kvb,
-    )
     all_stats = from_behind(stats, "outer", N_OUT)
-    all_stats, xs = lax.optimization_barrier((all_stats, xs))
 
     half = (KHALF, 2 * HEAD)
     dq, dq1, dq2, dq3, keep, send = kernel_call(
@@ -277,17 +310,19 @@
         [((ROWS, WIDE), f32)] + [((ROWS, WIDE), bf16)] * 3 + [(half, f32), (half, bf16)],
         row_scratch + [((2, ALL_ROWS), f32), acc_rows, ((KEYS, 2 * HEAD), f32)],
         cost(ALL_ROWS * KEYS, 5, 8 << 20), {}, 1,
-        ordk, posq, *all_stats, *ps, kva, kvb,
-    )
+        ordk, posq, *all_stats, *qs, *gs, kva, kvb,
+    )
+    send, dq1, dq2, dq3, xs = lax.optimization_barrier((send, dq1, dq2, dq3, xs))
     got = shift(send, "core", 1, 2)
     dq_parts = [shift(part, "outer", -d, N_OUT) for d, part in ((1, dq1), (2, dq2), (3, dq3))]
     dkv = (keep + got.astype(f32)).astype(bf16).reshape(8, ROWS, 2 * HEAD)
     dkv = lax.all_to_all(dkv, ("x", "yh"), 0, 0, tiled=True)
-    dkv = jnp.sum(dkv.astype(f32), axis=0)
-    dkv_all = from_behind(dkv.astype(bf16), "outer", N_OUT)
+    dkv = jnp.sum(dkv.astype(f32), axis=0).astype(bf16)
+    dkv_all = from_behind(dkv, "outer", N_OUT)
     for part in dq_parts:
         dq = dq + part.astype(f32)
     dq_all = from_behind(dq.astype(bf16), "outer", N_OUT)
+    dq_all, dkv = lax.optimization_barrier((dq_all, dkv))
 
     dq_other = shift(jnp.stack(dq_all), "core", 1, 2)
     dkv_other = shift(jnp.stack(dkv_all), "core", 1, 2)
@@ -298,9 +333,10 @@
         *xs, *dq_all, *dkv_all, dq_other, dkv_other,
     )
     dw = lax.all_to_all(dw, ("dp", "x", "yh"), 0, 0, tiled=True)
-    dw = jnp.sum(dw.astype(f32), axis=0)
-    wide = HEADS * HEAD
-    return dw[:, :wide], dw[:, wide : wide + HEAD], dw[:, wide + HEAD :]
+    return kernel_call(
+        last_sum, "last_sum", [((32, WIDE), f32), ((32, HEAD), f32), ((32, HEAD), f32)], [],
+        cost(32 * 16, 3, 1 << 20), {}, 0, dw,
+    )
 
 
 def solution(mesh):

time: 140 us -> 138 us (0.986)
  waiting for transfers between devices: 39.1 us -> 19.8 us
  starting transfers between devices: 32 us -> 42.1 us
  local copies, waits for them, and re-layouts: 4.26 us -> 7.8 us
  Pallas kernels: 36.1 us -> 38.9 us
    ppermute x23 -> x26, waiting for transfers between devices: 28.3 us -> 12.7 us  [shift(): return lax.ppermute(x, axis, [(i, (i + d) % n) for i in range(n)])]
    all_to_all x1, waiting for transfers between devices: 10.8 us -> 1.15 us  [per_device(): lax.all_to_all(kva, ('x', 'yh'), 0, 0, tiled=True).reshape(KHALF, 2 * HEAD)]
    ppermute x23 -> x26, starting transfers between devices: 20.6 us -> 29.9 us  [shift(): return lax.ppermute(x, axis, [(i, (i + d) % n) for i in range(n)])]
    all_to_all x1, waiting for transfers between devices: 0.01 us -> 5.94 us  [per_device(): dkv = lax.all_to_all(dkv, ('x', 'yh'), 0, 0, tiled=True)]
    unnamed x32 -> x46, local copies, waits for them, and re-layouts: 1.77 us -> 6.54 us
    pallas_call x4 -> x6, Pallas kernels: 36.1 us -> 38.9 us  [kernel_call(): pl.pallas_call(body, out_shape=tuple((jax.ShapeDtypeStruct(*o) for o in o...]
  transfers between devices with their start and end apart: 25 -> 28, of which waited for: 13 -> 10; matrix products, arithmetic and copies ran while one was open for 4% -> 4% of each run, Pallas kernels for 10% -> 22%
where the time goes in v6:
time: 138 us; the launch traced here: 137 us
  starting transfers between devices  42.1 us (31%)
  Pallas kernels  38.9 us (28%)
  waiting for transfers between devices  19.8 us (14%)
  blocking collectives  19.5 us (14%)
  local copies, waits for them, and re-layouts  7.8 us (6%)
  matrix products  4.57 us (3%)
  other arithmetic  3.19 us (2%)
    pallas_call x6, Pallas kernels, kernel_call(): pl.pallas_call(body, out_shape=tuple((jax.ShapeDtypeStruct(*o) for o in o...  38.9 us
    ppermute x26, starting transfers between devices, shift(): return lax.ppermute(x, axis, [(i, (i + d) % n) for i in range(n)])  29.9 us
    all_to_all x1, blocking collectives, per_device(): dw = lax.all_to_all(dw, ('dp', 'x', 'yh'), 0, 0, tiled=True)  19.5 us
    ppermute x26, waiting for transfers between devices, shift(): return lax.ppermute(x, axis, [(i, (i + d) % n) for i in range(n)])  12.7 us
    all_to_all x1, starting transfers between devices, per_device(): lax.all_to_all(kva, ('x', 'yh'), 0, 0, tiled=True).reshape(KHALF, 2 * HEAD)  6.93 us
    unnamed x46, local copies, waits for them, and re-layouts  6.54 us
    all_to_all x1, waiting for transfers between devices, per_device(): dkv = lax.all_to_all(dkv, ('x', 'yh'), 0, 0, tiled=True)  5.94 us
    all_to_all x1, starting transfers between devices, per_device(): dkv = lax.all_to_all(dkv, ('x', 'yh'), 0, 0, tiled=True)  5.23 us
  transfers between devices with their start and end apart: 28, of which 10 were waited for; matrix products, arithmetic and copies ran while one was open for 4% of the time, Pallas kernels for 22%

profile of v6, /device:TPU:0, one launch (start us, length us, event | category | flops | bytes accessed | tf_op | source)
XLA Modules:
  0.0 137.0 jit_solution(11974422836961364759)
XLA Ops:
  0.7 3.6 %convolution_convert_fusion.q0 = bf16[160,512]{1,0:T(8,128)(2,1)S(1)} fusion(bf16[4096,512]{1,0:T(8,128)(2,1)} %param.13, bf16[1,160,4096]{2,1,0:T(8,128)(2,1)} %param.11), kind=kOutput, calls=%fused_computation.1 | convolution fusion | flops 671170560 | bytes 5668864 | tf_op jit(solution)/shard_map/dot_general | solution.py:36
  4.3 4.2 %collective-permute-start.2 = (bf16[160,512]{1,0:T(8,128)(2,1)S(1)}, bf16[160,512]{1,0:T(8,128)(2,1)}, u32[]{:S(2)}, u32[]{:S(2)}) collective-permute-start(bf16[160,512]{1,0:T(8,128)(2,1)S(1)} %convolution_convert_fusion.q0), channel_id=1, source_target_pairs={{0,48},{16,0},{32,16},{48,32},{1,49},{17,1},{33,17},{49,33},{2,50}... | collective-permute-start | bytes 491528 | tf_op jit(solution)/shard_map/ppermute | solution.py:243
  8.4 3.2 %collective-permute-start.4 = (bf16[160,512]{1,0:T(8,128)(2,1)}, bf16[160,512]{1,0:T(8,128)(2,1)}, u32[]{:S(2)}, u32[]{:S(2)}) collective-permute-start(bf16[160,512]{1,0:T(8,128)(2,1)} %bitcast.5.g0), channel_id=1, source_target_pairs={{0,48},{16,0},{32,16},{48,32},{1,49},{17,1},{33,17},{49,33},{2,50}... | collective-permute-start | bytes 491528 | tf_op jit(solution)/shard_map/ppermute | solution.py:243
  12.2 0.5 convolution_convert_fusion.1
  12.8 0.9 broadcast_in_dim.47
  13.7 6.9 %all-to-all-start = ((bf16[8,160,256]{2,1,0:T(8,128)(2,1)}), bf16[8,160,256]{2,1,0:T(8,128)(2,1)S(1)}, u32[]{:S(2)}, u32[]{:S(2)}) async-start(bf16[8,160,256]{2,1,0:T(8,128)(2,1)} %broadcast_in_dim.47), calls=%async_computation | async-start | bytes 1310720 | tf_op jit(solution)/shard_map/all_to_all | solution.py:276
  21.2 3.3 %collective-permute-start.5 = (bf16[160,512]{1,0:T(8,128)(2,1)}, bf16[160,512]{1,0:T(8,128)(2,1)S(1)}, u32[]{:S(2)}, u32[]{:S(2)}) collective-permute-start(bf16[160,512]{1,0:T(8,128)(2,1)} %collective-permute-done.4.g3), channel_id=1, source_target_pairs={{0,48},{16,0},{32,16},{48,32},{1,49},{17,1},{33,17},{49,33},{2,50}... | collective-permute-start | bytes 491528 | tf_op jit(solution)/shard_map/ppermute | solution.py:243
  24.6 2.2 %columns.1 = (bf16[2,160,512]{2,1,0:T(8,128)(2,1)S(1)}, bf16[2,160,512]{2,1,0:T(8,128)(2,1)S(1)}, bf16[2,160,512]{2,1,0:T(8,128)(2,1)S(1)}, bf16[2,160,512]{2,1,0:T(8,128)(2,1)S(1)}) custom-call(s32[2]{0:T(128)S(1)} %pad_add_fusion.place_ref, bf16[160,4096]{1,0:T(8,128)(2,1)S(1)} %bitcast.29, bf16[160,4096]{1,0:T(8,128)(2,1)} %collective-permute-done.6.other), custom_call_target="tpu_custom_call" | custom-call | flops 671088640 | bytes 5242880 | tf_op jit(solution)/shard_map/columns/pallas_call | solution.py:224
  26.9 0.7 copy-done.8
  27.6 0.7 copy-done.10
  28.3 0.7 copy-done.12
  29.5 0.7 copy-done.14
  30.2 0.7 copy-done.16
  30.9 1.1 all-to-all-done
  32.6 0.9 copy-done.15
  33.5 0.9 copy-done.17
  34.4 6.6 %stats_own.1.before = f32[3,2560]{1,0:T(4,128)S(1)} custom-call(s32[32]{0:T(128)S(1)} %select_reduce_fusion.ordk, s32[1,2560]{1,0:T(1,128)S(1)} %reshape.101.posq.posq_ref, bf16[160,512]{1,0:T(8,128)(2,1)S(1)} %convolution_convert_fusion.q0, bf16[160,512]{1,0:T(8,128)(2,1)} %collective-permute-done.q1, bf16[160,512]{1,0:T(8,128)(2,1)S(1)} %copy-done.15, ...), custom_call_target="tpu_custom_call" | custom-call | flops 1677721600 | bytes 4194304 | tf_op jit(solution)/shard_map/stats_own/pallas_call | solution.py:224
  41.0 6.9 %stats_other.1.s0 = f32[3,2560]{1,0:T(4,128)S(1)} custom-call(s32[32]{0:T(128)S(1)} %select_reduce_fusion.ordk, s32[1,2560]{1,0:T(1,128)S(1)} %reshape.101.posq.posq_ref, bf16[160,512]{1,0:T(8,128)(2,1)S(1)} %convolution_convert_fusion.q0, bf16[160,512]{1,0:T(8,128)(2,1)} %collective-permute-done.q1, bf16[160,512]{1,0:T(8,128)(2,1)S(1)} %copy-done.15, ...), custom_call_target="tpu_custom_call" | custom-call | flops 1677721600 | bytes 4194304 | tf_op jit(solution)/shard_map/stats_other/pallas_call | solution.py:224
  47.9 3.3 %collective-permute-start.10 = (f32[3,2560]{1,0:T(4,128)S(1)}, f32[3,2560]{1,0:T(4,128)S(1)}, u32[]{:S(2)}, u32[]{:S(2)}) collective-permute-start(f32[3,2560]{1,0:T(4,128)S(1)} %stats_other.1.s0), channel_id=1, source_target_pairs={{0,48},{16,0},{32,16},{48,32},{1,49},{17,1},{33,17},{49,33},{2,50}... | collective-permute-start | bytes 92168 | tf_op jit(solution)/shard_map/ppermute | solution.py:243
  51.2 1.1 collective-permute-start.8
  52.3 2.4 %collective-permute-start.11 = (bf16[2,160,512]{2,1,0:T(8,128)(2,1)S(1)}, bf16[2,160,512]{2,1,0:T(8,128)(2,1)S(1)}, u32[]{:S(2)}, u32[]{:S(2)}) collective-permute-start(bf16[2,160,512]{2,1,0:T(8,128)(2,1)S(1)} %copy-done.13), channel_id=1, source_target_pairs={{0,16},{16,32},{32,48},{48,0},{1,17},{17,33},{33,49},{49,1},{2,18}... | collective-permute-start | bytes 983048 | tf_op jit(solution)/shard_map/ppermute | solution.py:243
  54.7 1.2 collective-permute-start.12
  55.9 1.5 %collective-permute-start.13 = (bf16[2,160,512]{2,1,0:T(8,128)(2,1)S(1)}, bf16[2,160,512]{2,1,0:T(8,128)(2,1)S(1)}, u32[]{:S(2)}, u32[]{:S(2)}) collective-permute-start(bf16[2,160,512]{2,1,0:T(8,128)(2,1)S(1)} %copy-done.9), channel_id=1, source_target_pairs={{0,48},{16,0},{32,16},{48,32},{1,49},{17,1},{33,17},{49,33},{2,50}... | collective-permute-start | bytes 983048 | tf_op jit(solution)/shard_map/ppermute | solution.py:243
  57.5 1.1 copy-done.7
  58.5 21.3 %grads.1 = (f32[160,512]{1,0:T(8,128)S(1)}, bf16[160,512]{1,0:T(8,128)(2,1)}, bf16[160,512]{1,0:T(8,128)(2,1)S(1)}, bf16[160,512]{1,0:T(8,128)(2,1)S(1)}, f32[12...) custom-call(s32[32]{0:T(128)S(1)} %select_reduce_fusion.ordk, s32[1,2560]{1,0:T(1,128)S(1)} %reshape.101.posq.posq_ref, ...), custom_call_target="tpu_custom_call" | custom-call | flops 8388608000 | bytes 8388608 | tf_op jit(solution)/shard_map/grads/pallas_call | solution.py:224
  80.2 1.4 %collective-permute-start.14 = (bf16[160,512]{1,0:T(8,128)(2,1)}, bf16[160,512]{1,0:T(8,128)(2,1)S(1)}, u32[]{:S(2)}, u32[]{:S(2)}) collective-permute-start(bf16[160,512]{1,0:T(8,128)(2,1)} %get-tuple-element.78), channel_id=1, source_target_pairs={{0,48},{16,0},{32,16},{48,32},{1,49},{17,1},{33,17},{49,33},{2,50}... | collective-permute-start | bytes 491528 | tf_op jit(solution)/shard_map/ppermute | solution.py:243
  81.6 1.2 collective-permute-start.15
  82.8 0.6 collective-permute-start.16
  83.4 1.0 add_convert_fusion
  84.4 5.2 %all-to-all-start.1 = ((bf16[8,160,256]{2,1,0:T(8,128)(2,1)}), bf16[8,160,256]{2,1,0:T(8,128)(2,1)}, u32[]{:S(2)}, u32[]{:S(2)}) async-start(bf16[8,160,256]{2,1,0:T(8,128)(2,1)} %bitcast.8), calls=%async_computation.1 | async-start | bytes 1310720 | tf_op jit(solution)/shard_map/all_to_all | solution.py:319
  89.7 0.5 collective-permute-done.15
  90.2 2.7 %collective-permute-done.16 = bf16[160,512]{1,0:T(8,128)(2,1)S(1)} collective-permute-done((bf16[160,512]{1,0:T(8,128)(2,1)S(1)}, bf16[160,512]{1,0:T(8,128)(2,1)S(1)}, u32[]{:S(2)}, u32[]{:S(2)}) %collective-permute-start.16) | collective-permute-done | bytes 163872 | tf_op jit(solution)/shard_map/ppermute | solution.py:243
  93.0 0.7 collective-permute-start.19
  93.7 1.2 collective-permute-start.18
  94.9 0.8 collective-permute-start.17
  95.7 5.9 %all-to-all-done.1 = bf16[8,160,256]{2,1,0:T(8,128)(2,1)} async-done(((bf16[8,160,256]{2,1,0:T(8,128)(2,1)}), bf16[8,160,256]{2,1,0:T(8,128)(2,1)}, u32[]{:S(2)}, u32[]{:S(2)}) %all-to-all-start.1) | async-done | bytes 655392 | tf_op jit(solution)/shard_map/all_to_all | solution.py:319
  101.7 1.2 reduce_sum.32.k0
  102.9 1.4 %collective-permute-done.17.q1 = bf16[160,512]{1,0:T(8,128)(2,1)S(1)} collective-permute-done((bf16[160,512]{1,0:T(8,128)(2,1)S(1)}, bf16[160,512]{1,0:T(8,128)(2,1)S(1)}, u32[]{:S(2)}, u32[]{:S(2)}) %collective-permute-start.17) | collective-permute-done | bytes 163872 | tf_op jit(solution)/shard_map/ppermute | solution.py:243
  104.5 1.5 %collective-permute-start.23 = (bf16[160,256]{1,0:T(8,128)(2,1)S(1)}, bf16[160,256]{1,0:T(8,128)(2,1)S(1)}, u32[]{:S(2)}, u32[]{:S(2)}) collective-permute-start(bf16[160,256]{1,0:T(8,128)(2,1)S(1)} %reduce_sum.32.k0), channel_id=1, source_target_pairs={{0,48},{16,0},{32,16},{48,32},{1,49},{17,1},{33,17},{49,33},{2,50}... | collective-permute-start | bytes 245768 | tf_op jit(solution)/shard_map/ppermute | solution.py:243
  105.9 0.9 collective-permute-start.22
  106.9 0.9 collective-permute-start.21
  107.8 2.0 %collective-permute-done.23.k3 = bf16[160,256]{1,0:T(8,128)(2,1)S(1)} collective-permute-done((bf16[160,256]{1,0:T(8,128)(2,1)S(1)}, bf16[160,256]{1,0:T(8,128)(2,1)S(1)}, u32[]{:S(2)}, u32[]{:S(2)}) %collective-permute-start.23) | collective-permute-done | bytes 81952 | tf_op jit(solution)/shard_map/ppermute | solution.py:243
  109.8 2.9 %collective-permute-done.22.k2 = bf16[160,256]{1,0:T(8,128)(2,1)S(1)} collective-permute-done((bf16[160,256]{1,0:T(8,128)(2,1)S(1)}, bf16[160,256]{1,0:T(8,128)(2,1)S(1)}, u32[]{:S(2)}, u32[]{:S(2)}) %collective-permute-start.22) | collective-permute-done | bytes 81952 | tf_op jit(solution)/shard_map/ppermute | solution.py:243
  112.7 1.0 collective-permute-done.21.k1
  113.9 1.6 %collective-permute-done.25.ko = bf16[4,160,256]{2,1,0:T(8,128)(2,1)S(1)} collective-permute-done((bf16[4,160,256]{2,1,0:T(8,128)(2,1)S(1)}, bf16[4,160,256]{2,1,0:T(8,128)(2,1)S(1)}, u32[]{:S(2)}, u32[]{:S(2)}) %collective-permute-start.25) | collective-permute-done | bytes 327712 | tf_op jit(solution)/shard_map/ppermute | solution.py:243
  115.5 1.2 weights.1
  116.7 19.5 %all_to_all.15.parts = bf16[16,32,768]{2,1,0:T(8,128)(2,1)S(1)} all-to-all(bf16[16,32,768]{2,1,0:T(8,128)(2,1)S(1)} %weights.1), channel_id=1, replica_groups=mesh['dp'=2,'outer'=4,'x'=4,'yh'=2,'core'=2] {'dp','x','yh'}, dimensions={0} | all-to-all | bytes 1572864 | tf_op jit(solution)/shard_map/all_to_all | solution.py:335
  136.2 0.7 last_sum.1
  (87 shorter events, 3.0 us)
Async XLA Ops:
  0.6 11.1 %copy-start = (bf16[4096,128]{1,0:T(8,128)(2,1)S(1)}, bf16[4096,128]{1,0:T(8,128)(2,1)}, u32[]{:S(2)}) copy-start(bf16[4096,128]{1,0:T(8,128)(2,1)} %param.14) | copy-start | bytes 3145732
  0.6 11.0 %copy-start.1 = (bf16[1,160,4096]{2,1,0:T(8,128)(2,1)S(1)}, bf16[1,160,4096]{2,1,0:T(8,128)(2,1)}, u32[]{:S(2)}) copy-start(bf16[1,160,4096]{2,1,0:T(8,128)(2,1)} %param.11) | copy-start | bytes 3932164
  4.2 7.9 %copy-start.18 = (bf16[4096,128]{1,0:T(8,128)(2,1)S(1)}, bf16[4096,128]{1,0:T(8,128)(2,1)}, u32[]{:S(2)}) copy-start(bf16[4096,128]{1,0:T(8,128)(2,1)} %param.15) | copy-start | bytes 3145732
  4.3 24.8 %collective-permute-start.2 = (bf16[160,512]{1,0:T(8,128)(2,1)S(1)}, bf16[160,512]{1,0:T(8,128)(2,1)}, u32[]{:S(2)}, u32[]{:S(2)}) collective-permute-start(bf16[160,512]{1,0:T(8,128)(2,1)S(1)} %convolution_convert_fusion.q0), channel_id=1, source_target_pairs={{0,48},{16,0},{32,16},{48,32},{1,49},{17,1},{33,17},{49,33},{2,50}... | collective-permute-start | bytes 491528 | tf_op jit(solution)/shard_map/ppermute | solution.py:243
  8.4 12.8 %collective-permute-start = (bf16[160,512]{1,0:T(8,128)(2,1)S(1)}, bf16[160,512]{1,0:T(8,128)(2,1)}, u32[]{:S(2)}, u32[]{:S(2)}) collective-permute-start(bf16[160,512]{1,0:T(8,128)(2,1)S(1)} %convolution_convert_fusion.q0), channel_id=1, source_target_pairs={{0,16},{16,32},{32,48},{48,0},{1,17},{17,33},{33,49},{49,1},{2,18}... | collective-permute-start | bytes 491528 | tf_op jit(solution)/shard_map/ppermute | solution.py:243
  8.4 12.8 %collective-permute-start.4 = (bf16[160,512]{1,0:T(8,128)(2,1)}, bf16[160,512]{1,0:T(8,128)(2,1)}, u32[]{:S(2)}, u32[]{:S(2)}) collective-permute-start(bf16[160,512]{1,0:T(8,128)(2,1)} %bitcast.5.g0), channel_id=1, source_target_pairs={{0,48},{16,0},{32,16},{48,32},{1,49},{17,1},{33,17},{49,33},{2,50}... | collective-permute-start | bytes 491528 | tf_op jit(solution)/shard_map/ppermute | solution.py:243
  11.7 17.4 %collective-permute-start.3 = (bf16[160,512]{1,0:T(8,128)(2,1)}, bf16[160,512]{1,0:T(8,128)(2,1)}, u32[]{:S(2)}, u32[]{:S(2)}) collective-permute-start(bf16[160,512]{1,0:T(8,128)(2,1)} %bitcast.5.g0), channel_id=1, source_target_pairs={{0,16},{16,32},{32,48},{48,0},{1,17},{17,33},{33,49},{49,1},{2,18}... | collective-permute-start | bytes 491528 | tf_op jit(solution)/shard_map/ppermute | solution.py:243
  12.7 7.9 %copy-start.19 = (s32[4]{0:T(128)S(1)}, s32[4]{0:T(128)}, u32[]{:S(2)}) copy-start(s32[4]{0:T(128)} %constant.76) | copy-start | bytes 52
  12.7 8.1 %copy-start.20 = (s32[1,128]{1,0:T(1,128)S(1)}, s32[1,128]{1,0:T(1,128)}, u32[]{:S(2)}) copy-start(s32[1,128]{1,0:T(1,128)} %param.12) | copy-start | bytes 1540
  12.7 8.3 %copy-start.22 = (s32[2,1,1]{0,2,1:T(1,128)S(1)}, s32[2,1,1]{0,2,1:T(1,128)}, u32[]{:S(2)}) copy-start(s32[2,1,1]{0,2,1:T(1,128)} %constant.68.clone) | copy-start | bytes 28
  12.7 8.4 %copy-start.21 = (s32[1,8,1]{1,2,0:T(1,128)S(1)}, s32[1,8,1]{1,2,0:T(1,128)}, u32[]{:S(2)}) copy-start(s32[1,8,1]{1,2,0:T(1,128)} %constant.67.clone) | copy-start | bytes 100
  13.7 18.3 %all-to-all-start = ((bf16[8,160,256]{2,1,0:T(8,128)(2,1)}), bf16[8,160,256]{2,1,0:T(8,128)(2,1)S(1)}, u32[]{:S(2)}, u32[]{:S(2)}) async-start(bf16[8,160,256]{2,1,0:T(8,128)(2,1)} %broadcast_in_dim.47), calls=%async_computation | async-start | bytes 1310720 | tf_op jit(solution)/shard_map/all_to_all | solution.py:276
  20.6 4.0 %collective-permute-start.6 = (bf16[160,4096]{1,0:T(8,128)(2,1)S(1)}, bf16[160,4096]{1,0:T(8,128)(2,1)}, u32[]{:S(2)}, u32[]{:S(2)}) collective-permute-start(bf16[160,4096]{1,0:T(8,128)(2,1)S(1)} %bitcast.28), channel_id=1, source_target_pairs={{0,1},{1,0},{2,3},{3,2},{4,5},{5,4},{6,7},{7,6},{8,9},{9,8},{10,11... | collective-permute-start | bytes 3932168 | tf_op jit(solution)/shard_map/ppermute | solution.py:243
  21.2 8.3 %collective-permute-start.1 = (bf16[160,512]{1,0:T(8,128)(2,1)}, bf16[160,512]{1,0:T(8,128)(2,1)S(1)}, u32[]{:S(2)}, u32[]{:S(2)}) collective-permute-start(bf16[160,512]{1,0:T(8,128)(2,1)} %collective-permute-done.q1), channel_id=1, source_target_pairs={{0,16},{16,32},{32,48},{48,0},{1,17},{17,33},{33,49},{49,1},{2,18}... | collective-permute-start | bytes 491528 | tf_op jit(solution)/shard_map/ppermute | solution.py:243
  21.2 8.9 %collective-permute-start.5 = (bf16[160,512]{1,0:T(8,128)(2,1)}, bf16[160,512]{1,0:T(8,128)(2,1)S(1)}, u32[]{:S(2)}, u32[]{:S(2)}) collective-permute-start(bf16[160,512]{1,0:T(8,128)(2,1)} %collective-permute-done.4.g3), channel_id=1, source_target_pairs={{0,48},{16,0},{32,16},{48,32},{1,49},{17,1},{33,17},{49,33},{2,50}... | collective-permute-start | bytes 491528 | tf_op jit(solution)/shard_map/ppermute | solution.py:243
  26.8 0.7 copy-start.8
  27.6 0.7 copy-start.10
  32.0 9.0 %collective-permute-start.7 = (bf16[1280,256]{1,0:T(8,128)(2,1)S(1)}, bf16[1280,256]{1,0:T(8,128)(2,1)S(1)}, u32[]{:S(2)}, u32[]{:S(2)}) collective-permute-start(bf16[1280,256]{1,0:T(8,128)(2,1)S(1)} %bitcast.35), channel_id=1, source_target_pairs={{0,1},{1,0},{2,3},{3,2},{4,5},{5,4},{6,7},{7,6},{8,9},{9,8},{10,11... | collective-permute-start | bytes 1966088 | tf_op jit(solution)/shard_map/ppermute | solution.py:243
  32.5 0.9 copy-start.15
  33.5 0.9 copy-start.17
  41.0 11.3 %copy-start.13 = (bf16[2,160,512]{2,1,0:T(8,128)(2,1)S(1)}, bf16[2,160,512]{2,1,0:T(8,128)(2,1)}, u32[]{:S(2)}) copy-start(bf16[2,160,512]{2,1,0:T(8,128)(2,1)} %copy-done.12) | copy-start | bytes 983044
  41.0 13.7 %copy-start.11 = (bf16[2,160,512]{2,1,0:T(8,128)(2,1)S(1)}, bf16[2,160,512]{2,1,0:T(8,128)(2,1)}, u32[]{:S(2)}) copy-start(bf16[2,160,512]{2,1,0:T(8,128)(2,1)} %copy-done.10) | copy-start | bytes 983044
  41.0 14.9 %copy-start.9 = (bf16[2,160,512]{2,1,0:T(8,128)(2,1)S(1)}, bf16[2,160,512]{2,1,0:T(8,128)(2,1)}, u32[]{:S(2)}) copy-start(bf16[2,160,512]{2,1,0:T(8,128)(2,1)} %copy-done.8) | copy-start | bytes 983044
  41.0 6.9 %copy-start.6 = (bf16[1280,256]{1,0:T(8,128)(2,1)}, bf16[1280,256]{1,0:T(8,128)(2,1)S(1)}, u32[]{:S(2)}) copy-start(bf16[1280,256]{1,0:T(8,128)(2,1)S(1)} %collective-permute-done.7.kvb) | copy-start | bytes 1966084
  47.9 8.0 %collective-permute-start.10 = (f32[3,2560]{1,0:T(4,128)S(1)}, f32[3,2560]{1,0:T(4,128)S(1)}, u32[]{:S(2)}, u32[]{:S(2)}) collective-permute-start(f32[3,2560]{1,0:T(4,128)S(1)} %stats_other.1.s0), channel_id=1, source_target_pairs={{0,48},{16,0},{32,16},{48,32},{1,49},{17,1},{33,17},{49,33},{2,50}... | collective-permute-start | bytes 92168 | tf_op jit(solution)/shard_map/ppermute | solution.py:243
  51.2 6.3 %collective-permute-start.9 = (f32[3,2560]{1,0:T(4,128)S(1)}, f32[3,2560]{1,0:T(4,128)S(1)}, u32[]{:S(2)}, u32[]{:S(2)}) collective-permute-start(f32[3,2560]{1,0:T(4,128)S(1)} %stats_other.1.s0), channel_id=1, source_target_pairs={{0,32},{16,48},{32,0},{48,16},{1,33},{17,49},{33,1},{49,17},{2,34}... | collective-permute-start | bytes 92168 | tf_op jit(solution)/shard_map/ppermute | solution.py:243
  51.2 6.3 %collective-permute-start.8 = (f32[3,2560]{1,0:T(4,128)S(1)}, f32[3,2560]{1,0:T(4,128)S(1)}, u32[]{:S(2)}, u32[]{:S(2)}) collective-permute-start(f32[3,2560]{1,0:T(4,128)S(1)} %stats_other.1.s0), channel_id=1, source_target_pairs={{0,16},{16,32},{32,48},{48,0},{1,17},{17,33},{33,49},{49,1},{2,18}... | collective-permute-start | bytes 92168 | tf_op jit(solution)/shard_map/ppermute | solution.py:243
  52.3 27.5 %collective-permute-start.11 = (bf16[2,160,512]{2,1,0:T(8,128)(2,1)S(1)}, bf16[2,160,512]{2,1,0:T(8,128)(2,1)S(1)}, u32[]{:S(2)}, u32[]{:S(2)}) collective-permute-start(bf16[2,160,512]{2,1,0:T(8,128)(2,1)S(1)} %copy-done.13), channel_id=1, source_target_pairs={{0,16},{16,32},{32,48},{48,0},{1,17},{17,33},{33,49},{49,1},{2,18}... | collective-permute-start | bytes 983048 | tf_op jit(solution)/shard_map/ppermute | solution.py:243
  54.7 25.2 %collective-permute-start.12 = (bf16[2,160,512]{2,1,0:T(8,128)(2,1)S(1)}, bf16[2,160,512]{2,1,0:T(8,128)(2,1)S(1)}, u32[]{:S(2)}, u32[]{:S(2)}) collective-permute-start(bf16[2,160,512]{2,1,0:T(8,128)(2,1)S(1)} %copy-done.11), channel_id=1, source_target_pairs={{0,32},{16,48},{32,0},{48,16},{1,33},{17,49},{33,1},{49,17},{2,34}... | collective-permute-start | bytes 983048 | tf_op jit(solution)/shard_map/ppermute | solution.py:243
  55.9 24.0 %collective-permute-start.13 = (bf16[2,160,512]{2,1,0:T(8,128)(2,1)S(1)}, bf16[2,160,512]{2,1,0:T(8,128)(2,1)S(1)}, u32[]{:S(2)}, u32[]{:S(2)}) collective-permute-start(bf16[2,160,512]{2,1,0:T(8,128)(2,1)S(1)} %copy-done.9), channel_id=1, source_target_pairs={{0,48},{16,0},{32,16},{48,32},{1,49},{17,1},{33,17},{49,33},{2,50}... | collective-permute-start | bytes 983048 | tf_op jit(solution)/shard_map/ppermute | solution.py:243
  57.5 1.1 copy-start.7
  79.9 4.6 %copy-start.2 = (bf16[2,160,512]{2,1,0:T(8,128)(2,1)}, bf16[2,160,512]{2,1,0:T(8,128)(2,1)S(1)}, u32[]{:S(2)}) copy-start(bf16[2,160,512]{2,1,0:T(8,128)(2,1)S(1)} %collective-permute-done.12.x2) | copy-start | bytes 983044
  79.9 4.5 %copy-start.4 = (bf16[2,160,512]{2,1,0:T(8,128)(2,1)}, bf16[2,160,512]{2,1,0:T(8,128)(2,1)S(1)}, u32[]{:S(2)}) copy-start(bf16[2,160,512]{2,1,0:T(8,128)(2,1)S(1)} %collective-permute-done.13.x3) | copy-start | bytes 983044
  79.9 3.5 %collective-permute-start.20 = (bf16[1280,256]{1,0:T(8,128)(2,1)S(1)}, bf16[1280,256]{1,0:T(8,128)(2,1)S(1)}, u32[]{:S(2)}, u32[]{:S(2)}) collective-permute-start(bf16[1280,256]{1,0:T(8,128)(2,1)S(1)} %get-tuple-element.82), channel_id=1, source_target_pairs={{0,1},{1,0},{2,3},{3,2},{4,5},{5,4},{6,7},{7,6},{8,9},{9,8},{10,11... | collective-permute-start | bytes 1966088 | tf_op jit(solution)/shard_map/ppermute | solution.py:243
  80.2 9.5 %collective-permute-start.14 = (bf16[160,512]{1,0:T(8,128)(2,1)}, bf16[160,512]{1,0:T(8,128)(2,1)S(1)}, u32[]{:S(2)}, u32[]{:S(2)}) collective-permute-start(bf16[160,512]{1,0:T(8,128)(2,1)} %get-tuple-element.78), channel_id=1, source_target_pairs={{0,48},{16,0},{32,16},{48,32},{1,49},{17,1},{33,17},{49,33},{2,50}... | collective-permute-start | bytes 491528 | tf_op jit(solution)/shard_map/ppermute | solution.py:243
  81.6 8.6 %collective-permute-start.15 = (bf16[160,512]{1,0:T(8,128)(2,1)S(1)}, bf16[160,512]{1,0:T(8,128)(2,1)S(1)}, u32[]{:S(2)}, u32[]{:S(2)}) collective-permute-start(bf16[160,512]{1,0:T(8,128)(2,1)S(1)} %get-tuple-element.79), channel_id=1, source_target_pairs={{0,32},{16,48},{32,0},{48,16},{1,33},{17,49},{33,1},{49,17},{2,34}... | collective-permute-start | bytes 491528 | tf_op jit(solution)/shard_map/ppermute | solution.py:243
  82.8 10.1 %collective-permute-start.16 = (bf16[160,512]{1,0:T(8,128)(2,1)S(1)}, bf16[160,512]{1,0:T(8,128)(2,1)S(1)}, u32[]{:S(2)}, u32[]{:S(2)}) collective-permute-start(bf16[160,512]{1,0:T(8,128)(2,1)S(1)} %get-tuple-element.80), channel_id=1, source_target_pairs={{0,16},{16,32},{32,48},{48,0},{1,17},{17,33},{33,49},{49,1},{2,18}... | collective-permute-start | bytes 491528 | tf_op jit(solution)/shard_map/ppermute | solution.py:243
  84.4 17.2 %all-to-all-start.1 = ((bf16[8,160,256]{2,1,0:T(8,128)(2,1)}), bf16[8,160,256]{2,1,0:T(8,128)(2,1)}, u32[]{:S(2)}, u32[]{:S(2)}) async-start(bf16[8,160,256]{2,1,0:T(8,128)(2,1)} %bitcast.8), calls=%async_computation.1 | async-start | bytes 1310720 | tf_op jit(solution)/shard_map/all_to_all | solution.py:319
  93.0 22.5 %copy-start.3 = (bf16[2,160,512]{2,1,0:T(8,128)(2,1)S(1)}, bf16[2,160,512]{2,1,0:T(8,128)(2,1)}, u32[]{:S(2)}) copy-start(bf16[2,160,512]{2,1,0:T(8,128)(2,1)} %copy-done.2) | copy-start | bytes 983044
  93.0 22.5 %copy-start.5 = (bf16[2,160,512]{2,1,0:T(8,128)(2,1)S(1)}, bf16[2,160,512]{2,1,0:T(8,128)(2,1)}, u32[]{:S(2)}) copy-start(bf16[2,160,512]{2,1,0:T(8,128)(2,1)} %copy-done.4) | copy-start | bytes 983044
  93.0 9.8 %collective-permute-start.19 = (bf16[160,512]{1,0:T(8,128)(2,1)S(1)}, bf16[160,512]{1,0:T(8,128)(2,1)S(1)}, u32[]{:S(2)}, u32[]{:S(2)}) collective-permute-start(bf16[160,512]{1,0:T(8,128)(2,1)S(1)} %add_convert_fusion.1.q0), channel_id=1, source_target_pairs={{0,48},{16,0},{32,16},{48,32},{1,49},{17,1},{33,17},{49,33},{2,50}... | collective-permute-start | bytes 491528 | tf_op jit(solution)/shard_map/ppermute | solution.py:243
  93.7 9.2 %collective-permute-start.18 = (bf16[160,512]{1,0:T(8,128)(2,1)S(1)}, bf16[160,512]{1,0:T(8,128)(2,1)S(1)}, u32[]{:S(2)}, u32[]{:S(2)}) collective-permute-start(bf16[160,512]{1,0:T(8,128)(2,1)S(1)} %add_convert_fusion.1.q0), channel_id=1, source_target_pairs={{0,32},{16,48},{32,0},{48,16},{1,33},{17,49},{33,1},{49,17},{2,34}... | collective-permute-start | bytes 491528 | tf_op jit(solution)/shard_map/ppermute | solution.py:243
  94.9 9.4 %collective-permute-start.17 = (bf16[160,512]{1,0:T(8,128)(2,1)S(1)}, bf16[160,512]{1,0:T(8,128)(2,1)S(1)}, u32[]{:S(2)}, u32[]{:S(2)}) collective-permute-start(bf16[160,512]{1,0:T(8,128)(2,1)S(1)} %add_convert_fusion.1.q0), channel_id=1, source_target_pairs={{0,16},{16,32},{32,48},{48,0},{1,17},{17,33},{33,49},{49,1},{2,18}... | collective-permute-start | bytes 491528 | tf_op jit(solution)/shard_map/ppermute | solution.py:243
  104.4 11.1 %collective-permute-start.24 = (bf16[4,160,512]{2,1,0:T(8,128)(2,1)S(1)}, bf16[4,160,512]{2,1,0:T(8,128)(2,1)S(1)}, u32[]{:S(2)}, u32[]{:S(2)}) collective-permute-start(bf16[4,160,512]{2,1,0:T(8,128)(2,1)S(1)} %pad_maximum_fusion), channel_id=1, source_target_pairs={{0,1},{1,0},{2,3},{3,2},{4,5},{5,4},{6,7},{7,6},{8,9},{9,8},{10,11... | collective-permute-start | bytes 1966088 | tf_op jit(solution)/shard_map/ppermute | solution.py:243
  104.5 5.3 %collective-permute-start.23 = (bf16[160,256]{1,0:T(8,128)(2,1)S(1)}, bf16[160,256]{1,0:T(8,128)(2,1)S(1)}, u32[]{:S(2)}, u32[]{:S(2)}) collective-permute-start(bf16[160,256]{1,0:T(8,128)(2,1)S(1)} %reduce_sum.32.k0), channel_id=1, source_target_pairs={{0,48},{16,0},{32,16},{48,32},{1,49},{17,1},{33,17},{49,33},{2,50}... | collective-permute-start | bytes 245768 | tf_op jit(solution)/shard_map/ppermute | solution.py:243
  105.9 6.8 %collective-permute-start.22 = (bf16[160,256]{1,0:T(8,128)(2,1)S(1)}, bf16[160,256]{1,0:T(8,128)(2,1)S(1)}, u32[]{:S(2)}, u32[]{:S(2)}) collective-permute-start(bf16[160,256]{1,0:T(8,128)(2,1)S(1)} %reduce_sum.32.k0), channel_id=1, source_target_pairs={{0,32},{16,48},{32,0},{48,16},{1,33},{17,49},{33,1},{49,17},{2,34}... | collective-permute-start | bytes 245768 | tf_op jit(solution)/shard_map/ppermute | solution.py:243
  106.9 6.8 %collective-permute-start.21 = (bf16[160,256]{1,0:T(8,128)(2,1)S(1)}, bf16[160,256]{1,0:T(8,128)(2,1)S(1)}, u32[]{:S(2)}, u32[]{:S(2)}) collective-permute-start(bf16[160,256]{1,0:T(8,128)(2,1)S(1)} %reduce_sum.32.k0), channel_id=1, source_target_pairs={{0,16},{16,32},{32,48},{48,0},{1,17},{17,33},{33,49},{49,1},{2,18}... | collective-permute-start | bytes 245768 | tf_op jit(solution)/shard_map/ppermute | solution.py:243
  113.8 1.7 %collective-permute-start.25 = (bf16[4,160,256]{2,1,0:T(8,128)(2,1)S(1)}, bf16[4,160,256]{2,1,0:T(8,128)(2,1)S(1)}, u32[]{:S(2)}, u32[]{:S(2)}) collective-permute-start(bf16[4,160,256]{2,1,0:T(8,128)(2,1)S(1)} %pad_maximum_fusion.1), channel_id=1, source_target_pairs={{0,1},{1,0},{2,3},{3,2},{4,5},{5,4},{6,7},{7,6},{8,9},{9,8},{10,11... | collective-permute-start | bytes 983048 | tf_op jit(solution)/shard_map/ppermute | solution.py:243
  (3 other events, 2.1 us)

commit v7 on v6

--- a/solution.py
+++ b/solution.py
@@ -58,10 +58,7 @@
     return jnp.concatenate(parts, axis=0)
 
 
-def stats_pass(block, ordk_ref, posq_ref, qs, gs, kv, before, out_ref, qr, gr):
-    fill_rows(qs, qr)
-    fill_rows(gs, gr)
-
+def stats_pass(block, ordk_ref, posq_ref, qr, gr, kv, before, out_ref):
     def row_tile(rt, _):
         r0 = pl.multiple_of(rt * RT, RT)
         q = qr[pl.ds(r0, RT), :]
@@ -99,13 +96,13 @@
 
 
 def stats_own(ordk, posq, q0, q1, q2, q3, g0, g1, g2, g3, kva, out, qr, gr):
-    stats_pass(0, ordk, posq, (q0, q1, q2, q3), (g0, g1, g2, g3), kva, None, out, qr, gr)
-
-
-def stats_other(ordk, posq, q0, q1, q2, q3, g0, g1, g2, g3, kvb, before, out, qr, gr):
-    stats_pass(
-        KHALF // HALF, ordk, posq, (q0, q1, q2, q3), (g0, g1, g2, g3), kvb, before, out, qr, gr
-    )
+    fill_rows((q0, q1, q2, q3), qr)
+    fill_rows((g0, g1, g2, g3), gr)
+    stats_pass(0, ordk, posq, qr, gr, kva, None, out)
+
+
+def stats_other(ordk, posq, qr, gr, kvb, before, out):
+    stats_pass(KHALF // HALF, ordk, posq, qr, gr, kvb, before, out)
 
 
 def combine_stats(stats, rowstat_ref):
@@ -129,11 +126,9 @@
 
 
 def grads_kernel(
-    ordk, posq_ref, s0, s1, s2, s3, q0, q1, q2, q3, g0, g1, g2, g3, kva, kvb,
-    dq0, dq1, dq2, dq3, keep, send, qr, gr, rowstat, dqr, dkv,
+    ordk, posq_ref, s0, s1, s2, s3, qr, gr, kva, kvb,
+    dq0, dq1, dq2, dq3, keep, send, rowstat, dqr, dkv,
 ):
-    fill_rows((q0, q1, q2, q3), qr)
-    fill_rows((g0, g1, g2, g3), gr)
     combine_stats((s0, s1, s2, s3), rowstat)
     dkv[...] = jnp.zeros_like(dkv)
 
@@ -220,22 +215,20 @@
     )
 
 
-def kernel_call(body, name, outs, scratch, estimate, aliases, scalars, *args):
+def kernel_call(body, name, outs, scratch, estimate, spaces, *args):
     return pl.pallas_call(
         body,
         out_shape=tuple(jax.ShapeDtypeStruct(*o) for o in outs),
-        in_specs=[smem] * scalars + [vmem] * (len(args) - scalars),
+        in_specs=spaces + [vmem] * (len(args) - len(spaces)),
         out_specs=tuple(vmem for _ in outs),
         scratch_shapes=[pltpu.VMEM(*s) for s in scratch],
         compiler_params=params,
         cost_estimate=estimate,
-        input_output_aliases=aliases,
         name=name,
     )(*args)
 
 
 WIDE = HEADS * HEAD
-row_scratch = [((ALL_ROWS, HEAD), bf16)] * 2
 acc_rows = ((ALL_ROWS, HEAD), f32)
 
 
@@ -265,17 +258,12 @@
         ],
         axis=1,
     )
-    place = jnp.stack([o, ic])
-    later, kv = lax.optimization_barrier((tokens, kv))
-    other_tokens = shift(later, "core", 1, 2)
-    xs = kernel_call(
-        columns_kernel, "columns", [((2, ROWS, 512), bf16)] * N_OUT, [],
-        cost(ROWS * 4096, 4, 5 << 20), {}, 1, place, later, other_tokens,
-    )
     kva = jnp.broadcast_to(kv[None], (8,) + kv.shape)
     kva = lax.all_to_all(kva, ("x", "yh"), 0, 0, tiled=True).reshape(KHALF, 2 * HEAD)
-    kva, qs, gs, xs = lax.optimization_barrier((kva, qs, gs, xs))
+    kva, qs, gs = lax.optimization_barrier((kva, qs, gs))
     kvb = shift(kva, "core", 1, 2)
+    later, kva = lax.optimization_barrier((tokens, kva))
+    other_tokens = shift(later, "core", 1, 2)
 
     key_dev = (o * 8 + np.arange(8)[None, :, None]) * 2 + (ic + np.arange(2)[:, None, None]) % 2
     key_blocks = (key_dev * 2 + np.arange(2)[None, None, :]).reshape(-1)
@@ -293,14 +281,19 @@
 
     pairs = cost(ALL_ROWS * KHALF, 2, 4 << 20)
     row_stats = [((3, ALL_ROWS), f32)]
+    rows = ((ALL_ROWS, HEAD), bf16)
+    stats, qr, gr = kernel_call(
+        stats_own, "stats_own", row_stats + [rows, rows], [], pairs, [smem],
+        ordk, posq, *qs, *gs, kva,
+    )
     (stats,) = kernel_call(
-        stats_own, "stats_own", row_stats, row_scratch, pairs, {}, 1, ordk, posq, *qs, *gs, kva
-    )
-    (stats,) = kernel_call(
-        stats_other, "stats_other", row_stats, row_scratch, pairs, {}, 1,
-        ordk, posq, *qs, *gs, kvb, stats,
-    )
-    xs, stats = lax.optimization_barrier((xs, stats))
+        stats_other, "stats_other", row_stats, [], pairs, [smem], ordk, posq, qr, gr, kvb, stats
+    )
+    later, other_tokens, stats = lax.optimization_barrier((later, other_tokens, stats))
+    xs = kernel_call(
+        columns_kernel, "columns", [((2, ROWS, 512), bf16)] * N_OUT, [],
+        cost(ROWS * 4096, 4, 5 << 20), [smem], jnp.stack([o, ic]), later, other_tokens,
+    )
     xs = [xs[0]] + [shift(xs[d], "outer", d, N_OUT) for d in range(1, N_OUT)]
     all_stats = from_behind(stats, "outer", N_OUT)
 
@@ -308,9 +301,8 @@
     dq, dq1, dq2, dq3, keep, send = kernel_call(
         grads_kernel, "grads",
         [((ROWS, WIDE), f32)] + [((ROWS, WIDE), bf16)] * 3 + [(half, f32), (half, bf16)],
-        row_scratch + [((2, ALL_ROWS), f32), acc_rows, ((KEYS, 2 * HEAD), f32)],
-        cost(ALL_ROWS * KEYS, 5, 8 << 20), {}, 1,
-        ordk, posq, *all_stats, *qs, *gs, kva, kvb,
+        [((2, ALL_ROWS), f32), acc_rows, ((KEYS, 2 * HEAD), f32)],
+        cost(ALL_ROWS * KEYS, 5, 8 << 20), [smem], ordk, posq, *all_stats, qr, gr, kva, kvb,
     )
     send, dq1, dq2, dq3, xs = lax.optimization_barrier((send, dq1, dq2, dq3, xs))
     got = shift(send, "core", 1, 2)
@@ -329,13 +321,13 @@
     (dw,) = kernel_call(
         weights_kernel, "weights", [((16, 32, 768), bf16)],
         [((2 * N_OUT * ROWS, 512), bf16), ((2 * N_OUT * ROWS, 768), bf16)],
-        cost(1280 * 512, 6, 4 << 20), {}, 0,
+        cost(1280 * 512, 6, 4 << 20), [],
         *xs, *dq_all, *dkv_all, dq_other, dkv_other,
     )
     dw = lax.all_to_all(dw, ("dp", "x", "yh"), 0, 0, tiled=True)
     return kernel_call(
         last_sum, "last_sum", [((32, WIDE), f32), ((32, HEAD), f32), ((32, HEAD), f32)], [],
-        cost(32 * 16, 3, 1 << 20), {}, 0, dw,
+        cost(32 * 16, 3, 1 << 20), [], dw,
     )
 
 

time: 138 us -> 138 us (level)
  waiting for transfers between devices: 19.8 us -> 26.5 us
  local copies, waits for them, and re-layouts: 7.8 us -> 4.49 us
  starting transfers between devices: 42.1 us -> 40.6 us
    ppermute x26, waiting for transfers between devices: 12.7 us -> 19.9 us  [shift(): return lax.ppermute(x, axis, [(i, (i + d) % n) for i in range(n)])]
    unnamed x46 -> x32, local copies, waits for them, and re-layouts: 6.54 us -> 3.23 us
    all_to_all x1, waiting for transfers between devices: 5.94 us -> 3.62 us  [per_device(): dkv = lax.all_to_all(dkv, ('x', 'yh'), 0, 0, tiled=True)]
    all_to_all x1, waiting for transfers between devices: 1.15 us -> 3.04 us  [per_device(): lax.all_to_all(kva, ('x', 'yh'), 0, 0, tiled=True).reshape(KHALF, 2 * HEAD)]
  transfers between devices with their start and end apart: 28 -> 28, of which waited for: 10 -> 11; matrix products, arithmetic and copies ran while one was open for 4% -> 5% of each run, Pallas kernels for 22% -> 26%
where the time goes in v7:
time: 138 us
  starting transfers between devices  40.6 us (29%)
  Pallas kernels  37.8 us (27%)
  waiting for transfers between devices  26.5 us (19%)
  blocking collectives  18.5 us (13%)
  matrix products  4.59 us (3%)
  local copies, waits for them, and re-layouts  4.49 us (3%)
  other arithmetic  4.28 us (3%)
    pallas_call x6, Pallas kernels, kernel_call(): pl.pallas_call(body, out_shape=tuple((jax.ShapeDtypeStruct(*o) for o in o...  37.8 us
    ppermute x26, starting transfers between devices, shift(): return lax.ppermute(x, axis, [(i, (i + d) % n) for i in range(n)])  29.4 us
    ppermute x26, waiting for transfers between devices, shift(): return lax.ppermute(x, axis, [(i, (i + d) % n) for i in range(n)])  19.9 us
    all_to_all x1, blocking collectives, per_device(): dw = lax.all_to_all(dw, ('dp', 'x', 'yh'), 0, 0, tiled=True)  18.5 us
    all_to_all x1, starting transfers between devices, per_device(): lax.all_to_all(kva, ('x', 'yh'), 0, 0, tiled=True).reshape(KHALF, 2 * HEAD)  6.93 us
    dot_general x3, matrix products, dot(): return lax.dot_general(a, b, dims, preferred_element_type=f32)  4.59 us
    all_to_all x1, starting transfers between devices, per_device(): dkv = lax.all_to_all(dkv, ('x', 'yh'), 0, 0, tiled=True)  4.21 us
    all_to_all x1, waiting for transfers between devices, per_device(): dkv = lax.all_to_all(dkv, ('x', 'yh'), 0, 0, tiled=True)  3.62 us
  transfers between devices with their start and end apart: 28, of which 11 were waited for; matrix products, arithmetic and copies ran while one was open for 5% of the time, Pallas kernels for 26%

profile of v7, /device:TPU:0, one launch (start us, length us, event | category | flops | bytes accessed | tf_op | source)
XLA Modules:
  0.0 137.8 jit_solution(5143118453204959036)
XLA Ops:
  0.7 3.6 %convolution_convert_fusion.q0 = bf16[160,512]{1,0:T(8,128)(2,1)S(1)} fusion(bf16[4096,512]{1,0:T(8,128)(2,1)} %param.13, bf16[1,160,4096]{2,1,0:T(8,128)(2,1)} %param.11), kind=kOutput, calls=%fused_computation.1 | convolution fusion | flops 671170560 | bytes 5668864 | tf_op jit(solution)/shard_map/dot_general | solution.py:36
  4.3 4.2 %collective-permute-start.2 = (bf16[160,512]{1,0:T(8,128)(2,1)S(1)}, bf16[160,512]{1,0:T(8,128)(2,1)S(1)}, u32[]{:S(2)}, u32[]{:S(2)}) collective-permute-start(bf16[160,512]{1,0:T(8,128)(2,1)S(1)} %convolution_convert_fusion.q0), channel_id=1, source_target_pairs={{0,48},{16,0},{32,16},{48,32},{1,49},{17,1},{33,17},{49,33},{2,50}... | collective-permute-start | bytes 491528 | tf_op jit(solution)/shard_map/ppermute | solution.py:236
  8.5 3.2 %collective-permute-start.4 = (bf16[160,512]{1,0:T(8,128)(2,1)S(1)}, bf16[160,512]{1,0:T(8,128)(2,1)}, u32[]{:S(2)}, u32[]{:S(2)}) collective-permute-start(bf16[160,512]{1,0:T(8,128)(2,1)S(1)} %bitcast.41), channel_id=1, source_target_pairs={{0,48},{16,0},{32,16},{48,32},{1,49},{17,1},{33,17},{49,33},{2,50}... | collective-permute-start | bytes 491528 | tf_op jit(solution)/shard_map/ppermute | solution.py:236
  11.7 0.5 convolution_convert_fusion.2
  12.2 0.5 convolution_convert_fusion.1
  12.8 0.9 broadcast_in_dim.47
  13.7 6.9 %all-to-all-start = ((bf16[8,160,256]{2,1,0:T(8,128)(2,1)}), bf16[8,160,256]{2,1,0:T(8,128)(2,1)S(1)}, u32[]{:S(2)}, u32[]{:S(2)}) async-start(bf16[8,160,256]{2,1,0:T(8,128)(2,1)} %broadcast_in_dim.47), calls=%async_computation | async-start | bytes 1310720 | tf_op jit(solution)/shard_map/all_to_all | solution.py:262
  21.0 3.3 %collective-permute-start.5 = (bf16[160,512]{1,0:T(8,128)(2,1)}, bf16[160,512]{1,0:T(8,128)(2,1)S(1)}, u32[]{:S(2)}, u32[]{:S(2)}) collective-permute-start(bf16[160,512]{1,0:T(8,128)(2,1)} %collective-permute-done.4.g3), channel_id=1, source_target_pairs={{0,48},{16,0},{32,16},{48,32},{1,49},{17,1},{33,17},{49,33},{2,50}... | collective-permute-start | bytes 491528 | tf_op jit(solution)/shard_map/ppermute | solution.py:236
  24.3 3.3 %collective-permute-done.1.q2 = bf16[160,512]{1,0:T(8,128)(2,1)S(1)} collective-permute-done((bf16[160,512]{1,0:T(8,128)(2,1)}, bf16[160,512]{1,0:T(8,128)(2,1)S(1)}, u32[]{:S(2)}, u32[]{:S(2)}) %collective-permute-start.1) | collective-permute-done | bytes 163872 | tf_op jit(solution)/shard_map/ppermute | solution.py:236
  27.7 0.7 copy-done.7
  28.4 0.7 copy-done.9
  29.0 3.0 %all-to-all-done = bf16[8,160,256]{2,1,0:T(8,128)(2,1)S(1)} async-done(((bf16[8,160,256]{2,1,0:T(8,128)(2,1)}), bf16[8,160,256]{2,1,0:T(8,128)(2,1)S(1)}, u32[]{:S(2)}, u32[]{:S(2)}) %all-to-all-start) | async-done | bytes 655392 | tf_op jit(solution)/shard_map/all_to_all | solution.py:262
  32.3 0.5 collective-permute-start.7
  33.5 0.9 copy-done.8
  34.4 0.9 copy-done.10
  35.3 6.7 %stats_own.1 = (f32[3,2560]{1,0:T(4,128)S(1)}, bf16[2560,128]{1,0:T(8,128)(2,1)S(1)}, bf16[2560,128]{1,0:T(8,128)(2,1)S(1)}) custom-call(s32[32]{0:T(128)S(1)} %select_reduce_fusion.ordk, s32[1,2560]{1,0:T(1,128)S(1)} %reshape.101.posq.posq_ref, bf16[160,512]{1,0:T(8,128)(2,1)S(1)} %convolution_convert_fusion.q0, bf16[160,512]{1,0:T(8,128)(2,1)} %collective-permute-done.q1, ...), custom_call_target="tpu_custom_call" | custom-call | flops 1677721600 | bytes 4194304 | tf_op jit(solution)/shard_map/stats_own/pallas_call | solution.py:219
  42.0 6.6 %stats_other.1.s0 = f32[3,2560]{1,0:T(4,128)S(1)} custom-call(s32[32]{0:T(128)S(1)} %select_reduce_fusion.ordk, s32[1,2560]{1,0:T(1,128)S(1)} %reshape.101.posq.posq_ref, bf16[2560,128]{1,0:T(8,128)(2,1)S(1)} %get-tuple-element.53.qr, bf16[2560,128]{1,0:T(8,128)(2,1)S(1)} %get-tuple-element.54.gr, bf16[1280,256]{1,0:T(8,128)(2,1)} %collective-permute-done.7.kvb, ...), custom_call_target="tpu_custom_call" | custom-call | flops 1677721600 | bytes 4194304 | tf_op jit(solution)/shard_map/stats_other/pallas_call | solution.py:219
  48.6 3.3 %collective-permute-start.10 = (f32[3,2560]{1,0:T(4,128)S(1)}, f32[3,2560]{1,0:T(4,128)S(1)}, u32[]{:S(2)}, u32[]{:S(2)}) collective-permute-start(f32[3,2560]{1,0:T(4,128)S(1)} %stats_other.1.s0), channel_id=1, source_target_pairs={{0,48},{16,0},{32,16},{48,32},{1,49},{17,1},{33,17},{49,33},{2,50}... | collective-permute-start | bytes 92168 | tf_op jit(solution)/shard_map/ppermute | solution.py:236
  51.9 0.9 collective-permute-start.8
  52.8 2.2 %columns.1 = (bf16[2,160,512]{2,1,0:T(8,128)(2,1)S(1)}, bf16[2,160,512]{2,1,0:T(8,128)(2,1)S(1)}, bf16[2,160,512]{2,1,0:T(8,128)(2,1)S(1)}, bf16[2,160,512]{2,1,0:T(8,128)(2,1)S(1)}) custom-call(s32[2]{0:T(128)S(1)} %pad_add_fusion.place_ref, bf16[160,4096]{1,0:T(8,128)(2,1)S(1)} %bitcast.29, bf16[160,4096]{1,0:T(8,128)(2,1)} %collective-permute-done.6.other), custom_call_target="tpu_custom_call" | custom-call | flops 671088640 | bytes 5242880 | tf_op jit(solution)/shard_map/columns/pallas_call | solution.py:219
  55.1 2.6 %collective-permute-start.11 = (bf16[2,160,512]{2,1,0:T(8,128)(2,1)S(1)}, bf16[2,160,512]{2,1,0:T(8,128)(2,1)S(1)}, u32[]{:S(2)}, u32[]{:S(2)}) collective-permute-start(bf16[2,160,512]{2,1,0:T(8,128)(2,1)S(1)} %get-tuple-element.64), channel_id=1, source_target_pairs={{0,16},{16,32},{32,48},{48,0},{1,17},{17,33},{33,49},{49,1},{2,18}... | collective-permute-start | bytes 983048 | tf_op jit(solution)/shard_map/ppermute | solution.py:236
  57.7 1.2 collective-permute-start.12
  58.9 1.6 %collective-permute-start.13 = (bf16[2,160,512]{2,1,0:T(8,128)(2,1)S(1)}, bf16[2,160,512]{2,1,0:T(8,128)(2,1)S(1)}, u32[]{:S(2)}, u32[]{:S(2)}) collective-permute-start(bf16[2,160,512]{2,1,0:T(8,128)(2,1)S(1)} %get-tuple-element.66), channel_id=1, source_target_pairs={{0,48},{16,0},{32,16},{48,32},{1,49},{17,1},{33,17},{49,33},{2,50}... | collective-permute-start | bytes 983048 | tf_op jit(solution)/shard_map/ppermute | solution.py:236
  60.4 20.4 %grads.1 = (f32[160,512]{1,0:T(8,128)S(1)}, bf16[160,512]{1,0:T(8,128)(2,1)S(1)}, bf16[160,512]{1,0:T(8,128)(2,1)S(1)}, bf16[160,512]{1,0:T(8,128)(2,1)S(1)}, f3...) custom-call(s32[32]{0:T(128)S(1)} %select_reduce_fusion.ordk, s32[1,2560]{1,0:T(1,128)S(1)} %reshape.101.posq.posq_ref, ...), custom_call_target="tpu_custom_call" | custom-call | flops 8388608000 | bytes 8388608 | tf_op jit(solution)/shard_map/grads/pallas_call | solution.py:219
  81.2 1.4 %collective-permute-start.14 = (bf16[160,512]{1,0:T(8,128)(2,1)S(1)}, bf16[160,512]{1,0:T(8,128)(2,1)}, u32[]{:S(2)}, u32[]{:S(2)}) collective-permute-start(bf16[160,512]{1,0:T(8,128)(2,1)S(1)} %get-tuple-element.72), channel_id=1, source_target_pairs={{0,48},{16,0},{32,16},{48,32},{1,49},{17,1},{33,17},{49,33},{2,50}... | collective-permute-start | bytes 491528 | tf_op jit(solution)/shard_map/ppermute | solution.py:236
  82.6 1.2 collective-permute-start.15
  83.8 1.1 add_convert_fusion
  84.9 4.2 %all-to-all-start.1 = ((bf16[8,160,256]{2,1,0:T(8,128)(2,1)}), bf16[8,160,256]{2,1,0:T(8,128)(2,1)}, u32[]{:S(2)}, u32[]{:S(2)}) async-start(bf16[8,160,256]{2,1,0:T(8,128)(2,1)} %bitcast.8), calls=%async_computation.1 | async-start | bytes 1310720 | tf_op jit(solution)/shard_map/all_to_all | solution.py:311
  89.1 2.2 %collective-permute-done.15 = bf16[160,512]{1,0:T(8,128)(2,1)} collective-permute-done((bf16[160,512]{1,0:T(8,128)(2,1)S(1)}, bf16[160,512]{1,0:T(8,128)(2,1)}, u32[]{:S(2)}, u32[]{:S(2)}) %collective-permute-start.15) | collective-permute-done | bytes 163872 | tf_op jit(solution)/shard_map/ppermute | solution.py:236
  91.3 2.7 %collective-permute-done.16 = bf16[160,512]{1,0:T(8,128)(2,1)} collective-permute-done((bf16[160,512]{1,0:T(8,128)(2,1)S(1)}, bf16[160,512]{1,0:T(8,128)(2,1)}, u32[]{:S(2)}, u32[]{:S(2)}) %collective-permute-start.16) | collective-permute-done | bytes 163872 | tf_op jit(solution)/shard_map/ppermute | solution.py:236
  94.0 1.2 add_convert_fusion.1.q0
  95.2 0.7 collective-permute-start.19
  95.8 1.2 collective-permute-start.18
  97.0 0.8 collective-permute-start.17
  97.9 3.6 %all-to-all-done.1 = bf16[8,160,256]{2,1,0:T(8,128)(2,1)} async-done(((bf16[8,160,256]{2,1,0:T(8,128)(2,1)}), bf16[8,160,256]{2,1,0:T(8,128)(2,1)}, u32[]{:S(2)}, u32[]{:S(2)}) %all-to-all-start.1) | async-done | bytes 655392 | tf_op jit(solution)/shard_map/all_to_all | solution.py:311
  101.5 1.2 reduce_sum.32.k0
  102.7 1.8 %collective-permute-done.18.q2 = bf16[160,512]{1,0:T(8,128)(2,1)S(1)} collective-permute-done((bf16[160,512]{1,0:T(8,128)(2,1)S(1)}, bf16[160,512]{1,0:T(8,128)(2,1)S(1)}, u32[]{:S(2)}, u32[]{:S(2)}) %collective-permute-start.18) | collective-permute-done | bytes 163872 | tf_op jit(solution)/shard_map/ppermute | solution.py:236
  104.5 2.0 %collective-permute-done.17.q1 = bf16[160,512]{1,0:T(8,128)(2,1)S(1)} collective-permute-done((bf16[160,512]{1,0:T(8,128)(2,1)S(1)}, bf16[160,512]{1,0:T(8,128)(2,1)S(1)}, u32[]{:S(2)}, u32[]{:S(2)}) %collective-permute-start.17) | collective-permute-done | bytes 163872 | tf_op jit(solution)/shard_map/ppermute | solution.py:236
  106.6 1.1 collective-permute-start.23
  107.8 0.7 collective-permute-start.22
  108.5 0.9 collective-permute-start.21
  109.3 2.6 %collective-permute-done.23.k3 = bf16[160,256]{1,0:T(8,128)(2,1)S(1)} collective-permute-done((bf16[160,256]{1,0:T(8,128)(2,1)S(1)}, bf16[160,256]{1,0:T(8,128)(2,1)S(1)}, u32[]{:S(2)}, u32[]{:S(2)}) %collective-permute-start.23) | collective-permute-done | bytes 81952 | tf_op jit(solution)/shard_map/ppermute | solution.py:236
  112.0 2.4 %collective-permute-done.22.k2 = bf16[160,256]{1,0:T(8,128)(2,1)S(1)} collective-permute-done((bf16[160,256]{1,0:T(8,128)(2,1)S(1)}, bf16[160,256]{1,0:T(8,128)(2,1)S(1)}, u32[]{:S(2)}, u32[]{:S(2)}) %collective-permute-start.22) | collective-permute-done | bytes 81952 | tf_op jit(solution)/shard_map/ppermute | solution.py:236
  114.4 1.2 collective-permute-done.21.k1
  115.7 1.6 %collective-permute-done.25.ko = bf16[4,160,256]{2,1,0:T(8,128)(2,1)S(1)} collective-permute-done((bf16[4,160,256]{2,1,0:T(8,128)(2,1)S(1)}, bf16[4,160,256]{2,1,0:T(8,128)(2,1)S(1)}, u32[]{:S(2)}, u32[]{:S(2)}) %collective-permute-start.25) | collective-permute-done | bytes 327712 | tf_op jit(solution)/shard_map/ppermute | solution.py:236
  117.3 1.2 weights.1
  118.6 18.5 %all_to_all.15.parts = bf16[16,32,768]{2,1,0:T(8,128)(2,1)S(1)} all-to-all(bf16[16,32,768]{2,1,0:T(8,128)(2,1)S(1)} %weights.1), channel_id=1, replica_groups=mesh['dp'=2,'outer'=4,'x'=4,'yh'=2,'core'=2] {'dp','x','yh'}, dimensions={0} | all-to-all | bytes 1572864 | tf_op jit(solution)/shard_map/all_to_all | solution.py:327
  137.1 0.7 last_sum.1
  (73 shorter events, 2.0 us)
Async XLA Ops:
  0.6 11.1 %copy-start = (bf16[4096,128]{1,0:T(8,128)(2,1)S(1)}, bf16[4096,128]{1,0:T(8,128)(2,1)}, u32[]{:S(2)}) copy-start(bf16[4096,128]{1,0:T(8,128)(2,1)} %param.14) | copy-start | bytes 3145732
  0.6 11.1 %copy-start.1 = (bf16[1,160,4096]{2,1,0:T(8,128)(2,1)S(1)}, bf16[1,160,4096]{2,1,0:T(8,128)(2,1)}, u32[]{:S(2)}) copy-start(bf16[1,160,4096]{2,1,0:T(8,128)(2,1)} %param.11) | copy-start | bytes 3932164
  0.7 7.8 %copy-start.6 = (bf16[1,160,512]{2,1,0:T(8,128)(2,1)S(1)}, bf16[1,160,512]{2,1,0:T(8,128)(2,1)}, u32[]{:S(2)}) copy-start(bf16[1,160,512]{2,1,0:T(8,128)(2,1)} %param.16) | copy-start | bytes 491524
  4.3 8.0 %copy-start.11 = (bf16[4096,128]{1,0:T(8,128)(2,1)S(1)}, bf16[4096,128]{1,0:T(8,128)(2,1)}, u32[]{:S(2)}) copy-start(bf16[4096,128]{1,0:T(8,128)(2,1)} %param.15) | copy-start | bytes 3145732
  4.3 20.1 %collective-permute-start.2 = (bf16[160,512]{1,0:T(8,128)(2,1)S(1)}, bf16[160,512]{1,0:T(8,128)(2,1)S(1)}, u32[]{:S(2)}, u32[]{:S(2)}) collective-permute-start(bf16[160,512]{1,0:T(8,128)(2,1)S(1)} %convolution_convert_fusion.q0), channel_id=1, source_target_pairs={{0,48},{16,0},{32,16},{48,32},{1,49},{17,1},{33,17},{49,33},{2,50}... | collective-permute-start | bytes 491528 | tf_op jit(solution)/shard_map/ppermute | solution.py:236
  8.5 12.4 %collective-permute-start = (bf16[160,512]{1,0:T(8,128)(2,1)S(1)}, bf16[160,512]{1,0:T(8,128)(2,1)}, u32[]{:S(2)}, u32[]{:S(2)}) collective-permute-start(bf16[160,512]{1,0:T(8,128)(2,1)S(1)} %convolution_convert_fusion.q0), channel_id=1, source_target_pairs={{0,16},{16,32},{32,48},{48,0},{1,17},{17,33},{33,49},{49,1},{2,18}... | collective-permute-start | bytes 491528 | tf_op jit(solution)/shard_map/ppermute | solution.py:236
  8.5 12.5 %collective-permute-start.4 = (bf16[160,512]{1,0:T(8,128)(2,1)S(1)}, bf16[160,512]{1,0:T(8,128)(2,1)}, u32[]{:S(2)}, u32[]{:S(2)}) collective-permute-start(bf16[160,512]{1,0:T(8,128)(2,1)S(1)} %bitcast.41), channel_id=1, source_target_pairs={{0,48},{16,0},{32,16},{48,32},{1,49},{17,1},{33,17},{49,33},{2,50}... | collective-permute-start | bytes 491528 | tf_op jit(solution)/shard_map/ppermute | solution.py:236
  11.7 12.6 %collective-permute-start.3 = (bf16[160,512]{1,0:T(8,128)(2,1)S(1)}, bf16[160,512]{1,0:T(8,128)(2,1)}, u32[]{:S(2)}, u32[]{:S(2)}) collective-permute-start(bf16[160,512]{1,0:T(8,128)(2,1)S(1)} %bitcast.42), channel_id=1, source_target_pairs={{0,16},{16,32},{32,48},{48,0},{1,17},{17,33},{33,49},{49,1},{2,18}... | collective-permute-start | bytes 491528 | tf_op jit(solution)/shard_map/ppermute | solution.py:236
  12.7 7.9 %copy-start.12 = (s32[4]{0:T(128)S(1)}, s32[4]{0:T(128)}, u32[]{:S(2)}) copy-start(s32[4]{0:T(128)} %constant.76) | copy-start | bytes 52
  12.8 8.1 %copy-start.15 = (s32[2,1,1]{0,2,1:T(1,128)S(1)}, s32[2,1,1]{0,2,1:T(1,128)}, u32[]{:S(2)}) copy-start(s32[2,1,1]{0,2,1:T(1,128)} %constant.68.clone) | copy-start | bytes 28
  12.8 8.1 %copy-start.14 = (s32[1,8,1]{1,2,0:T(1,128)S(1)}, s32[1,8,1]{1,2,0:T(1,128)}, u32[]{:S(2)}) copy-start(s32[1,8,1]{1,2,0:T(1,128)} %constant.67.clone) | copy-start | bytes 100
  12.8 19.3 %copy-start.13 = (s32[1,128]{1,0:T(1,128)S(1)}, s32[1,128]{1,0:T(1,128)}, u32[]{:S(2)}) copy-start(s32[1,128]{1,0:T(1,128)} %param.12) | copy-start | bytes 1540
  13.7 18.3 %all-to-all-start = ((bf16[8,160,256]{2,1,0:T(8,128)(2,1)}), bf16[8,160,256]{2,1,0:T(8,128)(2,1)S(1)}, u32[]{:S(2)}, u32[]{:S(2)}) async-start(bf16[8,160,256]{2,1,0:T(8,128)(2,1)} %broadcast_in_dim.47), calls=%async_computation | async-start | bytes 1310720 | tf_op jit(solution)/shard_map/all_to_all | solution.py:262
  20.9 6.8 %collective-permute-start.1 = (bf16[160,512]{1,0:T(8,128)(2,1)}, bf16[160,512]{1,0:T(8,128)(2,1)S(1)}, u32[]{:S(2)}, u32[]{:S(2)}) collective-permute-start(bf16[160,512]{1,0:T(8,128)(2,1)} %collective-permute-done.q1), channel_id=1, source_target_pairs={{0,16},{16,32},{32,48},{48,0},{1,17},{17,33},{33,49},{49,1},{2,18}... | collective-permute-start | bytes 491528 | tf_op jit(solution)/shard_map/ppermute | solution.py:236
  21.0 7.4 %collective-permute-start.5 = (bf16[160,512]{1,0:T(8,128)(2,1)}, bf16[160,512]{1,0:T(8,128)(2,1)S(1)}, u32[]{:S(2)}, u32[]{:S(2)}) collective-permute-start(bf16[160,512]{1,0:T(8,128)(2,1)} %collective-permute-done.4.g3), channel_id=1, source_target_pairs={{0,48},{16,0},{32,16},{48,32},{1,49},{17,1},{33,17},{49,33},{2,50}... | collective-permute-start | bytes 491528 | tf_op jit(solution)/shard_map/ppermute | solution.py:236
  27.7 0.7 copy-start.7
  28.4 0.7 copy-start.9
  32.1 16.5 %collective-permute-start.6 = (bf16[160,4096]{1,0:T(8,128)(2,1)S(1)}, bf16[160,4096]{1,0:T(8,128)(2,1)}, u32[]{:S(2)}, u32[]{:S(2)}) collective-permute-start(bf16[160,4096]{1,0:T(8,128)(2,1)S(1)} %bitcast.28), channel_id=1, source_target_pairs={{0,1},{1,0},{2,3},{3,2},{4,5},{5,4},{6,7},{7,6},{8,9},{9,8},{10,11... | collective-permute-start | bytes 3932168 | tf_op jit(solution)/shard_map/ppermute | solution.py:236
  32.3 9.7 %collective-permute-start.7 = (bf16[1280,256]{1,0:T(8,128)(2,1)S(1)}, bf16[1280,256]{1,0:T(8,128)(2,1)}, u32[]{:S(2)}, u32[]{:S(2)}) collective-permute-start(bf16[1280,256]{1,0:T(8,128)(2,1)S(1)} %bitcast.35), channel_id=1, source_target_pairs={{0,1},{1,0},{2,3},{3,2},{4,5},{5,4},{6,7},{7,6},{8,9},{9,8},{10,11... | collective-permute-start | bytes 1966088 | tf_op jit(solution)/shard_map/ppermute | solution.py:236
  33.5 0.9 copy-start.8
  34.4 0.9 copy-start.10
  48.6 10.3 %collective-permute-start.10 = (f32[3,2560]{1,0:T(4,128)S(1)}, f32[3,2560]{1,0:T(4,128)S(1)}, u32[]{:S(2)}, u32[]{:S(2)}) collective-permute-start(f32[3,2560]{1,0:T(4,128)S(1)} %stats_other.1.s0), channel_id=1, source_target_pairs={{0,48},{16,0},{32,16},{48,32},{1,49},{17,1},{33,17},{49,33},{2,50}... | collective-permute-start | bytes 92168 | tf_op jit(solution)/shard_map/ppermute | solution.py:236
  51.9 8.5 %collective-permute-start.9 = (f32[3,2560]{1,0:T(4,128)S(1)}, f32[3,2560]{1,0:T(4,128)S(1)}, u32[]{:S(2)}, u32[]{:S(2)}) collective-permute-start(f32[3,2560]{1,0:T(4,128)S(1)} %stats_other.1.s0), channel_id=1, source_target_pairs={{0,32},{16,48},{32,0},{48,16},{1,33},{17,49},{33,1},{49,17},{2,34}... | collective-permute-start | bytes 92168 | tf_op jit(solution)/shard_map/ppermute | solution.py:236
  51.9 8.5 %collective-permute-start.8 = (f32[3,2560]{1,0:T(4,128)S(1)}, f32[3,2560]{1,0:T(4,128)S(1)}, u32[]{:S(2)}, u32[]{:S(2)}) collective-permute-start(f32[3,2560]{1,0:T(4,128)S(1)} %stats_other.1.s0), channel_id=1, source_target_pairs={{0,16},{16,32},{32,48},{48,0},{1,17},{17,33},{33,49},{49,1},{2,18}... | collective-permute-start | bytes 92168 | tf_op jit(solution)/shard_map/ppermute | solution.py:236
  55.1 25.8 %collective-permute-start.11 = (bf16[2,160,512]{2,1,0:T(8,128)(2,1)S(1)}, bf16[2,160,512]{2,1,0:T(8,128)(2,1)S(1)}, u32[]{:S(2)}, u32[]{:S(2)}) collective-permute-start(bf16[2,160,512]{2,1,0:T(8,128)(2,1)S(1)} %get-tuple-element.64), channel_id=1, source_target_pairs={{0,16},{16,32},{32,48},{48,0},{1,17},{17,33},{33,49},{49,1},{2,18}... | collective-permute-start | bytes 983048 | tf_op jit(solution)/shard_map/ppermute | solution.py:236
  57.7 23.2 %collective-permute-start.12 = (bf16[2,160,512]{2,1,0:T(8,128)(2,1)S(1)}, bf16[2,160,512]{2,1,0:T(8,128)(2,1)S(1)}, u32[]{:S(2)}, u32[]{:S(2)}) collective-permute-start(bf16[2,160,512]{2,1,0:T(8,128)(2,1)S(1)} %get-tuple-element.65), channel_id=1, source_target_pairs={{0,32},{16,48},{32,0},{48,16},{1,33},{17,49},{33,1},{49,17},{2,34}... | collective-permute-start | bytes 983048 | tf_op jit(solution)/shard_map/ppermute | solution.py:236
  58.9 22.0 %collective-permute-start.13 = (bf16[2,160,512]{2,1,0:T(8,128)(2,1)S(1)}, bf16[2,160,512]{2,1,0:T(8,128)(2,1)S(1)}, u32[]{:S(2)}, u32[]{:S(2)}) collective-permute-start(bf16[2,160,512]{2,1,0:T(8,128)(2,1)S(1)} %get-tuple-element.66), channel_id=1, source_target_pairs={{0,48},{16,0},{32,16},{48,32},{1,49},{17,1},{33,17},{49,33},{2,50}... | collective-permute-start | bytes 983048 | tf_op jit(solution)/shard_map/ppermute | solution.py:236
  80.9 4.0 %copy-start.2 = (bf16[2,160,512]{2,1,0:T(8,128)(2,1)}, bf16[2,160,512]{2,1,0:T(8,128)(2,1)S(1)}, u32[]{:S(2)}) copy-start(bf16[2,160,512]{2,1,0:T(8,128)(2,1)S(1)} %collective-permute-done.12.x2) | copy-start | bytes 983044
  80.9 4.0 %copy-start.4 = (bf16[2,160,512]{2,1,0:T(8,128)(2,1)}, bf16[2,160,512]{2,1,0:T(8,128)(2,1)S(1)}, u32[]{:S(2)}) copy-start(bf16[2,160,512]{2,1,0:T(8,128)(2,1)S(1)} %collective-permute-done.13.x3) | copy-start | bytes 983044
  80.9 2.9 %collective-permute-start.20 = (bf16[1280,256]{1,0:T(8,128)(2,1)S(1)}, bf16[1280,256]{1,0:T(8,128)(2,1)S(1)}, u32[]{:S(2)}, u32[]{:S(2)}) collective-permute-start(bf16[1280,256]{1,0:T(8,128)(2,1)S(1)} %get-tuple-element.76), channel_id=1, source_target_pairs={{0,1},{1,0},{2,3},{3,2},{4,5},{5,4},{6,7},{7,6},{8,9},{9,8},{10,11... | collective-permute-start | bytes 1966088 | tf_op jit(solution)/shard_map/ppermute | solution.py:236
  81.2 7.9 %collective-permute-start.14 = (bf16[160,512]{1,0:T(8,128)(2,1)S(1)}, bf16[160,512]{1,0:T(8,128)(2,1)}, u32[]{:S(2)}, u32[]{:S(2)}) collective-permute-start(bf16[160,512]{1,0:T(8,128)(2,1)S(1)} %get-tuple-element.72), channel_id=1, source_target_pairs={{0,48},{16,0},{32,16},{48,32},{1,49},{17,1},{33,17},{49,33},{2,50}... | collective-permute-start | bytes 491528 | tf_op jit(solution)/shard_map/ppermute | solution.py:236
  82.6 8.7 %collective-permute-start.15 = (bf16[160,512]{1,0:T(8,128)(2,1)S(1)}, bf16[160,512]{1,0:T(8,128)(2,1)}, u32[]{:S(2)}, u32[]{:S(2)}) collective-permute-start(bf16[160,512]{1,0:T(8,128)(2,1)S(1)} %get-tuple-element.73), channel_id=1, source_target_pairs={{0,32},{16,48},{32,0},{48,16},{1,33},{17,49},{33,1},{49,17},{2,34}... | collective-permute-start | bytes 491528 | tf_op jit(solution)/shard_map/ppermute | solution.py:236
  83.8 10.2 %collective-permute-start.16 = (bf16[160,512]{1,0:T(8,128)(2,1)S(1)}, bf16[160,512]{1,0:T(8,128)(2,1)}, u32[]{:S(2)}, u32[]{:S(2)}) collective-permute-start(bf16[160,512]{1,0:T(8,128)(2,1)S(1)} %get-tuple-element.74), channel_id=1, source_target_pairs={{0,16},{16,32},{32,48},{48,0},{1,17},{17,33},{33,49},{49,1},{2,18}... | collective-permute-start | bytes 491528 | tf_op jit(solution)/shard_map/ppermute | solution.py:236
  84.9 16.6 %all-to-all-start.1 = ((bf16[8,160,256]{2,1,0:T(8,128)(2,1)}), bf16[8,160,256]{2,1,0:T(8,128)(2,1)}, u32[]{:S(2)}, u32[]{:S(2)}) async-start(bf16[8,160,256]{2,1,0:T(8,128)(2,1)} %bitcast.8), calls=%async_computation.1 | async-start | bytes 1310720 | tf_op jit(solution)/shard_map/all_to_all | solution.py:311
  95.1 22.2 %copy-start.3 = (bf16[2,160,512]{2,1,0:T(8,128)(2,1)S(1)}, bf16[2,160,512]{2,1,0:T(8,128)(2,1)}, u32[]{:S(2)}) copy-start(bf16[2,160,512]{2,1,0:T(8,128)(2,1)} %copy-done.2) | copy-start | bytes 983044
  95.1 22.2 %copy-start.5 = (bf16[2,160,512]{2,1,0:T(8,128)(2,1)S(1)}, bf16[2,160,512]{2,1,0:T(8,128)(2,1)}, u32[]{:S(2)}) copy-start(bf16[2,160,512]{2,1,0:T(8,128)(2,1)} %copy-done.4) | copy-start | bytes 983044
  95.2 7.5 %collective-permute-start.19 = (bf16[160,512]{1,0:T(8,128)(2,1)S(1)}, bf16[160,512]{1,0:T(8,128)(2,1)S(1)}, u32[]{:S(2)}, u32[]{:S(2)}) collective-permute-start(bf16[160,512]{1,0:T(8,128)(2,1)S(1)} %add_convert_fusion.1.q0), channel_id=1, source_target_pairs={{0,48},{16,0},{32,16},{48,32},{1,49},{17,1},{33,17},{49,33},{2,50}... | collective-permute-start | bytes 491528 | tf_op jit(solution)/shard_map/ppermute | solution.py:236
  95.8 8.6 %collective-permute-start.18 = (bf16[160,512]{1,0:T(8,128)(2,1)S(1)}, bf16[160,512]{1,0:T(8,128)(2,1)S(1)}, u32[]{:S(2)}, u32[]{:S(2)}) collective-permute-start(bf16[160,512]{1,0:T(8,128)(2,1)S(1)} %add_convert_fusion.1.q0), channel_id=1, source_target_pairs={{0,32},{16,48},{32,0},{48,16},{1,33},{17,49},{33,1},{49,17},{2,34}... | collective-permute-start | bytes 491528 | tf_op jit(solution)/shard_map/ppermute | solution.py:236
  97.0 9.4 %collective-permute-start.17 = (bf16[160,512]{1,0:T(8,128)(2,1)S(1)}, bf16[160,512]{1,0:T(8,128)(2,1)S(1)}, u32[]{:S(2)}, u32[]{:S(2)}) collective-permute-start(bf16[160,512]{1,0:T(8,128)(2,1)S(1)} %add_convert_fusion.1.q0), channel_id=1, source_target_pairs={{0,16},{16,32},{32,48},{48,0},{1,17},{17,33},{33,49},{49,1},{2,18}... | collective-permute-start | bytes 491528 | tf_op jit(solution)/shard_map/ppermute | solution.py:236
  106.5 10.8 %collective-permute-start.24 = (bf16[4,160,512]{2,1,0:T(8,128)(2,1)S(1)}, bf16[4,160,512]{2,1,0:T(8,128)(2,1)S(1)}, u32[]{:S(2)}, u32[]{:S(2)}) collective-permute-start(bf16[4,160,512]{2,1,0:T(8,128)(2,1)S(1)} %pad_maximum_fusion), channel_id=1, source_target_pairs={{0,1},{1,0},{2,3},{3,2},{4,5},{5,4},{6,7},{7,6},{8,9},{9,8},{10,11... | collective-permute-start | bytes 1966088 | tf_op jit(solution)/shard_map/ppermute | solution.py:236
  106.6 5.3 %collective-permute-start.23 = (bf16[160,256]{1,0:T(8,128)(2,1)S(1)}, bf16[160,256]{1,0:T(8,128)(2,1)S(1)}, u32[]{:S(2)}, u32[]{:S(2)}) collective-permute-start(bf16[160,256]{1,0:T(8,128)(2,1)S(1)} %reduce_sum.32.k0), channel_id=1, source_target_pairs={{0,48},{16,0},{32,16},{48,32},{1,49},{17,1},{33,17},{49,33},{2,50}... | collective-permute-start | bytes 245768 | tf_op jit(solution)/shard_map/ppermute | solution.py:236
  107.8 6.6 %collective-permute-start.22 = (bf16[160,256]{1,0:T(8,128)(2,1)S(1)}, bf16[160,256]{1,0:T(8,128)(2,1)S(1)}, u32[]{:S(2)}, u32[]{:S(2)}) collective-permute-start(bf16[160,256]{1,0:T(8,128)(2,1)S(1)} %reduce_sum.32.k0), channel_id=1, source_target_pairs={{0,32},{16,48},{32,0},{48,16},{1,33},{17,49},{33,1},{49,17},{2,34}... | collective-permute-start | bytes 245768 | tf_op jit(solution)/shard_map/ppermute | solution.py:236
  108.5 7.1 %collective-permute-start.21 = (bf16[160,256]{1,0:T(8,128)(2,1)S(1)}, bf16[160,256]{1,0:T(8,128)(2,1)S(1)}, u32[]{:S(2)}, u32[]{:S(2)}) collective-permute-start(bf16[160,256]{1,0:T(8,128)(2,1)S(1)} %reduce_sum.32.k0), channel_id=1, source_target_pairs={{0,16},{16,32},{32,48},{48,0},{1,17},{17,33},{33,49},{49,1},{2,18}... | collective-permute-start | bytes 245768 | tf_op jit(solution)/shard_map/ppermute | solution.py:236
  115.6 1.7 %collective-permute-start.25 = (bf16[4,160,256]{2,1,0:T(8,128)(2,1)S(1)}, bf16[4,160,256]{2,1,0:T(8,128)(2,1)S(1)}, u32[]{:S(2)}, u32[]{:S(2)}) collective-permute-start(bf16[4,160,256]{2,1,0:T(8,128)(2,1)S(1)} %pad_maximum_fusion.1), channel_id=1, source_target_pairs={{0,1},{1,0},{2,3},{3,2},{4,5},{5,4},{6,7},{7,6},{8,9},{9,8},{10,11... | collective-permute-start | bytes 983048 | tf_op jit(solution)/shard_map/ppermute | solution.py:236

commit v8 on v7

--- a/solution.py
+++ b/solution.py
@@ -179,7 +179,7 @@
                 out[t, :, p * 256 : (p + 1) * 256] = dot(cols, pick, NN).astype(bf16)
 
 
-def weights_kernel(x0, x1, x2, x3, q0, q1, q2, q3, k0, k1, k2, k3, qo, ko, out, xr, gr):
+def weights_kernel(x0, x1, x2, x3, q0, q1, q2, q3, k0, k1, k2, k3, grads, out, xr, gr):
     wide = HEADS * HEAD
     for d, x in enumerate((x0, x1, x2, x3)):
         rows = slice(d * ROWS, (d + 1) * ROWS)
@@ -188,8 +188,7 @@
         xr[other, :] = x[1]
         gr[rows, :wide] = (q0, q1, q2, q3)[d][...]
         gr[rows, wide:] = (k0, k1, k2, k3)[d][...]
-        gr[other, :wide] = qo[d]
-        gr[other, wide:] = ko[d]
+        gr[other, :] = grads[d]
     dw = dot(xr[...], gr[...], TN).astype(bf16)
     for p in range(16):
         out[p] = dw[p * 32 : (p + 1) * 32]
@@ -260,10 +259,10 @@
     )
     kva = jnp.broadcast_to(kv[None], (8,) + kv.shape)
     kva = lax.all_to_all(kva, ("x", "yh"), 0, 0, tiled=True).reshape(KHALF, 2 * HEAD)
-    kva, qs, gs = lax.optimization_barrier((kva, qs, gs))
+    other_tokens = shift(tokens, "core", 1, 2)
+    later = tokens
+    kva, qs, gs, other_tokens = lax.optimization_barrier((kva, qs, gs, other_tokens))
     kvb = shift(kva, "core", 1, 2)
-    later, kva = lax.optimization_barrier((tokens, kva))
-    other_tokens = shift(later, "core", 1, 2)
 
     key_dev = (o * 8 + np.arange(8)[None, :, None]) * 2 + (ic + np.arange(2)[:, None, None]) % 2
     key_blocks = (key_dev * 2 + np.arange(2)[None, None, :]).reshape(-1)
@@ -314,15 +313,15 @@
     for part in dq_parts:
         dq = dq + part.astype(f32)
     dq_all = from_behind(dq.astype(bf16), "outer", N_OUT)
-    dq_all, dkv = lax.optimization_barrier((dq_all, dkv))
-
-    dq_other = shift(jnp.stack(dq_all), "core", 1, 2)
-    dkv_other = shift(jnp.stack(dkv_all), "core", 1, 2)
+    dq_all, dkv_all = lax.optimization_barrier((dq_all, dkv_all))
+
+    grads = [jnp.concatenate(pair, axis=1) for pair in zip(dq_all, dkv_all)]
+    other_grads = shift(jnp.stack(grads), "core", 1, 2)
     (dw,) = kernel_call(
         weights_kernel, "weights", [((16, 32, 768), bf16)],
         [((2 * N_OUT * ROWS, 512), bf16), ((2 * N_OUT * ROWS, 768), bf16)],
         cost(1280 * 512, 6, 4 << 20), [],
-        *xs, *dq_all, *dkv_all, dq_other, dkv_other,
+        *xs, *dq_all, *dkv_all, other_grads,
     )
     dw = lax.all_to_all(dw, ("dp", "x", "yh"), 0, 0, tiled=True)
     return kernel_call(

time: 138 us -> 133 us (0.964)
  local copies, waits for them, and re-layouts: 4.49 us -> 1.31 us
  waiting for transfers between devices: 26.5 us -> 23.5 us
  starting transfers between devices: 40.6 us -> 42.2 us
    unnamed x32 -> x24, local copies, waits for them, and re-layouts: 3.23 us -> 0.07 us
    ppermute x26 -> x25, waiting for transfers between devices: 19.9 us -> 17 us  [shift(): return lax.ppermute(x, axis, [(i, (i + d) % n) for i in range(n)])]
    ppermute x26 -> x25, starting transfers between devices: 29.4 us -> 30.8 us  [shift(): return lax.ppermute(x, axis, [(i, (i + d) % n) for i in range(n)])]
  transfers between devices with their start and end apart: 28 -> 27, of which waited for: 11 -> 10; matrix products, arithmetic and copies ran while one was open for 5% -> 4% of each run, Pallas kernels for 26% -> 22%
where the time goes in v8:
time: 133 us; the launch traced here: 132 us
  starting transfers between devices  42.2 us (32%)
  Pallas kernels  38 us (29%)
  waiting for transfers between devices  23.5 us (18%)
  blocking collectives  18.2 us (14%)
  matrix products  4.59 us (3%)
  other arithmetic  3.29 us (2%)
    pallas_call x6, Pallas kernels, kernel_call(): pl.pallas_call(body, out_shape=tuple((jax.ShapeDtypeStruct(*o) for o in o...  38 us
    ppermute x25, starting transfers between devices, shift(): return lax.ppermute(x, axis, [(i, (i + d) % n) for i in range(n)])  30.8 us
    all_to_all x1, blocking collectives, per_device(): dw = lax.all_to_all(dw, ('dp', 'x', 'yh'), 0, 0, tiled=True)  18.2 us
    ppermute x25, waiting for transfers between devices, shift(): return lax.ppermute(x, axis, [(i, (i + d) % n) for i in range(n)])  17 us
    all_to_all x1, starting transfers between devices, per_device(): lax.all_to_all(kva, ('x', 'yh'), 0, 0, tiled=True).reshape(KHALF, 2 * HEAD)  6.93 us
    dot_general x3, matrix products, dot(): return lax.dot_general(a, b, dims, preferred_element_type=f32)  4.59 us
    all_to_all x1, starting transfers between devices, per_device(): dkv = lax.all_to_all(dkv, ('x', 'yh'), 0, 0, tiled=True)  4.5 us
    all_to_all x1, waiting for transfers between devices, per_device(): dkv = lax.all_to_all(dkv, ('x', 'yh'), 0, 0, tiled=True)  3.72 us
  transfers between devices with their start and end apart: 27, of which 10 were waited for; matrix products, arithmetic and copies ran while one was open for 4% of the time, Pallas kernels for 22%

profile of v8, /device:TPU:0, one launch (start us, length us, event | category | flops | bytes accessed | tf_op | source)
XLA Modules:
  0.0 132.1 jit_solution(517269134155745911)
XLA Ops:
  0.7 3.6 %convolution_convert_fusion.q0 = bf16[160,512]{1,0:T(8,128)(2,1)S(1)} fusion(bf16[4096,512]{1,0:T(8,128)(2,1)} %param.13, bf16[1,160,4096]{2,1,0:T(8,128)(2,1)} %param.11), kind=kOutput, calls=%fused_computation.1 | convolution fusion | flops 671170560 | bytes 5668864 | tf_op jit(solution)/shard_map/dot_general | solution.py:36
  4.3 4.2 %collective-permute-start.2 = (bf16[160,512]{1,0:T(8,128)(2,1)S(1)}, bf16[160,512]{1,0:T(8,128)(2,1)S(1)}, u32[]{:S(2)}, u32[]{:S(2)}) collective-permute-start(bf16[160,512]{1,0:T(8,128)(2,1)S(1)} %convolution_convert_fusion.q0), channel_id=1, source_target_pairs={{0,48},{16,0},{32,16},{48,32},{1,49},{17,1},{33,17},{49,33},{2,50}... | collective-permute-start | bytes 491528 | tf_op jit(solution)/shard_map/ppermute | solution.py:235
  8.5 3.2 %collective-permute-start.4 = (bf16[160,512]{1,0:T(8,128)(2,1)S(1)}, bf16[160,512]{1,0:T(8,128)(2,1)}, u32[]{:S(2)}, u32[]{:S(2)}) collective-permute-start(bf16[160,512]{1,0:T(8,128)(2,1)S(1)} %bitcast.33), channel_id=1, source_target_pairs={{0,48},{16,0},{32,16},{48,32},{1,49},{17,1},{33,17},{49,33},{2,50}... | collective-permute-start | bytes 491528 | tf_op jit(solution)/shard_map/ppermute | solution.py:235
  11.7 0.5 convolution_convert_fusion.2
  12.2 0.5 convolution_convert_fusion.1
  12.8 0.9 broadcast_in_dim.47
  13.7 6.9 %all-to-all-start = ((bf16[8,160,256]{2,1,0:T(8,128)(2,1)}), bf16[8,160,256]{2,1,0:T(8,128)(2,1)S(1)}, u32[]{:S(2)}, u32[]{:S(2)}) async-start(bf16[8,160,256]{2,1,0:T(8,128)(2,1)} %broadcast_in_dim.47), calls=%async_computation | async-start | bytes 1310720 | tf_op jit(solution)/shard_map/all_to_all | solution.py:261
  21.0 3.3 %collective-permute-start.5 = (bf16[160,512]{1,0:T(8,128)(2,1)}, bf16[160,512]{1,0:T(8,128)(2,1)}, u32[]{:S(2)}, u32[]{:S(2)}) collective-permute-start(bf16[160,512]{1,0:T(8,128)(2,1)} %collective-permute-done.4.g3), channel_id=1, source_target_pairs={{0,48},{16,0},{32,16},{48,32},{1,49},{17,1},{33,17},{49,33},{2,50}... | collective-permute-start | bytes 491528 | tf_op jit(solution)/shard_map/ppermute | solution.py:235
  24.4 0.2 select_reduce_fusion.1
  24.6 4.7 %collective-permute-done.1.q2 = bf16[160,512]{1,0:T(8,128)(2,1)} collective-permute-done((bf16[160,512]{1,0:T(8,128)(2,1)}, bf16[160,512]{1,0:T(8,128)(2,1)}, u32[]{:S(2)}, u32[]{:S(2)}) %collective-permute-start.1) | collective-permute-done | bytes 163872 | tf_op jit(solution)/shard_map/ppermute | solution.py:235
  29.3 2.7 %all-to-all-done = bf16[8,160,256]{2,1,0:T(8,128)(2,1)S(1)} async-done(((bf16[8,160,256]{2,1,0:T(8,128)(2,1)}), bf16[8,160,256]{2,1,0:T(8,128)(2,1)S(1)}, u32[]{:S(2)}, u32[]{:S(2)}) %all-to-all-start) | async-done | bytes 655392 | tf_op jit(solution)/shard_map/all_to_all | solution.py:261
  32.1 0.1 add.152
  32.3 0.1 reshape.101.posq.posq_ref
  32.5 0.2 select_reduce_fusion.ordk
  32.7 6.9 %stats_own.1 = (f32[3,2560]{1,0:T(4,128)S(1)}, bf16[2560,128]{1,0:T(8,128)(2,1)S(1)}, bf16[2560,128]{1,0:T(8,128)(2,1)S(1)}) custom-call(s32[32]{0:T(128)S(1)} %select_reduce_fusion.ordk, s32[1,2560]{1,0:T(1,128)S(1)} %reshape.101.posq.posq_ref, bf16[160,512]{1,0:T(8,128)(2,1)S(1)} %convolution_convert_fusion.q0, bf16[160,512]{1,0:T(8,128)(2,1)} %collective-permute-done.q1, ...), custom_call_target="tpu_custom_call" | custom-call | flops 1677721600 | bytes 4194304 | tf_op jit(solution)/shard_map/stats_own/pallas_call | solution.py:218
  39.6 6.6 %stats_other.1.s0 = f32[3,2560]{1,0:T(4,128)S(1)} custom-call(s32[32]{0:T(128)S(1)} %select_reduce_fusion.ordk, s32[1,2560]{1,0:T(1,128)S(1)} %reshape.101.posq.posq_ref, bf16[2560,128]{1,0:T(8,128)(2,1)S(1)} %get-tuple-element.55.qr, bf16[2560,128]{1,0:T(8,128)(2,1)S(1)} %get-tuple-element.56.gr, bf16[1280,256]{1,0:T(8,128)(2,1)} %collective-permute-done.7.kvb, ...), custom_call_target="tpu_custom_call" | custom-call | flops 1677721600 | bytes 4194304 | tf_op jit(solution)/shard_map/stats_other/pallas_call | solution.py:218
  46.1 3.3 %collective-permute-start.10 = (f32[3,2560]{1,0:T(4,128)S(1)}, f32[3,2560]{1,0:T(4,128)S(1)}, u32[]{:S(2)}, u32[]{:S(2)}) collective-permute-start(f32[3,2560]{1,0:T(4,128)S(1)} %stats_other.1.s0), channel_id=1, source_target_pairs={{0,48},{16,0},{32,16},{48,32},{1,49},{17,1},{33,17},{49,33},{2,50}... | collective-permute-start | bytes 92168 | tf_op jit(solution)/shard_map/ppermute | solution.py:235
  49.4 0.9 collective-permute-start.8
  50.4 2.2 %columns.1 = (bf16[2,160,512]{2,1,0:T(8,128)(2,1)S(1)}, bf16[2,160,512]{2,1,0:T(8,128)(2,1)S(1)}, bf16[2,160,512]{2,1,0:T(8,128)(2,1)S(1)}, bf16[2,160,512]{2,1,0:T(8,128)(2,1)S(1)}) custom-call(s32[2]{0:T(128)S(1)} %pad_add_fusion.place_ref, bf16[160,4096]{1,0:T(8,128)(2,1)S(1)} %bitcast.29, bf16[160,4096]{1,0:T(8,128)(2,1)} %collective-permute-done.6.other), custom_call_target="tpu_custom_call" | custom-call | flops 671088640 | bytes 5242880 | tf_op jit(solution)/shard_map/columns/pallas_call | solution.py:218
  52.6 2.6 %collective-permute-start.11 = (bf16[2,160,512]{2,1,0:T(8,128)(2,1)S(1)}, bf16[2,160,512]{2,1,0:T(8,128)(2,1)S(1)}, u32[]{:S(2)}, u32[]{:S(2)}) collective-permute-start(bf16[2,160,512]{2,1,0:T(8,128)(2,1)S(1)} %get-tuple-element.66), channel_id=1, source_target_pairs={{0,16},{16,32},{32,48},{48,0},{1,17},{17,33},{33,49},{49,1},{2,18}... | collective-permute-start | bytes 983048 | tf_op jit(solution)/shard_map/ppermute | solution.py:235
  55.2 1.2 collective-permute-start.12
  56.4 1.6 %collective-permute-start.13 = (bf16[2,160,512]{2,1,0:T(8,128)(2,1)S(1)}, bf16[2,160,512]{2,1,0:T(8,128)(2,1)S(1)}, u32[]{:S(2)}, u32[]{:S(2)}) collective-permute-start(bf16[2,160,512]{2,1,0:T(8,128)(2,1)S(1)} %get-tuple-element.68), channel_id=1, source_target_pairs={{0,48},{16,0},{32,16},{48,32},{1,49},{17,1},{33,17},{49,33},{2,50}... | collective-permute-start | bytes 983048 | tf_op jit(solution)/shard_map/ppermute | solution.py:235
  58.0 20.4 %grads.1 = (f32[160,512]{1,0:T(8,128)S(1)}, bf16[160,512]{1,0:T(8,128)(2,1)S(1)}, bf16[160,512]{1,0:T(8,128)(2,1)S(1)}, bf16[160,512]{1,0:T(8,128)(2,1)S(1)}, f3...) custom-call(s32[32]{0:T(128)S(1)} %select_reduce_fusion.ordk, s32[1,2560]{1,0:T(1,128)S(1)} %reshape.101.posq.posq_ref, ...), custom_call_target="tpu_custom_call" | custom-call | flops 8388608000 | bytes 8388608 | tf_op jit(solution)/shard_map/grads/pallas_call | solution.py:218
  78.4 0.3 collective-permute-start.20
  78.7 1.4 %collective-permute-start.14 = (bf16[160,512]{1,0:T(8,128)(2,1)S(1)}, bf16[160,512]{1,0:T(8,128)(2,1)}, u32[]{:S(2)}, u32[]{:S(2)}) collective-permute-start(bf16[160,512]{1,0:T(8,128)(2,1)S(1)} %get-tuple-element.74), channel_id=1, source_target_pairs={{0,48},{16,0},{32,16},{48,32},{1,49},{17,1},{33,17},{49,33},{2,50}... | collective-permute-start | bytes 491528 | tf_op jit(solution)/shard_map/ppermute | solution.py:235
  80.1 1.2 collective-permute-start.15
  81.4 1.1 add_convert_fusion
  82.4 4.5 %all-to-all-start.1 = ((bf16[8,160,256]{2,1,0:T(8,128)(2,1)}), bf16[8,160,256]{2,1,0:T(8,128)(2,1)S(1)}, u32[]{:S(2)}, u32[]{:S(2)}) async-start(bf16[8,160,256]{2,1,0:T(8,128)(2,1)} %bitcast.8), calls=%async_computation.1 | async-start | bytes 1310720 | tf_op jit(solution)/shard_map/all_to_all | solution.py:310
  86.9 1.9 %collective-permute-done.15 = bf16[160,512]{1,0:T(8,128)(2,1)} collective-permute-done((bf16[160,512]{1,0:T(8,128)(2,1)S(1)}, bf16[160,512]{1,0:T(8,128)(2,1)}, u32[]{:S(2)}, u32[]{:S(2)}) %collective-permute-start.15) | collective-permute-done | bytes 163872 | tf_op jit(solution)/shard_map/ppermute | solution.py:235
  88.8 2.7 %collective-permute-done.16 = bf16[160,512]{1,0:T(8,128)(2,1)} collective-permute-done((bf16[160,512]{1,0:T(8,128)(2,1)S(1)}, bf16[160,512]{1,0:T(8,128)(2,1)}, u32[]{:S(2)}, u32[]{:S(2)}) %collective-permute-start.16) | collective-permute-done | bytes 163872 | tf_op jit(solution)/shard_map/ppermute | solution.py:235
  91.5 1.2 add_convert_fusion.1.q0
  92.7 0.7 collective-permute-start.19
  93.3 1.2 collective-permute-start.18
  94.6 0.8 collective-permute-start.17
  95.4 3.7 %all-to-all-done.1 = bf16[8,160,256]{2,1,0:T(8,128)(2,1)S(1)} async-done(((bf16[8,160,256]{2,1,0:T(8,128)(2,1)}), bf16[8,160,256]{2,1,0:T(8,128)(2,1)S(1)}, u32[]{:S(2)}, u32[]{:S(2)}) %all-to-all-start.1) | async-done | bytes 655392 | tf_op jit(solution)/shard_map/all_to_all | solution.py:310
  99.1 0.1 reduce_sum.32.k0
  99.2 3.0 %collective-permute-start.23 = (bf16[160,256]{1,0:T(8,128)(2,1)S(1)}, bf16[160,256]{1,0:T(8,128)(2,1)S(1)}, u32[]{:S(2)}, u32[]{:S(2)}) collective-permute-start(bf16[160,256]{1,0:T(8,128)(2,1)S(1)} %reduce_sum.32.k0), channel_id=1, source_target_pairs={{0,48},{16,0},{32,16},{48,32},{1,49},{17,1},{33,17},{49,33},{2,50}... | collective-permute-start | bytes 245768 | tf_op jit(solution)/shard_map/ppermute | solution.py:235
  102.2 0.9 collective-permute-start.22
  103.2 0.7 collective-permute-start.21
  103.9 0.1 collective-permute-done.17.q1
  104.0 1.0 collective-permute-done.23.k3
  105.0 3.2 %collective-permute-done.22.k2 = bf16[160,256]{1,0:T(8,128)(2,1)S(1)} collective-permute-done((bf16[160,256]{1,0:T(8,128)(2,1)S(1)}, bf16[160,256]{1,0:T(8,128)(2,1)S(1)}, u32[]{:S(2)}, u32[]{:S(2)}) %collective-permute-start.22) | collective-permute-done | bytes 81952 | tf_op jit(solution)/shard_map/ppermute | solution.py:235
  108.2 0.9 collective-permute-done.21.k1
  109.1 0.1 pad_maximum_fusion
  109.4 2.6 %collective-permute-done.24.grads = bf16[4,160,768]{2,1,0:T(8,128)(2,1)S(1)} collective-permute-done((bf16[4,160,768]{2,1,0:T(8,128)(2,1)S(1)}, bf16[4,160,768]{2,1,0:T(8,128)(2,1)S(1)}, u32[]{:S(2)}, u32[]{:S(2)}) %collective-permute-start.24) | collective-permute-done | bytes 983072 | tf_op jit(solution)/shard_map/ppermute | solution.py:235
  111.9 1.2 weights.1
  113.2 18.2 %all_to_all.15.parts = bf16[16,32,768]{2,1,0:T(8,128)(2,1)S(1)} all-to-all(bf16[16,32,768]{2,1,0:T(8,128)(2,1)S(1)} %weights.1), channel_id=1, replica_groups=mesh['dp'=2,'outer'=4,'x'=4,'yh'=2,'core'=2] {'dp','x','yh'}, dimensions={0} | all-to-all | bytes 1572864 | tf_op jit(solution)/shard_map/all_to_all | solution.py:326
  131.4 0.7 last_sum.1
  (64 shorter events, 0.9 us)
Async XLA Ops:
  0.6 11.1 %copy-start = (bf16[4096,128]{1,0:T(8,128)(2,1)S(1)}, bf16[4096,128]{1,0:T(8,128)(2,1)}, u32[]{:S(2)}) copy-start(bf16[4096,128]{1,0:T(8,128)(2,1)} %param.14) | copy-start | bytes 3145732
  0.6 11.1 %copy-start.1 = (bf16[1,160,4096]{2,1,0:T(8,128)(2,1)S(1)}, bf16[1,160,4096]{2,1,0:T(8,128)(2,1)}, u32[]{:S(2)}) copy-start(bf16[1,160,4096]{2,1,0:T(8,128)(2,1)} %param.11) | copy-start | bytes 3932164
  0.7 7.8 %copy-start.6 = (bf16[1,160,512]{2,1,0:T(8,128)(2,1)S(1)}, bf16[1,160,512]{2,1,0:T(8,128)(2,1)}, u32[]{:S(2)}) copy-start(bf16[1,160,512]{2,1,0:T(8,128)(2,1)} %param.16) | copy-start | bytes 491524
  4.3 8.0 %copy-start.7 = (bf16[4096,128]{1,0:T(8,128)(2,1)S(1)}, bf16[4096,128]{1,0:T(8,128)(2,1)}, u32[]{:S(2)}) copy-start(bf16[4096,128]{1,0:T(8,128)(2,1)} %param.15) | copy-start | bytes 3145732
  4.3 20.3 %collective-permute-start.2 = (bf16[160,512]{1,0:T(8,128)(2,1)S(1)}, bf16[160,512]{1,0:T(8,128)(2,1)S(1)}, u32[]{:S(2)}, u32[]{:S(2)}) collective-permute-start(bf16[160,512]{1,0:T(8,128)(2,1)S(1)} %convolution_convert_fusion.q0), channel_id=1, source_target_pairs={{0,48},{16,0},{32,16},{48,32},{1,49},{17,1},{33,17},{49,33},{2,50}... | collective-permute-start | bytes 491528 | tf_op jit(solution)/shard_map/ppermute | solution.py:235
  8.5 12.4 %collective-permute-start = (bf16[160,512]{1,0:T(8,128)(2,1)S(1)}, bf16[160,512]{1,0:T(8,128)(2,1)}, u32[]{:S(2)}, u32[]{:S(2)}) collective-permute-start(bf16[160,512]{1,0:T(8,128)(2,1)S(1)} %convolution_convert_fusion.q0), channel_id=1, source_target_pairs={{0,16},{16,32},{32,48},{48,0},{1,17},{17,33},{33,49},{49,1},{2,18}... | collective-permute-start | bytes 491528 | tf_op jit(solution)/shard_map/ppermute | solution.py:235
  8.5 12.5 %collective-permute-start.4 = (bf16[160,512]{1,0:T(8,128)(2,1)S(1)}, bf16[160,512]{1,0:T(8,128)(2,1)}, u32[]{:S(2)}, u32[]{:S(2)}) collective-permute-start(bf16[160,512]{1,0:T(8,128)(2,1)S(1)} %bitcast.33), channel_id=1, source_target_pairs={{0,48},{16,0},{32,16},{48,32},{1,49},{17,1},{33,17},{49,33},{2,50}... | collective-permute-start | bytes 491528 | tf_op jit(solution)/shard_map/ppermute | solution.py:235
  11.7 12.9 %collective-permute-start.3 = (bf16[160,512]{1,0:T(8,128)(2,1)S(1)}, bf16[160,512]{1,0:T(8,128)(2,1)}, u32[]{:S(2)}, u32[]{:S(2)}) collective-permute-start(bf16[160,512]{1,0:T(8,128)(2,1)S(1)} %bitcast.34), channel_id=1, source_target_pairs={{0,16},{16,32},{32,48},{48,0},{1,17},{17,33},{33,49},{49,1},{2,18}... | collective-permute-start | bytes 491528 | tf_op jit(solution)/shard_map/ppermute | solution.py:235
  12.7 7.9 %copy-start.11 = (s32[1,8,1]{1,2,0:T(1,128)S(1)}, s32[1,8,1]{1,2,0:T(1,128)}, u32[]{:S(2)}) copy-start(s32[1,8,1]{1,2,0:T(1,128)} %constant.67.clone) | copy-start | bytes 100
  12.8 7.9 %copy-start.10 = (s32[2,1,1]{0,2,1:T(1,128)S(1)}, s32[2,1,1]{0,2,1:T(1,128)}, u32[]{:S(2)}) copy-start(s32[2,1,1]{0,2,1:T(1,128)} %constant.68.clone) | copy-start | bytes 28
  12.8 8.1 %copy-start.8 = (s32[4]{0:T(128)S(1)}, s32[4]{0:T(128)}, u32[]{:S(2)}) copy-start(s32[4]{0:T(128)} %constant.76) | copy-start | bytes 52
  12.8 11.6 %copy-start.9 = (s32[1,128]{1,0:T(1,128)S(1)}, s32[1,128]{1,0:T(1,128)}, u32[]{:S(2)}) copy-start(s32[1,128]{1,0:T(1,128)} %param.12) | copy-start | bytes 1540
  13.7 18.3 %all-to-all-start = ((bf16[8,160,256]{2,1,0:T(8,128)(2,1)}), bf16[8,160,256]{2,1,0:T(8,128)(2,1)S(1)}, u32[]{:S(2)}, u32[]{:S(2)}) async-start(bf16[8,160,256]{2,1,0:T(8,128)(2,1)} %broadcast_in_dim.47), calls=%async_computation | async-start | bytes 1310720 | tf_op jit(solution)/shard_map/all_to_all | solution.py:261
  20.6 11.4 %collective-permute-start.6 = (bf16[160,4096]{1,0:T(8,128)(2,1)S(1)}, bf16[160,4096]{1,0:T(8,128)(2,1)}, u32[]{:S(2)}, u32[]{:S(2)}) collective-permute-start(bf16[160,4096]{1,0:T(8,128)(2,1)S(1)} %bitcast.28), channel_id=1, source_target_pairs={{0,1},{1,0},{2,3},{3,2},{4,5},{5,4},{6,7},{7,6},{8,9},{9,8},{10,11... | collective-permute-start | bytes 3932168 | tf_op jit(solution)/shard_map/ppermute | solution.py:235
  20.9 8.4 %collective-permute-start.1 = (bf16[160,512]{1,0:T(8,128)(2,1)}, bf16[160,512]{1,0:T(8,128)(2,1)}, u32[]{:S(2)}, u32[]{:S(2)}) collective-permute-start(bf16[160,512]{1,0:T(8,128)(2,1)} %collective-permute-done.q1), channel_id=1, source_target_pairs={{0,16},{16,32},{32,48},{48,0},{1,17},{17,33},{33,49},{49,1},{2,18}... | collective-permute-start | bytes 491528 | tf_op jit(solution)/shard_map/ppermute | solution.py:235
  21.0 8.4 %collective-permute-start.5 = (bf16[160,512]{1,0:T(8,128)(2,1)}, bf16[160,512]{1,0:T(8,128)(2,1)}, u32[]{:S(2)}, u32[]{:S(2)}) collective-permute-start(bf16[160,512]{1,0:T(8,128)(2,1)} %collective-permute-done.4.g3), channel_id=1, source_target_pairs={{0,48},{16,0},{32,16},{48,32},{1,49},{17,1},{33,17},{49,33},{2,50}... | collective-permute-start | bytes 491528 | tf_op jit(solution)/shard_map/ppermute | solution.py:235
  32.0 7.5 %collective-permute-start.7 = (bf16[1280,256]{1,0:T(8,128)(2,1)S(1)}, bf16[1280,256]{1,0:T(8,128)(2,1)}, u32[]{:S(2)}, u32[]{:S(2)}) collective-permute-start(bf16[1280,256]{1,0:T(8,128)(2,1)S(1)} %bitcast.30), channel_id=1, source_target_pairs={{0,1},{1,0},{2,3},{3,2},{4,5},{5,4},{6,7},{7,6},{8,9},{9,8},{10,11... | collective-permute-start | bytes 1966088 | tf_op jit(solution)/shard_map/ppermute | solution.py:235
  46.1 10.3 %collective-permute-start.10 = (f32[3,2560]{1,0:T(4,128)S(1)}, f32[3,2560]{1,0:T(4,128)S(1)}, u32[]{:S(2)}, u32[]{:S(2)}) collective-permute-start(f32[3,2560]{1,0:T(4,128)S(1)} %stats_other.1.s0), channel_id=1, source_target_pairs={{0,48},{16,0},{32,16},{48,32},{1,49},{17,1},{33,17},{49,33},{2,50}... | collective-permute-start | bytes 92168 | tf_op jit(solution)/shard_map/ppermute | solution.py:235
  49.4 8.5 %collective-permute-start.9 = (f32[3,2560]{1,0:T(4,128)S(1)}, f32[3,2560]{1,0:T(4,128)S(1)}, u32[]{:S(2)}, u32[]{:S(2)}) collective-permute-start(f32[3,2560]{1,0:T(4,128)S(1)} %stats_other.1.s0), channel_id=1, source_target_pairs={{0,32},{16,48},{32,0},{48,16},{1,33},{17,49},{33,1},{49,17},{2,34}... | collective-permute-start | bytes 92168 | tf_op jit(solution)/shard_map/ppermute | solution.py:235
  49.4 8.5 %collective-permute-start.8 = (f32[3,2560]{1,0:T(4,128)S(1)}, f32[3,2560]{1,0:T(4,128)S(1)}, u32[]{:S(2)}, u32[]{:S(2)}) collective-permute-start(f32[3,2560]{1,0:T(4,128)S(1)} %stats_other.1.s0), channel_id=1, source_target_pairs={{0,16},{16,32},{32,48},{48,0},{1,17},{17,33},{33,49},{49,1},{2,18}... | collective-permute-start | bytes 92168 | tf_op jit(solution)/shard_map/ppermute | solution.py:235
  52.6 25.8 %collective-permute-start.11 = (bf16[2,160,512]{2,1,0:T(8,128)(2,1)S(1)}, bf16[2,160,512]{2,1,0:T(8,128)(2,1)S(1)}, u32[]{:S(2)}, u32[]{:S(2)}) collective-permute-start(bf16[2,160,512]{2,1,0:T(8,128)(2,1)S(1)} %get-tuple-element.66), channel_id=1, source_target_pairs={{0,16},{16,32},{32,48},{48,0},{1,17},{17,33},{33,49},{49,1},{2,18}... | collective-permute-start | bytes 983048 | tf_op jit(solution)/shard_map/ppermute | solution.py:235
  55.2 23.2 %collective-permute-start.12 = (bf16[2,160,512]{2,1,0:T(8,128)(2,1)S(1)}, bf16[2,160,512]{2,1,0:T(8,128)(2,1)S(1)}, u32[]{:S(2)}, u32[]{:S(2)}) collective-permute-start(bf16[2,160,512]{2,1,0:T(8,128)(2,1)S(1)} %get-tuple-element.67), channel_id=1, source_target_pairs={{0,32},{16,48},{32,0},{48,16},{1,33},{17,49},{33,1},{49,17},{2,34}... | collective-permute-start | bytes 983048 | tf_op jit(solution)/shard_map/ppermute | solution.py:235
  56.4 22.0 %collective-permute-start.13 = (bf16[2,160,512]{2,1,0:T(8,128)(2,1)S(1)}, bf16[2,160,512]{2,1,0:T(8,128)(2,1)S(1)}, u32[]{:S(2)}, u32[]{:S(2)}) collective-permute-start(bf16[2,160,512]{2,1,0:T(8,128)(2,1)S(1)} %get-tuple-element.68), channel_id=1, source_target_pairs={{0,48},{16,0},{32,16},{48,32},{1,49},{17,1},{33,17},{49,33},{2,50}... | collective-permute-start | bytes 983048 | tf_op jit(solution)/shard_map/ppermute | solution.py:235
  78.4 4.0 %copy-start.2 = (bf16[2,160,512]{2,1,0:T(8,128)(2,1)}, bf16[2,160,512]{2,1,0:T(8,128)(2,1)S(1)}, u32[]{:S(2)}) copy-start(bf16[2,160,512]{2,1,0:T(8,128)(2,1)S(1)} %collective-permute-done.12.x2) | copy-start | bytes 983044
  78.4 4.0 %copy-start.4 = (bf16[2,160,512]{2,1,0:T(8,128)(2,1)}, bf16[2,160,512]{2,1,0:T(8,128)(2,1)S(1)}, u32[]{:S(2)}) copy-start(bf16[2,160,512]{2,1,0:T(8,128)(2,1)S(1)} %collective-permute-done.13.x3) | copy-start | bytes 983044
  78.4 2.9 %collective-permute-start.20 = (bf16[1280,256]{1,0:T(8,128)(2,1)S(1)}, bf16[1280,256]{1,0:T(8,128)(2,1)S(1)}, u32[]{:S(2)}, u32[]{:S(2)}) collective-permute-start(bf16[1280,256]{1,0:T(8,128)(2,1)S(1)} %get-tuple-element.78), channel_id=1, source_target_pairs={{0,1},{1,0},{2,3},{3,2},{4,5},{5,4},{6,7},{7,6},{8,9},{9,8},{10,11... | collective-permute-start | bytes 1966088 | tf_op jit(solution)/shard_map/ppermute | solution.py:235
  78.7 8.2 %collective-permute-start.14 = (bf16[160,512]{1,0:T(8,128)(2,1)S(1)}, bf16[160,512]{1,0:T(8,128)(2,1)}, u32[]{:S(2)}, u32[]{:S(2)}) collective-permute-start(bf16[160,512]{1,0:T(8,128)(2,1)S(1)} %get-tuple-element.74), channel_id=1, source_target_pairs={{0,48},{16,0},{32,16},{48,32},{1,49},{17,1},{33,17},{49,33},{2,50}... | collective-permute-start | bytes 491528 | tf_op jit(solution)/shard_map/ppermute | solution.py:235
  80.1 8.7 %collective-permute-start.15 = (bf16[160,512]{1,0:T(8,128)(2,1)S(1)}, bf16[160,512]{1,0:T(8,128)(2,1)}, u32[]{:S(2)}, u32[]{:S(2)}) collective-permute-start(bf16[160,512]{1,0:T(8,128)(2,1)S(1)} %get-tuple-element.75), channel_id=1, source_target_pairs={{0,32},{16,48},{32,0},{48,16},{1,33},{17,49},{33,1},{49,17},{2,34}... | collective-permute-start | bytes 491528 | tf_op jit(solution)/shard_map/ppermute | solution.py:235
  81.3 10.2 %collective-permute-start.16 = (bf16[160,512]{1,0:T(8,128)(2,1)S(1)}, bf16[160,512]{1,0:T(8,128)(2,1)}, u32[]{:S(2)}, u32[]{:S(2)}) collective-permute-start(bf16[160,512]{1,0:T(8,128)(2,1)S(1)} %get-tuple-element.76), channel_id=1, source_target_pairs={{0,16},{16,32},{32,48},{48,0},{1,17},{17,33},{33,49},{49,1},{2,18}... | collective-permute-start | bytes 491528 | tf_op jit(solution)/shard_map/ppermute | solution.py:235
  82.4 16.7 %all-to-all-start.1 = ((bf16[8,160,256]{2,1,0:T(8,128)(2,1)}), bf16[8,160,256]{2,1,0:T(8,128)(2,1)S(1)}, u32[]{:S(2)}, u32[]{:S(2)}) async-start(bf16[8,160,256]{2,1,0:T(8,128)(2,1)} %bitcast.8), calls=%async_computation.1 | async-start | bytes 1310720 | tf_op jit(solution)/shard_map/all_to_all | solution.py:310
  92.7 10.5 %collective-permute-start.19 = (bf16[160,512]{1,0:T(8,128)(2,1)S(1)}, bf16[160,512]{1,0:T(8,128)(2,1)S(1)}, u32[]{:S(2)}, u32[]{:S(2)}) collective-permute-start(bf16[160,512]{1,0:T(8,128)(2,1)S(1)} %add_convert_fusion.1.q0), channel_id=1, source_target_pairs={{0,48},{16,0},{32,16},{48,32},{1,49},{17,1},{33,17},{49,33},{2,50}... | collective-permute-start | bytes 491528 | tf_op jit(solution)/shard_map/ppermute | solution.py:235
  93.3 10.5 %collective-permute-start.18 = (bf16[160,512]{1,0:T(8,128)(2,1)S(1)}, bf16[160,512]{1,0:T(8,128)(2,1)S(1)}, u32[]{:S(2)}, u32[]{:S(2)}) collective-permute-start(bf16[160,512]{1,0:T(8,128)(2,1)S(1)} %add_convert_fusion.1.q0), channel_id=1, source_target_pairs={{0,32},{16,48},{32,0},{48,16},{1,33},{17,49},{33,1},{49,17},{2,34}... | collective-permute-start | bytes 491528 | tf_op jit(solution)/shard_map/ppermute | solution.py:235
  94.6 9.4 %collective-permute-start.17 = (bf16[160,512]{1,0:T(8,128)(2,1)S(1)}, bf16[160,512]{1,0:T(8,128)(2,1)S(1)}, u32[]{:S(2)}, u32[]{:S(2)}) collective-permute-start(bf16[160,512]{1,0:T(8,128)(2,1)S(1)} %add_convert_fusion.1.q0), channel_id=1, source_target_pairs={{0,16},{16,32},{32,48},{48,0},{1,17},{17,33},{33,49},{49,1},{2,18}... | collective-permute-start | bytes 491528 | tf_op jit(solution)/shard_map/ppermute | solution.py:235
  99.2 5.8 %collective-permute-start.23 = (bf16[160,256]{1,0:T(8,128)(2,1)S(1)}, bf16[160,256]{1,0:T(8,128)(2,1)S(1)}, u32[]{:S(2)}, u32[]{:S(2)}) collective-permute-start(bf16[160,256]{1,0:T(8,128)(2,1)S(1)} %reduce_sum.32.k0), channel_id=1, source_target_pairs={{0,48},{16,0},{32,16},{48,32},{1,49},{17,1},{33,17},{49,33},{2,50}... | collective-permute-start | bytes 245768 | tf_op jit(solution)/shard_map/ppermute | solution.py:235
  102.2 6.0 %collective-permute-start.22 = (bf16[160,256]{1,0:T(8,128)(2,1)S(1)}, bf16[160,256]{1,0:T(8,128)(2,1)S(1)}, u32[]{:S(2)}, u32[]{:S(2)}) collective-permute-start(bf16[160,256]{1,0:T(8,128)(2,1)S(1)} %reduce_sum.32.k0), channel_id=1, source_target_pairs={{0,32},{16,48},{32,0},{48,16},{1,33},{17,49},{33,1},{49,17},{2,34}... | collective-permute-start | bytes 245768 | tf_op jit(solution)/shard_map/ppermute | solution.py:235
  103.2 5.9 %collective-permute-start.21 = (bf16[160,256]{1,0:T(8,128)(2,1)S(1)}, bf16[160,256]{1,0:T(8,128)(2,1)S(1)}, u32[]{:S(2)}, u32[]{:S(2)}) collective-permute-start(bf16[160,256]{1,0:T(8,128)(2,1)S(1)} %reduce_sum.32.k0), channel_id=1, source_target_pairs={{0,16},{16,32},{32,48},{48,0},{1,17},{17,33},{33,49},{49,1},{2,18}... | collective-permute-start | bytes 245768 | tf_op jit(solution)/shard_map/ppermute | solution.py:235
  109.1 2.8 %copy-start.3 = (bf16[2,160,512]{2,1,0:T(8,128)(2,1)S(1)}, bf16[2,160,512]{2,1,0:T(8,128)(2,1)}, u32[]{:S(2)}) copy-start(bf16[2,160,512]{2,1,0:T(8,128)(2,1)} %copy-done.2) | copy-start | bytes 983044
  109.1 2.8 %copy-start.5 = (bf16[2,160,512]{2,1,0:T(8,128)(2,1)S(1)}, bf16[2,160,512]{2,1,0:T(8,128)(2,1)}, u32[]{:S(2)}) copy-start(bf16[2,160,512]{2,1,0:T(8,128)(2,1)} %copy-done.4) | copy-start | bytes 983044
  109.3 2.6 %collective-permute-start.24 = (bf16[4,160,768]{2,1,0:T(8,128)(2,1)S(1)}, bf16[4,160,768]{2,1,0:T(8,128)(2,1)S(1)}, u32[]{:S(2)}, u32[]{:S(2)}) collective-permute-start(bf16[4,160,768]{2,1,0:T(8,128)(2,1)S(1)} %pad_maximum_fusion), channel_id=1, source_target_pairs={{0,1},{1,0},{2,3},{3,2},{4,5},{5,4},{6,7},{7,6},{8,9},{9,8},{10,11... | collective-permute-start | bytes 2949128 | tf_op jit(solution)/shard_map/ppermute | solution.py:235

commit v9 on v8

--- a/solution.py
+++ b/solution.py
@@ -64,19 +64,26 @@
         q = qr[pl.ds(r0, RT), :]
         g = gr[pl.ds(r0, RT), :]
         posq = posq_ref[:, pl.ds(r0, RT)]
-        top = jnp.full((8, RT), masked_fill, f32)
-        total = jnp.zeros((8, RT), f32)
-        weighted = jnp.zeros((8, RT), f32)
-        for k0 in range(0, KHALF, KS):
-            score = masked_scores(kv[k0 : k0 + KS, :HEAD], q, posq, ordk_ref, block + k0 // HALF)
-            dprob = dot(kv[k0 : k0 + KS, HEAD:], g, NT)
+        def chunk(k0, carry):
+            top, total, weighted = carry
+            score = masked_scores(kv[pl.ds(k0, KS), :HEAD], q, posq, ordk_ref, block + k0 // HALF)
+            dprob = dot(kv[pl.ds(k0, KS), HEAD:], g, NT)
             score = score.reshape(KS // 8, 8, RT)
             new_top = jnp.maximum(top, jnp.max(score, axis=0))
             weights = jnp.exp2(score - new_top[None])
             factor = jnp.exp2(top - new_top)
             total = total * factor + jnp.sum(weights, axis=0)
             weighted = weighted * factor + jnp.sum(weights * dprob.reshape(KS // 8, 8, RT), axis=0)
-            top = new_top
+            return new_top, total, weighted
+
+        def chunks(i, carry):
+            for j in range(2):
+                carry = chunk(pl.multiple_of((i * 2 + j) * KS, KS), carry)
+            return carry
+
+        empty = jnp.zeros((8, RT), f32)
+        carry = (jnp.full((8, RT), masked_fill, f32), empty, empty)
+        top, total, weighted = lax.fori_loop(0, KHALF // (2 * KS), chunks, carry)
         row_top = jnp.max(top, axis=0, keepdims=True)
         if before is not None:
             row_top = jnp.maximum(row_top, before[0:1, pl.ds(r0, RT)])
@@ -105,64 +112,66 @@
     stats_pass(KHALF // HALF, ordk, posq, qr, gr, kvb, before, out)
 
 
-def combine_stats(stats, rowstat_ref):
-    for d in range(N_OUT):
-        parts = []
-        for e in range(N_OUT):
-            c0 = slot_start(d - e)
-            parts.append(stats[e][:, c0 : c0 + SLOT])
-        row_top = parts[0][0:1]
-        for part in parts[1:]:
-            row_top = jnp.maximum(row_top, part[0:1])
-        total = jnp.zeros_like(row_top)
-        weighted = jnp.zeros_like(row_top)
-        for part in parts:
-            factor = jnp.exp2(part[0:1] - row_top)
-            total = total + part[1:2] * factor
-            weighted = weighted + part[2:3] * factor
-        r0 = slot_start(d)
-        rowstat_ref[0:1, r0 : r0 + SLOT] = row_top + jnp.log2(total)
-        rowstat_ref[1:2, r0 : r0 + SLOT] = weighted / total
-
-
-def grads_kernel(
-    ordk, posq_ref, s0, s1, s2, s3, qr, gr, kva, kvb,
-    dq0, dq1, dq2, dq3, keep, send, rowstat, dqr, dkv,
-):
-    combine_stats((s0, s1, s2, s3), rowstat)
-    dkv[...] = jnp.zeros_like(dkv)
-
-    def row_tile(rt, _):
-        r0 = pl.multiple_of(rt * RT, RT)
-        q = qr[pl.ds(r0, RT), :]
-        g = gr[pl.ds(r0, RT), :]
-        posq = posq_ref[:, pl.ds(r0, RT)]
-        lse = rowstat[0:1, pl.ds(r0, RT)]
-        delta = rowstat[1:2, pl.ds(r0, RT)]
-        dq = jnp.zeros((RT, HEAD), f32)
-        for chunk in range(KEYS // KC):
-            kv = kva if chunk * KC < KHALF else kvb
-            k0 = chunk * KC % KHALF
-            key_rows = kv[k0 : k0 + KC, :HEAD]
-            score = masked_scores(key_rows, q, posq, ordk, chunk * (KC // HALF))
-            prob = jnp.exp2(score - lse)
-            dprob = dot(kv[k0 : k0 + KC, HEAD:], g, NT)
-            dscore = (prob * (dprob - delta)).astype(bf16)
-            prob_low = prob.astype(bf16)
-            dkv[chunk * KC : (chunk + 1) * KC, HEAD:] += dot(prob_low, g, NN)
-            dkv[chunk * KC : (chunk + 1) * KC, :HEAD] += dot(dscore, q, NN)
-            dq = dq + dot(dscore, key_rows, TN)
-        dqr[pl.ds(r0, RT), :] = dq
-        return 0
-
-    lax.fori_loop(0, ALL_ROWS // RT, row_tile, 0)
-    for d, out in enumerate((dq0, dq1, dq2, dq3)):
+def combined_stats(stats, d):
+    parts = []
+    for e in range(N_OUT):
+        c0 = slot_start(d - e)
+        parts.append(stats[e][:, c0 : c0 + SLOT])
+    row_top = parts[0][0:1]
+    for part in parts[1:]:
+        row_top = jnp.maximum(row_top, part[0:1])
+    total = jnp.zeros_like(row_top)
+    weighted = jnp.zeros_like(row_top)
+    for part in parts:
+        factor = jnp.exp2(part[0:1] - row_top)
+        total = total + part[1:2] * factor
+        weighted = weighted + part[2:3] * factor
+    return row_top + jnp.log2(total), weighted / total
+
+
+def grads_tile(slots, ordk, posq_ref, stats, qr, gr, kva, kvb, dqs, put):
+    r0 = slot_start(slots[0])
+    q = qr[r0 : r0 + RT, :]
+    g = gr[r0 : r0 + RT, :]
+    posq = posq_ref[:, r0 : r0 + RT]
+    pairs = [combined_stats(stats, d) for d in slots]
+    lse = jnp.concatenate([p[0] for p in pairs], axis=1)
+    delta = jnp.concatenate([p[1] for p in pairs], axis=1)
+    dq = jnp.zeros((RT, HEAD), f32)
+    for chunk in range(KEYS // KC):
+        kv = kva if chunk * KC < KHALF else kvb
+        k0 = chunk * KC % KHALF
+        key_rows = kv[k0 : k0 + KC, :HEAD]
+        score = masked_scores(key_rows, q, posq, ordk, chunk * (KC // HALF))
+        prob = jnp.exp2(score - lse)
+        dprob = dot(kv[k0 : k0 + KC, HEAD:], g, NT)
+        dscore = (prob * (dprob - delta)).astype(bf16)
+        prob_low = prob.astype(bf16)
+        put(chunk, dot(dscore, q, NN), dot(prob_low, g, NN))
+        dq = dq + dot(dscore, key_rows, TN)
+    for i, out in enumerate(dqs):
         for h in range(HEADS):
-            r0 = slot_start(d) + h * ROWS
-            out[:, h * HEAD : (h + 1) * HEAD] = (dqr[r0 : r0 + ROWS, :] * SCALE).astype(out.dtype)
-    for out, k0 in ((keep, 0), (send, KHALF)):
-        out[:, :HEAD] = (dkv[k0 : k0 + KHALF, :HEAD] * SCALE).astype(out.dtype)
-        out[:, HEAD:] = dkv[k0 : k0 + KHALF, HEAD:].astype(out.dtype)
+            rows = dq[i * SLOT + h * ROWS : i * SLOT + (h + 1) * ROWS, :] * SCALE
+            out[:, h * HEAD : (h + 1) * HEAD] = rows.astype(out.dtype)
+
+
+def grads_first(ordk, posq, s0, s1, s2, s3, qr, gr, kva, kvb, dq1, dq2, acc):
+    def put(chunk, dk, dv):
+        acc[chunk * KC : (chunk + 1) * KC, :HEAD] = dk
+        acc[chunk * KC : (chunk + 1) * KC, HEAD:] = dv
+
+    grads_tile((1, 2), ordk, posq, (s0, s1, s2, s3), qr, gr, kva, kvb, (dq1, dq2), put)
+
+
+def grads_second(ordk, posq, s0, s1, s2, s3, qr, gr, kva, kvb, acc, dq3, dq0, keep, send):
+    def put(chunk, dk, dv):
+        k0 = chunk * KC % KHALF
+        out = keep if chunk * KC < KHALF else send
+        before = acc[chunk * KC : (chunk + 1) * KC, :]
+        out[k0 : k0 + KC, :HEAD] = ((before[:, :HEAD] + dk) * SCALE).astype(out.dtype)
+        out[k0 : k0 + KC, HEAD:] = (before[:, HEAD:] + dv).astype(out.dtype)
+
+    grads_tile((3, 0), ordk, posq, (s0, s1, s2, s3), qr, gr, kva, kvb, (dq3, dq0), put)
 
 
 def columns_kernel(place_ref, own, other, x0, x1, x2, x3):
@@ -228,7 +237,6 @@
 
 
 WIDE = HEADS * HEAD
-acc_rows = ((ALL_ROWS, HEAD), f32)
 
 
 def shift(x, axis, d, n):
@@ -297,15 +305,21 @@
     all_stats = from_behind(stats, "outer", N_OUT)
 
     half = (KHALF, 2 * HEAD)
-    dq, dq1, dq2, dq3, keep, send = kernel_call(
-        grads_kernel, "grads",
-        [((ROWS, WIDE), f32)] + [((ROWS, WIDE), bf16)] * 3 + [(half, f32), (half, bf16)],
-        [((2, ALL_ROWS), f32), acc_rows, ((KEYS, 2 * HEAD), f32)],
-        cost(ALL_ROWS * KEYS, 5, 8 << 20), [smem], ordk, posq, *all_stats, qr, gr, kva, kvb,
+    low_rows = ((ROWS, WIDE), bf16)
+    pairs = cost(RT * KEYS, 5, 8 << 20)
+    dq1, dq2, acc = kernel_call(
+        grads_first, "grads_first", [low_rows, low_rows, ((KEYS, 2 * HEAD), f32)], [],
+        pairs, [smem], ordk, posq, *all_stats, qr, gr, kva, kvb,
+    )
+    dq1, dq2 = shift(dq1, "outer", -1, N_OUT), shift(dq2, "outer", -2, N_OUT)
+    dq3, dq, keep, send = kernel_call(
+        grads_second, "grads_second",
+        [low_rows, ((ROWS, WIDE), f32), (half, f32), (half, bf16)], [],
+        pairs, [smem], ordk, posq, *all_stats, qr, gr, kva, kvb, acc,
     )
     send, dq1, dq2, dq3, xs = lax.optimization_barrier((send, dq1, dq2, dq3, xs))
     got = shift(send, "core", 1, 2)
-    dq_parts = [shift(part, "outer", -d, N_OUT) for d, part in ((1, dq1), (2, dq2), (3, dq3))]
+    dq_parts = [dq1, dq2, shift(dq3, "outer", -3, N_OUT)]
     dkv = (keep + got.astype(f32)).astype(bf16).reshape(8, ROWS, 2 * HEAD)
     dkv = lax.all_to_all(dkv, ("x", "yh"), 0, 0, tiled=True)
     dkv = jnp.sum(dkv.astype(f32), axis=0).astype(bf16)

time: 133 us -> 137 us (1.030)
  waiting for transfers between devices: 23.5 us -> 26 us
  Pallas kernels: 38 us -> 40.4 us
    all_to_all x1, waiting for transfers between devices: 3.72 us -> 8.62 us  [per_device(): dkv = lax.all_to_all(dkv, ('x', 'yh'), 0, 0, tiled=True)]
    pallas_call x6 -> x7, Pallas kernels: 38 us -> 40.4 us  [kernel_call(): pl.pallas_call(body, out_shape=tuple((jax.ShapeDtypeStruct(*o) for o in o...]
    ppermute x25, waiting for transfers between devices: 17 us -> 14.7 us  [shift(): return lax.ppermute(x, axis, [(i, (i + d) % n) for i in range(n)])]
  transfers between devices with their start and end apart: 27 -> 27, of which waited for: 10 -> 9; matrix products, arithmetic and copies ran while one was open for 4% -> 3% of each run, Pallas kernels for 22% -> 23%
where the time goes in v9:
time: 137 us
  starting transfers between devices  42.2 us (31%)
  Pallas kernels  40.4 us (29%)
  waiting for transfers between devices  26 us (19%)
  blocking collectives  18.3 us (13%)
  matrix products  4.59 us (3%)
  other arithmetic  2.14 us (2%)
  local copies, waits for them, and re-layouts  1.92 us (1%)
    pallas_call x7, Pallas kernels, kernel_call(): pl.pallas_call(body, out_shape=tuple((jax.ShapeDtypeStruct(*o) for o in o...  40.4 us
    ppermute x25, starting transfers between devices, shift(): return lax.ppermute(x, axis, [(i, (i + d) % n) for i in range(n)])  30.6 us
    all_to_all x1, blocking collectives, per_device(): dw = lax.all_to_all(dw, ('dp', 'x', 'yh'), 0, 0, tiled=True)  18.3 us
    ppermute x25, waiting for transfers between devices, shift(): return lax.ppermute(x, axis, [(i, (i + d) % n) for i in range(n)])  14.7 us
    all_to_all x1, waiting for transfers between devices, per_device(): dkv = lax.all_to_all(dkv, ('x', 'yh'), 0, 0, tiled=True)  8.62 us
    all_to_all x1, starting transfers between devices, per_device(): lax.all_to_all(kva, ('x', 'yh'), 0, 0, tiled=True).reshape(KHALF, 2 * HEAD)  6.93 us
    all_to_all x1, starting transfers between devices, per_device(): dkv = lax.all_to_all(dkv, ('x', 'yh'), 0, 0, tiled=True)  4.64 us
    dot_general x3, matrix products, dot(): return lax.dot_general(a, b, dims, preferred_element_type=f32)  4.59 us
  transfers between devices with their start and end apart: 27, of which 9 were waited for; matrix products, arithmetic and copies ran while one was open for 3% of the time, Pallas kernels for 23%

profile of v9, /device:TPU:0, one launch (start us, length us, event | category | flops | bytes accessed | tf_op | source)
XLA Modules:
  0.0 136.5 jit_solution(9050372031873859885)
XLA Ops:
  0.7 3.6 %convolution_convert_fusion.q0 = bf16[160,512]{1,0:T(8,128)(2,1)S(1)} fusion(bf16[4096,512]{1,0:T(8,128)(2,1)} %param.13, bf16[1,160,4096]{2,1,0:T(8,128)(2,1)} %param.11), kind=kOutput, calls=%fused_computation.1 | convolution fusion | flops 671170560 | bytes 5668864 | tf_op jit(solution)/shard_map/dot_general | solution.py:36
  4.3 4.2 %collective-permute-start.2 = (bf16[160,512]{1,0:T(8,128)(2,1)S(1)}, bf16[160,512]{1,0:T(8,128)(2,1)S(1)}, u32[]{:S(2)}, u32[]{:S(2)}) collective-permute-start(bf16[160,512]{1,0:T(8,128)(2,1)S(1)} %convolution_convert_fusion.q0), channel_id=1, source_target_pairs={{0,48},{16,0},{32,16},{48,32},{1,49},{17,1},{33,17},{49,33},{2,50}... | collective-permute-start | bytes 491528 | tf_op jit(solution)/shard_map/ppermute | solution.py:243
  8.5 3.2 %collective-permute-start.4 = (bf16[160,512]{1,0:T(8,128)(2,1)S(1)}, bf16[160,512]{1,0:T(8,128)(2,1)}, u32[]{:S(2)}, u32[]{:S(2)}) collective-permute-start(bf16[160,512]{1,0:T(8,128)(2,1)S(1)} %bitcast.34), channel_id=1, source_target_pairs={{0,48},{16,0},{32,16},{48,32},{1,49},{17,1},{33,17},{49,33},{2,50}... | collective-permute-start | bytes 491528 | tf_op jit(solution)/shard_map/ppermute | solution.py:243
  11.7 0.5 convolution_convert_fusion.2
  12.2 0.5 convolution_convert_fusion.1
  12.8 0.9 broadcast_in_dim.47
  13.7 6.9 %all-to-all-start = ((bf16[8,160,256]{2,1,0:T(8,128)(2,1)}), bf16[8,160,256]{2,1,0:T(8,128)(2,1)S(1)}, u32[]{:S(2)}, u32[]{:S(2)}) async-start(bf16[8,160,256]{2,1,0:T(8,128)(2,1)} %broadcast_in_dim.47), calls=%async_computation | async-start | bytes 1310720 | tf_op jit(solution)/shard_map/all_to_all | solution.py:269
  21.0 3.3 %collective-permute-start.5 = (bf16[160,512]{1,0:T(8,128)(2,1)}, bf16[160,512]{1,0:T(8,128)(2,1)}, u32[]{:S(2)}, u32[]{:S(2)}) collective-permute-start(bf16[160,512]{1,0:T(8,128)(2,1)} %collective-permute-done.4.g3), channel_id=1, source_target_pairs={{0,48},{16,0},{32,16},{48,32},{1,49},{17,1},{33,17},{49,33},{2,50}... | collective-permute-start | bytes 491528 | tf_op jit(solution)/shard_map/ppermute | solution.py:243
  24.3 0.1 add.164
  24.4 0.2 select_reduce_fusion.1
  24.6 4.7 %collective-permute-done.1.q2 = bf16[160,512]{1,0:T(8,128)(2,1)} collective-permute-done((bf16[160,512]{1,0:T(8,128)(2,1)}, bf16[160,512]{1,0:T(8,128)(2,1)}, u32[]{:S(2)}, u32[]{:S(2)}) %collective-permute-start.1) | collective-permute-done | bytes 163872 | tf_op jit(solution)/shard_map/ppermute | solution.py:243
  29.3 2.7 %all-to-all-done = bf16[8,160,256]{2,1,0:T(8,128)(2,1)S(1)} async-done(((bf16[8,160,256]{2,1,0:T(8,128)(2,1)}), bf16[8,160,256]{2,1,0:T(8,128)(2,1)S(1)}, u32[]{:S(2)}, u32[]{:S(2)}) %all-to-all-start) | async-done | bytes 655392 | tf_op jit(solution)/shard_map/all_to_all | solution.py:269
  32.1 0.1 add.152
  32.3 0.1 reshape.101.posq
  32.5 0.2 select_reduce_fusion.ordk
  32.7 7.7 %stats_own.1 = (f32[3,2560]{1,0:T(4,128)S(1)}, bf16[2560,128]{1,0:T(8,128)(2,1)S(1)}, bf16[2560,128]{1,0:T(8,128)(2,1)S(1)}) custom-call(s32[32]{0:T(128)S(1)} %select_reduce_fusion.ordk, s32[1,2560]{1,0:T(1,128)S(1)} %reshape.101.posq, bf16[160,512]{1,0:T(8,128)(2,1)S(1)} %convolution_convert_fusion.q0, bf16[160,512]{1,0:T(8,128)(2,1)} %collective-permute-done.q1, ...), custom_call_target="tpu_custom_call" | custom-call | flops 1677721600 | bytes 4194304 | tf_op jit(solution)/shard_map/stats_own/pallas_call | solution.py:227
  40.4 7.4 %stats_other.1.s0 = f32[3,2560]{1,0:T(4,128)S(1)} custom-call(s32[32]{0:T(128)S(1)} %select_reduce_fusion.ordk, s32[1,2560]{1,0:T(1,128)S(1)} %reshape.101.posq, bf16[2560,128]{1,0:T(8,128)(2,1)S(1)} %get-tuple-element.56.qr, bf16[2560,128]{1,0:T(8,128)(2,1)S(1)} %get-tuple-element.57.gr, bf16[1280,256]{1,0:T(8,128)(2,1)} %collective-permute-done.7.kvb, ...), custom_call_target="tpu_custom_call" | custom-call | flops 1677721600 | bytes 4194304 | tf_op jit(solution)/shard_map/stats_other/pallas_call | solution.py:227
  47.9 3.3 %collective-permute-start.10 = (f32[3,2560]{1,0:T(4,128)S(1)}, f32[3,2560]{1,0:T(4,128)S(1)}, u32[]{:S(2)}, u32[]{:S(2)}) collective-permute-start(f32[3,2560]{1,0:T(4,128)S(1)} %stats_other.1.s0), channel_id=1, source_target_pairs={{0,48},{16,0},{32,16},{48,32},{1,49},{17,1},{33,17},{49,33},{2,50}... | collective-permute-start | bytes 92168 | tf_op jit(solution)/shard_map/ppermute | solution.py:243
  51.1 0.9 collective-permute-start.8
  52.1 2.2 %columns.1 = (bf16[2,160,512]{2,1,0:T(8,128)(2,1)S(1)}, bf16[2,160,512]{2,1,0:T(8,128)(2,1)S(1)}, bf16[2,160,512]{2,1,0:T(8,128)(2,1)S(1)}, bf16[2,160,512]{2,1,0:T(8,128)(2,1)S(1)}) custom-call(s32[2]{0:T(128)S(1)} %pad_add_fusion.place_ref, bf16[160,4096]{1,0:T(8,128)(2,1)S(1)} %bitcast.29, bf16[160,4096]{1,0:T(8,128)(2,1)} %collective-permute-done.6.other), custom_call_target="tpu_custom_call" | custom-call | flops 671088640 | bytes 5242880 | tf_op jit(solution)/shard_map/columns/pallas_call | solution.py:227
  54.3 2.6 %collective-permute-start.13 = (bf16[2,160,512]{2,1,0:T(8,128)(2,1)S(1)}, bf16[2,160,512]{2,1,0:T(8,128)(2,1)S(1)}, u32[]{:S(2)}, u32[]{:S(2)}) collective-permute-start(bf16[2,160,512]{2,1,0:T(8,128)(2,1)S(1)} %get-tuple-element.68), channel_id=1, source_target_pairs={{0,16},{16,32},{32,48},{48,0},{1,17},{17,33},{33,49},{49,1},{2,18}... | collective-permute-start | bytes 983048 | tf_op jit(solution)/shard_map/ppermute | solution.py:243
  56.9 1.2 collective-permute-start.14
  58.1 1.6 %collective-permute-start.15 = (bf16[2,160,512]{2,1,0:T(8,128)(2,1)S(1)}, bf16[2,160,512]{2,1,0:T(8,128)(2,1)S(1)}, u32[]{:S(2)}, u32[]{:S(2)}) collective-permute-start(bf16[2,160,512]{2,1,0:T(8,128)(2,1)S(1)} %get-tuple-element.70), channel_id=1, source_target_pairs={{0,48},{16,0},{32,16},{48,32},{1,49},{17,1},{33,17},{49,33},{2,50}... | collective-permute-start | bytes 983048 | tf_op jit(solution)/shard_map/ppermute | solution.py:243
  59.7 10.5 %grads_first.1 = (bf16[160,512]{1,0:T(8,128)(2,1)S(1)}, bf16[160,512]{1,0:T(8,128)(2,1)S(1)}, f32[2560,256]{1,0:T(8,128)S(1)}) custom-call(s32[32]{0:T(128)S(1)} %select_reduce_fusion.ordk, s32[1,2560]{1,0:T(1,128)S(1)} %reshape.101.posq, f32[3,2560]{1,0:T(4,128)S(1)} %stats_other.1.s0, f32[3,2560]{1,0:T(4,128)S(1)} %collective-permute-done.8.s1, ...), custom_call_target="tpu_custom_call" | custom-call | flops 4194304000 | bytes 8388608 | tf_op jit(solution)/shard_map/grads_first/pallas_call | solution.py:227
  70.1 1.4 %collective-permute-start.11 = (bf16[160,512]{1,0:T(8,128)(2,1)S(1)}, bf16[160,512]{1,0:T(8,128)(2,1)S(1)}, u32[]{:S(2)}, u32[]{:S(2)}) collective-permute-start(bf16[160,512]{1,0:T(8,128)(2,1)S(1)} %get-tuple-element.62), channel_id=1, source_target_pairs={{0,48},{16,0},{32,16},{48,32},{1,49},{17,1},{33,17},{49,33},{2,50}... | collective-permute-start | bytes 491528 | tf_op jit(solution)/shard_map/ppermute | solution.py:243
  71.5 1.2 collective-permute-start.12
  72.8 10.7 %grads_second.1 = (bf16[160,512]{1,0:T(8,128)(2,1)S(1)}, f32[160,512]{1,0:T(8,128)S(1)}, f32[1280,256]{1,0:T(8,128)S(1)}, bf16[1280,256]{1,0:T(8,128)(2,1)S(1)}) custom-call(s32[32]{0:T(128)S(1)} %select_reduce_fusion.ordk, s32[1,2560]{1,0:T(1,128)S(1)} %reshape.101.posq, f32[3,2560]{1,0:T(4,128)S(1)} %stats_other.1.s0, ...), custom_call_target="tpu_custom_call" | custom-call | flops 4194304000 | bytes 8388608 | tf_op jit(solution)/shard_map/grads_second/pallas_call | solution.py:227
  83.5 0.6 copy-done.8
  84.1 2.1 %collective-permute-done.20 = bf16[1280,256]{1,0:T(8,128)(2,1)S(1)} collective-permute-done((bf16[1280,256]{1,0:T(8,128)(2,1)S(1)}, bf16[1280,256]{1,0:T(8,128)(2,1)S(1)}, u32[]{:S(2)}, u32[]{:S(2)}) %collective-permute-start.20) | collective-permute-done | bytes 655392 | tf_op jit(solution)/shard_map/ppermute | solution.py:243
  86.2 1.0 add_convert_fusion
  87.2 4.6 %all-to-all-start.1 = ((bf16[8,160,256]{2,1,0:T(8,128)(2,1)}), bf16[8,160,256]{2,1,0:T(8,128)(2,1)S(1)}, u32[]{:S(2)}, u32[]{:S(2)}) async-start(bf16[8,160,256]{2,1,0:T(8,128)(2,1)} %bitcast.8), calls=%async_computation.1 | async-start | bytes 1310720 | tf_op jit(solution)/shard_map/all_to_all | solution.py:324
  92.0 2.0 %collective-permute-start.19 = (bf16[160,512]{1,0:T(8,128)(2,1)S(1)}, bf16[160,512]{1,0:T(8,128)(2,1)S(1)}, u32[]{:S(2)}, u32[]{:S(2)}) collective-permute-start(bf16[160,512]{1,0:T(8,128)(2,1)S(1)} %add_convert_fusion.1.q0), channel_id=1, source_target_pairs={{0,48},{16,0},{32,16},{48,32},{1,49},{17,1},{33,17},{49,33},{2,50}... | collective-permute-start | bytes 491528 | tf_op jit(solution)/shard_map/ppermute | solution.py:243
  94.0 0.3 collective-permute-start.18
  94.3 1.3 collective-permute-start.17
  95.6 8.6 %all-to-all-done.1 = bf16[8,160,256]{2,1,0:T(8,128)(2,1)S(1)} async-done(((bf16[8,160,256]{2,1,0:T(8,128)(2,1)}), bf16[8,160,256]{2,1,0:T(8,128)(2,1)S(1)}, u32[]{:S(2)}, u32[]{:S(2)}) %all-to-all-start.1) | async-done | bytes 655392 | tf_op jit(solution)/shard_map/all_to_all | solution.py:324
  104.2 0.1 reduce_sum.32.k0
  104.3 2.3 %collective-permute-start.23 = (bf16[160,256]{1,0:T(8,128)(2,1)S(1)}, bf16[160,256]{1,0:T(8,128)(2,1)S(1)}, u32[]{:S(2)}, u32[]{:S(2)}) collective-permute-start(bf16[160,256]{1,0:T(8,128)(2,1)S(1)} %reduce_sum.32.k0), channel_id=1, source_target_pairs={{0,48},{16,0},{32,16},{48,32},{1,49},{17,1},{33,17},{49,33},{2,50}... | collective-permute-start | bytes 245768 | tf_op jit(solution)/shard_map/ppermute | solution.py:243
  106.6 0.3 collective-permute-start.22
  106.9 1.3 collective-permute-start.21
  108.2 1.3 collective-permute-done.23.k3
  109.6 3.1 %collective-permute-done.22.k2 = bf16[160,256]{1,0:T(8,128)(2,1)S(1)} collective-permute-done((bf16[160,256]{1,0:T(8,128)(2,1)S(1)}, bf16[160,256]{1,0:T(8,128)(2,1)S(1)}, u32[]{:S(2)}, u32[]{:S(2)}) %collective-permute-start.22) | collective-permute-done | bytes 81952 | tf_op jit(solution)/shard_map/ppermute | solution.py:243
  112.6 0.8 collective-permute-done.21.k1
  113.5 0.1 pad_maximum_fusion
  113.7 0.1 collective-permute-start.24
  113.7 2.6 %collective-permute-done.24.grads = bf16[4,160,768]{2,1,0:T(8,128)(2,1)S(1)} collective-permute-done((bf16[4,160,768]{2,1,0:T(8,128)(2,1)S(1)}, bf16[4,160,768]{2,1,0:T(8,128)(2,1)S(1)}, u32[]{:S(2)}, u32[]{:S(2)}) %collective-permute-start.24) | collective-permute-done | bytes 983072 | tf_op jit(solution)/shard_map/ppermute | solution.py:243
  116.3 1.2 weights.1
  117.5 18.3 %all_to_all.15.parts = bf16[16,32,768]{2,1,0:T(8,128)(2,1)S(1)} all-to-all(bf16[16,32,768]{2,1,0:T(8,128)(2,1)S(1)} %weights.1), channel_id=1, replica_groups=mesh['dp'=2,'outer'=4,'x'=4,'yh'=2,'core'=2] {'dp','x','yh'}, dimensions={0} | all-to-all | bytes 1572864 | tf_op jit(solution)/shard_map/all_to_all | solution.py:340
  135.8 0.7 last_sum.1
  (69 shorter events, 0.9 us)
Async XLA Ops:
  0.6 11.1 %copy-start = (bf16[4096,128]{1,0:T(8,128)(2,1)S(1)}, bf16[4096,128]{1,0:T(8,128)(2,1)}, u32[]{:S(2)}) copy-start(bf16[4096,128]{1,0:T(8,128)(2,1)} %param.14) | copy-start | bytes 3145732
  0.6 11.1 %copy-start.1 = (bf16[1,160,4096]{2,1,0:T(8,128)(2,1)S(1)}, bf16[1,160,4096]{2,1,0:T(8,128)(2,1)}, u32[]{:S(2)}) copy-start(bf16[1,160,4096]{2,1,0:T(8,128)(2,1)} %param.11) | copy-start | bytes 3932164
  0.7 7.8 %copy-start.6 = (bf16[1,160,512]{2,1,0:T(8,128)(2,1)S(1)}, bf16[1,160,512]{2,1,0:T(8,128)(2,1)}, u32[]{:S(2)}) copy-start(bf16[1,160,512]{2,1,0:T(8,128)(2,1)} %param.16) | copy-start | bytes 491524
  4.3 8.0 %copy-start.7 = (bf16[4096,128]{1,0:T(8,128)(2,1)S(1)}, bf16[4096,128]{1,0:T(8,128)(2,1)}, u32[]{:S(2)}) copy-start(bf16[4096,128]{1,0:T(8,128)(2,1)} %param.15) | copy-start | bytes 3145732
  4.3 20.3 %collective-permute-start.2 = (bf16[160,512]{1,0:T(8,128)(2,1)S(1)}, bf16[160,512]{1,0:T(8,128)(2,1)S(1)}, u32[]{:S(2)}, u32[]{:S(2)}) collective-permute-start(bf16[160,512]{1,0:T(8,128)(2,1)S(1)} %convolution_convert_fusion.q0), channel_id=1, source_target_pairs={{0,48},{16,0},{32,16},{48,32},{1,49},{17,1},{33,17},{49,33},{2,50}... | collective-permute-start | bytes 491528 | tf_op jit(solution)/shard_map/ppermute | solution.py:243
  8.5 12.4 %collective-permute-start = (bf16[160,512]{1,0:T(8,128)(2,1)S(1)}, bf16[160,512]{1,0:T(8,128)(2,1)}, u32[]{:S(2)}, u32[]{:S(2)}) collective-permute-start(bf16[160,512]{1,0:T(8,128)(2,1)S(1)} %convolution_convert_fusion.q0), channel_id=1, source_target_pairs={{0,16},{16,32},{32,48},{48,0},{1,17},{17,33},{33,49},{49,1},{2,18}... | collective-permute-start | bytes 491528 | tf_op jit(solution)/shard_map/ppermute | solution.py:243
  8.5 12.5 %collective-permute-start.4 = (bf16[160,512]{1,0:T(8,128)(2,1)S(1)}, bf16[160,512]{1,0:T(8,128)(2,1)}, u32[]{:S(2)}, u32[]{:S(2)}) collective-permute-start(bf16[160,512]{1,0:T(8,128)(2,1)S(1)} %bitcast.34), channel_id=1, source_target_pairs={{0,48},{16,0},{32,16},{48,32},{1,49},{17,1},{33,17},{49,33},{2,50}... | collective-permute-start | bytes 491528 | tf_op jit(solution)/shard_map/ppermute | solution.py:243
  11.7 12.9 %collective-permute-start.3 = (bf16[160,512]{1,0:T(8,128)(2,1)S(1)}, bf16[160,512]{1,0:T(8,128)(2,1)}, u32[]{:S(2)}, u32[]{:S(2)}) collective-permute-start(bf16[160,512]{1,0:T(8,128)(2,1)S(1)} %bitcast.35), channel_id=1, source_target_pairs={{0,16},{16,32},{32,48},{48,0},{1,17},{17,33},{33,49},{49,1},{2,18}... | collective-permute-start | bytes 491528 | tf_op jit(solution)/shard_map/ppermute | solution.py:243
  12.7 7.9 %copy-start.13 = (s32[1,8,1]{1,2,0:T(1,128)S(1)}, s32[1,8,1]{1,2,0:T(1,128)}, u32[]{:S(2)}) copy-start(s32[1,8,1]{1,2,0:T(1,128)} %constant.67.clone) | copy-start | bytes 100
  12.8 7.9 %copy-start.12 = (s32[2,1,1]{0,2,1:T(1,128)S(1)}, s32[2,1,1]{0,2,1:T(1,128)}, u32[]{:S(2)}) copy-start(s32[2,1,1]{0,2,1:T(1,128)} %constant.68.clone) | copy-start | bytes 28
  12.8 8.1 %copy-start.10 = (s32[4]{0:T(128)S(1)}, s32[4]{0:T(128)}, u32[]{:S(2)}) copy-start(s32[4]{0:T(128)} %constant.76) | copy-start | bytes 52
  12.8 11.6 %copy-start.11 = (s32[1,128]{1,0:T(1,128)S(1)}, s32[1,128]{1,0:T(1,128)}, u32[]{:S(2)}) copy-start(s32[1,128]{1,0:T(1,128)} %param.12) | copy-start | bytes 1540
  13.7 18.3 %all-to-all-start = ((bf16[8,160,256]{2,1,0:T(8,128)(2,1)}), bf16[8,160,256]{2,1,0:T(8,128)(2,1)S(1)}, u32[]{:S(2)}, u32[]{:S(2)}) async-start(bf16[8,160,256]{2,1,0:T(8,128)(2,1)} %broadcast_in_dim.47), calls=%async_computation | async-start | bytes 1310720 | tf_op jit(solution)/shard_map/all_to_all | solution.py:269
  20.6 11.4 %collective-permute-start.6 = (bf16[160,4096]{1,0:T(8,128)(2,1)S(1)}, bf16[160,4096]{1,0:T(8,128)(2,1)}, u32[]{:S(2)}, u32[]{:S(2)}) collective-permute-start(bf16[160,4096]{1,0:T(8,128)(2,1)S(1)} %bitcast.28), channel_id=1, source_target_pairs={{0,1},{1,0},{2,3},{3,2},{4,5},{5,4},{6,7},{7,6},{8,9},{9,8},{10,11... | collective-permute-start | bytes 3932168 | tf_op jit(solution)/shard_map/ppermute | solution.py:243
  20.9 8.4 %collective-permute-start.1 = (bf16[160,512]{1,0:T(8,128)(2,1)}, bf16[160,512]{1,0:T(8,128)(2,1)}, u32[]{:S(2)}, u32[]{:S(2)}) collective-permute-start(bf16[160,512]{1,0:T(8,128)(2,1)} %collective-permute-done.q1), channel_id=1, source_target_pairs={{0,16},{16,32},{32,48},{48,0},{1,17},{17,33},{33,49},{49,1},{2,18}... | collective-permute-start | bytes 491528 | tf_op jit(solution)/shard_map/ppermute | solution.py:243
  21.0 8.4 %collective-permute-start.5 = (bf16[160,512]{1,0:T(8,128)(2,1)}, bf16[160,512]{1,0:T(8,128)(2,1)}, u32[]{:S(2)}, u32[]{:S(2)}) collective-permute-start(bf16[160,512]{1,0:T(8,128)(2,1)} %collective-permute-done.4.g3), channel_id=1, source_target_pairs={{0,48},{16,0},{32,16},{48,32},{1,49},{17,1},{33,17},{49,33},{2,50}... | collective-permute-start | bytes 491528 | tf_op jit(solution)/shard_map/ppermute | solution.py:243
  32.0 8.4 %collective-permute-start.7 = (bf16[1280,256]{1,0:T(8,128)(2,1)S(1)}, bf16[1280,256]{1,0:T(8,128)(2,1)}, u32[]{:S(2)}, u32[]{:S(2)}) collective-permute-start(bf16[1280,256]{1,0:T(8,128)(2,1)S(1)} %bitcast.30), channel_id=1, source_target_pairs={{0,1},{1,0},{2,3},{3,2},{4,5},{5,4},{6,7},{7,6},{8,9},{9,8},{10,11... | collective-permute-start | bytes 1966088 | tf_op jit(solution)/shard_map/ppermute | solution.py:243
  47.9 10.3 %collective-permute-start.10 = (f32[3,2560]{1,0:T(4,128)S(1)}, f32[3,2560]{1,0:T(4,128)S(1)}, u32[]{:S(2)}, u32[]{:S(2)}) collective-permute-start(f32[3,2560]{1,0:T(4,128)S(1)} %stats_other.1.s0), channel_id=1, source_target_pairs={{0,48},{16,0},{32,16},{48,32},{1,49},{17,1},{33,17},{49,33},{2,50}... | collective-permute-start | bytes 92168 | tf_op jit(solution)/shard_map/ppermute | solution.py:243
  51.1 8.5 %collective-permute-start.9 = (f32[3,2560]{1,0:T(4,128)S(1)}, f32[3,2560]{1,0:T(4,128)S(1)}, u32[]{:S(2)}, u32[]{:S(2)}) collective-permute-start(f32[3,2560]{1,0:T(4,128)S(1)} %stats_other.1.s0), channel_id=1, source_target_pairs={{0,32},{16,48},{32,0},{48,16},{1,33},{17,49},{33,1},{49,17},{2,34}... | collective-permute-start | bytes 92168 | tf_op jit(solution)/shard_map/ppermute | solution.py:243
  51.1 8.5 %collective-permute-start.8 = (f32[3,2560]{1,0:T(4,128)S(1)}, f32[3,2560]{1,0:T(4,128)S(1)}, u32[]{:S(2)}, u32[]{:S(2)}) collective-permute-start(f32[3,2560]{1,0:T(4,128)S(1)} %stats_other.1.s0), channel_id=1, source_target_pairs={{0,16},{16,32},{32,48},{48,0},{1,17},{17,33},{33,49},{49,1},{2,18}... | collective-permute-start | bytes 92168 | tf_op jit(solution)/shard_map/ppermute | solution.py:243
  54.3 29.2 %collective-permute-start.13 = (bf16[2,160,512]{2,1,0:T(8,128)(2,1)S(1)}, bf16[2,160,512]{2,1,0:T(8,128)(2,1)S(1)}, u32[]{:S(2)}, u32[]{:S(2)}) collective-permute-start(bf16[2,160,512]{2,1,0:T(8,128)(2,1)S(1)} %get-tuple-element.68), channel_id=1, source_target_pairs={{0,16},{16,32},{32,48},{48,0},{1,17},{17,33},{33,49},{49,1},{2,18}... | collective-permute-start | bytes 983048 | tf_op jit(solution)/shard_map/ppermute | solution.py:243
  56.9 26.6 %collective-permute-start.14 = (bf16[2,160,512]{2,1,0:T(8,128)(2,1)S(1)}, bf16[2,160,512]{2,1,0:T(8,128)(2,1)S(1)}, u32[]{:S(2)}, u32[]{:S(2)}) collective-permute-start(bf16[2,160,512]{2,1,0:T(8,128)(2,1)S(1)} %get-tuple-element.69), channel_id=1, source_target_pairs={{0,32},{16,48},{32,0},{48,16},{1,33},{17,49},{33,1},{49,17},{2,34}... | collective-permute-start | bytes 983048 | tf_op jit(solution)/shard_map/ppermute | solution.py:243
  58.1 25.4 %collective-permute-start.15 = (bf16[2,160,512]{2,1,0:T(8,128)(2,1)S(1)}, bf16[2,160,512]{2,1,0:T(8,128)(2,1)S(1)}, u32[]{:S(2)}, u32[]{:S(2)}) collective-permute-start(bf16[2,160,512]{2,1,0:T(8,128)(2,1)S(1)} %get-tuple-element.70), channel_id=1, source_target_pairs={{0,48},{16,0},{32,16},{48,32},{1,49},{17,1},{33,17},{49,33},{2,50}... | collective-permute-start | bytes 983048 | tf_op jit(solution)/shard_map/ppermute | solution.py:243
  70.1 13.3 %collective-permute-start.11 = (bf16[160,512]{1,0:T(8,128)(2,1)S(1)}, bf16[160,512]{1,0:T(8,128)(2,1)S(1)}, u32[]{:S(2)}, u32[]{:S(2)}) collective-permute-start(bf16[160,512]{1,0:T(8,128)(2,1)S(1)} %get-tuple-element.62), channel_id=1, source_target_pairs={{0,48},{16,0},{32,16},{48,32},{1,49},{17,1},{33,17},{49,33},{2,50}... | collective-permute-start | bytes 491528 | tf_op jit(solution)/shard_map/ppermute | solution.py:243
  71.5 11.9 %collective-permute-start.12 = (bf16[160,512]{1,0:T(8,128)(2,1)S(1)}, bf16[160,512]{1,0:T(8,128)(2,1)S(1)}, u32[]{:S(2)}, u32[]{:S(2)}) collective-permute-start(bf16[160,512]{1,0:T(8,128)(2,1)S(1)} %get-tuple-element.63), channel_id=1, source_target_pairs={{0,32},{16,48},{32,0},{48,16},{1,33},{17,49},{33,1},{49,17},{2,34}... | collective-permute-start | bytes 491528 | tf_op jit(solution)/shard_map/ppermute | solution.py:243
  83.4 0.7 copy-start.8
  83.5 3.7 %copy-start.2 = (bf16[2,160,512]{2,1,0:T(8,128)(2,1)}, bf16[2,160,512]{2,1,0:T(8,128)(2,1)S(1)}, u32[]{:S(2)}) copy-start(bf16[2,160,512]{2,1,0:T(8,128)(2,1)S(1)} %collective-permute-done.14.x2) | copy-start | bytes 983044
  83.5 3.7 %copy-start.4 = (bf16[2,160,512]{2,1,0:T(8,128)(2,1)}, bf16[2,160,512]{2,1,0:T(8,128)(2,1)S(1)}, u32[]{:S(2)}) copy-start(bf16[2,160,512]{2,1,0:T(8,128)(2,1)S(1)} %collective-permute-done.15.x3) | copy-start | bytes 983044
  84.1 2.1 %collective-permute-start.20 = (bf16[1280,256]{1,0:T(8,128)(2,1)S(1)}, bf16[1280,256]{1,0:T(8,128)(2,1)S(1)}, u32[]{:S(2)}, u32[]{:S(2)}) collective-permute-start(bf16[1280,256]{1,0:T(8,128)(2,1)S(1)} %get-tuple-element.80), channel_id=1, source_target_pairs={{0,1},{1,0},{2,3},{3,2},{4,5},{5,4},{6,7},{7,6},{8,9},{9,8},{10,11... | collective-permute-start | bytes 1966088 | tf_op jit(solution)/shard_map/ppermute | solution.py:243
  84.1 7.8 %collective-permute-start.16 = (bf16[160,512]{1,0:T(8,128)(2,1)S(1)}, bf16[160,512]{1,0:T(8,128)(2,1)S(1)}, u32[]{:S(2)}, u32[]{:S(2)}) collective-permute-start(bf16[160,512]{1,0:T(8,128)(2,1)S(1)} %get-tuple-element.78), channel_id=1, source_target_pairs={{0,16},{16,32},{32,48},{48,0},{1,17},{17,33},{33,49},{49,1},{2,18}... | collective-permute-start | bytes 491528 | tf_op jit(solution)/shard_map/ppermute | solution.py:243
  87.2 4.7 %copy-start.9 = (bf16[160,512]{1,0:T(8,128)(2,1)S(1)}, bf16[160,512]{1,0:T(8,128)(2,1)}, u32[]{:S(2)}) copy-start(bf16[160,512]{1,0:T(8,128)(2,1)} %copy-done.8) | copy-start | bytes 491524
  87.2 17.0 %all-to-all-start.1 = ((bf16[8,160,256]{2,1,0:T(8,128)(2,1)}), bf16[8,160,256]{2,1,0:T(8,128)(2,1)S(1)}, u32[]{:S(2)}, u32[]{:S(2)}) async-start(bf16[8,160,256]{2,1,0:T(8,128)(2,1)} %bitcast.8), calls=%async_computation.1 | async-start | bytes 1310720 | tf_op jit(solution)/shard_map/all_to_all | solution.py:324
  92.0 14.9 %collective-permute-start.19 = (bf16[160,512]{1,0:T(8,128)(2,1)S(1)}, bf16[160,512]{1,0:T(8,128)(2,1)S(1)}, u32[]{:S(2)}, u32[]{:S(2)}) collective-permute-start(bf16[160,512]{1,0:T(8,128)(2,1)S(1)} %add_convert_fusion.1.q0), channel_id=1, source_target_pairs={{0,48},{16,0},{32,16},{48,32},{1,49},{17,1},{33,17},{49,33},{2,50}... | collective-permute-start | bytes 491528 | tf_op jit(solution)/shard_map/ppermute | solution.py:243
  94.0 14.2 %collective-permute-start.18 = (bf16[160,512]{1,0:T(8,128)(2,1)S(1)}, bf16[160,512]{1,0:T(8,128)(2,1)S(1)}, u32[]{:S(2)}, u32[]{:S(2)}) collective-permute-start(bf16[160,512]{1,0:T(8,128)(2,1)S(1)} %add_convert_fusion.1.q0), channel_id=1, source_target_pairs={{0,32},{16,48},{32,0},{48,16},{1,33},{17,49},{33,1},{49,17},{2,34}... | collective-permute-start | bytes 491528 | tf_op jit(solution)/shard_map/ppermute | solution.py:243
  94.3 14.0 %collective-permute-start.17 = (bf16[160,512]{1,0:T(8,128)(2,1)S(1)}, bf16[160,512]{1,0:T(8,128)(2,1)S(1)}, u32[]{:S(2)}, u32[]{:S(2)}) collective-permute-start(bf16[160,512]{1,0:T(8,128)(2,1)S(1)} %add_convert_fusion.1.q0), channel_id=1, source_target_pairs={{0,16},{16,32},{32,48},{48,0},{1,17},{17,33},{33,49},{49,1},{2,18}... | collective-permute-start | bytes 491528 | tf_op jit(solution)/shard_map/ppermute | solution.py:243
  104.3 5.2 %collective-permute-start.23 = (bf16[160,256]{1,0:T(8,128)(2,1)S(1)}, bf16[160,256]{1,0:T(8,128)(2,1)S(1)}, u32[]{:S(2)}, u32[]{:S(2)}) collective-permute-start(bf16[160,256]{1,0:T(8,128)(2,1)S(1)} %reduce_sum.32.k0), channel_id=1, source_target_pairs={{0,48},{16,0},{32,16},{48,32},{1,49},{17,1},{33,17},{49,33},{2,50}... | collective-permute-start | bytes 245768 | tf_op jit(solution)/shard_map/ppermute | solution.py:243
  106.6 6.0 %collective-permute-start.22 = (bf16[160,256]{1,0:T(8,128)(2,1)S(1)}, bf16[160,256]{1,0:T(8,128)(2,1)S(1)}, u32[]{:S(2)}, u32[]{:S(2)}) collective-permute-start(bf16[160,256]{1,0:T(8,128)(2,1)S(1)} %reduce_sum.32.k0), channel_id=1, source_target_pairs={{0,32},{16,48},{32,0},{48,16},{1,33},{17,49},{33,1},{49,17},{2,34}... | collective-permute-start | bytes 245768 | tf_op jit(solution)/shard_map/ppermute | solution.py:243
  106.9 6.5 %collective-permute-start.21 = (bf16[160,256]{1,0:T(8,128)(2,1)S(1)}, bf16[160,256]{1,0:T(8,128)(2,1)S(1)}, u32[]{:S(2)}, u32[]{:S(2)}) collective-permute-start(bf16[160,256]{1,0:T(8,128)(2,1)S(1)} %reduce_sum.32.k0), channel_id=1, source_target_pairs={{0,16},{16,32},{32,48},{48,0},{1,17},{17,33},{33,49},{49,1},{2,18}... | collective-permute-start | bytes 245768 | tf_op jit(solution)/shard_map/ppermute | solution.py:243
  113.5 2.8 %copy-start.3 = (bf16[2,160,512]{2,1,0:T(8,128)(2,1)S(1)}, bf16[2,160,512]{2,1,0:T(8,128)(2,1)}, u32[]{:S(2)}) copy-start(bf16[2,160,512]{2,1,0:T(8,128)(2,1)} %copy-done.2) | copy-start | bytes 983044
  113.5 2.8 %copy-start.5 = (bf16[2,160,512]{2,1,0:T(8,128)(2,1)S(1)}, bf16[2,160,512]{2,1,0:T(8,128)(2,1)}, u32[]{:S(2)}) copy-start(bf16[2,160,512]{2,1,0:T(8,128)(2,1)} %copy-done.4) | copy-start | bytes 983044
  113.7 2.6 %collective-permute-start.24 = (bf16[4,160,768]{2,1,0:T(8,128)(2,1)S(1)}, bf16[4,160,768]{2,1,0:T(8,128)(2,1)S(1)}, u32[]{:S(2)}, u32[]{:S(2)}) collective-permute-start(bf16[4,160,768]{2,1,0:T(8,128)(2,1)S(1)} %pad_maximum_fusion), channel_id=1, source_target_pairs={{0,1},{1,0},{2,3},{3,2},{4,5},{5,4},{6,7},{7,6},{8,9},{9,8},{10,11... | collective-permute-start | bytes 2949128 | tf_op jit(solution)/shard_map/ppermute | solution.py:243

commit v10 on v8

--- a/solution.py
+++ b/solution.py
@@ -257,11 +257,12 @@
         ],
         axis=1,
     )
-    kva = jnp.broadcast_to(kv[None], (8,) + kv.shape)
-    kva = lax.all_to_all(kva, ("x", "yh"), 0, 0, tiled=True).reshape(KHALF, 2 * HEAD)
     other_tokens = shift(tokens, "core", 1, 2)
     later = tokens
-    kva, qs, gs, other_tokens = lax.optimization_barrier((kva, qs, gs, other_tokens))
+    kva = jnp.broadcast_to(kv[None], (8,) + kv.shape)
+    kva, other_tokens = lax.optimization_barrier((kva, other_tokens))
+    kva = lax.all_to_all(kva, ("x", "yh"), 0, 0, tiled=True).reshape(KHALF, 2 * HEAD)
+    kva, qs, gs = lax.optimization_barrier((kva, qs, gs))
     kvb = shift(kva, "core", 1, 2)
 
     key_dev = (o * 8 + np.arange(8)[None, :, None]) * 2 + (ic + np.arange(2)[:, None, None]) % 2

time: 133 us -> 135 us (1.015)
  waiting for transfers between devices: 23.5 us -> 25.7 us
    all_to_all x1, waiting for transfers between devices: 2.72 us -> 4.42 us  [per_device(): lax.all_to_all(kva, ('x', 'yh'), 0, 0, tiled=True).reshape(KHALF, 2 * HEAD)]
  transfers between devices with their start and end apart: 27 -> 27, of which waited for: 10 -> 11; matrix products, arithmetic and copies ran while one was open for 4% -> 4% of each run, Pallas kernels for 22% -> 22%
where the time goes in v10:
time: 135 us; the launch traced here: 134 us
  starting transfers between devices  41.6 us (31%)
  Pallas kernels  38 us (28%)
  waiting for transfers between devices  25.7 us (19%)
  blocking collectives  18.2 us (13%)
  matrix products  4.59 us (3%)
  other arithmetic  3.28 us (2%)
  local copies, waits for them, and re-layouts  2.13 us (2%)
    pallas_call x6, Pallas kernels, kernel_call(): pl.pallas_call(body, out_shape=tuple((jax.ShapeDtypeStruct(*o) for o in o...  38 us
    ppermute x25, starting transfers between devices, shift(): return lax.ppermute(x, axis, [(i, (i + d) % n) for i in range(n)])  31 us
    ppermute x25, waiting for transfers between devices, shift(): return lax.ppermute(x, axis, [(i, (i + d) % n) for i in range(n)])  18.3 us
    all_to_all x1, blocking collectives, per_device(): dw = lax.all_to_all(dw, ('dp', 'x', 'yh'), 0, 0, tiled=True)  18.2 us
    all_to_all x1, starting transfers between devices, per_device(): lax.all_to_all(kva, ('x', 'yh'), 0, 0, tiled=True).reshape(KHALF, 2 * HEAD)  6.93 us
    dot_general x3, matrix products, dot(): return lax.dot_general(a, b, dims, preferred_element_type=f32)  4.59 us
    all_to_all x1, waiting for transfers between devices, per_device(): lax.all_to_all(kva, ('x', 'yh'), 0, 0, tiled=True).reshape(KHALF, 2 * HEAD)  4.42 us
    all_to_all x1, starting transfers between devices, per_device(): dkv = lax.all_to_all(dkv, ('x', 'yh'), 0, 0, tiled=True)  3.66 us
  transfers between devices with their start and end apart: 27, of which 11 were waited for; matrix products, arithmetic and copies ran while one was open for 4% of the time, Pallas kernels for 22%

profile of v10, /device:TPU:0, one launch (start us, length us, event | category | flops | bytes accessed | tf_op | source)
XLA Modules:
  0.0 134.4 jit_solution(10312673519736443026)
XLA Ops:
  0.7 3.6 %convolution_convert_fusion.q0 = bf16[160,512]{1,0:T(8,128)(2,1)S(1)} fusion(bf16[4096,512]{1,0:T(8,128)(2,1)} %param.13, bf16[1,160,4096]{2,1,0:T(8,128)(2,1)} %param.11), kind=kOutput, calls=%fused_computation.1 | convolution fusion | flops 671170560 | bytes 5668864 | tf_op jit(solution)/shard_map/dot_general | solution.py:36
  4.3 4.2 %collective-permute-start.3 = (bf16[160,512]{1,0:T(8,128)(2,1)S(1)}, bf16[160,512]{1,0:T(8,128)(2,1)S(1)}, u32[]{:S(2)}, u32[]{:S(2)}) collective-permute-start(bf16[160,512]{1,0:T(8,128)(2,1)S(1)} %convolution_convert_fusion.q0), channel_id=1, source_target_pairs={{0,48},{16,0},{32,16},{48,32},{1,49},{17,1},{33,17},{49,33},{2,50}... | collective-permute-start | bytes 491528 | tf_op jit(solution)/shard_map/ppermute | solution.py:235
  8.5 3.2 %collective-permute-start.5 = (bf16[160,512]{1,0:T(8,128)(2,1)S(1)}, bf16[160,512]{1,0:T(8,128)(2,1)}, u32[]{:S(2)}, u32[]{:S(2)}) collective-permute-start(bf16[160,512]{1,0:T(8,128)(2,1)S(1)} %bitcast.33), channel_id=1, source_target_pairs={{0,48},{16,0},{32,16},{48,32},{1,49},{17,1},{33,17},{49,33},{2,50}... | collective-permute-start | bytes 491528 | tf_op jit(solution)/shard_map/ppermute | solution.py:235
  11.7 0.5 convolution_convert_fusion.2
  12.2 0.7 copy-done.7
  13.0 0.5 convolution_convert_fusion.1
  13.7 1.2 collective-permute-done.other
  14.9 0.9 broadcast_in_dim.47
  15.7 6.9 %all-to-all-start = ((bf16[8,160,256]{2,1,0:T(8,128)(2,1)}), bf16[8,160,256]{2,1,0:T(8,128)(2,1)S(1)}, u32[]{:S(2)}, u32[]{:S(2)}) async-start(bf16[8,160,256]{2,1,0:T(8,128)(2,1)} %broadcast_in_dim.47), calls=%async_computation | async-start | bytes 1310720 | tf_op jit(solution)/shard_map/all_to_all | solution.py:264
  22.9 3.3 %collective-permute-start.6 = (bf16[160,512]{1,0:T(8,128)(2,1)}, bf16[160,512]{1,0:T(8,128)(2,1)}, u32[]{:S(2)}, u32[]{:S(2)}) collective-permute-start(bf16[160,512]{1,0:T(8,128)(2,1)} %collective-permute-done.5.g3), channel_id=1, source_target_pairs={{0,48},{16,0},{32,16},{48,32},{1,49},{17,1},{33,17},{49,33},{2,50}... | collective-permute-start | bytes 491528 | tf_op jit(solution)/shard_map/ppermute | solution.py:235
  26.3 0.2 select_reduce_fusion.1
  26.5 4.1 %collective-permute-done.2.q2 = bf16[160,512]{1,0:T(8,128)(2,1)} collective-permute-done((bf16[160,512]{1,0:T(8,128)(2,1)}, bf16[160,512]{1,0:T(8,128)(2,1)}, u32[]{:S(2)}, u32[]{:S(2)}) %collective-permute-start.2) | collective-permute-done | bytes 163872 | tf_op jit(solution)/shard_map/ppermute | solution.py:235
  30.6 4.4 %all-to-all-done = bf16[8,160,256]{2,1,0:T(8,128)(2,1)S(1)} async-done(((bf16[8,160,256]{2,1,0:T(8,128)(2,1)}), bf16[8,160,256]{2,1,0:T(8,128)(2,1)S(1)}, u32[]{:S(2)}, u32[]{:S(2)}) %all-to-all-start) | async-done | bytes 655392 | tf_op jit(solution)/shard_map/all_to_all | solution.py:264
  35.3 0.1 reshape.101.posq.posq_ref
  35.5 0.2 select_reduce_fusion.ordk
  35.7 6.9 %stats_own.1 = (f32[3,2560]{1,0:T(4,128)S(1)}, bf16[2560,128]{1,0:T(8,128)(2,1)S(1)}, bf16[2560,128]{1,0:T(8,128)(2,1)S(1)}) custom-call(s32[32]{0:T(128)S(1)} %select_reduce_fusion.ordk, s32[1,2560]{1,0:T(1,128)S(1)} %reshape.101.posq.posq_ref, bf16[160,512]{1,0:T(8,128)(2,1)S(1)} %convolution_convert_fusion.q0, ...), custom_call_target="tpu_custom_call" | custom-call | flops 1677721600 | bytes 4194304 | tf_op jit(solution)/shard_map/stats_own/pallas_call | solution.py:218
  42.6 6.6 %stats_other.1.s0 = f32[3,2560]{1,0:T(4,128)S(1)} custom-call(s32[32]{0:T(128)S(1)} %select_reduce_fusion.ordk, s32[1,2560]{1,0:T(1,128)S(1)} %reshape.101.posq.posq_ref, bf16[2560,128]{1,0:T(8,128)(2,1)S(1)} %get-tuple-element.57.qr, bf16[2560,128]{1,0:T(8,128)(2,1)S(1)} %get-tuple-element.58.gr, bf16[1280,256]{1,0:T(8,128)(2,1)} %collective-permute-done.7.kvb, ...), custom_call_target="tpu_custom_call" | custom-call | flops 1677721600 | bytes 4194304 | tf_op jit(solution)/shard_map/stats_other/pallas_call | solution.py:218
  49.2 3.3 %collective-permute-start.10 = (f32[3,2560]{1,0:T(4,128)S(1)}, f32[3,2560]{1,0:T(4,128)S(1)}, u32[]{:S(2)}, u32[]{:S(2)}) collective-permute-start(f32[3,2560]{1,0:T(4,128)S(1)} %stats_other.1.s0), channel_id=1, source_target_pairs={{0,48},{16,0},{32,16},{48,32},{1,49},{17,1},{33,17},{49,33},{2,50}... | collective-permute-start | bytes 92168 | tf_op jit(solution)/shard_map/ppermute | solution.py:235
  52.4 0.9 collective-permute-start.8
  53.4 2.2 %columns.1 = (bf16[2,160,512]{2,1,0:T(8,128)(2,1)S(1)}, bf16[2,160,512]{2,1,0:T(8,128)(2,1)S(1)}, bf16[2,160,512]{2,1,0:T(8,128)(2,1)S(1)}, bf16[2,160,512]{2,1,0:T(8,128)(2,1)S(1)}) custom-call(s32[2]{0:T(128)S(1)} %pad_add_fusion.place_ref, bf16[160,4096]{1,0:T(8,128)(2,1)S(1)} %bitcast.29, bf16[160,4096]{1,0:T(8,128)(2,1)} %collective-permute-done.other), custom_call_target="tpu_custom_call" | custom-call | flops 671088640 | bytes 5242880 | tf_op jit(solution)/shard_map/columns/pallas_call | solution.py:218
  55.6 2.6 %collective-permute-start.11 = (bf16[2,160,512]{2,1,0:T(8,128)(2,1)S(1)}, bf16[2,160,512]{2,1,0:T(8,128)(2,1)S(1)}, u32[]{:S(2)}, u32[]{:S(2)}) collective-permute-start(bf16[2,160,512]{2,1,0:T(8,128)(2,1)S(1)} %get-tuple-element.68), channel_id=1, source_target_pairs={{0,16},{16,32},{32,48},{48,0},{1,17},{17,33},{33,49},{49,1},{2,18}... | collective-permute-start | bytes 983048 | tf_op jit(solution)/shard_map/ppermute | solution.py:235
  58.2 1.2 collective-permute-start.12
  59.4 1.6 %collective-permute-start.13 = (bf16[2,160,512]{2,1,0:T(8,128)(2,1)S(1)}, bf16[2,160,512]{2,1,0:T(8,128)(2,1)S(1)}, u32[]{:S(2)}, u32[]{:S(2)}) collective-permute-start(bf16[2,160,512]{2,1,0:T(8,128)(2,1)S(1)} %get-tuple-element.70), channel_id=1, source_target_pairs={{0,48},{16,0},{32,16},{48,32},{1,49},{17,1},{33,17},{49,33},{2,50}... | collective-permute-start | bytes 983048 | tf_op jit(solution)/shard_map/ppermute | solution.py:235
  61.0 20.4 %grads.1 = (f32[160,512]{1,0:T(8,128)S(1)}, bf16[160,512]{1,0:T(8,128)(2,1)S(1)}, bf16[160,512]{1,0:T(8,128)(2,1)S(1)}, bf16[160,512]{1,0:T(8,128)(2,1)S(1)}, f3...) custom-call(s32[32]{0:T(128)S(1)} %select_reduce_fusion.ordk, s32[1,2560]{1,0:T(1,128)S(1)} %reshape.101.posq.posq_ref, ...), custom_call_target="tpu_custom_call" | custom-call | flops 8388608000 | bytes 8388608 | tf_op jit(solution)/shard_map/grads/pallas_call | solution.py:218
  81.5 0.3 collective-permute-start.20
  81.8 1.4 %collective-permute-start.14 = (bf16[160,512]{1,0:T(8,128)(2,1)S(1)}, bf16[160,512]{1,0:T(8,128)(2,1)}, u32[]{:S(2)}, u32[]{:S(2)}) collective-permute-start(bf16[160,512]{1,0:T(8,128)(2,1)S(1)} %get-tuple-element.76), channel_id=1, source_target_pairs={{0,48},{16,0},{32,16},{48,32},{1,49},{17,1},{33,17},{49,33},{2,50}... | collective-permute-start | bytes 491528 | tf_op jit(solution)/shard_map/ppermute | solution.py:235
  83.2 1.2 collective-permute-start.15
  84.4 1.1 add_convert_fusion
  85.5 3.7 %all-to-all-start.1 = ((bf16[8,160,256]{2,1,0:T(8,128)(2,1)}), bf16[8,160,256]{2,1,0:T(8,128)(2,1)S(1)}, u32[]{:S(2)}, u32[]{:S(2)}) async-start(bf16[8,160,256]{2,1,0:T(8,128)(2,1)} %bitcast.8), calls=%async_computation.1 | async-start | bytes 1310720 | tf_op jit(solution)/shard_map/all_to_all | solution.py:311
  89.1 2.7 %collective-permute-done.15 = bf16[160,512]{1,0:T(8,128)(2,1)} collective-permute-done((bf16[160,512]{1,0:T(8,128)(2,1)S(1)}, bf16[160,512]{1,0:T(8,128)(2,1)}, u32[]{:S(2)}, u32[]{:S(2)}) %collective-permute-start.15) | collective-permute-done | bytes 163872 | tf_op jit(solution)/shard_map/ppermute | solution.py:235
  91.9 2.7 %collective-permute-done.16 = bf16[160,512]{1,0:T(8,128)(2,1)} collective-permute-done((bf16[160,512]{1,0:T(8,128)(2,1)S(1)}, bf16[160,512]{1,0:T(8,128)(2,1)}, u32[]{:S(2)}, u32[]{:S(2)}) %collective-permute-start.16) | collective-permute-done | bytes 163872 | tf_op jit(solution)/shard_map/ppermute | solution.py:235
  94.5 1.2 add_convert_fusion.1.q0
  95.7 0.7 collective-permute-start.19
  96.4 1.2 collective-permute-start.18
  97.6 0.8 collective-permute-start.17
  98.4 3.0 %all-to-all-done.1 = bf16[8,160,256]{2,1,0:T(8,128)(2,1)S(1)} async-done(((bf16[8,160,256]{2,1,0:T(8,128)(2,1)}), bf16[8,160,256]{2,1,0:T(8,128)(2,1)S(1)}, u32[]{:S(2)}, u32[]{:S(2)}) %all-to-all-start.1) | async-done | bytes 655392 | tf_op jit(solution)/shard_map/all_to_all | solution.py:311
  101.5 3.0 %collective-permute-start.23 = (bf16[160,256]{1,0:T(8,128)(2,1)S(1)}, bf16[160,256]{1,0:T(8,128)(2,1)S(1)}, u32[]{:S(2)}, u32[]{:S(2)}) collective-permute-start(bf16[160,256]{1,0:T(8,128)(2,1)S(1)} %reduce_sum.32.k0), channel_id=1, source_target_pairs={{0,48},{16,0},{32,16},{48,32},{1,49},{17,1},{33,17},{49,33},{2,50}... | collective-permute-start | bytes 245768 | tf_op jit(solution)/shard_map/ppermute | solution.py:235
  104.5 1.1 collective-permute-start.22
  105.6 0.7 collective-permute-start.21
  106.3 0.7 collective-permute-done.17.q1
  107.0 1.0 collective-permute-done.23.k3
  108.0 2.4 %collective-permute-done.22.k2 = bf16[160,256]{1,0:T(8,128)(2,1)S(1)} collective-permute-done((bf16[160,256]{1,0:T(8,128)(2,1)S(1)}, bf16[160,256]{1,0:T(8,128)(2,1)S(1)}, u32[]{:S(2)}, u32[]{:S(2)}) %collective-permute-start.22) | collective-permute-done | bytes 81952 | tf_op jit(solution)/shard_map/ppermute | solution.py:235
  110.5 0.9 collective-permute-done.21.k1
  111.4 0.1 pad_maximum_fusion
  111.7 2.6 %collective-permute-done.24.grads = bf16[4,160,768]{2,1,0:T(8,128)(2,1)S(1)} collective-permute-done((bf16[4,160,768]{2,1,0:T(8,128)(2,1)S(1)}, bf16[4,160,768]{2,1,0:T(8,128)(2,1)S(1)}, u32[]{:S(2)}, u32[]{:S(2)}) %collective-permute-start.24) | collective-permute-done | bytes 983072 | tf_op jit(solution)/shard_map/ppermute | solution.py:235
  114.2 1.2 weights.1
  115.5 18.2 %all_to_all.15.parts = bf16[16,32,768]{2,1,0:T(8,128)(2,1)S(1)} all-to-all(bf16[16,32,768]{2,1,0:T(8,128)(2,1)S(1)} %weights.1), channel_id=1, replica_groups=mesh['dp'=2,'outer'=4,'x'=4,'yh'=2,'core'=2] {'dp','x','yh'}, dimensions={0} | all-to-all | bytes 1572864 | tf_op jit(solution)/shard_map/all_to_all | solution.py:327
  133.7 0.7 last_sum.1
  (64 shorter events, 1.2 us)
Async XLA Ops:
  0.6 11.1 %copy-start = (bf16[4096,128]{1,0:T(8,128)(2,1)S(1)}, bf16[4096,128]{1,0:T(8,128)(2,1)}, u32[]{:S(2)}) copy-start(bf16[4096,128]{1,0:T(8,128)(2,1)} %param.14) | copy-start | bytes 3145732
  0.6 11.1 %copy-start.1 = (bf16[1,160,4096]{2,1,0:T(8,128)(2,1)S(1)}, bf16[1,160,4096]{2,1,0:T(8,128)(2,1)}, u32[]{:S(2)}) copy-start(bf16[1,160,4096]{2,1,0:T(8,128)(2,1)} %param.11) | copy-start | bytes 3932164
  0.7 7.8 %copy-start.6 = (bf16[1,160,512]{2,1,0:T(8,128)(2,1)S(1)}, bf16[1,160,512]{2,1,0:T(8,128)(2,1)}, u32[]{:S(2)}) copy-start(bf16[1,160,512]{2,1,0:T(8,128)(2,1)} %param.16) | copy-start | bytes 491524
  4.3 22.3 %collective-permute-start.3 = (bf16[160,512]{1,0:T(8,128)(2,1)S(1)}, bf16[160,512]{1,0:T(8,128)(2,1)S(1)}, u32[]{:S(2)}, u32[]{:S(2)}) collective-permute-start(bf16[160,512]{1,0:T(8,128)(2,1)S(1)} %convolution_convert_fusion.q0), channel_id=1, source_target_pairs={{0,48},{16,0},{32,16},{48,32},{1,49},{17,1},{33,17},{49,33},{2,50}... | collective-permute-start | bytes 491528 | tf_op jit(solution)/shard_map/ppermute | solution.py:235
  8.5 14.3 %collective-permute-start.1 = (bf16[160,512]{1,0:T(8,128)(2,1)S(1)}, bf16[160,512]{1,0:T(8,128)(2,1)}, u32[]{:S(2)}, u32[]{:S(2)}) collective-permute-start(bf16[160,512]{1,0:T(8,128)(2,1)S(1)} %convolution_convert_fusion.q0), channel_id=1, source_target_pairs={{0,16},{16,32},{32,48},{48,0},{1,17},{17,33},{33,49},{49,1},{2,18}... | collective-permute-start | bytes 491528 | tf_op jit(solution)/shard_map/ppermute | solution.py:235
  8.5 14.4 %collective-permute-start.5 = (bf16[160,512]{1,0:T(8,128)(2,1)S(1)}, bf16[160,512]{1,0:T(8,128)(2,1)}, u32[]{:S(2)}, u32[]{:S(2)}) collective-permute-start(bf16[160,512]{1,0:T(8,128)(2,1)S(1)} %bitcast.33), channel_id=1, source_target_pairs={{0,48},{16,0},{32,16},{48,32},{1,49},{17,1},{33,17},{49,33},{2,50}... | collective-permute-start | bytes 491528 | tf_op jit(solution)/shard_map/ppermute | solution.py:235
  11.7 14.8 %collective-permute-start.4 = (bf16[160,512]{1,0:T(8,128)(2,1)S(1)}, bf16[160,512]{1,0:T(8,128)(2,1)}, u32[]{:S(2)}, u32[]{:S(2)}) collective-permute-start(bf16[160,512]{1,0:T(8,128)(2,1)S(1)} %bitcast.34), channel_id=1, source_target_pairs={{0,16},{16,32},{32,48},{48,0},{1,17},{17,33},{33,49},{49,1},{2,18}... | collective-permute-start | bytes 491528 | tf_op jit(solution)/shard_map/ppermute | solution.py:235
  11.7 3.2 %collective-permute-start = (bf16[160,4096]{1,0:T(8,128)(2,1)S(1)}, bf16[160,4096]{1,0:T(8,128)(2,1)}, u32[]{:S(2)}, u32[]{:S(2)}) collective-permute-start(bf16[160,4096]{1,0:T(8,128)(2,1)S(1)} %bitcast.28), channel_id=1, source_target_pairs={{0,1},{1,0},{2,3},{3,2},{4,5},{5,4},{6,7},{7,6},{8,9},{9,8},{10,11... | collective-permute-start | bytes 3932168 | tf_op jit(solution)/shard_map/ppermute | solution.py:235
  11.7 1.2 copy-start.7
  13.0 0.7 copy-start.11
  13.0 0.7 copy-start.10
  13.5 9.3 %copy-start.8 = (s32[4]{0:T(128)S(1)}, s32[4]{0:T(128)}, u32[]{:S(2)}) copy-start(s32[4]{0:T(128)} %constant.76) | copy-start | bytes 52
  13.5 12.9 %copy-start.9 = (s32[1,128]{1,0:T(1,128)S(1)}, s32[1,128]{1,0:T(1,128)}, u32[]{:S(2)}) copy-start(s32[1,128]{1,0:T(1,128)} %param.12) | copy-start | bytes 1540
  15.7 19.3 %all-to-all-start = ((bf16[8,160,256]{2,1,0:T(8,128)(2,1)}), bf16[8,160,256]{2,1,0:T(8,128)(2,1)S(1)}, u32[]{:S(2)}, u32[]{:S(2)}) async-start(bf16[8,160,256]{2,1,0:T(8,128)(2,1)} %broadcast_in_dim.47), calls=%async_computation | async-start | bytes 1310720 | tf_op jit(solution)/shard_map/all_to_all | solution.py:264
  22.8 7.8 %collective-permute-start.2 = (bf16[160,512]{1,0:T(8,128)(2,1)}, bf16[160,512]{1,0:T(8,128)(2,1)}, u32[]{:S(2)}, u32[]{:S(2)}) collective-permute-start(bf16[160,512]{1,0:T(8,128)(2,1)} %collective-permute-done.1.q1), channel_id=1, source_target_pairs={{0,16},{16,32},{32,48},{48,0},{1,17},{17,33},{33,49},{49,1},{2,18}... | collective-permute-start | bytes 491528 | tf_op jit(solution)/shard_map/ppermute | solution.py:235
  22.9 7.7 %collective-permute-start.6 = (bf16[160,512]{1,0:T(8,128)(2,1)}, bf16[160,512]{1,0:T(8,128)(2,1)}, u32[]{:S(2)}, u32[]{:S(2)}) collective-permute-start(bf16[160,512]{1,0:T(8,128)(2,1)} %collective-permute-done.5.g3), channel_id=1, source_target_pairs={{0,48},{16,0},{32,16},{48,32},{1,49},{17,1},{33,17},{49,33},{2,50}... | collective-permute-start | bytes 491528 | tf_op jit(solution)/shard_map/ppermute | solution.py:235
  35.0 7.5 %collective-permute-start.7 = (bf16[1280,256]{1,0:T(8,128)(2,1)S(1)}, bf16[1280,256]{1,0:T(8,128)(2,1)}, u32[]{:S(2)}, u32[]{:S(2)}) collective-permute-start(bf16[1280,256]{1,0:T(8,128)(2,1)S(1)} %bitcast.30), channel_id=1, source_target_pairs={{0,1},{1,0},{2,3},{3,2},{4,5},{5,4},{6,7},{7,6},{8,9},{9,8},{10,11... | collective-permute-start | bytes 1966088 | tf_op jit(solution)/shard_map/ppermute | solution.py:235
  49.2 10.3 %collective-permute-start.10 = (f32[3,2560]{1,0:T(4,128)S(1)}, f32[3,2560]{1,0:T(4,128)S(1)}, u32[]{:S(2)}, u32[]{:S(2)}) collective-permute-start(f32[3,2560]{1,0:T(4,128)S(1)} %stats_other.1.s0), channel_id=1, source_target_pairs={{0,48},{16,0},{32,16},{48,32},{1,49},{17,1},{33,17},{49,33},{2,50}... | collective-permute-start | bytes 92168 | tf_op jit(solution)/shard_map/ppermute | solution.py:235
  52.4 8.5 %collective-permute-start.9 = (f32[3,2560]{1,0:T(4,128)S(1)}, f32[3,2560]{1,0:T(4,128)S(1)}, u32[]{:S(2)}, u32[]{:S(2)}) collective-permute-start(f32[3,2560]{1,0:T(4,128)S(1)} %stats_other.1.s0), channel_id=1, source_target_pairs={{0,32},{16,48},{32,0},{48,16},{1,33},{17,49},{33,1},{49,17},{2,34}... | collective-permute-start | bytes 92168 | tf_op jit(solution)/shard_map/ppermute | solution.py:235
  52.4 8.5 %collective-permute-start.8 = (f32[3,2560]{1,0:T(4,128)S(1)}, f32[3,2560]{1,0:T(4,128)S(1)}, u32[]{:S(2)}, u32[]{:S(2)}) collective-permute-start(f32[3,2560]{1,0:T(4,128)S(1)} %stats_other.1.s0), channel_id=1, source_target_pairs={{0,16},{16,32},{32,48},{48,0},{1,17},{17,33},{33,49},{49,1},{2,18}... | collective-permute-start | bytes 92168 | tf_op jit(solution)/shard_map/ppermute | solution.py:235
  55.6 25.8 %collective-permute-start.11 = (bf16[2,160,512]{2,1,0:T(8,128)(2,1)S(1)}, bf16[2,160,512]{2,1,0:T(8,128)(2,1)S(1)}, u32[]{:S(2)}, u32[]{:S(2)}) collective-permute-start(bf16[2,160,512]{2,1,0:T(8,128)(2,1)S(1)} %get-tuple-element.68), channel_id=1, source_target_pairs={{0,16},{16,32},{32,48},{48,0},{1,17},{17,33},{33,49},{49,1},{2,18}... | collective-permute-start | bytes 983048 | tf_op jit(solution)/shard_map/ppermute | solution.py:235
  58.2 23.2 %collective-permute-start.12 = (bf16[2,160,512]{2,1,0:T(8,128)(2,1)S(1)}, bf16[2,160,512]{2,1,0:T(8,128)(2,1)S(1)}, u32[]{:S(2)}, u32[]{:S(2)}) collective-permute-start(bf16[2,160,512]{2,1,0:T(8,128)(2,1)S(1)} %get-tuple-element.69), channel_id=1, source_target_pairs={{0,32},{16,48},{32,0},{48,16},{1,33},{17,49},{33,1},{49,17},{2,34}... | collective-permute-start | bytes 983048 | tf_op jit(solution)/shard_map/ppermute | solution.py:235
  59.4 22.0 %collective-permute-start.13 = (bf16[2,160,512]{2,1,0:T(8,128)(2,1)S(1)}, bf16[2,160,512]{2,1,0:T(8,128)(2,1)S(1)}, u32[]{:S(2)}, u32[]{:S(2)}) collective-permute-start(bf16[2,160,512]{2,1,0:T(8,128)(2,1)S(1)} %get-tuple-element.70), channel_id=1, source_target_pairs={{0,48},{16,0},{32,16},{48,32},{1,49},{17,1},{33,17},{49,33},{2,50}... | collective-permute-start | bytes 983048 | tf_op jit(solution)/shard_map/ppermute | solution.py:235
  81.4 4.0 %copy-start.2 = (bf16[2,160,512]{2,1,0:T(8,128)(2,1)}, bf16[2,160,512]{2,1,0:T(8,128)(2,1)S(1)}, u32[]{:S(2)}) copy-start(bf16[2,160,512]{2,1,0:T(8,128)(2,1)S(1)} %collective-permute-done.12.x2) | copy-start | bytes 983044
  81.4 4.0 %copy-start.4 = (bf16[2,160,512]{2,1,0:T(8,128)(2,1)}, bf16[2,160,512]{2,1,0:T(8,128)(2,1)S(1)}, u32[]{:S(2)}) copy-start(bf16[2,160,512]{2,1,0:T(8,128)(2,1)S(1)} %collective-permute-done.13.x3) | copy-start | bytes 983044
  81.5 2.9 %collective-permute-start.20 = (bf16[1280,256]{1,0:T(8,128)(2,1)S(1)}, bf16[1280,256]{1,0:T(8,128)(2,1)S(1)}, u32[]{:S(2)}, u32[]{:S(2)}) collective-permute-start(bf16[1280,256]{1,0:T(8,128)(2,1)S(1)} %get-tuple-element.80), channel_id=1, source_target_pairs={{0,1},{1,0},{2,3},{3,2},{4,5},{5,4},{6,7},{7,6},{8,9},{9,8},{10,11... | collective-permute-start | bytes 1966088 | tf_op jit(solution)/shard_map/ppermute | solution.py:235
  81.8 7.4 %collective-permute-start.14 = (bf16[160,512]{1,0:T(8,128)(2,1)S(1)}, bf16[160,512]{1,0:T(8,128)(2,1)}, u32[]{:S(2)}, u32[]{:S(2)}) collective-permute-start(bf16[160,512]{1,0:T(8,128)(2,1)S(1)} %get-tuple-element.76), channel_id=1, source_target_pairs={{0,48},{16,0},{32,16},{48,32},{1,49},{17,1},{33,17},{49,33},{2,50}... | collective-permute-start | bytes 491528 | tf_op jit(solution)/shard_map/ppermute | solution.py:235
  83.2 8.7 %collective-permute-start.15 = (bf16[160,512]{1,0:T(8,128)(2,1)S(1)}, bf16[160,512]{1,0:T(8,128)(2,1)}, u32[]{:S(2)}, u32[]{:S(2)}) collective-permute-start(bf16[160,512]{1,0:T(8,128)(2,1)S(1)} %get-tuple-element.77), channel_id=1, source_target_pairs={{0,32},{16,48},{32,0},{48,16},{1,33},{17,49},{33,1},{49,17},{2,34}... | collective-permute-start | bytes 491528 | tf_op jit(solution)/shard_map/ppermute | solution.py:235
  84.4 10.2 %collective-permute-start.16 = (bf16[160,512]{1,0:T(8,128)(2,1)S(1)}, bf16[160,512]{1,0:T(8,128)(2,1)}, u32[]{:S(2)}, u32[]{:S(2)}) collective-permute-start(bf16[160,512]{1,0:T(8,128)(2,1)S(1)} %get-tuple-element.78), channel_id=1, source_target_pairs={{0,16},{16,32},{32,48},{48,0},{1,17},{17,33},{33,49},{49,1},{2,18}... | collective-permute-start | bytes 491528 | tf_op jit(solution)/shard_map/ppermute | solution.py:235
  85.5 15.9 %all-to-all-start.1 = ((bf16[8,160,256]{2,1,0:T(8,128)(2,1)}), bf16[8,160,256]{2,1,0:T(8,128)(2,1)S(1)}, u32[]{:S(2)}, u32[]{:S(2)}) async-start(bf16[8,160,256]{2,1,0:T(8,128)(2,1)} %bitcast.8), calls=%async_computation.1 | async-start | bytes 1310720 | tf_op jit(solution)/shard_map/all_to_all | solution.py:311
  95.7 9.9 %collective-permute-start.19 = (bf16[160,512]{1,0:T(8,128)(2,1)S(1)}, bf16[160,512]{1,0:T(8,128)(2,1)S(1)}, u32[]{:S(2)}, u32[]{:S(2)}) collective-permute-start(bf16[160,512]{1,0:T(8,128)(2,1)S(1)} %add_convert_fusion.1.q0), channel_id=1, source_target_pairs={{0,48},{16,0},{32,16},{48,32},{1,49},{17,1},{33,17},{49,33},{2,50}... | collective-permute-start | bytes 491528 | tf_op jit(solution)/shard_map/ppermute | solution.py:235
  96.4 9.9 %collective-permute-start.18 = (bf16[160,512]{1,0:T(8,128)(2,1)S(1)}, bf16[160,512]{1,0:T(8,128)(2,1)S(1)}, u32[]{:S(2)}, u32[]{:S(2)}) collective-permute-start(bf16[160,512]{1,0:T(8,128)(2,1)S(1)} %add_convert_fusion.1.q0), channel_id=1, source_target_pairs={{0,32},{16,48},{32,0},{48,16},{1,33},{17,49},{33,1},{49,17},{2,34}... | collective-permute-start | bytes 491528 | tf_op jit(solution)/shard_map/ppermute | solution.py:235
  97.6 9.4 %collective-permute-start.17 = (bf16[160,512]{1,0:T(8,128)(2,1)S(1)}, bf16[160,512]{1,0:T(8,128)(2,1)S(1)}, u32[]{:S(2)}, u32[]{:S(2)}) collective-permute-start(bf16[160,512]{1,0:T(8,128)(2,1)S(1)} %add_convert_fusion.1.q0), channel_id=1, source_target_pairs={{0,16},{16,32},{32,48},{48,0},{1,17},{17,33},{33,49},{49,1},{2,18}... | collective-permute-start | bytes 491528 | tf_op jit(solution)/shard_map/ppermute | solution.py:235
  101.5 6.5 %collective-permute-start.23 = (bf16[160,256]{1,0:T(8,128)(2,1)S(1)}, bf16[160,256]{1,0:T(8,128)(2,1)S(1)}, u32[]{:S(2)}, u32[]{:S(2)}) collective-permute-start(bf16[160,256]{1,0:T(8,128)(2,1)S(1)} %reduce_sum.32.k0), channel_id=1, source_target_pairs={{0,48},{16,0},{32,16},{48,32},{1,49},{17,1},{33,17},{49,33},{2,50}... | collective-permute-start | bytes 245768 | tf_op jit(solution)/shard_map/ppermute | solution.py:235
  104.5 6.0 %collective-permute-start.22 = (bf16[160,256]{1,0:T(8,128)(2,1)S(1)}, bf16[160,256]{1,0:T(8,128)(2,1)S(1)}, u32[]{:S(2)}, u32[]{:S(2)}) collective-permute-start(bf16[160,256]{1,0:T(8,128)(2,1)S(1)} %reduce_sum.32.k0), channel_id=1, source_target_pairs={{0,32},{16,48},{32,0},{48,16},{1,33},{17,49},{33,1},{49,17},{2,34}... | collective-permute-start | bytes 245768 | tf_op jit(solution)/shard_map/ppermute | solution.py:235
  105.6 5.7 %collective-permute-start.21 = (bf16[160,256]{1,0:T(8,128)(2,1)S(1)}, bf16[160,256]{1,0:T(8,128)(2,1)S(1)}, u32[]{:S(2)}, u32[]{:S(2)}) collective-permute-start(bf16[160,256]{1,0:T(8,128)(2,1)S(1)} %reduce_sum.32.k0), channel_id=1, source_target_pairs={{0,16},{16,32},{32,48},{48,0},{1,17},{17,33},{33,49},{49,1},{2,18}... | collective-permute-start | bytes 245768 | tf_op jit(solution)/shard_map/ppermute | solution.py:235
  111.4 2.8 %copy-start.3 = (bf16[2,160,512]{2,1,0:T(8,128)(2,1)S(1)}, bf16[2,160,512]{2,1,0:T(8,128)(2,1)}, u32[]{:S(2)}) copy-start(bf16[2,160,512]{2,1,0:T(8,128)(2,1)} %copy-done.2) | copy-start | bytes 983044
  111.4 2.8 %copy-start.5 = (bf16[2,160,512]{2,1,0:T(8,128)(2,1)S(1)}, bf16[2,160,512]{2,1,0:T(8,128)(2,1)}, u32[]{:S(2)}) copy-start(bf16[2,160,512]{2,1,0:T(8,128)(2,1)} %copy-done.4) | copy-start | bytes 983044
  111.6 2.6 %collective-permute-start.24 = (bf16[4,160,768]{2,1,0:T(8,128)(2,1)S(1)}, bf16[4,160,768]{2,1,0:T(8,128)(2,1)S(1)}, u32[]{:S(2)}, u32[]{:S(2)}) collective-permute-start(bf16[4,160,768]{2,1,0:T(8,128)(2,1)S(1)} %pad_maximum_fusion), channel_id=1, source_target_pairs={{0,1},{1,0},{2,3},{3,2},{4,5},{5,4},{6,7},{7,6},{8,9},{9,8},{10,11... | collective-permute-start | bytes 2949128 | tf_op jit(solution)/shard_map/ppermute | solution.py:235

commit v11 on v8

--- a/solution.py
+++ b/solution.py
@@ -202,6 +202,24 @@
     dwv[...] = total[:, wide + HEAD :]
 
 
+def project_kernel(tok, wq, wk, wv, query, kv, acc):
+    step = pl.program_id(0)
+
+    @pl.when(step == 0)
+    def _():
+        acc[...] = jnp.zeros_like(acc)
+
+    wide = HEADS * HEAD
+    for out, w in ((slice(0, wide), wq), (slice(wide, wide + HEAD), wk), (slice(wide + HEAD, wide + 2 * HEAD), wv)):
+        acc[:, out] += dot(tok[...], w[...], NN)
+
+    @pl.when(step == pl.num_programs(0) - 1)
+    def _():
+        query[...] = acc[:, :wide].astype(bf16)
+        for i in range(8):
+            kv[i] = acc[:, wide:].astype(bf16)
+
+
 VM = 24
 smem = pl.BlockSpec(memory_space=pltpu.SMEM)
 vmem = pl.BlockSpec(memory_space=pltpu.VMEM)
@@ -231,6 +249,32 @@
 acc_rows = ((ALL_ROWS, HEAD), f32)
 
 
+def project_call(tokens, w_query, w_key, w_value):
+    depth = 1024
+    return pl.pallas_call(
+        project_kernel,
+        grid=(tokens.shape[1] // depth,),
+        out_shape=(
+            jax.ShapeDtypeStruct((ROWS, WIDE), bf16),
+            jax.ShapeDtypeStruct((8, ROWS, 2 * HEAD), bf16),
+        ),
+        in_specs=[
+            pl.BlockSpec((ROWS, depth), lambda i: (0, i)),
+            pl.BlockSpec((depth, WIDE), lambda i: (i, 0)),
+            pl.BlockSpec((depth, HEAD), lambda i: (i, 0)),
+            pl.BlockSpec((depth, HEAD), lambda i: (i, 0)),
+        ],
+        out_specs=(
+            pl.BlockSpec((ROWS, WIDE), lambda i: (0, 0)),
+            pl.BlockSpec((8, ROWS, 2 * HEAD), lambda i: (0, 0, 0)),
+        ),
+        scratch_shapes=[pltpu.VMEM((ROWS, WIDE + 2 * HEAD), f32)],
+        compiler_params=params,
+        cost_estimate=cost(ROWS * 4096, 6, 8 << 20),
+        name="project",
+    )(tokens, w_query, w_key, w_value)
+
+
 def shift(x, axis, d, n):
     return lax.ppermute(x, axis, [(i, (i + d) % n) for i in range(n)])
 
@@ -245,19 +289,11 @@
     dout = grad_out[0]
     o, ix, iy, ic = (lax.axis_index(a) for a in ("outer", "x", "yh", "core"))
 
-    query = dot(tokens, w_query, NN).astype(bf16)
+    query, kva = project_call(tokens, w_query, w_key, w_value)
     q1, q3 = shift(query, "outer", 1, N_OUT), shift(query, "outer", -1, N_OUT)
     g1, g3 = shift(dout, "outer", 1, N_OUT), shift(dout, "outer", -1, N_OUT)
     qs = [query, q1, shift(q1, "outer", 1, N_OUT), q3]
     gs = [dout, g1, shift(g3, "outer", -1, N_OUT), g3]
-    kv = jnp.concatenate(
-        [
-            dot(tokens, w_key, NN).astype(bf16),
-            dot(tokens, w_value, NN).astype(bf16),
-        ],
-        axis=1,
-    )
-    kva = jnp.broadcast_to(kv[None], (8,) + kv.shape)
     kva = lax.all_to_all(kva, ("x", "yh"), 0, 0, tiled=True).reshape(KHALF, 2 * HEAD)
     other_tokens = shift(tokens, "core", 1, 2)
     later = tokens

time: 133 us -> 135 us (1.015)
  matrix products: 4.59 us -> 0 us
  local copies, waits for them, and re-layouts: 1.31 us -> 5.02 us
  Pallas kernels: 38 us -> 41 us
  waiting for transfers between devices: 23.5 us -> 25 us
    dot_general x3 -> x0, matrix products: 4.59 us -> none  [dot(): return lax.dot_general(a, b, dims, preferred_element_type=f32)]
    unnamed x24 -> x16, local copies, waits for them, and re-layouts: 0.07 us -> 4.66 us
    pallas_call x0 -> x1, Pallas kernels: none -> 4.46 us  [project_call(): pl.pallas_call(project_kernel, grid=(tokens.shape[1] // depth,), out_shap...]
    ppermute x25, waiting for transfers between devices: 17 us -> 19 us  [shift(): return lax.ppermute(x, axis, [(i, (i + d) % n) for i in range(n)])]
    pallas_call x6, Pallas kernels: 38 us -> 36.5 us  [kernel_call(): pl.pallas_call(body, out_shape=tuple((jax.ShapeDtypeStruct(*o) for o in o...]
  transfers between devices with their start and end apart: 27 -> 27, of which waited for: 10 -> 10; matrix products, arithmetic and copies ran while one was open for 4% -> 2% of each run, Pallas kernels for 22% -> 24%
where the time goes in v11:
time: 135 us; the launch traced here: 134 us
  starting transfers between devices  42.2 us (31%)
  Pallas kernels  41 us (30%)
  waiting for transfers between devices  25 us (19%)
  blocking collectives  18.2 us (13%)
  local copies, waits for them, and re-layouts  5.02 us (4%)
  other arithmetic  2.11 us (2%)
    pallas_call x6, Pallas kernels, kernel_call(): pl.pallas_call(body, out_shape=tuple((jax.ShapeDtypeStruct(*o) for o in o...  36.5 us
    ppermute x25, starting transfers between devices, shift(): return lax.ppermute(x, axis, [(i, (i + d) % n) for i in range(n)])  31.3 us
    ppermute x25, waiting for transfers between devices, shift(): return lax.ppermute(x, axis, [(i, (i + d) % n) for i in range(n)])  19 us
    all_to_all x1, blocking collectives, per_device(): dw = lax.all_to_all(dw, ('dp', 'x', 'yh'), 0, 0, tiled=True)  18.2 us
    all_to_all x1, starting transfers between devices, per_device(): lax.all_to_all(kva, ('x', 'yh'), 0, 0, tiled=True).reshape(KHALF, 2 * HEAD)  6.93 us
    unnamed x16, local copies, waits for them, and re-layouts  4.66 us
    pallas_call x1, Pallas kernels, project_call(): pl.pallas_call(project_kernel, grid=(tokens.shape[1] // depth,), out_shap...  4.46 us
    all_to_all x1, waiting for transfers between devices, per_device(): dkv = lax.all_to_all(dkv, ('x', 'yh'), 0, 0, tiled=True)  4.3 us
  transfers between devices with their start and end apart: 27, of which 10 were waited for; matrix products, arithmetic and copies ran while one was open for 2% of the time, Pallas kernels for 24%

profile of v11, /device:TPU:0, one launch (start us, length us, event | category | flops | bytes accessed | tf_op | source)
XLA Modules:
  0.0 134.4 jit_solution(12420834604413965224)
XLA Ops:
  0.6 4.2 %collective-permute-start.4 = (bf16[160,512]{1,0:T(8,128)(2,1)}, bf16[160,512]{1,0:T(8,128)(2,1)S(1)}, u32[]{:S(2)}, u32[]{:S(2)}) collective-permute-start(bf16[160,512]{1,0:T(8,128)(2,1)} %bitcast.22), channel_id=1, source_target_pairs={{0,48},{16,0},{32,16},{48,32},{1,49},{17,1},{33,17},{49,33},{2,50}... | collective-permute-start | bytes 491528 | tf_op jit(solution)/shard_map/ppermute | solution.py:279
  4.8 2.2 %copy-done = bf16[4096,512]{1,0:T(8,128)(2,1)S(1)} copy-done((bf16[4096,512]{1,0:T(8,128)(2,1)S(1)}, bf16[4096,512]{1,0:T(8,128)(2,1)}, u32[]{:S(2)}) %copy-start) | copy-done | bytes 4194328
  7.0 1.2 copy-done.1
  8.2 1.2 copy-done.2
  9.5 4.5 %project.1 = (bf16[160,512]{1,0:T(8,128)(2,1)S(1)}, bf16[8,160,256]{2,1,0:T(8,128)(2,1)}) custom-call(bf16[160,4096]{1,0:T(8,128)(2,1)} %bitcast.3.tok.own, bf16[4096,512]{1,0:T(8,128)(2,1)S(1)} %copy-done, bf16[4096,128]{1,0:T(8,128)(2,1)S(1)} %copy-done.1, bf16[4096,128]{1,0:T(8,128)(2,1)S(1)} %copy-done.2), custom_call_target="tpu_custom_call" | custom-call | flops 1006632960 | bytes 8388608 | tf_op jit(solution)/shard_map/project/pallas_call | solution.py:254
  13.9 3.3 %collective-permute-start.2 = (bf16[160,512]{1,0:T(8,128)(2,1)S(1)}, bf16[160,512]{1,0:T(8,128)(2,1)S(1)}, u32[]{:S(2)}, u32[]{:S(2)}) collective-permute-start(bf16[160,512]{1,0:T(8,128)(2,1)S(1)} %get-tuple-element.50.q0), channel_id=1, source_target_pairs={{0,48},{16,0},{32,16},{48,32},{1,49},{17,1},{33,17},{49,33},{2,50}... | collective-permute-start | bytes 491528 | tf_op jit(solution)/shard_map/ppermute | solution.py:279
  17.3 6.9 %all-to-all-start = ((bf16[8,160,256]{2,1,0:T(8,128)(2,1)}), bf16[8,160,256]{2,1,0:T(8,128)(2,1)S(1)}, u32[]{:S(2)}, u32[]{:S(2)}) async-start(bf16[8,160,256]{2,1,0:T(8,128)(2,1)} %get-tuple-element.47), calls=%async_computation | async-start | bytes 1310720 | tf_op jit(solution)/shard_map/all_to_all | solution.py:297
  24.4 3.3 %collective-permute-start.5 = (bf16[160,512]{1,0:T(8,128)(2,1)S(1)}, bf16[160,512]{1,0:T(8,128)(2,1)S(1)}, u32[]{:S(2)}, u32[]{:S(2)}) collective-permute-start(bf16[160,512]{1,0:T(8,128)(2,1)S(1)} %collective-permute-done.4.g3), channel_id=1, source_target_pairs={{0,48},{16,0},{32,16},{48,32},{1,49},{17,1},{33,17},{49,33},{2,50}... | collective-permute-start | bytes 491528 | tf_op jit(solution)/shard_map/ppermute | solution.py:279
  27.8 0.1 add.164
  27.9 0.2 select_reduce_fusion.1
  28.1 3.5 %collective-permute-done.5.g2 = bf16[160,512]{1,0:T(8,128)(2,1)S(1)} collective-permute-done((bf16[160,512]{1,0:T(8,128)(2,1)S(1)}, bf16[160,512]{1,0:T(8,128)(2,1)S(1)}, u32[]{:S(2)}, u32[]{:S(2)}) %collective-permute-start.5) | collective-permute-done | bytes 163872 | tf_op jit(solution)/shard_map/ppermute | solution.py:279
  31.6 3.4 %collective-permute-done.1.q2 = bf16[160,512]{1,0:T(8,128)(2,1)S(1)} collective-permute-done((bf16[160,512]{1,0:T(8,128)(2,1)S(1)}, bf16[160,512]{1,0:T(8,128)(2,1)S(1)}, u32[]{:S(2)}, u32[]{:S(2)}) %collective-permute-start.1) | collective-permute-done | bytes 163872 | tf_op jit(solution)/shard_map/ppermute | solution.py:279
  35.0 1.7 %all-to-all-done = bf16[8,160,256]{2,1,0:T(8,128)(2,1)S(1)} async-done(((bf16[8,160,256]{2,1,0:T(8,128)(2,1)}), bf16[8,160,256]{2,1,0:T(8,128)(2,1)S(1)}, u32[]{:S(2)}, u32[]{:S(2)}) %all-to-all-start) | async-done | bytes 655392 | tf_op jit(solution)/shard_map/all_to_all | solution.py:297
  36.8 0.1 add.152
  36.9 0.1 reshape.100.posq.posq_ref
  37.1 0.2 select_reduce_fusion.ordk
  37.3 5.9 %stats_own.1 = (f32[3,2560]{1,0:T(4,128)S(1)}, bf16[2560,128]{1,0:T(8,128)(2,1)S(1)}, bf16[2560,128]{1,0:T(8,128)(2,1)S(1)}) custom-call(s32[32]{0:T(128)S(1)} %select_reduce_fusion.ordk, s32[1,2560]{1,0:T(1,128)S(1)} %reshape.100.posq.posq_ref, bf16[160,512]{1,0:T(8,128)(2,1)S(1)} %get-tuple-element.50.q0, bf16[160,512]{1,0:T(8,128)(2,1)S(1)} %collective-permute-done.q1, ...), custom_call_target="tpu_custom_call" | custom-call | flops 1677721600 | bytes 4194304 | tf_op jit(solution)/shard_map/stats_own/pallas_call | solution.py:236
  43.2 6.3 %stats_other.1.s0 = f32[3,2560]{1,0:T(4,128)S(1)} custom-call(s32[32]{0:T(128)S(1)} %select_reduce_fusion.ordk, s32[1,2560]{1,0:T(1,128)S(1)} %reshape.100.posq.posq_ref, bf16[2560,128]{1,0:T(8,128)(2,1)S(1)} %get-tuple-element.59.qr, bf16[2560,128]{1,0:T(8,128)(2,1)S(1)} %get-tuple-element.60.gr, bf16[1280,256]{1,0:T(8,128)(2,1)} %collective-permute-done.7.kvb, ...), custom_call_target="tpu_custom_call" | custom-call | flops 1677721600 | bytes 4194304 | tf_op jit(solution)/shard_map/stats_other/pallas_call | solution.py:236
  49.5 3.3 %collective-permute-start.10 = (f32[3,2560]{1,0:T(4,128)S(1)}, f32[3,2560]{1,0:T(4,128)S(1)}, u32[]{:S(2)}, u32[]{:S(2)}) collective-permute-start(f32[3,2560]{1,0:T(4,128)S(1)} %stats_other.1.s0), channel_id=1, source_target_pairs={{0,48},{16,0},{32,16},{48,32},{1,49},{17,1},{33,17},{49,33},{2,50}... | collective-permute-start | bytes 92168 | tf_op jit(solution)/shard_map/ppermute | solution.py:279
  52.8 0.9 collective-permute-start.8
  53.8 2.2 %columns.1 = (bf16[2,160,512]{2,1,0:T(8,128)(2,1)S(1)}, bf16[2,160,512]{2,1,0:T(8,128)(2,1)S(1)}, bf16[2,160,512]{2,1,0:T(8,128)(2,1)S(1)}, bf16[2,160,512]{2,1,0:T(8,128)(2,1)S(1)}) custom-call(s32[2]{0:T(128)S(1)} %pad_add_fusion.place_ref, bf16[160,4096]{1,0:T(8,128)(2,1)} %bitcast.3.tok.own, bf16[160,4096]{1,0:T(8,128)(2,1)S(1)} %collective-permute-done.6.other), custom_call_target="tpu_custom_call" | custom-call | flops 671088640 | bytes 5242880 | tf_op jit(solution)/shard_map/columns/pallas_call | solution.py:236
  56.0 2.6 %collective-permute-start.11 = (bf16[2,160,512]{2,1,0:T(8,128)(2,1)S(1)}, bf16[2,160,512]{2,1,0:T(8,128)(2,1)S(1)}, u32[]{:S(2)}, u32[]{:S(2)}) collective-permute-start(bf16[2,160,512]{2,1,0:T(8,128)(2,1)S(1)} %get-tuple-element.70), channel_id=1, source_target_pairs={{0,16},{16,32},{32,48},{48,0},{1,17},{17,33},{33,49},{49,1},{2,18}... | collective-permute-start | bytes 983048 | tf_op jit(solution)/shard_map/ppermute | solution.py:279
  58.6 1.2 collective-permute-start.12
  59.8 1.6 %collective-permute-start.13 = (bf16[2,160,512]{2,1,0:T(8,128)(2,1)S(1)}, bf16[2,160,512]{2,1,0:T(8,128)(2,1)S(1)}, u32[]{:S(2)}, u32[]{:S(2)}) collective-permute-start(bf16[2,160,512]{2,1,0:T(8,128)(2,1)S(1)} %get-tuple-element.72), channel_id=1, source_target_pairs={{0,48},{16,0},{32,16},{48,32},{1,49},{17,1},{33,17},{49,33},{2,50}... | collective-permute-start | bytes 983048 | tf_op jit(solution)/shard_map/ppermute | solution.py:279
  61.4 20.2 %grads.1 = (f32[160,512]{1,0:T(8,128)S(1)}, bf16[160,512]{1,0:T(8,128)(2,1)S(1)}, bf16[160,512]{1,0:T(8,128)(2,1)S(1)}, bf16[160,512]{1,0:T(8,128)(2,1)S(1)}, f3...) custom-call(s32[32]{0:T(128)S(1)} %select_reduce_fusion.ordk, s32[1,2560]{1,0:T(1,128)S(1)} %reshape.100.posq.posq_ref, ...), custom_call_target="tpu_custom_call" | custom-call | flops 8388608000 | bytes 8388608 | tf_op jit(solution)/shard_map/grads/pallas_call | solution.py:236
  81.6 0.1 collective-permute-start.20
  81.7 1.4 %collective-permute-start.14 = (bf16[160,512]{1,0:T(8,128)(2,1)S(1)}, bf16[160,512]{1,0:T(8,128)(2,1)S(1)}, u32[]{:S(2)}, u32[]{:S(2)}) collective-permute-start(bf16[160,512]{1,0:T(8,128)(2,1)S(1)} %get-tuple-element.78), channel_id=1, source_target_pairs={{0,48},{16,0},{32,16},{48,32},{1,49},{17,1},{33,17},{49,33},{2,50}... | collective-permute-start | bytes 491528 | tf_op jit(solution)/shard_map/ppermute | solution.py:279
  83.1 1.2 collective-permute-start.15
  84.3 1.0 add_convert_fusion
  85.3 4.0 %all-to-all-start.1 = ((bf16[8,160,256]{2,1,0:T(8,128)(2,1)}), bf16[8,160,256]{2,1,0:T(8,128)(2,1)S(1)}, u32[]{:S(2)}, u32[]{:S(2)}) async-start(bf16[8,160,256]{2,1,0:T(8,128)(2,1)} %bitcast.8), calls=%async_computation.1 | async-start | bytes 1310720 | tf_op jit(solution)/shard_map/all_to_all | solution.py:346
  89.3 2.4 %collective-permute-done.15 = bf16[160,512]{1,0:T(8,128)(2,1)S(1)} collective-permute-done((bf16[160,512]{1,0:T(8,128)(2,1)S(1)}, bf16[160,512]{1,0:T(8,128)(2,1)S(1)}, u32[]{:S(2)}, u32[]{:S(2)}) %collective-permute-start.15) | collective-permute-done | bytes 163872 | tf_op jit(solution)/shard_map/ppermute | solution.py:279
  91.7 2.7 %collective-permute-done.16 = bf16[160,512]{1,0:T(8,128)(2,1)S(1)} collective-permute-done((bf16[160,512]{1,0:T(8,128)(2,1)S(1)}, bf16[160,512]{1,0:T(8,128)(2,1)S(1)}, u32[]{:S(2)}, u32[]{:S(2)}) %collective-permute-start.16) | collective-permute-done | bytes 163872 | tf_op jit(solution)/shard_map/ppermute | solution.py:279
  94.5 0.9 collective-permute-start.19
  95.4 1.2 collective-permute-start.18
  96.6 0.8 collective-permute-start.17
  97.4 4.3 %all-to-all-done.1 = bf16[8,160,256]{2,1,0:T(8,128)(2,1)S(1)} async-done(((bf16[8,160,256]{2,1,0:T(8,128)(2,1)}), bf16[8,160,256]{2,1,0:T(8,128)(2,1)S(1)}, u32[]{:S(2)}, u32[]{:S(2)}) %all-to-all-start.1) | async-done | bytes 655392 | tf_op jit(solution)/shard_map/all_to_all | solution.py:346
  101.7 0.1 reduce_sum.32.k0
  101.8 2.7 %collective-permute-start.23 = (bf16[160,256]{1,0:T(8,128)(2,1)S(1)}, bf16[160,256]{1,0:T(8,128)(2,1)S(1)}, u32[]{:S(2)}, u32[]{:S(2)}) collective-permute-start(bf16[160,256]{1,0:T(8,128)(2,1)S(1)} %reduce_sum.32.k0), channel_id=1, source_target_pairs={{0,48},{16,0},{32,16},{48,32},{1,49},{17,1},{33,17},{49,33},{2,50}... | collective-permute-start | bytes 245768 | tf_op jit(solution)/shard_map/ppermute | solution.py:279
  104.5 1.1 collective-permute-start.22
  105.6 1.3 collective-permute-start.21
  106.9 0.1 collective-permute-done.23.k3
  107.1 3.4 %collective-permute-done.22.k2 = bf16[160,256]{1,0:T(8,128)(2,1)S(1)} collective-permute-done((bf16[160,256]{1,0:T(8,128)(2,1)S(1)}, bf16[160,256]{1,0:T(8,128)(2,1)S(1)}, u32[]{:S(2)}, u32[]{:S(2)}) %collective-permute-start.22) | collective-permute-done | bytes 81952 | tf_op jit(solution)/shard_map/ppermute | solution.py:279
  110.5 0.9 collective-permute-done.21.k1
  111.4 0.1 pad_maximum_fusion
  111.7 2.6 %collective-permute-done.24.grads = bf16[4,160,768]{2,1,0:T(8,128)(2,1)S(1)} collective-permute-done((bf16[4,160,768]{2,1,0:T(8,128)(2,1)S(1)}, bf16[4,160,768]{2,1,0:T(8,128)(2,1)S(1)}, u32[]{:S(2)}, u32[]{:S(2)}) %collective-permute-start.24) | collective-permute-done | bytes 983072 | tf_op jit(solution)/shard_map/ppermute | solution.py:279
  114.2 1.2 weights.1
  115.4 18.2 %all_to_all.15.parts = bf16[16,32,768]{2,1,0:T(8,128)(2,1)S(1)} all-to-all(bf16[16,32,768]{2,1,0:T(8,128)(2,1)S(1)} %weights.1), channel_id=1, replica_groups=mesh['dp'=2,'outer'=4,'x'=4,'yh'=2,'core'=2] {'dp','x','yh'}, dimensions={0} | all-to-all | bytes 1572864 | tf_op jit(solution)/shard_map/all_to_all | solution.py:362
  133.7 0.7 last_sum.1
  (52 shorter events, 0.8 us)
Async XLA Ops:
  0.6 23.8 %collective-permute-start.4 = (bf16[160,512]{1,0:T(8,128)(2,1)}, bf16[160,512]{1,0:T(8,128)(2,1)S(1)}, u32[]{:S(2)}, u32[]{:S(2)}) collective-permute-start(bf16[160,512]{1,0:T(8,128)(2,1)} %bitcast.22), channel_id=1, source_target_pairs={{0,48},{16,0},{32,16},{48,32},{1,49},{17,1},{33,17},{49,33},{2,50}... | collective-permute-start | bytes 491528 | tf_op jit(solution)/shard_map/ppermute | solution.py:279
  4.8 23.2 %collective-permute-start.3 = (bf16[160,512]{1,0:T(8,128)(2,1)}, bf16[160,512]{1,0:T(8,128)(2,1)S(1)}, u32[]{:S(2)}, u32[]{:S(2)}) collective-permute-start(bf16[160,512]{1,0:T(8,128)(2,1)} %bitcast.23), channel_id=1, source_target_pairs={{0,16},{16,32},{32,48},{48,0},{1,17},{17,33},{33,49},{49,1},{2,18}... | collective-permute-start | bytes 491528 | tf_op jit(solution)/shard_map/ppermute | solution.py:279
  4.8 2.2 %copy-start = (bf16[4096,512]{1,0:T(8,128)(2,1)S(1)}, bf16[4096,512]{1,0:T(8,128)(2,1)}, u32[]{:S(2)}) copy-start(bf16[4096,512]{1,0:T(8,128)(2,1)} %wq.1) | copy-start | bytes 12582916
  7.0 1.2 copy-start.1
  8.2 1.2 copy-start.2
  13.9 10.3 %copy-start.7 = (s32[1,8,1]{1,2,0:T(1,128)S(1)}, s32[1,8,1]{1,2,0:T(1,128)}, u32[]{:S(2)}) copy-start(s32[1,8,1]{1,2,0:T(1,128)} %constant.67.clone) | copy-start | bytes 100
  13.9 10.3 %copy-start.6 = (s32[2,1,1]{0,2,1:T(1,128)S(1)}, s32[2,1,1]{0,2,1:T(1,128)}, u32[]{:S(2)}) copy-start(s32[2,1,1]{0,2,1:T(1,128)} %constant.68.clone) | copy-start | bytes 28
  13.9 10.5 %copy-start.4 = (s32[4]{0:T(128)S(1)}, s32[4]{0:T(128)}, u32[]{:S(2)}) copy-start(s32[4]{0:T(128)} %constant.76) | copy-start | bytes 52
  13.9 14.0 %copy-start.5 = (s32[1,128]{1,0:T(1,128)S(1)}, s32[1,128]{1,0:T(1,128)}, u32[]{:S(2)}) copy-start(s32[1,128]{1,0:T(1,128)} %param.12) | copy-start | bytes 1540
  13.9 23.4 %copy-start.3 = (bf16[1,160,512]{2,1,0:T(8,128)(2,1)S(1)}, bf16[1,160,512]{2,1,0:T(8,128)(2,1)}, u32[]{:S(2)}) copy-start(bf16[1,160,512]{2,1,0:T(8,128)(2,1)} %param.16) | copy-start | bytes 491524
  13.9 14.1 %collective-permute-start.2 = (bf16[160,512]{1,0:T(8,128)(2,1)S(1)}, bf16[160,512]{1,0:T(8,128)(2,1)S(1)}, u32[]{:S(2)}, u32[]{:S(2)}) collective-permute-start(bf16[160,512]{1,0:T(8,128)(2,1)S(1)} %get-tuple-element.50.q0), channel_id=1, source_target_pairs={{0,48},{16,0},{32,16},{48,32},{1,49},{17,1},{33,17},{49,33},{2,50}... | collective-permute-start | bytes 491528 | tf_op jit(solution)/shard_map/ppermute | solution.py:279
  17.2 10.5 %collective-permute-start = (bf16[160,512]{1,0:T(8,128)(2,1)S(1)}, bf16[160,512]{1,0:T(8,128)(2,1)S(1)}, u32[]{:S(2)}, u32[]{:S(2)}) collective-permute-start(bf16[160,512]{1,0:T(8,128)(2,1)S(1)} %get-tuple-element.50.q0), channel_id=1, source_target_pairs={{0,16},{16,32},{32,48},{48,0},{1,17},{17,33},{33,49},{49,1},{2,18}... | collective-permute-start | bytes 491528 | tf_op jit(solution)/shard_map/ppermute | solution.py:279
  17.3 19.4 %collective-permute-start.6 = (bf16[160,4096]{1,0:T(8,128)(2,1)}, bf16[160,4096]{1,0:T(8,128)(2,1)S(1)}, u32[]{:S(2)}, u32[]{:S(2)}) collective-permute-start(bf16[160,4096]{1,0:T(8,128)(2,1)} %bitcast.3.tok.own), channel_id=1, source_target_pairs={{0,1},{1,0},{2,3},{3,2},{4,5},{5,4},{6,7},{7,6},{8,9},{9,8},{10,11... | collective-permute-start | bytes 3932168 | tf_op jit(solution)/shard_map/ppermute | solution.py:279
  17.3 19.4 %all-to-all-start = ((bf16[8,160,256]{2,1,0:T(8,128)(2,1)}), bf16[8,160,256]{2,1,0:T(8,128)(2,1)S(1)}, u32[]{:S(2)}, u32[]{:S(2)}) async-start(bf16[8,160,256]{2,1,0:T(8,128)(2,1)} %get-tuple-element.47), calls=%async_computation | async-start | bytes 1310720 | tf_op jit(solution)/shard_map/all_to_all | solution.py:297
  24.4 7.2 %collective-permute-start.5 = (bf16[160,512]{1,0:T(8,128)(2,1)S(1)}, bf16[160,512]{1,0:T(8,128)(2,1)S(1)}, u32[]{:S(2)}, u32[]{:S(2)}) collective-permute-start(bf16[160,512]{1,0:T(8,128)(2,1)S(1)} %collective-permute-done.4.g3), channel_id=1, source_target_pairs={{0,48},{16,0},{32,16},{48,32},{1,49},{17,1},{33,17},{49,33},{2,50}... | collective-permute-start | bytes 491528 | tf_op jit(solution)/shard_map/ppermute | solution.py:279
  27.7 7.3 %collective-permute-start.1 = (bf16[160,512]{1,0:T(8,128)(2,1)S(1)}, bf16[160,512]{1,0:T(8,128)(2,1)S(1)}, u32[]{:S(2)}, u32[]{:S(2)}) collective-permute-start(bf16[160,512]{1,0:T(8,128)(2,1)S(1)} %collective-permute-done.q1), channel_id=1, source_target_pairs={{0,16},{16,32},{32,48},{48,0},{1,17},{17,33},{33,49},{49,1},{2,18}... | collective-permute-start | bytes 491528 | tf_op jit(solution)/shard_map/ppermute | solution.py:279
  36.7 6.5 %collective-permute-start.7 = (bf16[1280,256]{1,0:T(8,128)(2,1)S(1)}, bf16[1280,256]{1,0:T(8,128)(2,1)}, u32[]{:S(2)}, u32[]{:S(2)}) collective-permute-start(bf16[1280,256]{1,0:T(8,128)(2,1)S(1)} %bitcast.19), channel_id=1, source_target_pairs={{0,1},{1,0},{2,3},{3,2},{4,5},{5,4},{6,7},{7,6},{8,9},{9,8},{10,11... | collective-permute-start | bytes 1966088 | tf_op jit(solution)/shard_map/ppermute | solution.py:279
  49.5 10.3 %collective-permute-start.10 = (f32[3,2560]{1,0:T(4,128)S(1)}, f32[3,2560]{1,0:T(4,128)S(1)}, u32[]{:S(2)}, u32[]{:S(2)}) collective-permute-start(f32[3,2560]{1,0:T(4,128)S(1)} %stats_other.1.s0), channel_id=1, source_target_pairs={{0,48},{16,0},{32,16},{48,32},{1,49},{17,1},{33,17},{49,33},{2,50}... | collective-permute-start | bytes 92168 | tf_op jit(solution)/shard_map/ppermute | solution.py:279
  52.8 8.5 %collective-permute-start.9 = (f32[3,2560]{1,0:T(4,128)S(1)}, f32[3,2560]{1,0:T(4,128)S(1)}, u32[]{:S(2)}, u32[]{:S(2)}) collective-permute-start(f32[3,2560]{1,0:T(4,128)S(1)} %stats_other.1.s0), channel_id=1, source_target_pairs={{0,32},{16,48},{32,0},{48,16},{1,33},{17,49},{33,1},{49,17},{2,34}... | collective-permute-start | bytes 92168 | tf_op jit(solution)/shard_map/ppermute | solution.py:279
  52.8 8.5 %collective-permute-start.8 = (f32[3,2560]{1,0:T(4,128)S(1)}, f32[3,2560]{1,0:T(4,128)S(1)}, u32[]{:S(2)}, u32[]{:S(2)}) collective-permute-start(f32[3,2560]{1,0:T(4,128)S(1)} %stats_other.1.s0), channel_id=1, source_target_pairs={{0,16},{16,32},{32,48},{48,0},{1,17},{17,33},{33,49},{49,1},{2,18}... | collective-permute-start | bytes 92168 | tf_op jit(solution)/shard_map/ppermute | solution.py:279
  56.0 25.6 %collective-permute-start.11 = (bf16[2,160,512]{2,1,0:T(8,128)(2,1)S(1)}, bf16[2,160,512]{2,1,0:T(8,128)(2,1)S(1)}, u32[]{:S(2)}, u32[]{:S(2)}) collective-permute-start(bf16[2,160,512]{2,1,0:T(8,128)(2,1)S(1)} %get-tuple-element.70), channel_id=1, source_target_pairs={{0,16},{16,32},{32,48},{48,0},{1,17},{17,33},{33,49},{49,1},{2,18}... | collective-permute-start | bytes 983048 | tf_op jit(solution)/shard_map/ppermute | solution.py:279
  58.6 23.0 %collective-permute-start.12 = (bf16[2,160,512]{2,1,0:T(8,128)(2,1)S(1)}, bf16[2,160,512]{2,1,0:T(8,128)(2,1)S(1)}, u32[]{:S(2)}, u32[]{:S(2)}) collective-permute-start(bf16[2,160,512]{2,1,0:T(8,128)(2,1)S(1)} %get-tuple-element.71), channel_id=1, source_target_pairs={{0,32},{16,48},{32,0},{48,16},{1,33},{17,49},{33,1},{49,17},{2,34}... | collective-permute-start | bytes 983048 | tf_op jit(solution)/shard_map/ppermute | solution.py:279
  59.8 21.8 %collective-permute-start.13 = (bf16[2,160,512]{2,1,0:T(8,128)(2,1)S(1)}, bf16[2,160,512]{2,1,0:T(8,128)(2,1)S(1)}, u32[]{:S(2)}, u32[]{:S(2)}) collective-permute-start(bf16[2,160,512]{2,1,0:T(8,128)(2,1)S(1)} %get-tuple-element.72), channel_id=1, source_target_pairs={{0,48},{16,0},{32,16},{48,32},{1,49},{17,1},{33,17},{49,33},{2,50}... | collective-permute-start | bytes 983048 | tf_op jit(solution)/shard_map/ppermute | solution.py:279
  81.6 2.7 %collective-permute-start.20 = (bf16[1280,256]{1,0:T(8,128)(2,1)S(1)}, bf16[1280,256]{1,0:T(8,128)(2,1)S(1)}, u32[]{:S(2)}, u32[]{:S(2)}) collective-permute-start(bf16[1280,256]{1,0:T(8,128)(2,1)S(1)} %get-tuple-element.82), channel_id=1, source_target_pairs={{0,1},{1,0},{2,3},{3,2},{4,5},{5,4},{6,7},{7,6},{8,9},{9,8},{10,11... | collective-permute-start | bytes 1966088 | tf_op jit(solution)/shard_map/ppermute | solution.py:279
  81.7 7.6 %collective-permute-start.14 = (bf16[160,512]{1,0:T(8,128)(2,1)S(1)}, bf16[160,512]{1,0:T(8,128)(2,1)S(1)}, u32[]{:S(2)}, u32[]{:S(2)}) collective-permute-start(bf16[160,512]{1,0:T(8,128)(2,1)S(1)} %get-tuple-element.78), channel_id=1, source_target_pairs={{0,48},{16,0},{32,16},{48,32},{1,49},{17,1},{33,17},{49,33},{2,50}... | collective-permute-start | bytes 491528 | tf_op jit(solution)/shard_map/ppermute | solution.py:279
  83.1 8.6 %collective-permute-start.15 = (bf16[160,512]{1,0:T(8,128)(2,1)S(1)}, bf16[160,512]{1,0:T(8,128)(2,1)S(1)}, u32[]{:S(2)}, u32[]{:S(2)}) collective-permute-start(bf16[160,512]{1,0:T(8,128)(2,1)S(1)} %get-tuple-element.79), channel_id=1, source_target_pairs={{0,32},{16,48},{32,0},{48,16},{1,33},{17,49},{33,1},{49,17},{2,34}... | collective-permute-start | bytes 491528 | tf_op jit(solution)/shard_map/ppermute | solution.py:279
  84.3 10.1 %collective-permute-start.16 = (bf16[160,512]{1,0:T(8,128)(2,1)S(1)}, bf16[160,512]{1,0:T(8,128)(2,1)S(1)}, u32[]{:S(2)}, u32[]{:S(2)}) collective-permute-start(bf16[160,512]{1,0:T(8,128)(2,1)S(1)} %get-tuple-element.80), channel_id=1, source_target_pairs={{0,16},{16,32},{32,48},{48,0},{1,17},{17,33},{33,49},{49,1},{2,18}... | collective-permute-start | bytes 491528 | tf_op jit(solution)/shard_map/ppermute | solution.py:279
  85.3 16.4 %all-to-all-start.1 = ((bf16[8,160,256]{2,1,0:T(8,128)(2,1)}), bf16[8,160,256]{2,1,0:T(8,128)(2,1)S(1)}, u32[]{:S(2)}, u32[]{:S(2)}) async-start(bf16[8,160,256]{2,1,0:T(8,128)(2,1)} %bitcast.8), calls=%async_computation.1 | async-start | bytes 1310720 | tf_op jit(solution)/shard_map/all_to_all | solution.py:346
  94.5 11.2 %collective-permute-start.19 = (bf16[160,512]{1,0:T(8,128)(2,1)S(1)}, bf16[160,512]{1,0:T(8,128)(2,1)S(1)}, u32[]{:S(2)}, u32[]{:S(2)}) collective-permute-start(bf16[160,512]{1,0:T(8,128)(2,1)S(1)} %add_convert_fusion.1.q0), channel_id=1, source_target_pairs={{0,48},{16,0},{32,16},{48,32},{1,49},{17,1},{33,17},{49,33},{2,50}... | collective-permute-start | bytes 491528 | tf_op jit(solution)/shard_map/ppermute | solution.py:279
  95.4 11.6 %collective-permute-start.18 = (bf16[160,512]{1,0:T(8,128)(2,1)S(1)}, bf16[160,512]{1,0:T(8,128)(2,1)S(1)}, u32[]{:S(2)}, u32[]{:S(2)}) collective-permute-start(bf16[160,512]{1,0:T(8,128)(2,1)S(1)} %add_convert_fusion.1.q0), channel_id=1, source_target_pairs={{0,32},{16,48},{32,0},{48,16},{1,33},{17,49},{33,1},{49,17},{2,34}... | collective-permute-start | bytes 491528 | tf_op jit(solution)/shard_map/ppermute | solution.py:279
  96.6 10.4 %collective-permute-start.17 = (bf16[160,512]{1,0:T(8,128)(2,1)S(1)}, bf16[160,512]{1,0:T(8,128)(2,1)S(1)}, u32[]{:S(2)}, u32[]{:S(2)}) collective-permute-start(bf16[160,512]{1,0:T(8,128)(2,1)S(1)} %add_convert_fusion.1.q0), channel_id=1, source_target_pairs={{0,16},{16,32},{32,48},{48,0},{1,17},{17,33},{33,49},{49,1},{2,18}... | collective-permute-start | bytes 491528 | tf_op jit(solution)/shard_map/ppermute | solution.py:279
  101.8 5.3 %collective-permute-start.23 = (bf16[160,256]{1,0:T(8,128)(2,1)S(1)}, bf16[160,256]{1,0:T(8,128)(2,1)S(1)}, u32[]{:S(2)}, u32[]{:S(2)}) collective-permute-start(bf16[160,256]{1,0:T(8,128)(2,1)S(1)} %reduce_sum.32.k0), channel_id=1, source_target_pairs={{0,48},{16,0},{32,16},{48,32},{1,49},{17,1},{33,17},{49,33},{2,50}... | collective-permute-start | bytes 245768 | tf_op jit(solution)/shard_map/ppermute | solution.py:279
  104.5 6.0 %collective-permute-start.22 = (bf16[160,256]{1,0:T(8,128)(2,1)S(1)}, bf16[160,256]{1,0:T(8,128)(2,1)S(1)}, u32[]{:S(2)}, u32[]{:S(2)}) collective-permute-start(bf16[160,256]{1,0:T(8,128)(2,1)S(1)} %reduce_sum.32.k0), channel_id=1, source_target_pairs={{0,32},{16,48},{32,0},{48,16},{1,33},{17,49},{33,1},{49,17},{2,34}... | collective-permute-start | bytes 245768 | tf_op jit(solution)/shard_map/ppermute | solution.py:279
  105.6 5.7 %collective-permute-start.21 = (bf16[160,256]{1,0:T(8,128)(2,1)S(1)}, bf16[160,256]{1,0:T(8,128)(2,1)S(1)}, u32[]{:S(2)}, u32[]{:S(2)}) collective-permute-start(bf16[160,256]{1,0:T(8,128)(2,1)S(1)} %reduce_sum.32.k0), channel_id=1, source_target_pairs={{0,16},{16,32},{32,48},{48,0},{1,17},{17,33},{33,49},{49,1},{2,18}... | collective-permute-start | bytes 245768 | tf_op jit(solution)/shard_map/ppermute | solution.py:279
  111.6 2.6 %collective-permute-start.24 = (bf16[4,160,768]{2,1,0:T(8,128)(2,1)S(1)}, bf16[4,160,768]{2,1,0:T(8,128)(2,1)S(1)}, u32[]{:S(2)}, u32[]{:S(2)}) collective-permute-start(bf16[4,160,768]{2,1,0:T(8,128)(2,1)S(1)} %pad_maximum_fusion), channel_id=1, source_target_pairs={{0,1},{1,0},{2,3},{3,2},{4,5},{5,4},{6,7},{7,6},{8,9},{9,8},{10,11... | collective-permute-start | bytes 2949128 | tf_op jit(solution)/shard_map/ppermute | solution.py:279

commit v12 on v8

--- a/solution.py
+++ b/solution.py
@@ -101,8 +101,25 @@
     stats_pass(0, ordk, posq, qr, gr, kva, None, out)
 
 
-def stats_other(ordk, posq, qr, gr, kvb, before, out):
+def pick_columns(place_ref, own, other, xs):
+    ic = place_ref[1]
+    src = lax.broadcasted_iota(jnp.int32, (512, 256), 0)
+    dst = lax.broadcasted_iota(jnp.int32, (512, 256), 1)
+    home = dst // 32 * 64 + dst % 32 + ic * 32
+    pick = jnp.where(src == home, 1.0, 0.0).astype(bf16)
+    for d, out in enumerate(xs):
+        base = lax.rem(place_ref[0] + d, N_OUT) * 512
+        for t, tok in enumerate((own, other)):
+            for p in range(2):
+                cols = tok[:, pl.ds(pl.multiple_of(base + p * 2048, 512), 512)]
+                out[t, :, p * 256 : (p + 1) * 256] = dot(cols, pick, NN).astype(bf16)
+
+
+def stats_other(
+    ordk, place, posq, qr, gr, kvb, before, own, other, out, x0, x1, x2, x3
+):
     stats_pass(KHALF // HALF, ordk, posq, qr, gr, kvb, before, out)
+    pick_columns(place, own, other, (x0, x1, x2, x3))
 
 
 def combine_stats(stats, rowstat_ref):
@@ -165,20 +182,6 @@
         out[:, HEAD:] = dkv[k0 : k0 + KHALF, HEAD:].astype(out.dtype)
 
 
-def columns_kernel(place_ref, own, other, x0, x1, x2, x3):
-    ic = place_ref[1]
-    src = lax.broadcasted_iota(jnp.int32, (512, 256), 0)
-    dst = lax.broadcasted_iota(jnp.int32, (512, 256), 1)
-    home = dst // 32 * 64 + dst % 32 + ic * 32
-    pick = jnp.where(src == home, 1.0, 0.0).astype(bf16)
-    for d, out in enumerate((x0, x1, x2, x3)):
-        base = lax.rem(place_ref[0] + d, N_OUT) * 512
-        for t, tok in enumerate((own, other)):
-            for p in range(2):
-                cols = tok[:, pl.ds(pl.multiple_of(base + p * 2048, 512), 512)]
-                out[t, :, p * 256 : (p + 1) * 256] = dot(cols, pick, NN).astype(bf16)
-
-
 def weights_kernel(x0, x1, x2, x3, q0, q1, q2, q3, k0, k1, k2, k3, grads, out, xr, gr):
     wide = HEADS * HEAD
     for d, x in enumerate((x0, x1, x2, x3)):
@@ -260,7 +263,6 @@
     kva = jnp.broadcast_to(kv[None], (8,) + kv.shape)
     kva = lax.all_to_all(kva, ("x", "yh"), 0, 0, tiled=True).reshape(KHALF, 2 * HEAD)
     other_tokens = shift(tokens, "core", 1, 2)
-    later = tokens
     kva, qs, gs, other_tokens = lax.optimization_barrier((kva, qs, gs, other_tokens))
     kvb = shift(kva, "core", 1, 2)
 
@@ -285,13 +287,10 @@
         stats_own, "stats_own", row_stats + [rows, rows], [], pairs, [smem],
         ordk, posq, *qs, *gs, kva,
     )
-    (stats,) = kernel_call(
-        stats_other, "stats_other", row_stats, [], pairs, [smem], ordk, posq, qr, gr, kvb, stats
-    )
-    later, other_tokens, stats = lax.optimization_barrier((later, other_tokens, stats))
-    xs = kernel_call(
-        columns_kernel, "columns", [((2, ROWS, 512), bf16)] * N_OUT, [],
-        cost(ROWS * 4096, 4, 5 << 20), [smem], jnp.stack([o, ic]), later, other_tokens,
+    stats, *xs = kernel_call(
+        stats_other, "stats_other", row_stats + [((2, ROWS, 512), bf16)] * N_OUT, [], pairs,
+        [smem, smem],
+        ordk, jnp.stack([o, ic]), posq, qr, gr, kvb, stats, tokens, other_tokens,
     )
     xs = [xs[0]] + [shift(xs[d], "outer", d, N_OUT) for d in range(1, N_OUT)]
     all_stats = from_behind(stats, "outer", N_OUT)

time: 133 us -> 131 us (0.985)
    pallas_call x6 -> x5, Pallas kernels: 38 us -> 37.1 us  [kernel_call(): pl.pallas_call(body, out_shape=tuple((jax.ShapeDtypeStruct(*o) for o in o...]
  transfers between devices with their start and end apart: 27 -> 27, of which waited for: 10 -> 10; matrix products, arithmetic and copies ran while one was open for 4% -> 4% of each run, Pallas kernels for 22% -> 21%
where the time goes in v12:
time: 131 us
  starting transfers between devices  42.2 us (32%)
  Pallas kernels  37.1 us (28%)
  waiting for transfers between devices  23.2 us (18%)
  blocking collectives  18.2 us (14%)
  matrix products  4.59 us (4%)
  other arithmetic  3.22 us (2%)
  local copies, waits for them, and re-layouts  1.31 us (1%)
    pallas_call x5, Pallas kernels, kernel_call(): pl.pallas_call(body, out_shape=tuple((jax.ShapeDtypeStruct(*o) for o in o...  37.1 us
    ppermute x25, starting transfers between devices, shift(): return lax.ppermute(x, axis, [(i, (i + d) % n) for i in range(n)])  30.9 us
    all_to_all x1, blocking collectives, per_device(): dw = lax.all_to_all(dw, ('dp', 'x', 'yh'), 0, 0, tiled=True)  18.2 us
    ppermute x25, waiting for transfers between devices, shift(): return lax.ppermute(x, axis, [(i, (i + d) % n) for i in range(n)])  16.7 us
    all_to_all x1, starting transfers between devices, per_device(): lax.all_to_all(kva, ('x', 'yh'), 0, 0, tiled=True).reshape(KHALF, 2 * HEAD)  6.93 us
    dot_general x3, matrix products, dot(): return lax.dot_general(a, b, dims, preferred_element_type=f32)  4.59 us
    all_to_all x1, starting transfers between devices, per_device(): dkv = lax.all_to_all(dkv, ('x', 'yh'), 0, 0, tiled=True)  4.34 us
    all_to_all x1, waiting for transfers between devices, per_device(): dkv = lax.all_to_all(dkv, ('x', 'yh'), 0, 0, tiled=True)  3.79 us
  transfers between devices with their start and end apart: 27, of which 10 were waited for; matrix products, arithmetic and copies ran while one was open for 4% of the time, Pallas kernels for 21%

profile of v12, /device:TPU:0, one launch (start us, length us, event | category | flops | bytes accessed | tf_op | source)
XLA Modules:
  0.0 130.9 jit_solution(16884885591467875625)
XLA Ops:
  0.7 3.6 %convolution_convert_fusion.q0 = bf16[160,512]{1,0:T(8,128)(2,1)S(1)} fusion(bf16[4096,512]{1,0:T(8,128)(2,1)} %param.13, bf16[1,160,4096]{2,1,0:T(8,128)(2,1)} %param.11), kind=kOutput, calls=%fused_computation.1 | convolution fusion | flops 671170560 | bytes 5668864 | tf_op jit(solution)/shard_map/dot_general | solution.py:36
  4.3 4.2 %collective-permute-start.2 = (bf16[160,512]{1,0:T(8,128)(2,1)S(1)}, bf16[160,512]{1,0:T(8,128)(2,1)S(1)}, u32[]{:S(2)}, u32[]{:S(2)}) collective-permute-start(bf16[160,512]{1,0:T(8,128)(2,1)S(1)} %convolution_convert_fusion.q0), channel_id=1, source_target_pairs={{0,48},{16,0},{32,16},{48,32},{1,49},{17,1},{33,17},{49,33},{2,50}... | collective-permute-start | bytes 491528 | tf_op jit(solution)/shard_map/ppermute | solution.py:238
  8.5 3.2 %collective-permute-start.4 = (bf16[160,512]{1,0:T(8,128)(2,1)S(1)}, bf16[160,512]{1,0:T(8,128)(2,1)}, u32[]{:S(2)}, u32[]{:S(2)}) collective-permute-start(bf16[160,512]{1,0:T(8,128)(2,1)S(1)} %bitcast.33), channel_id=1, source_target_pairs={{0,48},{16,0},{32,16},{48,32},{1,49},{17,1},{33,17},{49,33},{2,50}... | collective-permute-start | bytes 491528 | tf_op jit(solution)/shard_map/ppermute | solution.py:238
  11.7 0.5 convolution_convert_fusion.2
  12.2 0.5 convolution_convert_fusion.1
  12.8 0.9 broadcast_in_dim.47
  13.7 6.9 %all-to-all-start = ((bf16[8,160,256]{2,1,0:T(8,128)(2,1)}), bf16[8,160,256]{2,1,0:T(8,128)(2,1)S(1)}, u32[]{:S(2)}, u32[]{:S(2)}) async-start(bf16[8,160,256]{2,1,0:T(8,128)(2,1)} %broadcast_in_dim.47), calls=%async_computation | async-start | bytes 1310720 | tf_op jit(solution)/shard_map/all_to_all | solution.py:264
  21.0 3.3 %collective-permute-start.5 = (bf16[160,512]{1,0:T(8,128)(2,1)}, bf16[160,512]{1,0:T(8,128)(2,1)}, u32[]{:S(2)}, u32[]{:S(2)}) collective-permute-start(bf16[160,512]{1,0:T(8,128)(2,1)} %collective-permute-done.4.g3), channel_id=1, source_target_pairs={{0,48},{16,0},{32,16},{48,32},{1,49},{17,1},{33,17},{49,33},{2,50}... | collective-permute-start | bytes 491528 | tf_op jit(solution)/shard_map/ppermute | solution.py:238
  24.3 0.1 add.164
  24.4 0.2 select_reduce_fusion.1
  24.6 4.7 %collective-permute-done.1.q2 = bf16[160,512]{1,0:T(8,128)(2,1)} collective-permute-done((bf16[160,512]{1,0:T(8,128)(2,1)}, bf16[160,512]{1,0:T(8,128)(2,1)}, u32[]{:S(2)}, u32[]{:S(2)}) %collective-permute-start.1) | collective-permute-done | bytes 163872 | tf_op jit(solution)/shard_map/ppermute | solution.py:238
  29.3 2.7 %all-to-all-done = bf16[8,160,256]{2,1,0:T(8,128)(2,1)S(1)} async-done(((bf16[8,160,256]{2,1,0:T(8,128)(2,1)}), bf16[8,160,256]{2,1,0:T(8,128)(2,1)S(1)}, u32[]{:S(2)}, u32[]{:S(2)}) %all-to-all-start) | async-done | bytes 655392 | tf_op jit(solution)/shard_map/all_to_all | solution.py:264
  32.1 0.1 add.152
  32.3 0.1 reshape.101.posq.posq_ref
  32.5 0.2 select_reduce_fusion.ordk
  32.7 6.9 %stats_own.1 = (f32[3,2560]{1,0:T(4,128)S(1)}, bf16[2560,128]{1,0:T(8,128)(2,1)S(1)}, bf16[2560,128]{1,0:T(8,128)(2,1)S(1)}) custom-call(s32[32]{0:T(128)S(1)} %select_reduce_fusion.ordk, s32[1,2560]{1,0:T(1,128)S(1)} %reshape.101.posq.posq_ref, bf16[160,512]{1,0:T(8,128)(2,1)S(1)} %convolution_convert_fusion.q0, bf16[160,512]{1,0:T(8,128)(2,1)} %collective-permute-done.q1, ...), custom_call_target="tpu_custom_call" | custom-call | flops 1677721600 | bytes 4194304 | tf_op jit(solution)/shard_map/stats_own/pallas_call | solution.py:221
  39.6 7.9 %stats_other.1 = (f32[3,2560]{1,0:T(4,128)S(1)}, bf16[2,160,512]{2,1,0:T(8,128)(2,1)S(1)}, bf16[2,160,512]{2,1,0:T(8,128)(2,1)S(1)}, bf16[2,160,512]{2,1,0:T(8,128)(2,1)S(1)}, bf16[2,160,512]{2,1,0:T(8,128)(2,1)S(1)}) custom-call(s32[32]{0:T(128)S(1)} %select_reduce_fusion.ordk, s32[2]{0:T(128)S(1)} %pad_add_fusion.place, ...), custom_call_target="tpu_custom_call" | custom-call | flops 1677721600 | bytes 4194304 | tf_op jit(solution)/shard_map/stats_other/pallas_call | solution.py:221
  47.5 3.3 %collective-permute-start.10 = (f32[3,2560]{1,0:T(4,128)S(1)}, f32[3,2560]{1,0:T(4,128)S(1)}, u32[]{:S(2)}, u32[]{:S(2)}) collective-permute-start(f32[3,2560]{1,0:T(4,128)S(1)} %get-tuple-element.56.s0), channel_id=1, source_target_pairs={{0,48},{16,0},{32,16},{48,32},{1,49},{17,1},{33,17},{49,33},{2,50}... | collective-permute-start | bytes 92168 | tf_op jit(solution)/shard_map/ppermute | solution.py:238
  50.8 0.9 collective-permute-start.8
  51.7 2.5 %collective-permute-start.11 = (bf16[2,160,512]{2,1,0:T(8,128)(2,1)S(1)}, bf16[2,160,512]{2,1,0:T(8,128)(2,1)S(1)}, u32[]{:S(2)}, u32[]{:S(2)}) collective-permute-start(bf16[2,160,512]{2,1,0:T(8,128)(2,1)S(1)} %get-tuple-element.62), channel_id=1, source_target_pairs={{0,16},{16,32},{32,48},{48,0},{1,17},{17,33},{33,49},{49,1},{2,18}... | collective-permute-start | bytes 983048 | tf_op jit(solution)/shard_map/ppermute | solution.py:238
  54.2 1.2 collective-permute-start.12
  55.5 1.5 %collective-permute-start.13 = (bf16[2,160,512]{2,1,0:T(8,128)(2,1)S(1)}, bf16[2,160,512]{2,1,0:T(8,128)(2,1)S(1)}, u32[]{:S(2)}, u32[]{:S(2)}) collective-permute-start(bf16[2,160,512]{2,1,0:T(8,128)(2,1)S(1)} %get-tuple-element.64), channel_id=1, source_target_pairs={{0,48},{16,0},{32,16},{48,32},{1,49},{17,1},{33,17},{49,33},{2,50}... | collective-permute-start | bytes 983048 | tf_op jit(solution)/shard_map/ppermute | solution.py:238
  57.0 20.4 %grads.1 = (f32[160,512]{1,0:T(8,128)S(1)}, bf16[160,512]{1,0:T(8,128)(2,1)S(1)}, bf16[160,512]{1,0:T(8,128)(2,1)S(1)}, bf16[160,512]{1,0:T(8,128)(2,1)S(1)}, f3...) custom-call(s32[32]{0:T(128)S(1)} %select_reduce_fusion.ordk, s32[1,2560]{1,0:T(1,128)S(1)} %reshape.101.posq.posq_ref, ...), custom_call_target="tpu_custom_call" | custom-call | flops 8388608000 | bytes 8388608 | tf_op jit(solution)/shard_map/grads/pallas_call | solution.py:221
  77.5 1.5 %collective-permute-start.14 = (bf16[160,512]{1,0:T(8,128)(2,1)S(1)}, bf16[160,512]{1,0:T(8,128)(2,1)}, u32[]{:S(2)}, u32[]{:S(2)}) collective-permute-start(bf16[160,512]{1,0:T(8,128)(2,1)S(1)} %get-tuple-element.70), channel_id=1, source_target_pairs={{0,48},{16,0},{32,16},{48,32},{1,49},{17,1},{33,17},{49,33},{2,50}... | collective-permute-start | bytes 491528 | tf_op jit(solution)/shard_map/ppermute | solution.py:238
  79.0 1.2 collective-permute-start.15
  80.2 0.6 collective-permute-start.16
  80.8 1.0 add_convert_fusion
  81.8 4.3 %all-to-all-start.1 = ((bf16[8,160,256]{2,1,0:T(8,128)(2,1)}), bf16[8,160,256]{2,1,0:T(8,128)(2,1)S(1)}, u32[]{:S(2)}, u32[]{:S(2)}) async-start(bf16[8,160,256]{2,1,0:T(8,128)(2,1)} %bitcast.8), calls=%async_computation.1 | async-start | bytes 1310720 | tf_op jit(solution)/shard_map/all_to_all | solution.py:309
  86.1 1.5 %collective-permute-done.15 = bf16[160,512]{1,0:T(8,128)(2,1)} collective-permute-done((bf16[160,512]{1,0:T(8,128)(2,1)S(1)}, bf16[160,512]{1,0:T(8,128)(2,1)}, u32[]{:S(2)}, u32[]{:S(2)}) %collective-permute-start.15) | collective-permute-done | bytes 163872 | tf_op jit(solution)/shard_map/ppermute | solution.py:238
  87.7 2.7 %collective-permute-done.16 = bf16[160,512]{1,0:T(8,128)(2,1)} collective-permute-done((bf16[160,512]{1,0:T(8,128)(2,1)S(1)}, bf16[160,512]{1,0:T(8,128)(2,1)}, u32[]{:S(2)}, u32[]{:S(2)}) %collective-permute-start.16) | collective-permute-done | bytes 163872 | tf_op jit(solution)/shard_map/ppermute | solution.py:238
  90.4 1.2 add_convert_fusion.1.q0
  91.5 0.7 collective-permute-start.19
  92.2 1.2 collective-permute-start.18
  93.4 0.8 collective-permute-start.17
  94.2 3.8 %all-to-all-done.1 = bf16[8,160,256]{2,1,0:T(8,128)(2,1)S(1)} async-done(((bf16[8,160,256]{2,1,0:T(8,128)(2,1)}), bf16[8,160,256]{2,1,0:T(8,128)(2,1)S(1)}, u32[]{:S(2)}, u32[]{:S(2)}) %all-to-all-start.1) | async-done | bytes 655392 | tf_op jit(solution)/shard_map/all_to_all | solution.py:309
  98.0 0.1 reduce_sum.32.k0
  98.1 2.9 %collective-permute-start.23 = (bf16[160,256]{1,0:T(8,128)(2,1)S(1)}, bf16[160,256]{1,0:T(8,128)(2,1)S(1)}, u32[]{:S(2)}, u32[]{:S(2)}) collective-permute-start(bf16[160,256]{1,0:T(8,128)(2,1)S(1)} %reduce_sum.32.k0), channel_id=1, source_target_pairs={{0,48},{16,0},{32,16},{48,32},{1,49},{17,1},{33,17},{49,33},{2,50}... | collective-permute-start | bytes 245768 | tf_op jit(solution)/shard_map/ppermute | solution.py:238
  101.0 0.9 collective-permute-start.22
  101.9 0.7 collective-permute-start.21
  102.6 0.2 collective-permute-done.17.q1
  102.8 1.0 collective-permute-done.23.k3
  103.8 3.1 %collective-permute-done.22.k2 = bf16[160,256]{1,0:T(8,128)(2,1)S(1)} collective-permute-done((bf16[160,256]{1,0:T(8,128)(2,1)S(1)}, bf16[160,256]{1,0:T(8,128)(2,1)S(1)}, u32[]{:S(2)}, u32[]{:S(2)}) %collective-permute-start.22) | collective-permute-done | bytes 81952 | tf_op jit(solution)/shard_map/ppermute | solution.py:238
  107.0 0.9 collective-permute-done.21.k1
  107.9 0.1 pad_maximum_fusion
  108.1 2.6 %collective-permute-done.24.grads = bf16[4,160,768]{2,1,0:T(8,128)(2,1)S(1)} collective-permute-done((bf16[4,160,768]{2,1,0:T(8,128)(2,1)S(1)}, bf16[4,160,768]{2,1,0:T(8,128)(2,1)S(1)}, u32[]{:S(2)}, u32[]{:S(2)}) %collective-permute-start.24) | collective-permute-done | bytes 983072 | tf_op jit(solution)/shard_map/ppermute | solution.py:238
  110.7 1.2 weights.1
  111.9 18.2 %all_to_all.15.parts = bf16[16,32,768]{2,1,0:T(8,128)(2,1)S(1)} all-to-all(bf16[16,32,768]{2,1,0:T(8,128)(2,1)S(1)} %weights.1), channel_id=1, replica_groups=mesh['dp'=2,'outer'=4,'x'=4,'yh'=2,'core'=2] {'dp','x','yh'}, dimensions={0} | all-to-all | bytes 1572864 | tf_op jit(solution)/shard_map/all_to_all | solution.py:325
  130.2 0.7 last_sum.1
  (63 shorter events, 0.9 us)
Async XLA Ops:
  0.6 11.1 %copy-start = (bf16[4096,128]{1,0:T(8,128)(2,1)S(1)}, bf16[4096,128]{1,0:T(8,128)(2,1)}, u32[]{:S(2)}) copy-start(bf16[4096,128]{1,0:T(8,128)(2,1)} %param.14) | copy-start | bytes 3145732
  0.6 11.1 %copy-start.1 = (bf16[1,160,4096]{2,1,0:T(8,128)(2,1)S(1)}, bf16[1,160,4096]{2,1,0:T(8,128)(2,1)}, u32[]{:S(2)}) copy-start(bf16[1,160,4096]{2,1,0:T(8,128)(2,1)} %param.11) | copy-start | bytes 3932164
  0.7 7.8 %copy-start.6 = (bf16[1,160,512]{2,1,0:T(8,128)(2,1)S(1)}, bf16[1,160,512]{2,1,0:T(8,128)(2,1)}, u32[]{:S(2)}) copy-start(bf16[1,160,512]{2,1,0:T(8,128)(2,1)} %param.16) | copy-start | bytes 491524
  4.3 8.0 %copy-start.7 = (bf16[4096,128]{1,0:T(8,128)(2,1)S(1)}, bf16[4096,128]{1,0:T(8,128)(2,1)}, u32[]{:S(2)}) copy-start(bf16[4096,128]{1,0:T(8,128)(2,1)} %param.15) | copy-start | bytes 3145732
  4.3 20.3 %collective-permute-start.2 = (bf16[160,512]{1,0:T(8,128)(2,1)S(1)}, bf16[160,512]{1,0:T(8,128)(2,1)S(1)}, u32[]{:S(2)}, u32[]{:S(2)}) collective-permute-start(bf16[160,512]{1,0:T(8,128)(2,1)S(1)} %convolution_convert_fusion.q0), channel_id=1, source_target_pairs={{0,48},{16,0},{32,16},{48,32},{1,49},{17,1},{33,17},{49,33},{2,50}... | collective-permute-start | bytes 491528 | tf_op jit(solution)/shard_map/ppermute | solution.py:238
  8.5 12.4 %collective-permute-start = (bf16[160,512]{1,0:T(8,128)(2,1)S(1)}, bf16[160,512]{1,0:T(8,128)(2,1)}, u32[]{:S(2)}, u32[]{:S(2)}) collective-permute-start(bf16[160,512]{1,0:T(8,128)(2,1)S(1)} %convolution_convert_fusion.q0), channel_id=1, source_target_pairs={{0,16},{16,32},{32,48},{48,0},{1,17},{17,33},{33,49},{49,1},{2,18}... | collective-permute-start | bytes 491528 | tf_op jit(solution)/shard_map/ppermute | solution.py:238
  8.5 12.5 %collective-permute-start.4 = (bf16[160,512]{1,0:T(8,128)(2,1)S(1)}, bf16[160,512]{1,0:T(8,128)(2,1)}, u32[]{:S(2)}, u32[]{:S(2)}) collective-permute-start(bf16[160,512]{1,0:T(8,128)(2,1)S(1)} %bitcast.33), channel_id=1, source_target_pairs={{0,48},{16,0},{32,16},{48,32},{1,49},{17,1},{33,17},{49,33},{2,50}... | collective-permute-start | bytes 491528 | tf_op jit(solution)/shard_map/ppermute | solution.py:238
  11.7 12.9 %collective-permute-start.3 = (bf16[160,512]{1,0:T(8,128)(2,1)S(1)}, bf16[160,512]{1,0:T(8,128)(2,1)}, u32[]{:S(2)}, u32[]{:S(2)}) collective-permute-start(bf16[160,512]{1,0:T(8,128)(2,1)S(1)} %bitcast.34), channel_id=1, source_target_pairs={{0,16},{16,32},{32,48},{48,0},{1,17},{17,33},{33,49},{49,1},{2,18}... | collective-permute-start | bytes 491528 | tf_op jit(solution)/shard_map/ppermute | solution.py:238
  12.7 7.9 %copy-start.11 = (s32[1,8,1]{1,2,0:T(1,128)S(1)}, s32[1,8,1]{1,2,0:T(1,128)}, u32[]{:S(2)}) copy-start(s32[1,8,1]{1,2,0:T(1,128)} %constant.67.clone) | copy-start | bytes 100
  12.8 7.9 %copy-start.10 = (s32[2,1,1]{0,2,1:T(1,128)S(1)}, s32[2,1,1]{0,2,1:T(1,128)}, u32[]{:S(2)}) copy-start(s32[2,1,1]{0,2,1:T(1,128)} %constant.68.clone) | copy-start | bytes 28
  12.8 8.1 %copy-start.8 = (s32[4]{0:T(128)S(1)}, s32[4]{0:T(128)}, u32[]{:S(2)}) copy-start(s32[4]{0:T(128)} %constant.76) | copy-start | bytes 52
  12.8 11.6 %copy-start.9 = (s32[1,128]{1,0:T(1,128)S(1)}, s32[1,128]{1,0:T(1,128)}, u32[]{:S(2)}) copy-start(s32[1,128]{1,0:T(1,128)} %param.12) | copy-start | bytes 1540
  13.7 18.3 %all-to-all-start = ((bf16[8,160,256]{2,1,0:T(8,128)(2,1)}), bf16[8,160,256]{2,1,0:T(8,128)(2,1)S(1)}, u32[]{:S(2)}, u32[]{:S(2)}) async-start(bf16[8,160,256]{2,1,0:T(8,128)(2,1)} %broadcast_in_dim.47), calls=%async_computation | async-start | bytes 1310720 | tf_op jit(solution)/shard_map/all_to_all | solution.py:264
  20.6 11.4 %collective-permute-start.6 = (bf16[160,4096]{1,0:T(8,128)(2,1)S(1)}, bf16[160,4096]{1,0:T(8,128)(2,1)}, u32[]{:S(2)}, u32[]{:S(2)}) collective-permute-start(bf16[160,4096]{1,0:T(8,128)(2,1)S(1)} %bitcast.28), channel_id=1, source_target_pairs={{0,1},{1,0},{2,3},{3,2},{4,5},{5,4},{6,7},{7,6},{8,9},{9,8},{10,11... | collective-permute-start | bytes 3932168 | tf_op jit(solution)/shard_map/ppermute | solution.py:238
  20.9 8.4 %collective-permute-start.1 = (bf16[160,512]{1,0:T(8,128)(2,1)}, bf16[160,512]{1,0:T(8,128)(2,1)}, u32[]{:S(2)}, u32[]{:S(2)}) collective-permute-start(bf16[160,512]{1,0:T(8,128)(2,1)} %collective-permute-done.q1), channel_id=1, source_target_pairs={{0,16},{16,32},{32,48},{48,0},{1,17},{17,33},{33,49},{49,1},{2,18}... | collective-permute-start | bytes 491528 | tf_op jit(solution)/shard_map/ppermute | solution.py:238
  21.0 8.4 %collective-permute-start.5 = (bf16[160,512]{1,0:T(8,128)(2,1)}, bf16[160,512]{1,0:T(8,128)(2,1)}, u32[]{:S(2)}, u32[]{:S(2)}) collective-permute-start(bf16[160,512]{1,0:T(8,128)(2,1)} %collective-permute-done.4.g3), channel_id=1, source_target_pairs={{0,48},{16,0},{32,16},{48,32},{1,49},{17,1},{33,17},{49,33},{2,50}... | collective-permute-start | bytes 491528 | tf_op jit(solution)/shard_map/ppermute | solution.py:238
  32.0 7.5 %collective-permute-start.7 = (bf16[1280,256]{1,0:T(8,128)(2,1)S(1)}, bf16[1280,256]{1,0:T(8,128)(2,1)}, u32[]{:S(2)}, u32[]{:S(2)}) collective-permute-start(bf16[1280,256]{1,0:T(8,128)(2,1)S(1)} %bitcast.30), channel_id=1, source_target_pairs={{0,1},{1,0},{2,3},{3,2},{4,5},{5,4},{6,7},{7,6},{8,9},{9,8},{10,11... | collective-permute-start | bytes 1966088 | tf_op jit(solution)/shard_map/ppermute | solution.py:238
  47.5 8.0 %collective-permute-start.10 = (f32[3,2560]{1,0:T(4,128)S(1)}, f32[3,2560]{1,0:T(4,128)S(1)}, u32[]{:S(2)}, u32[]{:S(2)}) collective-permute-start(f32[3,2560]{1,0:T(4,128)S(1)} %get-tuple-element.56.s0), channel_id=1, source_target_pairs={{0,48},{16,0},{32,16},{48,32},{1,49},{17,1},{33,17},{49,33},{2,50}... | collective-permute-start | bytes 92168 | tf_op jit(solution)/shard_map/ppermute | solution.py:238
  50.8 6.2 %collective-permute-start.9 = (f32[3,2560]{1,0:T(4,128)S(1)}, f32[3,2560]{1,0:T(4,128)S(1)}, u32[]{:S(2)}, u32[]{:S(2)}) collective-permute-start(f32[3,2560]{1,0:T(4,128)S(1)} %get-tuple-element.56.s0), channel_id=1, source_target_pairs={{0,32},{16,48},{32,0},{48,16},{1,33},{17,49},{33,1},{49,17},{2,34}... | collective-permute-start | bytes 92168 | tf_op jit(solution)/shard_map/ppermute | solution.py:238
  50.8 6.2 %collective-permute-start.8 = (f32[3,2560]{1,0:T(4,128)S(1)}, f32[3,2560]{1,0:T(4,128)S(1)}, u32[]{:S(2)}, u32[]{:S(2)}) collective-permute-start(f32[3,2560]{1,0:T(4,128)S(1)} %get-tuple-element.56.s0), channel_id=1, source_target_pairs={{0,16},{16,32},{32,48},{48,0},{1,17},{17,33},{33,49},{49,1},{2,18}... | collective-permute-start | bytes 92168 | tf_op jit(solution)/shard_map/ppermute | solution.py:238
  51.7 25.7 %collective-permute-start.11 = (bf16[2,160,512]{2,1,0:T(8,128)(2,1)S(1)}, bf16[2,160,512]{2,1,0:T(8,128)(2,1)S(1)}, u32[]{:S(2)}, u32[]{:S(2)}) collective-permute-start(bf16[2,160,512]{2,1,0:T(8,128)(2,1)S(1)} %get-tuple-element.62), channel_id=1, source_target_pairs={{0,16},{16,32},{32,48},{48,0},{1,17},{17,33},{33,49},{49,1},{2,18}... | collective-permute-start | bytes 983048 | tf_op jit(solution)/shard_map/ppermute | solution.py:238
  54.2 23.1 %collective-permute-start.12 = (bf16[2,160,512]{2,1,0:T(8,128)(2,1)S(1)}, bf16[2,160,512]{2,1,0:T(8,128)(2,1)S(1)}, u32[]{:S(2)}, u32[]{:S(2)}) collective-permute-start(bf16[2,160,512]{2,1,0:T(8,128)(2,1)S(1)} %get-tuple-element.63), channel_id=1, source_target_pairs={{0,32},{16,48},{32,0},{48,16},{1,33},{17,49},{33,1},{49,17},{2,34}... | collective-permute-start | bytes 983048 | tf_op jit(solution)/shard_map/ppermute | solution.py:238
  55.5 21.9 %collective-permute-start.13 = (bf16[2,160,512]{2,1,0:T(8,128)(2,1)S(1)}, bf16[2,160,512]{2,1,0:T(8,128)(2,1)S(1)}, u32[]{:S(2)}, u32[]{:S(2)}) collective-permute-start(bf16[2,160,512]{2,1,0:T(8,128)(2,1)S(1)} %get-tuple-element.64), channel_id=1, source_target_pairs={{0,48},{16,0},{32,16},{48,32},{1,49},{17,1},{33,17},{49,33},{2,50}... | collective-permute-start | bytes 983048 | tf_op jit(solution)/shard_map/ppermute | solution.py:238
  77.4 4.4 %copy-start.2 = (bf16[2,160,512]{2,1,0:T(8,128)(2,1)}, bf16[2,160,512]{2,1,0:T(8,128)(2,1)S(1)}, u32[]{:S(2)}) copy-start(bf16[2,160,512]{2,1,0:T(8,128)(2,1)S(1)} %collective-permute-done.12.x2) | copy-start | bytes 983044
  77.4 4.4 %copy-start.4 = (bf16[2,160,512]{2,1,0:T(8,128)(2,1)}, bf16[2,160,512]{2,1,0:T(8,128)(2,1)S(1)}, u32[]{:S(2)}) copy-start(bf16[2,160,512]{2,1,0:T(8,128)(2,1)S(1)} %collective-permute-done.13.x3) | copy-start | bytes 983044
  77.4 3.4 %collective-permute-start.20 = (bf16[1280,256]{1,0:T(8,128)(2,1)S(1)}, bf16[1280,256]{1,0:T(8,128)(2,1)S(1)}, u32[]{:S(2)}, u32[]{:S(2)}) collective-permute-start(bf16[1280,256]{1,0:T(8,128)(2,1)S(1)} %get-tuple-element.74), channel_id=1, source_target_pairs={{0,1},{1,0},{2,3},{3,2},{4,5},{5,4},{6,7},{7,6},{8,9},{9,8},{10,11... | collective-permute-start | bytes 1966088 | tf_op jit(solution)/shard_map/ppermute | solution.py:238
  77.5 8.6 %collective-permute-start.14 = (bf16[160,512]{1,0:T(8,128)(2,1)S(1)}, bf16[160,512]{1,0:T(8,128)(2,1)}, u32[]{:S(2)}, u32[]{:S(2)}) collective-permute-start(bf16[160,512]{1,0:T(8,128)(2,1)S(1)} %get-tuple-element.70), channel_id=1, source_target_pairs={{0,48},{16,0},{32,16},{48,32},{1,49},{17,1},{33,17},{49,33},{2,50}... | collective-permute-start | bytes 491528 | tf_op jit(solution)/shard_map/ppermute | solution.py:238
  79.0 8.7 %collective-permute-start.15 = (bf16[160,512]{1,0:T(8,128)(2,1)S(1)}, bf16[160,512]{1,0:T(8,128)(2,1)}, u32[]{:S(2)}, u32[]{:S(2)}) collective-permute-start(bf16[160,512]{1,0:T(8,128)(2,1)S(1)} %get-tuple-element.71), channel_id=1, source_target_pairs={{0,32},{16,48},{32,0},{48,16},{1,33},{17,49},{33,1},{49,17},{2,34}... | collective-permute-start | bytes 491528 | tf_op jit(solution)/shard_map/ppermute | solution.py:238
  80.2 10.2 %collective-permute-start.16 = (bf16[160,512]{1,0:T(8,128)(2,1)S(1)}, bf16[160,512]{1,0:T(8,128)(2,1)}, u32[]{:S(2)}, u32[]{:S(2)}) collective-permute-start(bf16[160,512]{1,0:T(8,128)(2,1)S(1)} %get-tuple-element.72), channel_id=1, source_target_pairs={{0,16},{16,32},{32,48},{48,0},{1,17},{17,33},{33,49},{49,1},{2,18}... | collective-permute-start | bytes 491528 | tf_op jit(solution)/shard_map/ppermute | solution.py:238
  81.8 16.2 %all-to-all-start.1 = ((bf16[8,160,256]{2,1,0:T(8,128)(2,1)}), bf16[8,160,256]{2,1,0:T(8,128)(2,1)S(1)}, u32[]{:S(2)}, u32[]{:S(2)}) async-start(bf16[8,160,256]{2,1,0:T(8,128)(2,1)} %bitcast.8), calls=%async_computation.1 | async-start | bytes 1310720 | tf_op jit(solution)/shard_map/all_to_all | solution.py:309
  91.5 10.4 %collective-permute-start.19 = (bf16[160,512]{1,0:T(8,128)(2,1)S(1)}, bf16[160,512]{1,0:T(8,128)(2,1)S(1)}, u32[]{:S(2)}, u32[]{:S(2)}) collective-permute-start(bf16[160,512]{1,0:T(8,128)(2,1)S(1)} %add_convert_fusion.1.q0), channel_id=1, source_target_pairs={{0,48},{16,0},{32,16},{48,32},{1,49},{17,1},{33,17},{49,33},{2,50}... | collective-permute-start | bytes 491528 | tf_op jit(solution)/shard_map/ppermute | solution.py:238
  92.2 10.4 %collective-permute-start.18 = (bf16[160,512]{1,0:T(8,128)(2,1)S(1)}, bf16[160,512]{1,0:T(8,128)(2,1)S(1)}, u32[]{:S(2)}, u32[]{:S(2)}) collective-permute-start(bf16[160,512]{1,0:T(8,128)(2,1)S(1)} %add_convert_fusion.1.q0), channel_id=1, source_target_pairs={{0,32},{16,48},{32,0},{48,16},{1,33},{17,49},{33,1},{49,17},{2,34}... | collective-permute-start | bytes 491528 | tf_op jit(solution)/shard_map/ppermute | solution.py:238
  93.4 9.4 %collective-permute-start.17 = (bf16[160,512]{1,0:T(8,128)(2,1)S(1)}, bf16[160,512]{1,0:T(8,128)(2,1)S(1)}, u32[]{:S(2)}, u32[]{:S(2)}) collective-permute-start(bf16[160,512]{1,0:T(8,128)(2,1)S(1)} %add_convert_fusion.1.q0), channel_id=1, source_target_pairs={{0,16},{16,32},{32,48},{48,0},{1,17},{17,33},{33,49},{49,1},{2,18}... | collective-permute-start | bytes 491528 | tf_op jit(solution)/shard_map/ppermute | solution.py:238
  98.1 5.7 %collective-permute-start.23 = (bf16[160,256]{1,0:T(8,128)(2,1)S(1)}, bf16[160,256]{1,0:T(8,128)(2,1)S(1)}, u32[]{:S(2)}, u32[]{:S(2)}) collective-permute-start(bf16[160,256]{1,0:T(8,128)(2,1)S(1)} %reduce_sum.32.k0), channel_id=1, source_target_pairs={{0,48},{16,0},{32,16},{48,32},{1,49},{17,1},{33,17},{49,33},{2,50}... | collective-permute-start | bytes 245768 | tf_op jit(solution)/shard_map/ppermute | solution.py:238
  101.0 6.0 %collective-permute-start.22 = (bf16[160,256]{1,0:T(8,128)(2,1)S(1)}, bf16[160,256]{1,0:T(8,128)(2,1)S(1)}, u32[]{:S(2)}, u32[]{:S(2)}) collective-permute-start(bf16[160,256]{1,0:T(8,128)(2,1)S(1)} %reduce_sum.32.k0), channel_id=1, source_target_pairs={{0,32},{16,48},{32,0},{48,16},{1,33},{17,49},{33,1},{49,17},{2,34}... | collective-permute-start | bytes 245768 | tf_op jit(solution)/shard_map/ppermute | solution.py:238
  101.9 5.9 %collective-permute-start.21 = (bf16[160,256]{1,0:T(8,128)(2,1)S(1)}, bf16[160,256]{1,0:T(8,128)(2,1)S(1)}, u32[]{:S(2)}, u32[]{:S(2)}) collective-permute-start(bf16[160,256]{1,0:T(8,128)(2,1)S(1)} %reduce_sum.32.k0), channel_id=1, source_target_pairs={{0,16},{16,32},{32,48},{48,0},{1,17},{17,33},{33,49},{49,1},{2,18}... | collective-permute-start | bytes 245768 | tf_op jit(solution)/shard_map/ppermute | solution.py:238
  107.9 2.8 %copy-start.3 = (bf16[2,160,512]{2,1,0:T(8,128)(2,1)S(1)}, bf16[2,160,512]{2,1,0:T(8,128)(2,1)}, u32[]{:S(2)}) copy-start(bf16[2,160,512]{2,1,0:T(8,128)(2,1)} %copy-done.2) | copy-start | bytes 983044
  107.9 2.8 %copy-start.5 = (bf16[2,160,512]{2,1,0:T(8,128)(2,1)S(1)}, bf16[2,160,512]{2,1,0:T(8,128)(2,1)}, u32[]{:S(2)}) copy-start(bf16[2,160,512]{2,1,0:T(8,128)(2,1)} %copy-done.4) | copy-start | bytes 983044
  108.0 2.6 %collective-permute-start.24 = (bf16[4,160,768]{2,1,0:T(8,128)(2,1)S(1)}, bf16[4,160,768]{2,1,0:T(8,128)(2,1)S(1)}, u32[]{:S(2)}, u32[]{:S(2)}) collective-permute-start(bf16[4,160,768]{2,1,0:T(8,128)(2,1)S(1)} %pad_maximum_fusion), channel_id=1, source_target_pairs={{0,1},{1,0},{2,3},{3,2},{4,5},{5,4},{6,7},{7,6},{8,9},{9,8},{10,11... | collective-permute-start | bytes 2949128 | tf_op jit(solution)/shard_map/ppermute | solution.py:238

commit v13 on v12

--- a/solution.py
+++ b/solution.py
@@ -262,8 +262,9 @@
     )
     kva = jnp.broadcast_to(kv[None], (8,) + kv.shape)
     kva = lax.all_to_all(kva, ("x", "yh"), 0, 0, tiled=True).reshape(KHALF, 2 * HEAD)
-    other_tokens = shift(tokens, "core", 1, 2)
-    kva, qs, gs, other_tokens = lax.optimization_barrier((kva, qs, gs, other_tokens))
+    later, _ = lax.optimization_barrier((tokens, (qs[2], gs[2])))
+    other_tokens = shift(later, "core", 1, 2)
+    kva, qs, gs = lax.optimization_barrier((kva, qs, gs))
     kvb = shift(kva, "core", 1, 2)
 
     key_dev = (o * 8 + np.arange(8)[None, :, None]) * 2 + (ic + np.arange(2)[:, None, None]) % 2

time: 131 us -> 131 us (level)
    all_to_all x1, waiting for transfers between devices: 2.72 us -> 4.04 us  [per_device(): lax.all_to_all(kva, ('x', 'yh'), 0, 0, tiled=True).reshape(KHALF, 2 * HEAD)]
where the time goes in v13:
time: 131 us; the launch traced here: 130 us
  starting transfers between devices  41.8 us (32%)
  Pallas kernels  37.1 us (28%)
  waiting for transfers between devices  23.3 us (18%)
  blocking collectives  18.2 us (14%)
  matrix products  4.59 us (4%)
  other arithmetic  3.22 us (2%)
  local copies, waits for them, and re-layouts  1.32 us (1%)
    pallas_call x5, Pallas kernels, kernel_call(): pl.pallas_call(body, out_shape=tuple((jax.ShapeDtypeStruct(*o) for o in o...  37.1 us
    ppermute x25, starting transfers between devices, shift(): return lax.ppermute(x, axis, [(i, (i + d) % n) for i in range(n)])  30.9 us
    all_to_all x1, blocking collectives, per_device(): dw = lax.all_to_all(dw, ('dp', 'x', 'yh'), 0, 0, tiled=True)  18.2 us
    ppermute x25, waiting for transfers between devices, shift(): return lax.ppermute(x, axis, [(i, (i + d) % n) for i in range(n)])  15.8 us
    all_to_all x1, starting transfers between devices, per_device(): lax.all_to_all(kva, ('x', 'yh'), 0, 0, tiled=True).reshape(KHALF, 2 * HEAD)  6.93 us
    dot_general x3, matrix products, dot(): return lax.dot_general(a, b, dims, preferred_element_type=f32)  4.59 us
    all_to_all x1, waiting for transfers between devices, per_device(): lax.all_to_all(kva, ('x', 'yh'), 0, 0, tiled=True).reshape(KHALF, 2 * HEAD)  4.04 us
    all_to_all x1, starting transfers between devices, per_device(): dkv = lax.all_to_all(dkv, ('x', 'yh'), 0, 0, tiled=True)  3.92 us
  transfers between devices with their start and end apart: 27, of which 10 were waited for; matrix products, arithmetic and copies ran while one was open for 4% of the time, Pallas kernels for 21%

profile of v13, /device:TPU:0, one launch (start us, length us, event | category | flops | bytes accessed | tf_op | source)
XLA Modules:
  0.0 130.5 jit_solution(6453708416151914141)
XLA Ops:
  0.7 3.6 %convolution_convert_fusion.q0 = bf16[160,512]{1,0:T(8,128)(2,1)S(1)} fusion(bf16[4096,512]{1,0:T(8,128)(2,1)} %param.13, bf16[1,160,4096]{2,1,0:T(8,128)(2,1)} %param.11), kind=kOutput, calls=%fused_computation.1 | convolution fusion | flops 671170560 | bytes 5668864 | tf_op jit(solution)/shard_map/dot_general | solution.py:36
  4.3 4.2 %collective-permute-start.2 = (bf16[160,512]{1,0:T(8,128)(2,1)S(1)}, bf16[160,512]{1,0:T(8,128)(2,1)S(1)}, u32[]{:S(2)}, u32[]{:S(2)}) collective-permute-start(bf16[160,512]{1,0:T(8,128)(2,1)S(1)} %convolution_convert_fusion.q0), channel_id=1, source_target_pairs={{0,48},{16,0},{32,16},{48,32},{1,49},{17,1},{33,17},{49,33},{2,50}... | collective-permute-start | bytes 491528 | tf_op jit(solution)/shard_map/ppermute | solution.py:238
  8.5 3.2 %collective-permute-start.4 = (bf16[160,512]{1,0:T(8,128)(2,1)S(1)}, bf16[160,512]{1,0:T(8,128)(2,1)}, u32[]{:S(2)}, u32[]{:S(2)}) collective-permute-start(bf16[160,512]{1,0:T(8,128)(2,1)S(1)} %bitcast.33), channel_id=1, source_target_pairs={{0,48},{16,0},{32,16},{48,32},{1,49},{17,1},{33,17},{49,33},{2,50}... | collective-permute-start | bytes 491528 | tf_op jit(solution)/shard_map/ppermute | solution.py:238
  11.7 0.5 convolution_convert_fusion.2
  12.2 0.5 convolution_convert_fusion.1
  12.8 0.9 broadcast_in_dim.47
  13.7 6.9 %all-to-all-start = ((bf16[8,160,256]{2,1,0:T(8,128)(2,1)}), bf16[8,160,256]{2,1,0:T(8,128)(2,1)S(1)}, u32[]{:S(2)}, u32[]{:S(2)}) async-start(bf16[8,160,256]{2,1,0:T(8,128)(2,1)} %broadcast_in_dim.47), calls=%async_computation | async-start | bytes 1310720 | tf_op jit(solution)/shard_map/all_to_all | solution.py:264
  20.8 3.3 %collective-permute-start.5 = (bf16[160,512]{1,0:T(8,128)(2,1)}, bf16[160,512]{1,0:T(8,128)(2,1)}, u32[]{:S(2)}, u32[]{:S(2)}) collective-permute-start(bf16[160,512]{1,0:T(8,128)(2,1)} %collective-permute-done.4.g3), channel_id=1, source_target_pairs={{0,48},{16,0},{32,16},{48,32},{1,49},{17,1},{33,17},{49,33},{2,50}... | collective-permute-start | bytes 491528 | tf_op jit(solution)/shard_map/ppermute | solution.py:238
  24.2 3.5 %collective-permute-done.1.q2 = bf16[160,512]{1,0:T(8,128)(2,1)} collective-permute-done((bf16[160,512]{1,0:T(8,128)(2,1)}, bf16[160,512]{1,0:T(8,128)(2,1)}, u32[]{:S(2)}, u32[]{:S(2)}) %collective-permute-start.1) | collective-permute-done | bytes 163872 | tf_op jit(solution)/shard_map/ppermute | solution.py:238
  27.7 0.1 add.164
  27.8 0.2 select_reduce_fusion.1
  28.0 4.0 %all-to-all-done = bf16[8,160,256]{2,1,0:T(8,128)(2,1)S(1)} async-done(((bf16[8,160,256]{2,1,0:T(8,128)(2,1)}), bf16[8,160,256]{2,1,0:T(8,128)(2,1)S(1)}, u32[]{:S(2)}, u32[]{:S(2)}) %all-to-all-start) | async-done | bytes 655392 | tf_op jit(solution)/shard_map/all_to_all | solution.py:264
  32.1 0.1 add.152
  32.3 0.1 reshape.101.posq.posq_ref
  32.5 0.2 select_reduce_fusion.ordk
  32.7 6.9 %stats_own.1 = (f32[3,2560]{1,0:T(4,128)S(1)}, bf16[2560,128]{1,0:T(8,128)(2,1)S(1)}, bf16[2560,128]{1,0:T(8,128)(2,1)S(1)}) custom-call(s32[32]{0:T(128)S(1)} %select_reduce_fusion.ordk, s32[1,2560]{1,0:T(1,128)S(1)} %reshape.101.posq.posq_ref, bf16[160,512]{1,0:T(8,128)(2,1)S(1)} %convolution_convert_fusion.q0, bf16[160,512]{1,0:T(8,128)(2,1)} %collective-permute-done.q1, ...), custom_call_target="tpu_custom_call" | custom-call | flops 1677721600 | bytes 4194304 | tf_op jit(solution)/shard_map/stats_own/pallas_call | solution.py:221
  39.6 7.9 %stats_other.1 = (f32[3,2560]{1,0:T(4,128)S(1)}, bf16[2,160,512]{2,1,0:T(8,128)(2,1)S(1)}, bf16[2,160,512]{2,1,0:T(8,128)(2,1)S(1)}, bf16[2,160,512]{2,1,0:T(8,128)(2,1)S(1)}, bf16[2,160,512]{2,1,0:T(8,128)(2,1)S(1)}) custom-call(s32[32]{0:T(128)S(1)} %select_reduce_fusion.ordk, s32[2]{0:T(128)S(1)} %pad_add_fusion.place, ...), custom_call_target="tpu_custom_call" | custom-call | flops 1677721600 | bytes 4194304 | tf_op jit(solution)/shard_map/stats_other/pallas_call | solution.py:221
  47.5 3.3 %collective-permute-start.10 = (f32[3,2560]{1,0:T(4,128)S(1)}, f32[3,2560]{1,0:T(4,128)S(1)}, u32[]{:S(2)}, u32[]{:S(2)}) collective-permute-start(f32[3,2560]{1,0:T(4,128)S(1)} %get-tuple-element.56.s0), channel_id=1, source_target_pairs={{0,48},{16,0},{32,16},{48,32},{1,49},{17,1},{33,17},{49,33},{2,50}... | collective-permute-start | bytes 92168 | tf_op jit(solution)/shard_map/ppermute | solution.py:238
  50.7 0.9 collective-permute-start.8
  51.7 2.5 %collective-permute-start.11 = (bf16[2,160,512]{2,1,0:T(8,128)(2,1)S(1)}, bf16[2,160,512]{2,1,0:T(8,128)(2,1)S(1)}, u32[]{:S(2)}, u32[]{:S(2)}) collective-permute-start(bf16[2,160,512]{2,1,0:T(8,128)(2,1)S(1)} %get-tuple-element.62), channel_id=1, source_target_pairs={{0,16},{16,32},{32,48},{48,0},{1,17},{17,33},{33,49},{49,1},{2,18}... | collective-permute-start | bytes 983048 | tf_op jit(solution)/shard_map/ppermute | solution.py:238
  54.2 1.2 collective-permute-start.12
  55.5 1.5 %collective-permute-start.13 = (bf16[2,160,512]{2,1,0:T(8,128)(2,1)S(1)}, bf16[2,160,512]{2,1,0:T(8,128)(2,1)S(1)}, u32[]{:S(2)}, u32[]{:S(2)}) collective-permute-start(bf16[2,160,512]{2,1,0:T(8,128)(2,1)S(1)} %get-tuple-element.64), channel_id=1, source_target_pairs={{0,48},{16,0},{32,16},{48,32},{1,49},{17,1},{33,17},{49,33},{2,50}... | collective-permute-start | bytes 983048 | tf_op jit(solution)/shard_map/ppermute | solution.py:238
  57.0 20.4 %grads.1 = (f32[160,512]{1,0:T(8,128)S(1)}, bf16[160,512]{1,0:T(8,128)(2,1)S(1)}, bf16[160,512]{1,0:T(8,128)(2,1)S(1)}, bf16[160,512]{1,0:T(8,128)(2,1)S(1)}, f3...) custom-call(s32[32]{0:T(128)S(1)} %select_reduce_fusion.ordk, s32[1,2560]{1,0:T(1,128)S(1)} %reshape.101.posq.posq_ref, ...), custom_call_target="tpu_custom_call" | custom-call | flops 8388608000 | bytes 8388608 | tf_op jit(solution)/shard_map/grads/pallas_call | solution.py:221
  77.5 1.5 %collective-permute-start.14 = (bf16[160,512]{1,0:T(8,128)(2,1)S(1)}, bf16[160,512]{1,0:T(8,128)(2,1)}, u32[]{:S(2)}, u32[]{:S(2)}) collective-permute-start(bf16[160,512]{1,0:T(8,128)(2,1)S(1)} %get-tuple-element.70), channel_id=1, source_target_pairs={{0,48},{16,0},{32,16},{48,32},{1,49},{17,1},{33,17},{49,33},{2,50}... | collective-permute-start | bytes 491528 | tf_op jit(solution)/shard_map/ppermute | solution.py:238
  79.0 1.2 collective-permute-start.15
  80.2 0.6 collective-permute-start.16
  80.8 1.0 add_convert_fusion
  81.8 3.9 %all-to-all-start.1 = ((bf16[8,160,256]{2,1,0:T(8,128)(2,1)}), bf16[8,160,256]{2,1,0:T(8,128)(2,1)S(1)}, u32[]{:S(2)}, u32[]{:S(2)}) async-start(bf16[8,160,256]{2,1,0:T(8,128)(2,1)} %bitcast.8), calls=%async_computation.1 | async-start | bytes 1310720 | tf_op jit(solution)/shard_map/all_to_all | solution.py:310
  85.7 2.0 %collective-permute-done.15 = bf16[160,512]{1,0:T(8,128)(2,1)} collective-permute-done((bf16[160,512]{1,0:T(8,128)(2,1)S(1)}, bf16[160,512]{1,0:T(8,128)(2,1)}, u32[]{:S(2)}, u32[]{:S(2)}) %collective-permute-start.15) | collective-permute-done | bytes 163872 | tf_op jit(solution)/shard_map/ppermute | solution.py:238
  87.7 2.7 %collective-permute-done.16 = bf16[160,512]{1,0:T(8,128)(2,1)} collective-permute-done((bf16[160,512]{1,0:T(8,128)(2,1)S(1)}, bf16[160,512]{1,0:T(8,128)(2,1)}, u32[]{:S(2)}, u32[]{:S(2)}) %collective-permute-start.16) | collective-permute-done | bytes 163872 | tf_op jit(solution)/shard_map/ppermute | solution.py:238
  90.3 1.2 add_convert_fusion.1.q0
  91.5 0.7 collective-permute-start.19
  92.2 1.2 collective-permute-start.18
  93.4 0.8 collective-permute-start.17
  94.2 3.4 %all-to-all-done.1 = bf16[8,160,256]{2,1,0:T(8,128)(2,1)S(1)} async-done(((bf16[8,160,256]{2,1,0:T(8,128)(2,1)}), bf16[8,160,256]{2,1,0:T(8,128)(2,1)S(1)}, u32[]{:S(2)}, u32[]{:S(2)}) %all-to-all-start.1) | async-done | bytes 655392 | tf_op jit(solution)/shard_map/all_to_all | solution.py:310
  97.6 0.1 reduce_sum.32.k0
  97.7 2.9 %collective-permute-start.23 = (bf16[160,256]{1,0:T(8,128)(2,1)S(1)}, bf16[160,256]{1,0:T(8,128)(2,1)S(1)}, u32[]{:S(2)}, u32[]{:S(2)}) collective-permute-start(bf16[160,256]{1,0:T(8,128)(2,1)S(1)} %reduce_sum.32.k0), channel_id=1, source_target_pairs={{0,48},{16,0},{32,16},{48,32},{1,49},{17,1},{33,17},{49,33},{2,50}... | collective-permute-start | bytes 245768 | tf_op jit(solution)/shard_map/ppermute | solution.py:238
  100.6 0.9 collective-permute-start.22
  101.4 0.8 collective-permute-start.21
  102.3 0.5 collective-permute-done.17.q1
  102.8 1.2 collective-permute-done.23.k3
  104.0 2.6 %collective-permute-done.22.k2 = bf16[160,256]{1,0:T(8,128)(2,1)S(1)} collective-permute-done((bf16[160,256]{1,0:T(8,128)(2,1)S(1)}, bf16[160,256]{1,0:T(8,128)(2,1)S(1)}, u32[]{:S(2)}, u32[]{:S(2)}) %collective-permute-start.22) | collective-permute-done | bytes 81952 | tf_op jit(solution)/shard_map/ppermute | solution.py:238
  106.6 0.8 collective-permute-done.21.k1
  107.5 0.1 pad_maximum_fusion
  107.7 2.6 %collective-permute-done.24.grads = bf16[4,160,768]{2,1,0:T(8,128)(2,1)S(1)} collective-permute-done((bf16[4,160,768]{2,1,0:T(8,128)(2,1)S(1)}, bf16[4,160,768]{2,1,0:T(8,128)(2,1)S(1)}, u32[]{:S(2)}, u32[]{:S(2)}) %collective-permute-start.24) | collective-permute-done | bytes 983072 | tf_op jit(solution)/shard_map/ppermute | solution.py:238
  110.3 1.2 weights.1
  111.5 18.2 %all_to_all.15.parts = bf16[16,32,768]{2,1,0:T(8,128)(2,1)S(1)} all-to-all(bf16[16,32,768]{2,1,0:T(8,128)(2,1)S(1)} %weights.1), channel_id=1, replica_groups=mesh['dp'=2,'outer'=4,'x'=4,'yh'=2,'core'=2] {'dp','x','yh'}, dimensions={0} | all-to-all | bytes 1572864 | tf_op jit(solution)/shard_map/all_to_all | solution.py:326
  129.8 0.7 last_sum.1
  (63 shorter events, 0.9 us)
Async XLA Ops:
  0.6 11.1 %copy-start = (bf16[4096,128]{1,0:T(8,128)(2,1)S(1)}, bf16[4096,128]{1,0:T(8,128)(2,1)}, u32[]{:S(2)}) copy-start(bf16[4096,128]{1,0:T(8,128)(2,1)} %param.14) | copy-start | bytes 3145732
  0.6 11.1 %copy-start.1 = (bf16[1,160,4096]{2,1,0:T(8,128)(2,1)S(1)}, bf16[1,160,4096]{2,1,0:T(8,128)(2,1)}, u32[]{:S(2)}) copy-start(bf16[1,160,4096]{2,1,0:T(8,128)(2,1)} %param.11) | copy-start | bytes 3932164
  0.7 7.8 %copy-start.6 = (bf16[1,160,512]{2,1,0:T(8,128)(2,1)S(1)}, bf16[1,160,512]{2,1,0:T(8,128)(2,1)}, u32[]{:S(2)}) copy-start(bf16[1,160,512]{2,1,0:T(8,128)(2,1)} %param.16) | copy-start | bytes 491524
  4.3 8.0 %copy-start.7 = (bf16[4096,128]{1,0:T(8,128)(2,1)S(1)}, bf16[4096,128]{1,0:T(8,128)(2,1)}, u32[]{:S(2)}) copy-start(bf16[4096,128]{1,0:T(8,128)(2,1)} %param.15) | copy-start | bytes 3145732
  4.3 23.7 %collective-permute-start.2 = (bf16[160,512]{1,0:T(8,128)(2,1)S(1)}, bf16[160,512]{1,0:T(8,128)(2,1)S(1)}, u32[]{:S(2)}, u32[]{:S(2)}) collective-permute-start(bf16[160,512]{1,0:T(8,128)(2,1)S(1)} %convolution_convert_fusion.q0), channel_id=1, source_target_pairs={{0,48},{16,0},{32,16},{48,32},{1,49},{17,1},{33,17},{49,33},{2,50}... | collective-permute-start | bytes 491528 | tf_op jit(solution)/shard_map/ppermute | solution.py:238
  8.5 12.3 %collective-permute-start = (bf16[160,512]{1,0:T(8,128)(2,1)S(1)}, bf16[160,512]{1,0:T(8,128)(2,1)}, u32[]{:S(2)}, u32[]{:S(2)}) collective-permute-start(bf16[160,512]{1,0:T(8,128)(2,1)S(1)} %convolution_convert_fusion.q0), channel_id=1, source_target_pairs={{0,16},{16,32},{32,48},{48,0},{1,17},{17,33},{33,49},{49,1},{2,18}... | collective-permute-start | bytes 491528 | tf_op jit(solution)/shard_map/ppermute | solution.py:238
  8.5 12.3 %collective-permute-start.4 = (bf16[160,512]{1,0:T(8,128)(2,1)S(1)}, bf16[160,512]{1,0:T(8,128)(2,1)}, u32[]{:S(2)}, u32[]{:S(2)}) collective-permute-start(bf16[160,512]{1,0:T(8,128)(2,1)S(1)} %bitcast.33), channel_id=1, source_target_pairs={{0,48},{16,0},{32,16},{48,32},{1,49},{17,1},{33,17},{49,33},{2,50}... | collective-permute-start | bytes 491528 | tf_op jit(solution)/shard_map/ppermute | solution.py:238
  11.7 16.3 %collective-permute-start.3 = (bf16[160,512]{1,0:T(8,128)(2,1)S(1)}, bf16[160,512]{1,0:T(8,128)(2,1)}, u32[]{:S(2)}, u32[]{:S(2)}) collective-permute-start(bf16[160,512]{1,0:T(8,128)(2,1)S(1)} %bitcast.34), channel_id=1, source_target_pairs={{0,16},{16,32},{32,48},{48,0},{1,17},{17,33},{33,49},{49,1},{2,18}... | collective-permute-start | bytes 491528 | tf_op jit(solution)/shard_map/ppermute | solution.py:238
  12.7 7.9 %copy-start.11 = (s32[1,8,1]{1,2,0:T(1,128)S(1)}, s32[1,8,1]{1,2,0:T(1,128)}, u32[]{:S(2)}) copy-start(s32[1,8,1]{1,2,0:T(1,128)} %constant.67.clone) | copy-start | bytes 100
  12.8 7.9 %copy-start.10 = (s32[2,1,1]{0,2,1:T(1,128)S(1)}, s32[2,1,1]{0,2,1:T(1,128)}, u32[]{:S(2)}) copy-start(s32[2,1,1]{0,2,1:T(1,128)} %constant.68.clone) | copy-start | bytes 28
  12.8 14.8 %copy-start.8 = (s32[4]{0:T(128)S(1)}, s32[4]{0:T(128)}, u32[]{:S(2)}) copy-start(s32[4]{0:T(128)} %constant.76) | copy-start | bytes 52
  12.8 15.0 %copy-start.9 = (s32[1,128]{1,0:T(1,128)S(1)}, s32[1,128]{1,0:T(1,128)}, u32[]{:S(2)}) copy-start(s32[1,128]{1,0:T(1,128)} %param.12) | copy-start | bytes 1540
  13.7 18.3 %all-to-all-start = ((bf16[8,160,256]{2,1,0:T(8,128)(2,1)}), bf16[8,160,256]{2,1,0:T(8,128)(2,1)S(1)}, u32[]{:S(2)}, u32[]{:S(2)}) async-start(bf16[8,160,256]{2,1,0:T(8,128)(2,1)} %broadcast_in_dim.47), calls=%async_computation | async-start | bytes 1310720 | tf_op jit(solution)/shard_map/all_to_all | solution.py:264
  20.7 6.9 %collective-permute-start.1 = (bf16[160,512]{1,0:T(8,128)(2,1)}, bf16[160,512]{1,0:T(8,128)(2,1)}, u32[]{:S(2)}, u32[]{:S(2)}) collective-permute-start(bf16[160,512]{1,0:T(8,128)(2,1)} %collective-permute-done.q1), channel_id=1, source_target_pairs={{0,16},{16,32},{32,48},{48,0},{1,17},{17,33},{33,49},{49,1},{2,18}... | collective-permute-start | bytes 491528 | tf_op jit(solution)/shard_map/ppermute | solution.py:238
  20.8 6.8 %collective-permute-start.5 = (bf16[160,512]{1,0:T(8,128)(2,1)}, bf16[160,512]{1,0:T(8,128)(2,1)}, u32[]{:S(2)}, u32[]{:S(2)}) collective-permute-start(bf16[160,512]{1,0:T(8,128)(2,1)} %collective-permute-done.4.g3), channel_id=1, source_target_pairs={{0,48},{16,0},{32,16},{48,32},{1,49},{17,1},{33,17},{49,33},{2,50}... | collective-permute-start | bytes 491528 | tf_op jit(solution)/shard_map/ppermute | solution.py:238
  27.6 12.0 %collective-permute-start.7 = (bf16[160,4096]{1,0:T(8,128)(2,1)S(1)}, bf16[160,4096]{1,0:T(8,128)(2,1)}, u32[]{:S(2)}, u32[]{:S(2)}) collective-permute-start(bf16[160,4096]{1,0:T(8,128)(2,1)S(1)} %bitcast.28), channel_id=1, source_target_pairs={{0,1},{1,0},{2,3},{3,2},{4,5},{5,4},{6,7},{7,6},{8,9},{9,8},{10,11... | collective-permute-start | bytes 3932168 | tf_op jit(solution)/shard_map/ppermute | solution.py:238
  32.0 7.5 %collective-permute-start.6 = (bf16[1280,256]{1,0:T(8,128)(2,1)S(1)}, bf16[1280,256]{1,0:T(8,128)(2,1)}, u32[]{:S(2)}, u32[]{:S(2)}) collective-permute-start(bf16[1280,256]{1,0:T(8,128)(2,1)S(1)} %bitcast.30), channel_id=1, source_target_pairs={{0,1},{1,0},{2,3},{3,2},{4,5},{5,4},{6,7},{7,6},{8,9},{9,8},{10,11... | collective-permute-start | bytes 1966088 | tf_op jit(solution)/shard_map/ppermute | solution.py:238
  47.5 8.0 %collective-permute-start.10 = (f32[3,2560]{1,0:T(4,128)S(1)}, f32[3,2560]{1,0:T(4,128)S(1)}, u32[]{:S(2)}, u32[]{:S(2)}) collective-permute-start(f32[3,2560]{1,0:T(4,128)S(1)} %get-tuple-element.56.s0), channel_id=1, source_target_pairs={{0,48},{16,0},{32,16},{48,32},{1,49},{17,1},{33,17},{49,33},{2,50}... | collective-permute-start | bytes 92168 | tf_op jit(solution)/shard_map/ppermute | solution.py:238
  50.7 6.2 %collective-permute-start.9 = (f32[3,2560]{1,0:T(4,128)S(1)}, f32[3,2560]{1,0:T(4,128)S(1)}, u32[]{:S(2)}, u32[]{:S(2)}) collective-permute-start(f32[3,2560]{1,0:T(4,128)S(1)} %get-tuple-element.56.s0), channel_id=1, source_target_pairs={{0,32},{16,48},{32,0},{48,16},{1,33},{17,49},{33,1},{49,17},{2,34}... | collective-permute-start | bytes 92168 | tf_op jit(solution)/shard_map/ppermute | solution.py:238
  50.7 6.2 %collective-permute-start.8 = (f32[3,2560]{1,0:T(4,128)S(1)}, f32[3,2560]{1,0:T(4,128)S(1)}, u32[]{:S(2)}, u32[]{:S(2)}) collective-permute-start(f32[3,2560]{1,0:T(4,128)S(1)} %get-tuple-element.56.s0), channel_id=1, source_target_pairs={{0,16},{16,32},{32,48},{48,0},{1,17},{17,33},{33,49},{49,1},{2,18}... | collective-permute-start | bytes 92168 | tf_op jit(solution)/shard_map/ppermute | solution.py:238
  51.7 25.7 %collective-permute-start.11 = (bf16[2,160,512]{2,1,0:T(8,128)(2,1)S(1)}, bf16[2,160,512]{2,1,0:T(8,128)(2,1)S(1)}, u32[]{:S(2)}, u32[]{:S(2)}) collective-permute-start(bf16[2,160,512]{2,1,0:T(8,128)(2,1)S(1)} %get-tuple-element.62), channel_id=1, source_target_pairs={{0,16},{16,32},{32,48},{48,0},{1,17},{17,33},{33,49},{49,1},{2,18}... | collective-permute-start | bytes 983048 | tf_op jit(solution)/shard_map/ppermute | solution.py:238
  54.2 23.1 %collective-permute-start.12 = (bf16[2,160,512]{2,1,0:T(8,128)(2,1)S(1)}, bf16[2,160,512]{2,1,0:T(8,128)(2,1)S(1)}, u32[]{:S(2)}, u32[]{:S(2)}) collective-permute-start(bf16[2,160,512]{2,1,0:T(8,128)(2,1)S(1)} %get-tuple-element.63), channel_id=1, source_target_pairs={{0,32},{16,48},{32,0},{48,16},{1,33},{17,49},{33,1},{49,17},{2,34}... | collective-permute-start | bytes 983048 | tf_op jit(solution)/shard_map/ppermute | solution.py:238
  55.5 21.9 %collective-permute-start.13 = (bf16[2,160,512]{2,1,0:T(8,128)(2,1)S(1)}, bf16[2,160,512]{2,1,0:T(8,128)(2,1)S(1)}, u32[]{:S(2)}, u32[]{:S(2)}) collective-permute-start(bf16[2,160,512]{2,1,0:T(8,128)(2,1)S(1)} %get-tuple-element.64), channel_id=1, source_target_pairs={{0,48},{16,0},{32,16},{48,32},{1,49},{17,1},{33,17},{49,33},{2,50}... | collective-permute-start | bytes 983048 | tf_op jit(solution)/shard_map/ppermute | solution.py:238
  77.4 4.4 %copy-start.2 = (bf16[2,160,512]{2,1,0:T(8,128)(2,1)}, bf16[2,160,512]{2,1,0:T(8,128)(2,1)S(1)}, u32[]{:S(2)}) copy-start(bf16[2,160,512]{2,1,0:T(8,128)(2,1)S(1)} %collective-permute-done.12.x2) | copy-start | bytes 983044
  77.4 4.4 %copy-start.4 = (bf16[2,160,512]{2,1,0:T(8,128)(2,1)}, bf16[2,160,512]{2,1,0:T(8,128)(2,1)S(1)}, u32[]{:S(2)}) copy-start(bf16[2,160,512]{2,1,0:T(8,128)(2,1)S(1)} %collective-permute-done.13.x3) | copy-start | bytes 983044
  77.4 3.4 %collective-permute-start.20 = (bf16[1280,256]{1,0:T(8,128)(2,1)S(1)}, bf16[1280,256]{1,0:T(8,128)(2,1)S(1)}, u32[]{:S(2)}, u32[]{:S(2)}) collective-permute-start(bf16[1280,256]{1,0:T(8,128)(2,1)S(1)} %get-tuple-element.74), channel_id=1, source_target_pairs={{0,1},{1,0},{2,3},{3,2},{4,5},{5,4},{6,7},{7,6},{8,9},{9,8},{10,11... | collective-permute-start | bytes 1966088 | tf_op jit(solution)/shard_map/ppermute | solution.py:238
  77.5 8.2 %collective-permute-start.14 = (bf16[160,512]{1,0:T(8,128)(2,1)S(1)}, bf16[160,512]{1,0:T(8,128)(2,1)}, u32[]{:S(2)}, u32[]{:S(2)}) collective-permute-start(bf16[160,512]{1,0:T(8,128)(2,1)S(1)} %get-tuple-element.70), channel_id=1, source_target_pairs={{0,48},{16,0},{32,16},{48,32},{1,49},{17,1},{33,17},{49,33},{2,50}... | collective-permute-start | bytes 491528 | tf_op jit(solution)/shard_map/ppermute | solution.py:238
  79.0 8.7 %collective-permute-start.15 = (bf16[160,512]{1,0:T(8,128)(2,1)S(1)}, bf16[160,512]{1,0:T(8,128)(2,1)}, u32[]{:S(2)}, u32[]{:S(2)}) collective-permute-start(bf16[160,512]{1,0:T(8,128)(2,1)S(1)} %get-tuple-element.71), channel_id=1, source_target_pairs={{0,32},{16,48},{32,0},{48,16},{1,33},{17,49},{33,1},{49,17},{2,34}... | collective-permute-start | bytes 491528 | tf_op jit(solution)/shard_map/ppermute | solution.py:238
  80.2 10.2 %collective-permute-start.16 = (bf16[160,512]{1,0:T(8,128)(2,1)S(1)}, bf16[160,512]{1,0:T(8,128)(2,1)}, u32[]{:S(2)}, u32[]{:S(2)}) collective-permute-start(bf16[160,512]{1,0:T(8,128)(2,1)S(1)} %get-tuple-element.72), channel_id=1, source_target_pairs={{0,16},{16,32},{32,48},{48,0},{1,17},{17,33},{33,49},{49,1},{2,18}... | collective-permute-start | bytes 491528 | tf_op jit(solution)/shard_map/ppermute | solution.py:238
  81.8 15.8 %all-to-all-start.1 = ((bf16[8,160,256]{2,1,0:T(8,128)(2,1)}), bf16[8,160,256]{2,1,0:T(8,128)(2,1)S(1)}, u32[]{:S(2)}, u32[]{:S(2)}) async-start(bf16[8,160,256]{2,1,0:T(8,128)(2,1)} %bitcast.8), calls=%async_computation.1 | async-start | bytes 1310720 | tf_op jit(solution)/shard_map/all_to_all | solution.py:310
  91.5 10.0 %collective-permute-start.19 = (bf16[160,512]{1,0:T(8,128)(2,1)S(1)}, bf16[160,512]{1,0:T(8,128)(2,1)S(1)}, u32[]{:S(2)}, u32[]{:S(2)}) collective-permute-start(bf16[160,512]{1,0:T(8,128)(2,1)S(1)} %add_convert_fusion.1.q0), channel_id=1, source_target_pairs={{0,48},{16,0},{32,16},{48,32},{1,49},{17,1},{33,17},{49,33},{2,50}... | collective-permute-start | bytes 491528 | tf_op jit(solution)/shard_map/ppermute | solution.py:238
  92.2 10.1 %collective-permute-start.18 = (bf16[160,512]{1,0:T(8,128)(2,1)S(1)}, bf16[160,512]{1,0:T(8,128)(2,1)S(1)}, u32[]{:S(2)}, u32[]{:S(2)}) collective-permute-start(bf16[160,512]{1,0:T(8,128)(2,1)S(1)} %add_convert_fusion.1.q0), channel_id=1, source_target_pairs={{0,32},{16,48},{32,0},{48,16},{1,33},{17,49},{33,1},{49,17},{2,34}... | collective-permute-start | bytes 491528 | tf_op jit(solution)/shard_map/ppermute | solution.py:238
  93.4 9.4 %collective-permute-start.17 = (bf16[160,512]{1,0:T(8,128)(2,1)S(1)}, bf16[160,512]{1,0:T(8,128)(2,1)S(1)}, u32[]{:S(2)}, u32[]{:S(2)}) collective-permute-start(bf16[160,512]{1,0:T(8,128)(2,1)S(1)} %add_convert_fusion.1.q0), channel_id=1, source_target_pairs={{0,16},{16,32},{32,48},{48,0},{1,17},{17,33},{33,49},{49,1},{2,18}... | collective-permute-start | bytes 491528 | tf_op jit(solution)/shard_map/ppermute | solution.py:238
  97.7 6.3 %collective-permute-start.23 = (bf16[160,256]{1,0:T(8,128)(2,1)S(1)}, bf16[160,256]{1,0:T(8,128)(2,1)S(1)}, u32[]{:S(2)}, u32[]{:S(2)}) collective-permute-start(bf16[160,256]{1,0:T(8,128)(2,1)S(1)} %reduce_sum.32.k0), channel_id=1, source_target_pairs={{0,48},{16,0},{32,16},{48,32},{1,49},{17,1},{33,17},{49,33},{2,50}... | collective-permute-start | bytes 245768 | tf_op jit(solution)/shard_map/ppermute | solution.py:238
  100.6 6.0 %collective-permute-start.22 = (bf16[160,256]{1,0:T(8,128)(2,1)S(1)}, bf16[160,256]{1,0:T(8,128)(2,1)S(1)}, u32[]{:S(2)}, u32[]{:S(2)}) collective-permute-start(bf16[160,256]{1,0:T(8,128)(2,1)S(1)} %reduce_sum.32.k0), channel_id=1, source_target_pairs={{0,32},{16,48},{32,0},{48,16},{1,33},{17,49},{33,1},{49,17},{2,34}... | collective-permute-start | bytes 245768 | tf_op jit(solution)/shard_map/ppermute | solution.py:238
  101.4 6.0 %collective-permute-start.21 = (bf16[160,256]{1,0:T(8,128)(2,1)S(1)}, bf16[160,256]{1,0:T(8,128)(2,1)S(1)}, u32[]{:S(2)}, u32[]{:S(2)}) collective-permute-start(bf16[160,256]{1,0:T(8,128)(2,1)S(1)} %reduce_sum.32.k0), channel_id=1, source_target_pairs={{0,16},{16,32},{32,48},{48,0},{1,17},{17,33},{33,49},{49,1},{2,18}... | collective-permute-start | bytes 245768 | tf_op jit(solution)/shard_map/ppermute | solution.py:238
  107.5 2.8 %copy-start.3 = (bf16[2,160,512]{2,1,0:T(8,128)(2,1)S(1)}, bf16[2,160,512]{2,1,0:T(8,128)(2,1)}, u32[]{:S(2)}) copy-start(bf16[2,160,512]{2,1,0:T(8,128)(2,1)} %copy-done.2) | copy-start | bytes 983044
  107.5 2.8 %copy-start.5 = (bf16[2,160,512]{2,1,0:T(8,128)(2,1)S(1)}, bf16[2,160,512]{2,1,0:T(8,128)(2,1)}, u32[]{:S(2)}) copy-start(bf16[2,160,512]{2,1,0:T(8,128)(2,1)} %copy-done.4) | copy-start | bytes 983044
  107.7 2.6 %collective-permute-start.24 = (bf16[4,160,768]{2,1,0:T(8,128)(2,1)S(1)}, bf16[4,160,768]{2,1,0:T(8,128)(2,1)S(1)}, u32[]{:S(2)}, u32[]{:S(2)}) collective-permute-start(bf16[4,160,768]{2,1,0:T(8,128)(2,1)S(1)} %pad_maximum_fusion), channel_id=1, source_target_pairs={{0,1},{1,0},{2,3},{3,2},{4,5},{5,4},{6,7},{7,6},{8,9},{9,8},{10,11... | collective-permute-start | bytes 2949128 | tf_op jit(solution)/shard_map/ppermute | solution.py:238

commit v14 on v13

--- a/solution.py
+++ b/solution.py
@@ -22,7 +22,7 @@
 KHALF = KEYS // 2
 RT = 1280
 KC = 640
-KS = 160
+KS = 640
 SCALE = 1.0 / math.sqrt(HEAD)
 SCALE2 = SCALE * math.log2(math.e)
 f32 = jnp.float32

time: 131 us -> 130 us (level)
  no operation moved by 1% of the time
where the time goes in v14:
time: 130 us
  starting transfers between devices  41.8 us (32%)
  Pallas kernels  36.3 us (28%)
  waiting for transfers between devices  23.3 us (18%)
  blocking collectives  18.2 us (14%)
  matrix products  4.59 us (4%)
  other arithmetic  3.22 us (2%)
  local copies, waits for them, and re-layouts  1.32 us (1%)
    pallas_call x5, Pallas kernels, kernel_call(): pl.pallas_call(body, out_shape=tuple((jax.ShapeDtypeStruct(*o) for o in o...  36.3 us
    ppermute x25, starting transfers between devices, shift(): return lax.ppermute(x, axis, [(i, (i + d) % n) for i in range(n)])  30.9 us
    all_to_all x1, blocking collectives, per_device(): dw = lax.all_to_all(dw, ('dp', 'x', 'yh'), 0, 0, tiled=True)  18.2 us
    ppermute x25, waiting for transfers between devices, shift(): return lax.ppermute(x, axis, [(i, (i + d) % n) for i in range(n)])  15.8 us
    all_to_all x1, starting transfers between devices, per_device(): lax.all_to_all(kva, ('x', 'yh'), 0, 0, tiled=True).reshape(KHALF, 2 * HEAD)  6.93 us
    dot_general x3, matrix products, dot(): return lax.dot_general(a, b, dims, preferred_element_type=f32)  4.59 us
    all_to_all x1, waiting for transfers between devices, per_device(): lax.all_to_all(kva, ('x', 'yh'), 0, 0, tiled=True).reshape(KHALF, 2 * HEAD)  4.04 us
    all_to_all x1, starting transfers between devices, per_device(): dkv = lax.all_to_all(dkv, ('x', 'yh'), 0, 0, tiled=True)  3.93 us
  transfers between devices with their start and end apart: 27, of which 10 were waited for; matrix products, arithmetic and copies ran while one was open for 4% of the time, Pallas kernels for 21%

profile of v14, /device:TPU:0, one launch (start us, length us, event | category | flops | bytes accessed | tf_op | source)
XLA Modules:
  0.0 129.7 jit_solution(10408891214012449038)
XLA Ops:
  0.7 3.6 %convolution_convert_fusion.q0 = bf16[160,512]{1,0:T(8,128)(2,1)S(1)} fusion(bf16[4096,512]{1,0:T(8,128)(2,1)} %param.13, bf16[1,160,4096]{2,1,0:T(8,128)(2,1)} %param.11), kind=kOutput, calls=%fused_computation.1 | convolution fusion | flops 671170560 | bytes 5668864 | tf_op jit(solution)/shard_map/dot_general | solution.py:36
  4.3 4.2 %collective-permute-start.2 = (bf16[160,512]{1,0:T(8,128)(2,1)S(1)}, bf16[160,512]{1,0:T(8,128)(2,1)S(1)}, u32[]{:S(2)}, u32[]{:S(2)}) collective-permute-start(bf16[160,512]{1,0:T(8,128)(2,1)S(1)} %convolution_convert_fusion.q0), channel_id=1, source_target_pairs={{0,48},{16,0},{32,16},{48,32},{1,49},{17,1},{33,17},{49,33},{2,50}... | collective-permute-start | bytes 491528 | tf_op jit(solution)/shard_map/ppermute | solution.py:238
  8.5 3.2 %collective-permute-start.4 = (bf16[160,512]{1,0:T(8,128)(2,1)S(1)}, bf16[160,512]{1,0:T(8,128)(2,1)}, u32[]{:S(2)}, u32[]{:S(2)}) collective-permute-start(bf16[160,512]{1,0:T(8,128)(2,1)S(1)} %bitcast.33), channel_id=1, source_target_pairs={{0,48},{16,0},{32,16},{48,32},{1,49},{17,1},{33,17},{49,33},{2,50}... | collective-permute-start | bytes 491528 | tf_op jit(solution)/shard_map/ppermute | solution.py:238
  11.7 0.5 convolution_convert_fusion.2
  12.2 0.5 convolution_convert_fusion.1
  12.8 0.9 broadcast_in_dim.47
  13.7 6.9 %all-to-all-start = ((bf16[8,160,256]{2,1,0:T(8,128)(2,1)}), bf16[8,160,256]{2,1,0:T(8,128)(2,1)S(1)}, u32[]{:S(2)}, u32[]{:S(2)}) async-start(bf16[8,160,256]{2,1,0:T(8,128)(2,1)} %broadcast_in_dim.47), calls=%async_computation | async-start | bytes 1310720 | tf_op jit(solution)/shard_map/all_to_all | solution.py:264
  20.8 3.3 %collective-permute-start.5 = (bf16[160,512]{1,0:T(8,128)(2,1)}, bf16[160,512]{1,0:T(8,128)(2,1)}, u32[]{:S(2)}, u32[]{:S(2)}) collective-permute-start(bf16[160,512]{1,0:T(8,128)(2,1)} %collective-permute-done.4.g3), channel_id=1, source_target_pairs={{0,48},{16,0},{32,16},{48,32},{1,49},{17,1},{33,17},{49,33},{2,50}... | collective-permute-start | bytes 491528 | tf_op jit(solution)/shard_map/ppermute | solution.py:238
  24.2 3.5 %collective-permute-done.1.q2 = bf16[160,512]{1,0:T(8,128)(2,1)} collective-permute-done((bf16[160,512]{1,0:T(8,128)(2,1)}, bf16[160,512]{1,0:T(8,128)(2,1)}, u32[]{:S(2)}, u32[]{:S(2)}) %collective-permute-start.1) | collective-permute-done | bytes 163872 | tf_op jit(solution)/shard_map/ppermute | solution.py:238
  27.7 0.1 add.164
  27.8 0.2 select_reduce_fusion.1
  28.0 4.0 %all-to-all-done = bf16[8,160,256]{2,1,0:T(8,128)(2,1)S(1)} async-done(((bf16[8,160,256]{2,1,0:T(8,128)(2,1)}), bf16[8,160,256]{2,1,0:T(8,128)(2,1)S(1)}, u32[]{:S(2)}, u32[]{:S(2)}) %all-to-all-start) | async-done | bytes 655392 | tf_op jit(solution)/shard_map/all_to_all | solution.py:264
  32.1 0.1 add.152
  32.3 0.1 reshape.101.posq.posq_ref
  32.5 0.2 select_reduce_fusion.ordk
  32.7 6.5 %stats_own.1 = (f32[3,2560]{1,0:T(4,128)S(1)}, bf16[2560,128]{1,0:T(8,128)(2,1)S(1)}, bf16[2560,128]{1,0:T(8,128)(2,1)S(1)}) custom-call(s32[32]{0:T(128)S(1)} %select_reduce_fusion.ordk, s32[1,2560]{1,0:T(1,128)S(1)} %reshape.101.posq.posq_ref, bf16[160,512]{1,0:T(8,128)(2,1)S(1)} %convolution_convert_fusion.q0, bf16[160,512]{1,0:T(8,128)(2,1)} %collective-permute-done.q1, ...), custom_call_target="tpu_custom_call" | custom-call | flops 1677721600 | bytes 4194304 | tf_op jit(solution)/shard_map/stats_own/pallas_call | solution.py:221
  39.2 7.5 %stats_other.1 = (f32[3,2560]{1,0:T(4,128)S(1)}, bf16[2,160,512]{2,1,0:T(8,128)(2,1)S(1)}, bf16[2,160,512]{2,1,0:T(8,128)(2,1)S(1)}, bf16[2,160,512]{2,1,0:T(8,128)(2,1)S(1)}, bf16[2,160,512]{2,1,0:T(8,128)(2,1)S(1)}) custom-call(s32[32]{0:T(128)S(1)} %select_reduce_fusion.ordk, s32[2]{0:T(128)S(1)} %pad_add_fusion.place, ...), custom_call_target="tpu_custom_call" | custom-call | flops 1677721600 | bytes 4194304 | tf_op jit(solution)/shard_map/stats_other/pallas_call | solution.py:221
  46.7 3.3 %collective-permute-start.10 = (f32[3,2560]{1,0:T(4,128)S(1)}, f32[3,2560]{1,0:T(4,128)S(1)}, u32[]{:S(2)}, u32[]{:S(2)}) collective-permute-start(f32[3,2560]{1,0:T(4,128)S(1)} %get-tuple-element.56.s0), channel_id=1, source_target_pairs={{0,48},{16,0},{32,16},{48,32},{1,49},{17,1},{33,17},{49,33},{2,50}... | collective-permute-start | bytes 92168 | tf_op jit(solution)/shard_map/ppermute | solution.py:238
  50.0 0.9 collective-permute-start.8
  50.9 2.5 %collective-permute-start.11 = (bf16[2,160,512]{2,1,0:T(8,128)(2,1)S(1)}, bf16[2,160,512]{2,1,0:T(8,128)(2,1)S(1)}, u32[]{:S(2)}, u32[]{:S(2)}) collective-permute-start(bf16[2,160,512]{2,1,0:T(8,128)(2,1)S(1)} %get-tuple-element.62), channel_id=1, source_target_pairs={{0,16},{16,32},{32,48},{48,0},{1,17},{17,33},{33,49},{49,1},{2,18}... | collective-permute-start | bytes 983048 | tf_op jit(solution)/shard_map/ppermute | solution.py:238
  53.5 1.2 collective-permute-start.12
  54.7 1.5 %collective-permute-start.13 = (bf16[2,160,512]{2,1,0:T(8,128)(2,1)S(1)}, bf16[2,160,512]{2,1,0:T(8,128)(2,1)S(1)}, u32[]{:S(2)}, u32[]{:S(2)}) collective-permute-start(bf16[2,160,512]{2,1,0:T(8,128)(2,1)S(1)} %get-tuple-element.64), channel_id=1, source_target_pairs={{0,48},{16,0},{32,16},{48,32},{1,49},{17,1},{33,17},{49,33},{2,50}... | collective-permute-start | bytes 983048 | tf_op jit(solution)/shard_map/ppermute | solution.py:238
  56.2 20.4 %grads.1 = (f32[160,512]{1,0:T(8,128)S(1)}, bf16[160,512]{1,0:T(8,128)(2,1)S(1)}, bf16[160,512]{1,0:T(8,128)(2,1)S(1)}, bf16[160,512]{1,0:T(8,128)(2,1)S(1)}, f3...) custom-call(s32[32]{0:T(128)S(1)} %select_reduce_fusion.ordk, s32[1,2560]{1,0:T(1,128)S(1)} %reshape.101.posq.posq_ref, ...), custom_call_target="tpu_custom_call" | custom-call | flops 8388608000 | bytes 8388608 | tf_op jit(solution)/shard_map/grads/pallas_call | solution.py:221
  76.7 1.5 %collective-permute-start.14 = (bf16[160,512]{1,0:T(8,128)(2,1)S(1)}, bf16[160,512]{1,0:T(8,128)(2,1)}, u32[]{:S(2)}, u32[]{:S(2)}) collective-permute-start(bf16[160,512]{1,0:T(8,128)(2,1)S(1)} %get-tuple-element.70), channel_id=1, source_target_pairs={{0,48},{16,0},{32,16},{48,32},{1,49},{17,1},{33,17},{49,33},{2,50}... | collective-permute-start | bytes 491528 | tf_op jit(solution)/shard_map/ppermute | solution.py:238
  78.2 1.2 collective-permute-start.15
  79.4 0.6 collective-permute-start.16
  80.0 1.0 add_convert_fusion
  81.0 3.9 %all-to-all-start.1 = ((bf16[8,160,256]{2,1,0:T(8,128)(2,1)}), bf16[8,160,256]{2,1,0:T(8,128)(2,1)S(1)}, u32[]{:S(2)}, u32[]{:S(2)}) async-start(bf16[8,160,256]{2,1,0:T(8,128)(2,1)} %bitcast.8), calls=%async_computation.1 | async-start | bytes 1310720 | tf_op jit(solution)/shard_map/all_to_all | solution.py:310
  84.9 2.0 %collective-permute-done.15 = bf16[160,512]{1,0:T(8,128)(2,1)} collective-permute-done((bf16[160,512]{1,0:T(8,128)(2,1)S(1)}, bf16[160,512]{1,0:T(8,128)(2,1)}, u32[]{:S(2)}, u32[]{:S(2)}) %collective-permute-start.15) | collective-permute-done | bytes 163872 | tf_op jit(solution)/shard_map/ppermute | solution.py:238
  86.9 2.7 %collective-permute-done.16 = bf16[160,512]{1,0:T(8,128)(2,1)} collective-permute-done((bf16[160,512]{1,0:T(8,128)(2,1)S(1)}, bf16[160,512]{1,0:T(8,128)(2,1)}, u32[]{:S(2)}, u32[]{:S(2)}) %collective-permute-start.16) | collective-permute-done | bytes 163872 | tf_op jit(solution)/shard_map/ppermute | solution.py:238
  89.6 1.2 add_convert_fusion.1.q0
  90.7 0.7 collective-permute-start.19
  91.4 1.2 collective-permute-start.18
  92.6 0.8 collective-permute-start.17
  93.4 3.4 %all-to-all-done.1 = bf16[8,160,256]{2,1,0:T(8,128)(2,1)S(1)} async-done(((bf16[8,160,256]{2,1,0:T(8,128)(2,1)}), bf16[8,160,256]{2,1,0:T(8,128)(2,1)S(1)}, u32[]{:S(2)}, u32[]{:S(2)}) %all-to-all-start.1) | async-done | bytes 655392 | tf_op jit(solution)/shard_map/all_to_all | solution.py:310
  96.8 0.1 reduce_sum.32.k0
  96.9 2.9 %collective-permute-start.23 = (bf16[160,256]{1,0:T(8,128)(2,1)S(1)}, bf16[160,256]{1,0:T(8,128)(2,1)S(1)}, u32[]{:S(2)}, u32[]{:S(2)}) collective-permute-start(bf16[160,256]{1,0:T(8,128)(2,1)S(1)} %reduce_sum.32.k0), channel_id=1, source_target_pairs={{0,48},{16,0},{32,16},{48,32},{1,49},{17,1},{33,17},{49,33},{2,50}... | collective-permute-start | bytes 245768 | tf_op jit(solution)/shard_map/ppermute | solution.py:238
  99.8 0.9 collective-permute-start.22
  100.7 0.8 collective-permute-start.21
  101.5 0.5 collective-permute-done.17.q1
  102.0 1.2 collective-permute-done.23.k3
  103.2 2.6 %collective-permute-done.22.k2 = bf16[160,256]{1,0:T(8,128)(2,1)S(1)} collective-permute-done((bf16[160,256]{1,0:T(8,128)(2,1)S(1)}, bf16[160,256]{1,0:T(8,128)(2,1)S(1)}, u32[]{:S(2)}, u32[]{:S(2)}) %collective-permute-start.22) | collective-permute-done | bytes 81952 | tf_op jit(solution)/shard_map/ppermute | solution.py:238
  105.8 0.8 collective-permute-done.21.k1
  106.7 0.1 pad_maximum_fusion
  107.0 2.6 %collective-permute-done.24.grads = bf16[4,160,768]{2,1,0:T(8,128)(2,1)S(1)} collective-permute-done((bf16[4,160,768]{2,1,0:T(8,128)(2,1)S(1)}, bf16[4,160,768]{2,1,0:T(8,128)(2,1)S(1)}, u32[]{:S(2)}, u32[]{:S(2)}) %collective-permute-start.24) | collective-permute-done | bytes 983072 | tf_op jit(solution)/shard_map/ppermute | solution.py:238
  109.5 1.2 weights.1
  110.8 18.2 %all_to_all.15.parts = bf16[16,32,768]{2,1,0:T(8,128)(2,1)S(1)} all-to-all(bf16[16,32,768]{2,1,0:T(8,128)(2,1)S(1)} %weights.1), channel_id=1, replica_groups=mesh['dp'=2,'outer'=4,'x'=4,'yh'=2,'core'=2] {'dp','x','yh'}, dimensions={0} | all-to-all | bytes 1572864 | tf_op jit(solution)/shard_map/all_to_all | solution.py:326
  129.0 0.7 last_sum.1
  (63 shorter events, 0.9 us)
Async XLA Ops:
  0.6 11.1 %copy-start = (bf16[4096,128]{1,0:T(8,128)(2,1)S(1)}, bf16[4096,128]{1,0:T(8,128)(2,1)}, u32[]{:S(2)}) copy-start(bf16[4096,128]{1,0:T(8,128)(2,1)} %param.14) | copy-start | bytes 3145732
  0.6 11.1 %copy-start.1 = (bf16[1,160,4096]{2,1,0:T(8,128)(2,1)S(1)}, bf16[1,160,4096]{2,1,0:T(8,128)(2,1)}, u32[]{:S(2)}) copy-start(bf16[1,160,4096]{2,1,0:T(8,128)(2,1)} %param.11) | copy-start | bytes 3932164
  0.7 7.8 %copy-start.6 = (bf16[1,160,512]{2,1,0:T(8,128)(2,1)S(1)}, bf16[1,160,512]{2,1,0:T(8,128)(2,1)}, u32[]{:S(2)}) copy-start(bf16[1,160,512]{2,1,0:T(8,128)(2,1)} %param.16) | copy-start | bytes 491524
  4.3 8.0 %copy-start.7 = (bf16[4096,128]{1,0:T(8,128)(2,1)S(1)}, bf16[4096,128]{1,0:T(8,128)(2,1)}, u32[]{:S(2)}) copy-start(bf16[4096,128]{1,0:T(8,128)(2,1)} %param.15) | copy-start | bytes 3145732
  4.3 23.7 %collective-permute-start.2 = (bf16[160,512]{1,0:T(8,128)(2,1)S(1)}, bf16[160,512]{1,0:T(8,128)(2,1)S(1)}, u32[]{:S(2)}, u32[]{:S(2)}) collective-permute-start(bf16[160,512]{1,0:T(8,128)(2,1)S(1)} %convolution_convert_fusion.q0), channel_id=1, source_target_pairs={{0,48},{16,0},{32,16},{48,32},{1,49},{17,1},{33,17},{49,33},{2,50}... | collective-permute-start | bytes 491528 | tf_op jit(solution)/shard_map/ppermute | solution.py:238
  8.5 12.3 %collective-permute-start = (bf16[160,512]{1,0:T(8,128)(2,1)S(1)}, bf16[160,512]{1,0:T(8,128)(2,1)}, u32[]{:S(2)}, u32[]{:S(2)}) collective-permute-start(bf16[160,512]{1,0:T(8,128)(2,1)S(1)} %convolution_convert_fusion.q0), channel_id=1, source_target_pairs={{0,16},{16,32},{32,48},{48,0},{1,17},{17,33},{33,49},{49,1},{2,18}... | collective-permute-start | bytes 491528 | tf_op jit(solution)/shard_map/ppermute | solution.py:238
  8.5 12.3 %collective-permute-start.4 = (bf16[160,512]{1,0:T(8,128)(2,1)S(1)}, bf16[160,512]{1,0:T(8,128)(2,1)}, u32[]{:S(2)}, u32[]{:S(2)}) collective-permute-start(bf16[160,512]{1,0:T(8,128)(2,1)S(1)} %bitcast.33), channel_id=1, source_target_pairs={{0,48},{16,0},{32,16},{48,32},{1,49},{17,1},{33,17},{49,33},{2,50}... | collective-permute-start | bytes 491528 | tf_op jit(solution)/shard_map/ppermute | solution.py:238
  11.7 16.3 %collective-permute-start.3 = (bf16[160,512]{1,0:T(8,128)(2,1)S(1)}, bf16[160,512]{1,0:T(8,128)(2,1)}, u32[]{:S(2)}, u32[]{:S(2)}) collective-permute-start(bf16[160,512]{1,0:T(8,128)(2,1)S(1)} %bitcast.34), channel_id=1, source_target_pairs={{0,16},{16,32},{32,48},{48,0},{1,17},{17,33},{33,49},{49,1},{2,18}... | collective-permute-start | bytes 491528 | tf_op jit(solution)/shard_map/ppermute | solution.py:238
  12.7 7.9 %copy-start.11 = (s32[1,8,1]{1,2,0:T(1,128)S(1)}, s32[1,8,1]{1,2,0:T(1,128)}, u32[]{:S(2)}) copy-start(s32[1,8,1]{1,2,0:T(1,128)} %constant.67.clone) | copy-start | bytes 100
  12.8 7.9 %copy-start.10 = (s32[2,1,1]{0,2,1:T(1,128)S(1)}, s32[2,1,1]{0,2,1:T(1,128)}, u32[]{:S(2)}) copy-start(s32[2,1,1]{0,2,1:T(1,128)} %constant.68.clone) | copy-start | bytes 28
  12.8 14.8 %copy-start.8 = (s32[4]{0:T(128)S(1)}, s32[4]{0:T(128)}, u32[]{:S(2)}) copy-start(s32[4]{0:T(128)} %constant.76) | copy-start | bytes 52
  12.8 15.0 %copy-start.9 = (s32[1,128]{1,0:T(1,128)S(1)}, s32[1,128]{1,0:T(1,128)}, u32[]{:S(2)}) copy-start(s32[1,128]{1,0:T(1,128)} %param.12) | copy-start | bytes 1540
  13.7 18.3 %all-to-all-start = ((bf16[8,160,256]{2,1,0:T(8,128)(2,1)}), bf16[8,160,256]{2,1,0:T(8,128)(2,1)S(1)}, u32[]{:S(2)}, u32[]{:S(2)}) async-start(bf16[8,160,256]{2,1,0:T(8,128)(2,1)} %broadcast_in_dim.47), calls=%async_computation | async-start | bytes 1310720 | tf_op jit(solution)/shard_map/all_to_all | solution.py:264
  20.7 6.9 %collective-permute-start.1 = (bf16[160,512]{1,0:T(8,128)(2,1)}, bf16[160,512]{1,0:T(8,128)(2,1)}, u32[]{:S(2)}, u32[]{:S(2)}) collective-permute-start(bf16[160,512]{1,0:T(8,128)(2,1)} %collective-permute-done.q1), channel_id=1, source_target_pairs={{0,16},{16,32},{32,48},{48,0},{1,17},{17,33},{33,49},{49,1},{2,18}... | collective-permute-start | bytes 491528 | tf_op jit(solution)/shard_map/ppermute | solution.py:238
  20.8 6.8 %collective-permute-start.5 = (bf16[160,512]{1,0:T(8,128)(2,1)}, bf16[160,512]{1,0:T(8,128)(2,1)}, u32[]{:S(2)}, u32[]{:S(2)}) collective-permute-start(bf16[160,512]{1,0:T(8,128)(2,1)} %collective-permute-done.4.g3), channel_id=1, source_target_pairs={{0,48},{16,0},{32,16},{48,32},{1,49},{17,1},{33,17},{49,33},{2,50}... | collective-permute-start | bytes 491528 | tf_op jit(solution)/shard_map/ppermute | solution.py:238
  27.6 11.6 %collective-permute-start.7 = (bf16[160,4096]{1,0:T(8,128)(2,1)S(1)}, bf16[160,4096]{1,0:T(8,128)(2,1)}, u32[]{:S(2)}, u32[]{:S(2)}) collective-permute-start(bf16[160,4096]{1,0:T(8,128)(2,1)S(1)} %bitcast.28), channel_id=1, source_target_pairs={{0,1},{1,0},{2,3},{3,2},{4,5},{5,4},{6,7},{7,6},{8,9},{9,8},{10,11... | collective-permute-start | bytes 3932168 | tf_op jit(solution)/shard_map/ppermute | solution.py:238
  32.0 7.2 %collective-permute-start.6 = (bf16[1280,256]{1,0:T(8,128)(2,1)S(1)}, bf16[1280,256]{1,0:T(8,128)(2,1)}, u32[]{:S(2)}, u32[]{:S(2)}) collective-permute-start(bf16[1280,256]{1,0:T(8,128)(2,1)S(1)} %bitcast.30), channel_id=1, source_target_pairs={{0,1},{1,0},{2,3},{3,2},{4,5},{5,4},{6,7},{7,6},{8,9},{9,8},{10,11... | collective-permute-start | bytes 1966088 | tf_op jit(solution)/shard_map/ppermute | solution.py:238
  46.7 8.0 %collective-permute-start.10 = (f32[3,2560]{1,0:T(4,128)S(1)}, f32[3,2560]{1,0:T(4,128)S(1)}, u32[]{:S(2)}, u32[]{:S(2)}) collective-permute-start(f32[3,2560]{1,0:T(4,128)S(1)} %get-tuple-element.56.s0), channel_id=1, source_target_pairs={{0,48},{16,0},{32,16},{48,32},{1,49},{17,1},{33,17},{49,33},{2,50}... | collective-permute-start | bytes 92168 | tf_op jit(solution)/shard_map/ppermute | solution.py:238
  50.0 6.2 %collective-permute-start.9 = (f32[3,2560]{1,0:T(4,128)S(1)}, f32[3,2560]{1,0:T(4,128)S(1)}, u32[]{:S(2)}, u32[]{:S(2)}) collective-permute-start(f32[3,2560]{1,0:T(4,128)S(1)} %get-tuple-element.56.s0), channel_id=1, source_target_pairs={{0,32},{16,48},{32,0},{48,16},{1,33},{17,49},{33,1},{49,17},{2,34}... | collective-permute-start | bytes 92168 | tf_op jit(solution)/shard_map/ppermute | solution.py:238
  50.0 6.2 %collective-permute-start.8 = (f32[3,2560]{1,0:T(4,128)S(1)}, f32[3,2560]{1,0:T(4,128)S(1)}, u32[]{:S(2)}, u32[]{:S(2)}) collective-permute-start(f32[3,2560]{1,0:T(4,128)S(1)} %get-tuple-element.56.s0), channel_id=1, source_target_pairs={{0,16},{16,32},{32,48},{48,0},{1,17},{17,33},{33,49},{49,1},{2,18}... | collective-permute-start | bytes 92168 | tf_op jit(solution)/shard_map/ppermute | solution.py:238
  50.9 25.7 %collective-permute-start.11 = (bf16[2,160,512]{2,1,0:T(8,128)(2,1)S(1)}, bf16[2,160,512]{2,1,0:T(8,128)(2,1)S(1)}, u32[]{:S(2)}, u32[]{:S(2)}) collective-permute-start(bf16[2,160,512]{2,1,0:T(8,128)(2,1)S(1)} %get-tuple-element.62), channel_id=1, source_target_pairs={{0,16},{16,32},{32,48},{48,0},{1,17},{17,33},{33,49},{49,1},{2,18}... | collective-permute-start | bytes 983048 | tf_op jit(solution)/shard_map/ppermute | solution.py:238
  53.5 23.1 %collective-permute-start.12 = (bf16[2,160,512]{2,1,0:T(8,128)(2,1)S(1)}, bf16[2,160,512]{2,1,0:T(8,128)(2,1)S(1)}, u32[]{:S(2)}, u32[]{:S(2)}) collective-permute-start(bf16[2,160,512]{2,1,0:T(8,128)(2,1)S(1)} %get-tuple-element.63), channel_id=1, source_target_pairs={{0,32},{16,48},{32,0},{48,16},{1,33},{17,49},{33,1},{49,17},{2,34}... | collective-permute-start | bytes 983048 | tf_op jit(solution)/shard_map/ppermute | solution.py:238
  54.7 21.9 %collective-permute-start.13 = (bf16[2,160,512]{2,1,0:T(8,128)(2,1)S(1)}, bf16[2,160,512]{2,1,0:T(8,128)(2,1)S(1)}, u32[]{:S(2)}, u32[]{:S(2)}) collective-permute-start(bf16[2,160,512]{2,1,0:T(8,128)(2,1)S(1)} %get-tuple-element.64), channel_id=1, source_target_pairs={{0,48},{16,0},{32,16},{48,32},{1,49},{17,1},{33,17},{49,33},{2,50}... | collective-permute-start | bytes 983048 | tf_op jit(solution)/shard_map/ppermute | solution.py:238
  76.6 4.4 %copy-start.2 = (bf16[2,160,512]{2,1,0:T(8,128)(2,1)}, bf16[2,160,512]{2,1,0:T(8,128)(2,1)S(1)}, u32[]{:S(2)}) copy-start(bf16[2,160,512]{2,1,0:T(8,128)(2,1)S(1)} %collective-permute-done.12.x2) | copy-start | bytes 983044
  76.6 4.4 %copy-start.4 = (bf16[2,160,512]{2,1,0:T(8,128)(2,1)}, bf16[2,160,512]{2,1,0:T(8,128)(2,1)S(1)}, u32[]{:S(2)}) copy-start(bf16[2,160,512]{2,1,0:T(8,128)(2,1)S(1)} %collective-permute-done.13.x3) | copy-start | bytes 983044
  76.6 3.3 %collective-permute-start.20 = (bf16[1280,256]{1,0:T(8,128)(2,1)S(1)}, bf16[1280,256]{1,0:T(8,128)(2,1)S(1)}, u32[]{:S(2)}, u32[]{:S(2)}) collective-permute-start(bf16[1280,256]{1,0:T(8,128)(2,1)S(1)} %get-tuple-element.74), channel_id=1, source_target_pairs={{0,1},{1,0},{2,3},{3,2},{4,5},{5,4},{6,7},{7,6},{8,9},{9,8},{10,11... | collective-permute-start | bytes 1966088 | tf_op jit(solution)/shard_map/ppermute | solution.py:238
  76.7 8.2 %collective-permute-start.14 = (bf16[160,512]{1,0:T(8,128)(2,1)S(1)}, bf16[160,512]{1,0:T(8,128)(2,1)}, u32[]{:S(2)}, u32[]{:S(2)}) collective-permute-start(bf16[160,512]{1,0:T(8,128)(2,1)S(1)} %get-tuple-element.70), channel_id=1, source_target_pairs={{0,48},{16,0},{32,16},{48,32},{1,49},{17,1},{33,17},{49,33},{2,50}... | collective-permute-start | bytes 491528 | tf_op jit(solution)/shard_map/ppermute | solution.py:238
  78.2 8.7 %collective-permute-start.15 = (bf16[160,512]{1,0:T(8,128)(2,1)S(1)}, bf16[160,512]{1,0:T(8,128)(2,1)}, u32[]{:S(2)}, u32[]{:S(2)}) collective-permute-start(bf16[160,512]{1,0:T(8,128)(2,1)S(1)} %get-tuple-element.71), channel_id=1, source_target_pairs={{0,32},{16,48},{32,0},{48,16},{1,33},{17,49},{33,1},{49,17},{2,34}... | collective-permute-start | bytes 491528 | tf_op jit(solution)/shard_map/ppermute | solution.py:238
  79.4 10.2 %collective-permute-start.16 = (bf16[160,512]{1,0:T(8,128)(2,1)S(1)}, bf16[160,512]{1,0:T(8,128)(2,1)}, u32[]{:S(2)}, u32[]{:S(2)}) collective-permute-start(bf16[160,512]{1,0:T(8,128)(2,1)S(1)} %get-tuple-element.72), channel_id=1, source_target_pairs={{0,16},{16,32},{32,48},{48,0},{1,17},{17,33},{33,49},{49,1},{2,18}... | collective-permute-start | bytes 491528 | tf_op jit(solution)/shard_map/ppermute | solution.py:238
  81.0 15.8 %all-to-all-start.1 = ((bf16[8,160,256]{2,1,0:T(8,128)(2,1)}), bf16[8,160,256]{2,1,0:T(8,128)(2,1)S(1)}, u32[]{:S(2)}, u32[]{:S(2)}) async-start(bf16[8,160,256]{2,1,0:T(8,128)(2,1)} %bitcast.8), calls=%async_computation.1 | async-start | bytes 1310720 | tf_op jit(solution)/shard_map/all_to_all | solution.py:310
  90.7 10.0 %collective-permute-start.19 = (bf16[160,512]{1,0:T(8,128)(2,1)S(1)}, bf16[160,512]{1,0:T(8,128)(2,1)S(1)}, u32[]{:S(2)}, u32[]{:S(2)}) collective-permute-start(bf16[160,512]{1,0:T(8,128)(2,1)S(1)} %add_convert_fusion.1.q0), channel_id=1, source_target_pairs={{0,48},{16,0},{32,16},{48,32},{1,49},{17,1},{33,17},{49,33},{2,50}... | collective-permute-start | bytes 491528 | tf_op jit(solution)/shard_map/ppermute | solution.py:238
  91.4 10.1 %collective-permute-start.18 = (bf16[160,512]{1,0:T(8,128)(2,1)S(1)}, bf16[160,512]{1,0:T(8,128)(2,1)S(1)}, u32[]{:S(2)}, u32[]{:S(2)}) collective-permute-start(bf16[160,512]{1,0:T(8,128)(2,1)S(1)} %add_convert_fusion.1.q0), channel_id=1, source_target_pairs={{0,32},{16,48},{32,0},{48,16},{1,33},{17,49},{33,1},{49,17},{2,34}... | collective-permute-start | bytes 491528 | tf_op jit(solution)/shard_map/ppermute | solution.py:238
  92.6 9.4 %collective-permute-start.17 = (bf16[160,512]{1,0:T(8,128)(2,1)S(1)}, bf16[160,512]{1,0:T(8,128)(2,1)S(1)}, u32[]{:S(2)}, u32[]{:S(2)}) collective-permute-start(bf16[160,512]{1,0:T(8,128)(2,1)S(1)} %add_convert_fusion.1.q0), channel_id=1, source_target_pairs={{0,16},{16,32},{32,48},{48,0},{1,17},{17,33},{33,49},{49,1},{2,18}... | collective-permute-start | bytes 491528 | tf_op jit(solution)/shard_map/ppermute | solution.py:238
  96.9 6.3 %collective-permute-start.23 = (bf16[160,256]{1,0:T(8,128)(2,1)S(1)}, bf16[160,256]{1,0:T(8,128)(2,1)S(1)}, u32[]{:S(2)}, u32[]{:S(2)}) collective-permute-start(bf16[160,256]{1,0:T(8,128)(2,1)S(1)} %reduce_sum.32.k0), channel_id=1, source_target_pairs={{0,48},{16,0},{32,16},{48,32},{1,49},{17,1},{33,17},{49,33},{2,50}... | collective-permute-start | bytes 245768 | tf_op jit(solution)/shard_map/ppermute | solution.py:238
  99.8 6.0 %collective-permute-start.22 = (bf16[160,256]{1,0:T(8,128)(2,1)S(1)}, bf16[160,256]{1,0:T(8,128)(2,1)S(1)}, u32[]{:S(2)}, u32[]{:S(2)}) collective-permute-start(bf16[160,256]{1,0:T(8,128)(2,1)S(1)} %reduce_sum.32.k0), channel_id=1, source_target_pairs={{0,32},{16,48},{32,0},{48,16},{1,33},{17,49},{33,1},{49,17},{2,34}... | collective-permute-start | bytes 245768 | tf_op jit(solution)/shard_map/ppermute | solution.py:238
  100.7 6.0 %collective-permute-start.21 = (bf16[160,256]{1,0:T(8,128)(2,1)S(1)}, bf16[160,256]{1,0:T(8,128)(2,1)S(1)}, u32[]{:S(2)}, u32[]{:S(2)}) collective-permute-start(bf16[160,256]{1,0:T(8,128)(2,1)S(1)} %reduce_sum.32.k0), channel_id=1, source_target_pairs={{0,16},{16,32},{32,48},{48,0},{1,17},{17,33},{33,49},{49,1},{2,18}... | collective-permute-start | bytes 245768 | tf_op jit(solution)/shard_map/ppermute | solution.py:238
  106.7 2.8 %copy-start.3 = (bf16[2,160,512]{2,1,0:T(8,128)(2,1)S(1)}, bf16[2,160,512]{2,1,0:T(8,128)(2,1)}, u32[]{:S(2)}) copy-start(bf16[2,160,512]{2,1,0:T(8,128)(2,1)} %copy-done.2) | copy-start | bytes 983044
  106.7 2.8 %copy-start.5 = (bf16[2,160,512]{2,1,0:T(8,128)(2,1)S(1)}, bf16[2,160,512]{2,1,0:T(8,128)(2,1)}, u32[]{:S(2)}) copy-start(bf16[2,160,512]{2,1,0:T(8,128)(2,1)} %copy-done.4) | copy-start | bytes 983044
  106.9 2.6 %collective-permute-start.24 = (bf16[4,160,768]{2,1,0:T(8,128)(2,1)S(1)}, bf16[4,160,768]{2,1,0:T(8,128)(2,1)S(1)}, u32[]{:S(2)}, u32[]{:S(2)}) collective-permute-start(bf16[4,160,768]{2,1,0:T(8,128)(2,1)S(1)} %pad_maximum_fusion), channel_id=1, source_target_pairs={{0,1},{1,0},{2,3},{3,2},{4,5},{5,4},{6,7},{7,6},{8,9},{9,8},{10,11... | collective-permute-start | bytes 2949128 | tf_op jit(solution)/shard_map/ppermute | solution.py:238
